TPU v7x, 128 devices: a whole 4x4x4 slice. The times are simulated.
128 devices in a mesh: seq: 32 (over y, z, core), head: 4 (over x).
Axes of the slice: x: 4, y: 4, z: 4, core: 2. Of those that a mesh axis runs over, the one named last changes fastest.
Arguments:
- hidden_in: bfloat16 [8192, 2048], P('seq'), may hold values from -6 to 6
- attn_gain: float32 [2048], replicated, may hold values from 0.1 to 1.9
- w_qkv: bfloat16 [2048, 3, 2048], P(None, None, 'head'), may hold values from -0.125 to 0.125
- out_gain: float32 [2048], P('head'), may hold values from 0.1 to 1.9
- w_out: bfloat16 [2048, 2048], P('head'), may hold values from -0.125 to 0.125
- moe_gain: float32 [2048], replicated, may hold values from 0.1 to 1.9
- routes: int32 [8192, 8], P(('seq', 'head')), may hold values from 0 to 63, all different within a row; in each aligned block of 64 rows (0 to 63, 64 to 127, ...) at most 9 rows name the same one
- gate_weights: float32 [8192, 8], P(('seq', 'head')), may hold values from 0.1 to 0.6
- w_gate_up: bfloat16 [64, 2, 2048, 1024], P('seq', None, None, 'head'), may hold values from -0.125 to 0.125
- w_down: bfloat16 [64, 1024, 2048], P('seq', 'head'), may hold values from -0.1875 to 0.1875
Outputs:
- layer_out: bfloat16 [8192, 2048], P(('seq', 'head'))
Inputs may be any that keep to these rules, and one draw needn't show every extreme that they name: `routes`: each row names 8 different experts; within each aligned block of 64 rows (the rows of one device) no expert is named more than 9 times, a bound that some block reaches.
All inputs are finite; a program needn't handle non-finite values.
Results may differ from a plain program's by a relative error of at most 0.015.
Values may be sent and summed in bfloat16 or wider, within the bound.
No kernel may reach another device: no remote copies, remote signals or barrier semaphores. Data moves between devices by JAX's collectives and lax.ppermute only.
A program may use at most 128 MiB of HBM per device.

v0:
```python
import jax
import jax.numpy as jnp
from jax import lax
from jax.experimental import pallas as pl
from jax.experimental.pallas import tpu as pltpu
from jax.sharding import PartitionSpec as P

D = 2048
DH = 128
HEADS = 4
WIDE = HEADS * DH
TOP = 8
CAP = 9
ROWS = 64
TOK = 256
MAIN = 512
SLOTS = 576
PACKED = D + 256
EPSILON = 1e-06
BF = jnp.bfloat16
F32 = jnp.float32


VMEM = pl.BlockSpec(memory_space=pltpu.VMEM)
SMEM = pl.BlockSpec(memory_space=pltpu.SMEM)
ANY = pl.BlockSpec(memory_space=pl.ANY)


def out(shape, dtype):
    return jax.ShapeDtypeStruct(shape, dtype)


def call(kernel, ins, outs, scratch=()):
    return pl.pallas_call(
        kernel,
        in_specs=ins,
        out_specs=[SMEM if o.dtype == jnp.int32 else VMEM for o in outs],
        out_shape=outs,
        scratch_shapes=list(scratch),
        compiler_params=pltpu.CompilerParams(vmem_limit_bytes=56 << 20),
    )


def rms_norm(values, gain):
    mean_square = jnp.mean(values * values, axis=-1, keepdims=True)
    return values * lax.rsqrt(mean_square + EPSILON) * gain


def dot(first, second):
    return jnp.dot(first, second, preferred_element_type=F32)


def dot_rows(first, second):
    return lax.dot_general(first, second, (((0,), (0,)), ((), ())), preferred_element_type=F32)


def dot_cols(first, second):
    return lax.dot_general(first, second, (((1,), (1,)), ((), ())), preferred_element_type=F32)


def of_head(h):
    return slice(h * DH, (h + 1) * DH)


def front_kernel(x_ref, gain_ref, wk_ref, wv_ref, normed_ref, k_ref, v_ref, state_ref, send_ref, zero_ref, wk, wv, sems):
    zero_ref[0] = 0
    copy_k = pltpu.make_async_copy(wk_ref, wk, sems.at[0])
    copy_v = pltpu.make_async_copy(wv_ref, wv, sems.at[1])
    copy_k.start()
    copy_v.start()
    normed = rms_norm(x_ref[...].astype(F32), gain_ref[...]).astype(BF)
    normed_ref[...] = normed
    copy_k.wait()
    key = dot(normed, wk[...]).astype(BF)
    k_ref[...] = key
    copy_v.wait()
    value = dot(normed, wv[...]).astype(BF)
    v_ref[...] = value
    for h in range(HEADS):
        state = dot_rows(key[:, of_head(h)], value[:, of_head(h)])
        state_ref[h] = state
        send_ref[h] = state.astype(BF)


def local_kernel(normed_ref, wq_ref, k_ref, v_ref, q_ref, local_ref):
    query = dot(normed_ref[...], wq_ref[...]).astype(BF)
    q_ref[...] = query
    row = lax.broadcasted_iota(jnp.int32, (TOK, TOK), 0)
    causal = lax.broadcasted_iota(jnp.int32, (TOK, TOK), 1) <= row
    for h in range(HEADS):
        scores = dot_cols(query[:, of_head(h)], k_ref[:, of_head(h)])
        scores = jnp.where(causal, scores, 0.0).astype(BF)
        local_ref[:, of_head(h)] = dot(scores, v_ref[:, of_head(h)])


def attend_kernel(
    place_ref, prefix_ref, g1, g2, g3, q_ref, local_ref, gain_ref, w_ref,
    own_ref, s1, s2, s3, mixed_ref, turned_ref,
):
    y = place_ref[0]
    head = place_ref[1]
    for h in range(HEADS):
        earlier = prefix_ref[h]
        for k, got in ((1, g1), (2, g2), (3, g3)):
            earlier = earlier + jnp.where(y >= k, got[h].astype(F32), 0.0)
        high = earlier.astype(BF)
        low = (earlier - high.astype(F32)).astype(BF)
        query = q_ref[:, of_head(h)]
        attended = local_ref[:, of_head(h)] + (dot(query, high) + dot(query, low))
        mixed_ref[:, of_head(h)] = rms_norm(attended, gain_ref[:, of_head(h)]).astype(BF)
    for k in range(4):
        start = pl.multiple_of(((head - k) % 4) * ROWS, ROWS)
        turned_ref[k * ROWS:(k + 1) * ROWS, :] = mixed_ref[pl.ds(start, ROWS), :]
    for n in range(4):
        cols = slice(n * 512, (n + 1) * 512)
        rows = dot(turned_ref[...], w_ref[:, cols])
        own_ref[:, cols] = rows[:ROWS]
        s3[:, cols] = rows[ROWS:2 * ROWS].astype(BF)
        s2[:, cols] = rows[2 * ROWS:3 * ROWS].astype(BF)
        s1[:, cols] = rows[3 * ROWS:].astype(BF)


def routing_kernel(head_ref, t0, t1, t2, t3, place_ref, weight_ref):
    head = head_ref[0]
    tables = jnp.concatenate([t0[...], t1[...], t2[...], t3[...]], axis=0)
    wanted = lax.broadcasted_iota(jnp.int32, (TOK, 16), 1) * 4 + head
    chosen = jnp.zeros((TOK, 16), F32)
    gates = jnp.zeros((TOK, 16), F32)
    for k in range(TOP):
        hit = tables[:, k:k + 1].astype(jnp.int32) == wanted
        chosen = chosen + hit.astype(F32)
        gates = gates + jnp.where(hit, tables[:, TOP + k:TOP + k + 1], 0.0)
    row = lax.broadcasted_iota(jnp.int32, (TOK, TOK), 0)
    col = lax.broadcasted_iota(jnp.int32, (TOK, TOK), 1)
    before = ((row // ROWS == col // ROWS) & (col < row)).astype(F32).astype(BF)
    rank = dot(before, chosen.astype(BF))
    block = (head - lax.broadcasted_iota(jnp.int32, (TOK, 16), 0) // ROWS) & 3
    base = ((block >> 1) * 18 + (block & 1) * CAP).astype(F32)
    slot = jnp.where(chosen > 0, base + rank, -1.0).astype(BF)
    high = gates.astype(BF)
    low = (gates - high.astype(F32)).astype(BF)

    def of_row(shape, axis):
        row = lax.broadcasted_iota(jnp.int32, shape, axis)
        is_main = row < MAIN
        chip = jnp.where(is_main, row >> 5, (row & 31) >> 1)
        core = jnp.where(is_main, (row >> 4) & 1, row & 1)
        within = jnp.where(is_main, row & 15, 16 + ((row - MAIN) >> 5))
        return chip, (core * 18 + within).astype(F32)

    chip, want = of_row((SLOTS, 16), 0)
    spread = (chip == lax.broadcasted_iota(jnp.int32, (SLOTS, 16), 1)).astype(F32).astype(BF)
    place_ref[...] = (dot_cols(spread, slot) == want[:, :1]).astype(F32).astype(BF)
    chip, want = of_row((16, SLOTS), 1)
    spread = (chip == lax.broadcasted_iota(jnp.int32, (16, SLOTS), 0)).astype(F32).astype(BF)
    at_row = dot(slot, spread) == want[:1, :]
    weight_ref[:TOK, :] = jnp.where(at_row, dot(high, spread), 0.0).astype(BF)
    weight_ref[TOK:, :] = jnp.where(at_row, dot(low, spread), 0.0).astype(BF)


def dispatch_kernel(place_ref, t0, t1, t2, t3, out_ref, tokens):
    for k, ref in enumerate((t0, t1, t2, t3)):
        tokens[k * ROWS:(k + 1) * ROWS, :] = ref[...]
    tail = []
    for n in range(4):
        cols = slice(n * 512, (n + 1) * 512)
        rows = dot(place_ref[...], tokens[:, cols])
        out_ref[:, cols] = rows[:MAIN].astype(BF)
        tail.append(rows[MAIN:])
    tail = jnp.concatenate(tail, axis=1)
    for t in range(2):
        piece = tail[t * 32:(t + 1) * 32].reshape(MAIN, 128).astype(BF)
        out_ref[:, D + t * 128:D + (t + 1) * 128] = piece


def expert_kernel(
    keep_ref, x_ref, gu0, gu1, gu2, gu3, gu4, gu5, dn0, dn1, dn2, dn3, dn4, dn5,
    out_ref, rows, ends, gate_up, down, act, tail, sems,
):
    copies = [
        pltpu.make_async_copy(x_ref.at[:, :D], rows.at[:MAIN], sems.at[8]),
        pltpu.make_async_copy(x_ref.at[:, D:], ends, sems.at[9]),
    ]

    def load(q, gu, dn):
        return [
            pltpu.make_async_copy(gu, gate_up.at[q], sems.at[q]),
            pltpu.make_async_copy(dn, down.at[q * 256:(q + 1) * 256], sems.at[4 + q]),
        ]

    copies += load(0, gu0, dn0) + load(1, gu1, dn1)
    for copy in copies:
        copy.start()
    keep = keep_ref[0] == 1

    @pl.when(keep)
    def _():
        for copy in load(2, gu2, dn2) + load(3, gu5, dn5):
            copy.start()

    @pl.when(jnp.logical_not(keep))
    def _():
        for copy in load(2, gu3, dn3) + load(3, gu4, dn4):
            copy.start()

    copies += load(2, gu2, dn2) + load(3, gu4, dn4)
    copies[1].wait()
    for t in range(2):
        piece = ends[:, t * 128:(t + 1) * 128].astype(F32).reshape(32, D)
        rows[MAIN + t * 32:MAIN + (t + 1) * 32, :] = piece.astype(BF)
    copies[0].wait()
    for q in range(4):
        copies[2 + 2 * q].wait()
        gate = dot(rows[...], gate_up[q, 0])
        up = dot(rows[...], gate_up[q, 1])
        act[:, q * 256:(q + 1) * 256] = (jax.nn.silu(gate) * up).astype(BF)
    for q in range(4):
        copies[3 + 2 * q].wait()
    for n in range(4):
        cols = slice(n * 512, (n + 1) * 512)
        result = dot(act[...], down[:, cols])
        out_ref[:, cols] = result[:MAIN].astype(BF)
        tail[:, cols] = result[MAIN:]
    for t in range(2):
        piece = tail[t * 32:(t + 1) * 32, :].reshape(MAIN, 128).astype(BF)
        out_ref[:, D + t * 128:D + (t + 1) * 128] = piece


def combine_kernel(weight_ref, y_ref, own_ref, s1, s2, s3, tail):
    for t in range(2):
        piece = y_ref[:, D + t * 128:D + (t + 1) * 128].astype(F32).reshape(32, D)
        tail[t * 32:(t + 1) * 32, :] = piece.astype(BF)
    for n in range(4):
        cols = slice(n * 512, (n + 1) * 512)
        rows = dot(weight_ref[:, :MAIN], y_ref[:, cols]) + dot(weight_ref[:, MAIN:], tail[:, cols])
        rows = rows[:TOK] + rows[TOK:]
        own_ref[:, cols] = rows[:ROWS]
        s3[:, cols] = rows[ROWS:2 * ROWS].astype(BF)
        s2[:, cols] = rows[2 * ROWS:3 * ROWS].astype(BF)
        s1[:, cols] = rows[3 * ROWS:].astype(BF)


BLOCKS_OUT = [out((ROWS, D), F32)] + [out((ROWS, D), BF)] * 3


def seq_perm(dy, dz, dc):
    return [
        ((y * 4 + z) * 2 + c, (((y + dy) % 4) * 4 + (z + dz) % 4) * 2 + (c ^ dc))
        for y in range(4)
        for z in range(4)
        for c in range(2)
    ]


def head_perm(shift):
    return [(h, (h + shift) % 4) for h in range(4)]


def device_perm(target):
    pairs = []
    for chip in range(16):
        for c in range(2):
            for h in range(4):
                to = target(c, h)
                if to is None:
                    continue
                pairs.append(((chip * 2 + c) * 4 + h, (chip * 2 + to[0]) * 4 + to[1]))
    return pairs


def near_target(c, h):
    chip = 2 * c + 1 - (h & 1)
    return (c, chip) if (chip - 1) % 4 == h else (1 - c, chip)


def far_target(c, h):
    return None if h // 2 == c else (1 - c, (h + 2) % 4)


def keep_target(c, h):
    return (1 - c, h) if h // 2 == c else None


def pass_target(c, h):
    return None if h // 2 == c else (1 - c, h)


def permute_all(arrays, axes, perm):
    return [lax.ppermute(a, axes, perm) for a in arrays]


def pick_kernel(index_ref, gu_ref, dn_ref, gu_out, dn_out, sems):
    index = index_ref[0]
    copies = []
    for half in range(2):
        for part in range(2):
            rows = pl.ds(part * (D // 2), D // 2)
            copies.append((gu_ref.at[index, half, rows], gu_out.at[half, rows]))
        rows = pl.ds(half * 128, 128)
        copies.append((dn_ref.at[index, rows], dn_out.at[rows]))
    copies = [pltpu.make_async_copy(a, b, sems.at[i]) for i, (a, b) in enumerate(copies)]
    for copy in copies:
        copy.start()
    for copy in copies:
        copy.wait()


def pick(w_gate_up, w_down, index):
    return pl.pallas_call(
        pick_kernel,
        in_specs=[SMEM, ANY, ANY],
        out_specs=[VMEM, VMEM],
        out_shape=[out((2, D, 256), BF), out((256, D), BF)],
        scratch_shapes=[pltpu.SemaphoreType.DMA((6,))],
        name="pick",
    )(index.astype(jnp.int32)[None], w_gate_up, w_down)


def exchange(array, step):
    dy, dz = step
    return [lax.ppermute(array, "seq", seq_perm(dy * k, dz * k, 0)) for k in range(1, 4)]


def gather_head(array):
    return [array] + [lax.ppermute(array, "head", head_perm(k)) for k in range(1, 4)]


def scatter_head(blocks):
    total = blocks[0]
    for k in range(1, 4):
        total = total + lax.ppermute(blocks[k], "head", head_perm(k)).astype(F32)
    return total


def on_device(
    hidden_in, attn_gain, w_qkv, out_gain, w_out, moe_gain, routes, gate_weights, w_gate_up, w_down
):
    seq = lax.axis_index("seq")
    head = lax.axis_index("head")
    core = seq % 2
    z = (seq // 2) % 4
    y = seq // 8

    both = ("seq", "head")
    near = permute_all(pick(w_gate_up, w_down, 1 - (head & 1)), both, device_perm(near_target))
    tables = gather_head(jnp.concatenate([routes.astype(F32), gate_weights], axis=1))
    place_rows, weight = call(
        routing_kernel, [SMEM] + [VMEM] * 4, [out((SLOTS, TOK), BF), out((2 * TOK, SLOTS), BF)]
    )(head.astype(jnp.int32)[None], *tables)

    normed, key, value, own_state, send_state, zero = call(
        front_kernel,
        [VMEM, VMEM, ANY, ANY],
        [
            out((TOK, D), BF),
            out((TOK, WIDE), BF),
            out((TOK, WIDE), BF),
            out((HEADS, DH, DH), F32),
            out((HEADS, DH, DH), BF),
            out((1,), jnp.int32),
        ],
        [pltpu.VMEM((D, WIDE), BF), pltpu.VMEM((D, WIDE), BF), pltpu.SemaphoreType.DMA((2,))],
    )(hidden_in, attn_gain[None, :], w_qkv[:, 1], w_qkv[:, 2])
    sibling = lax.ppermute(send_state, "seq", seq_perm(0, 0, 1)).astype(F32)
    odd = (head & 1) + zero[0]
    rest = pick(w_gate_up, w_down, odd)
    far = permute_all(rest, both, device_perm(far_target))
    rest_other = permute_all(rest, both, device_perm(keep_target))
    near_other = permute_all(near, "seq", seq_perm(0, 0, 1))
    far_other = permute_all(far, both, device_perm(pass_target))
    pieces = [near, near_other, rest, rest_other, far, far_other]
    prefix = jnp.where(core == 1, sibling, 0.0)
    total = own_state + sibling
    rows_z = exchange(total.astype(BF), (0, 1))
    for k, got in enumerate(rows_z):
        prefix = prefix + jnp.where(z > k, got.astype(F32), 0.0)
        total = total + got.astype(F32)
    rows_y = exchange(total.astype(BF), (1, 0))

    query, local = call(
        local_kernel, [VMEM] * 4, [out((TOK, WIDE), BF), out((TOK, WIDE), F32)]
    )(normed, w_qkv[:, 0], key, value)
    place = jnp.stack([y, head]).astype(jnp.int32)
    blocks = call(
        attend_kernel,
        [SMEM] + [VMEM] * 8,
        BLOCKS_OUT,
        [pltpu.VMEM((TOK, WIDE), BF), pltpu.VMEM((TOK, WIDE), BF)],
    )(place, prefix, *rows_y, query, local, out_gain[None, :], w_out)
    attn_rows = scatter_head(blocks)
    resid = lax.dynamic_slice_in_dim(hidden_in, head * ROWS, ROWS, 0).astype(F32) + attn_rows
    normed2 = rms_norm(resid, moe_gain).astype(BF)
    tokens = gather_head(normed2)

    sent = call(
        dispatch_kernel, [VMEM] * 5, [out((MAIN, PACKED), BF)], [pltpu.VMEM((TOK, D), BF)]
    )(place_rows, *tokens)[0]
    received = lax.all_to_all(sent.reshape(32, 16, PACKED), "seq", 0, 0, tiled=True)
    keep = (head // 2 == core).astype(jnp.int32)[None]
    results = call(
        expert_kernel,
        [SMEM] + [ANY] * 13,
        [out((MAIN, PACKED), BF)],
        [
            pltpu.VMEM((SLOTS, D), BF),
            pltpu.VMEM((MAIN, 256), BF),
            pltpu.VMEM((4, 2, D, 256), BF),
            pltpu.VMEM((1024, D), BF),
            pltpu.VMEM((SLOTS, 1024), BF),
            pltpu.VMEM((64, D), F32),
            pltpu.SemaphoreType.DMA((10,)),
        ],
    )(keep, received.reshape(MAIN, PACKED), *[p[0] for p in pieces], *[p[1] for p in pieces])[0]
    back = lax.all_to_all(results.reshape(32, 16, PACKED), "seq", 0, 0, tiled=True)
    blocks = call(
        combine_kernel, [VMEM] * 2, BLOCKS_OUT, [pltpu.VMEM((64, D), BF)]
    )(weight, back.reshape(MAIN, PACKED))
    moe_sum = scatter_head(blocks)
    return (resid + moe_sum).astype(BF)


def solution(mesh):
    placed = (
        P("seq", None),
        P(),
        P(None, None, "head"),
        P("head"),
        P("head", None),
        P(),
        P(("seq", "head"), None),
        P(("seq", "head"), None),
        P("seq", None, None, "head"),
        P("seq", "head", None),
    )

    return jax.shard_map(
        on_device, mesh=mesh, in_specs=placed, out_specs=P(("seq", "head"), None), check_vma=False
    )
```

profile of v0, /device:TPU:33, one launch (start us, length us, event | category | flops | bytes accessed | tf_op | source)
XLA Modules:
  0.0 237.9 jit_solution(10540319089884310797)
XLA Ops:
  0.0 5.6 %slice_bitcast_fusion = (bf16[2048,512]{1,0:T(8,128)(2,1)}, bf16[2048,512]{1,0:T(8,128)(2,1)}, bf16[2048,512]{1,0:T(8,128)(2,1)}) fusion(bf16[2048,3,512]{2,0,1:T(8,128)(2,1)} %param.12), kind=kLoop, calls=%fused_computation | loop fusion | bytes 12582912 | tf_op jit(solution)/shard_map/squeeze | solution.py:382
  5.6 5.2 %shard_map.100 = (bf16[256,2048]{1,0:T(8,128)(2,1)}, bf16[256,512]{1,0:T(8,128)(2,1)}, bf16[256,512]{1,0:T(8,128)(2,1)}, f32[4,128,128]{2,1,0:T(8,128)}, bf16[4,128,128]{2,1,0:T(8,128)(2,1)}, /*index=5*/s32[1]{0:T(128)}) custom-call(bf16[256,2048]{1,0:T(8,128)(2,1)} %x_ref.1, f32[1,2048]{1,0:T(1,128)} %bitcast.22, ...), custom_call_target="tpu_custom_call" | custom-call | tf_op jit(solution)/shard_map/pallas_call | solution.py:351
  18.6 3.5 %pick.2 = (bf16[2,2048,256]{2,1,0:T(8,128)(2,1)}, bf16[256,2048]{1,0:T(8,128)(2,1)}) custom-call(s32[1]{0:T(128)} %bitcast.10.index_ref, bf16[2,2,2048,256]{3,2,1,0:T(8,128)(2,1)} %gu_ref.3, bf16[2,256,2048]{2,1,0:T(8,128)(2,1)} %dn_ref.3), custom_call_target="tpu_custom_call" | custom-call | tf_op jit(solution)/shard_map/pick/pallas_call | solution.py:309
  22.1 3.6 %collective-permute-start.16 = (bf16[2,2048,256]{2,1,0:T(8,128)(2,1)}, bf16[2,2048,256]{2,1,0:T(8,128)(2,1)}, u32[]{:S(2)}, u32[]{:S(2)}) collective-permute-start(bf16[2,2048,256]{2,1,0:T(8,128)(2,1)} %get-tuple-element.40), channel_id=1, source_target_pairs={{0,1},{1,4},{2,5},{3,0},{4,3},{5,6},{6,7},{7,2},{8,9},{9,12},{10,1... | collective-permute-start | bytes 6291464 | tf_op jit(solution)/shard_map/ppermute | solution.py:289
  26.4 3.7 %pick.3 = (bf16[2,2048,256]{2,1,0:T(8,128)(2,1)}, bf16[256,2048]{1,0:T(8,128)(2,1)}) custom-call(s32[1]{0:T(128)} %bitcast.12.index_ref, bf16[2,2,2048,256]{3,2,1,0:T(8,128)(2,1)} %gu_ref.3, bf16[2,256,2048]{2,1,0:T(8,128)(2,1)} %dn_ref.3), custom_call_target="tpu_custom_call" | custom-call | tf_op jit(solution)/shard_map/pick/pallas_call | solution.py:309
  37.0 3.9 %shard_map.101 = (bf16[256,512]{1,0:T(8,128)(2,1)}, f32[256,512]{1,0:T(8,128)}) custom-call(bf16[256,2048]{1,0:T(8,128)(2,1)} %get-tuple-element.29.normed_ref, bf16[2048,512]{1,0:T(8,128)(2,1)} %get-tuple-element.51.wq_ref, bf16[256,512]{1,0:T(8,128)(2,1)} %get-tuple-element.30.k_ref, bf16[256,512]{1,0:T(8,128)(2,1)} %get-tuple-element.31.v_ref), custom_call_target="tpu_custom_call" | custom-call | tf_op jit(solution)/shard_map/pallas_call | solution.py:380
  46.1 4.3 %shard_map.102 = (f32[64,2048]{1,0:T(8,128)}, bf16[64,2048]{1,0:T(8,128)(2,1)}, bf16[64,2048]{1,0:T(8,128)(2,1)}, bf16[64,2048]{1,0:T(8,128)(2,1)}) custom-call(s32[2]{0:T(128)} %pad_add_fusion.place_ref, f32[4,128,128]{2,1,0:T(8,128)} %get-tuple-element.55.prefix_ref, bf16[4,128,128]{2,1,0:T(8,128)(2,1)} %copy-done.8, bf16[4,128,128]{2,1,0:T(8,128)(2,1)} %copy-done.7, ...), custom_call_target="tpu_custom_call" | custom-call | tf_op jit(solution)/shard_map/pallas_call | solution.py:384
  53.1 26.2 %collective-permute-done.7 = bf16[64,2048]{1,0:T(8,128)(2,1)S(1)} collective-permute-done((bf16[64,2048]{1,0:T(8,128)(2,1)}, bf16[64,2048]{1,0:T(8,128)(2,1)S(1)}, u32[]{:S(2)}, u32[]{:S(2)}) %collective-permute-start.7) | collective-permute-done | bytes 262176 | tf_op jit(solution)/shard_map/ppermute | solution.py:331
  79.3 3.8 %collective-permute-start.21 = (bf16[256,2048]{1,0:T(8,128)(2,1)}, bf16[256,2048]{1,0:T(8,128)(2,1)}, u32[]{:S(2)}, u32[]{:S(2)}) collective-permute-start(bf16[256,2048]{1,0:T(8,128)(2,1)} %get-tuple-element.43), channel_id=1, source_target_pairs={{0,1},{1,4},{2,5},{3,0},{4,3},{5,6},{6,7},{7,2},{8,9},{9,12},{10,1... | collective-permute-start | bytes 3145736 | tf_op jit(solution)/shard_map/ppermute | solution.py:289
  87.6 13.8 %collective-permute-done.12.t3 = f32[64,16]{1,0:T(8,128)S(1)} collective-permute-done((f32[64,16]{1,0:T(8,128)S(1)}, f32[64,16]{1,0:T(8,128)S(1)}, u32[]{:S(2)}, u32[]{:S(2)}) %collective-permute-start.12) | collective-permute-done | bytes 4128 | tf_op jit(solution)/shard_map/ppermute | solution.py:325
  102.4 3.6 %collective-permute-done.11.t2 = f32[64,16]{1,0:T(8,128)S(1)} collective-permute-done((f32[64,16]{1,0:T(8,128)S(1)}, f32[64,16]{1,0:T(8,128)S(1)}, u32[]{:S(2)}, u32[]{:S(2)}) %collective-permute-start.11) | collective-permute-done | bytes 4128 | tf_op jit(solution)/shard_map/ppermute | solution.py:325
  106.3 3.7 %collective-permute-done.10.t1 = f32[64,16]{1,0:T(8,128)S(1)} collective-permute-done((f32[64,16]{1,0:T(8,128)S(1)}, f32[64,16]{1,0:T(8,128)S(1)}, u32[]{:S(2)}, u32[]{:S(2)}) %collective-permute-start.10) | collective-permute-done | bytes 4128 | tf_op jit(solution)/shard_map/ppermute | solution.py:325
  118.0 7.4 %collective-permute-done.13.t1 = bf16[64,2048]{1,0:T(8,128)(2,1)S(1)} collective-permute-done((bf16[64,2048]{1,0:T(8,128)(2,1)S(1)}, bf16[64,2048]{1,0:T(8,128)(2,1)S(1)}, u32[]{:S(2)}, u32[]{:S(2)}) %collective-permute-start.13) | collective-permute-done | bytes 262176 | tf_op jit(solution)/shard_map/ppermute | solution.py:325
  126.1 3.5 %shard_map.104 = bf16[512,2304]{1,0:T(8,128)(2,1)} custom-call(bf16[576,256]{1,0:T(8,128)(2,1)} %get-tuple-element.39.place_ref, bf16[64,2048]{1,0:T(8,128)(2,1)} %copy-done.1, bf16[64,2048]{1,0:T(8,128)(2,1)} %copy-done.5, bf16[64,2048]{1,0:T(8,128)(2,1)} %copy-done.4, bf16[64,2048]{1,0:T(8,128)(2,1)} %copy-done.3), custom_call_target="tpu_custom_call" | custom-call | tf_op jit(solution)/shard_map/pallas_call | solution.py:395
  129.6 6.2 %all-to-all-start = ((bf16[32,16,2304]{2,1,0:T(8,128)(2,1)}), bf16[32,16,2304]{2,1,0:T(8,128)(2,1)S(1)}, u32[]{:S(2)}, u32[]{:S(2)}) async-start(bf16[32,16,2304]{2,1,0:T(8,128)(2,1)} %bitcast.20), calls=%async_computation | async-start | bytes 4718592 | tf_op jit(solution)/shard_map/all_to_all | solution.py:398
  141.5 3.5 %collective-permute-start.17 = (bf16[2,2048,256]{2,1,0:T(8,128)(2,1)}, bf16[2,2048,256]{2,1,0:T(8,128)(2,1)}, u32[]{:S(2)}, u32[]{:S(2)}) collective-permute-start(bf16[2,2048,256]{2,1,0:T(8,128)(2,1)} %collective-permute-done.16.gu0), channel_id=1, source_target_pairs={{0,4},{4,0},{8,12},{12,8},{16,20},{20,16},{24,28},{28,24},{32,36},... | collective-permute-start | bytes 6291464 | tf_op jit(solution)/shard_map/ppermute | solution.py:289
  145.0 3.2 %collective-permute-start.20 = (bf16[2,2048,256]{2,1,0:T(8,128)(2,1)}, bf16[2,2048,256]{2,1,0:T(8,128)(2,1)}, u32[]{:S(2)}, u32[]{:S(2)}) collective-permute-start(bf16[2,2048,256]{2,1,0:T(8,128)(2,1)} %collective-permute-done.19.gu4), channel_id=1, source_target_pairs={{2,6},{3,7},{4,0},{5,1},{10,14},{11,15},{12,8},{13,9},{18,22},{19,... | collective-permute-start | bytes 6291464 | tf_op jit(solution)/shard_map/ppermute | solution.py:289
  148.3 5.6 %collective-permute-done.24.dn4 = bf16[256,2048]{1,0:T(8,128)(2,1)} collective-permute-done((bf16[256,2048]{1,0:T(8,128)(2,1)}, bf16[256,2048]{1,0:T(8,128)(2,1)}, u32[]{:S(2)}, u32[]{:S(2)}) %collective-permute-start.24) | collective-permute-done | bytes 1048608 | tf_op jit(solution)/shard_map/ppermute | solution.py:289
  153.9 3.4 %collective-permute-start.25 = (bf16[256,2048]{1,0:T(8,128)(2,1)}, bf16[256,2048]{1,0:T(8,128)(2,1)}, u32[]{:S(2)}, u32[]{:S(2)}) collective-permute-start(bf16[256,2048]{1,0:T(8,128)(2,1)} %collective-permute-done.24.dn4), channel_id=1, source_target_pairs={{2,6},{3,7},{4,0},{5,1},{10,14},{11,15},{12,8},{13,9},{18,22},{19,... | collective-permute-start | bytes 3145736 | tf_op jit(solution)/shard_map/ppermute | solution.py:289
  158.9 6.1 %all-to-all-done = bf16[32,16,2304]{2,1,0:T(8,128)(2,1)S(1)} async-done(((bf16[32,16,2304]{2,1,0:T(8,128)(2,1)}), bf16[32,16,2304]{2,1,0:T(8,128)(2,1)S(1)}, u32[]{:S(2)}, u32[]{:S(2)}) %all-to-all-start) | async-done | bytes 2359328 | tf_op jit(solution)/shard_map/all_to_all | solution.py:398
  166.5 12.0 %shard_map.105 = bf16[512,2304]{1,0:T(8,128)(2,1)} custom-call(s32[1]{0:T(128)} %bitcast.7.keep_ref, bf16[512,2304]{1,0:T(8,128)(2,1)} %bitcast.18, bf16[2,2048,256]{2,1,0:T(8,128)(2,1)} %collective-permute-done.16.gu0, bf16[2,2048,256]{2,1,0:T(8,128)(2,1)} %collective-permute-done.17.gu1, bf16[2,2048,256]{2,1,0:T(8,128)(2,1)} %get-tuple-element.42.gu2, ...), custom_call_target="tpu_custom_call" | custom-call | tf_op jit(solution)/shard_map/pallas_call | solution.py:400
  178.5 37.6 %all_to_all.10 = bf16[32,16,2304]{2,1,0:T(8,128)(2,1)} all-to-all(bf16[32,16,2304]{2,1,0:T(8,128)(2,1)} %bitcast.19), channel_id=1, replica_groups=mesh['seq'=32,'head'=4] {'seq'}, dimensions={0} | all-to-all | bytes 4718592 | tf_op jit(solution)/shard_map/all_to_all | solution.py:414
  216.1 4.7 %shard_map.106 = (f32[64,2048]{1,0:T(8,128)}, bf16[64,2048]{1,0:T(8,128)(2,1)}, bf16[64,2048]{1,0:T(8,128)(2,1)}, bf16[64,2048]{1,0:T(8,128)(2,1)}) custom-call(bf16[512,576]{1,0:T(8,128)(2,1)} %get-tuple-element.38.weight_ref, bf16[512,2304]{1,0:T(8,128)(2,1)} %bitcast.21), custom_call_target="tpu_custom_call" | custom-call | tf_op jit(solution)/shard_map/pallas_call | solution.py:415
  223.7 12.0 %collective-permute-done.26 = bf16[64,2048]{1,0:T(8,128)(2,1)S(1)} collective-permute-done((bf16[64,2048]{1,0:T(8,128)(2,1)}, bf16[64,2048]{1,0:T(8,128)(2,1)S(1)}, u32[]{:S(2)}, u32[]{:S(2)}) %collective-permute-start.26) | collective-permute-done | bytes 262176 | tf_op jit(solution)/shard_map/ppermute | solution.py:331
  (89 shorter events, 51.0 us)
Async XLA Ops:
  13.7 18.5 %collective-permute-start.3 = (bf16[4,128,128]{2,1,0:T(8,128)(2,1)S(1)}, bf16[4,128,128]{2,1,0:T(8,128)(2,1)S(1)}, u32[]{:S(2)}, u32[]{:S(2)}) collective-permute-start(bf16[4,128,128]{2,1,0:T(8,128)(2,1)S(1)} %fusion.4), channel_id=1, source_target_pairs={{0,24},{4,28},{8,0},{12,4},{16,8},{20,12},{24,16},{28,20},{32,56},... | collective-permute-start | bytes 393224 | tf_op jit(solution)/shard_map/ppermute | solution.py:321
  13.8 18.5 %collective-permute-start.2 = (bf16[4,128,128]{2,1,0:T(8,128)(2,1)S(1)}, bf16[4,128,128]{2,1,0:T(8,128)(2,1)S(1)}, u32[]{:S(2)}, u32[]{:S(2)}) collective-permute-start(bf16[4,128,128]{2,1,0:T(8,128)(2,1)S(1)} %fusion.4), channel_id=1, source_target_pairs={{0,16},{4,20},{8,24},{12,28},{16,0},{20,4},{24,8},{28,12},{32,48},... | collective-permute-start | bytes 393224 | tf_op jit(solution)/shard_map/ppermute | solution.py:321
  16.6 15.7 %collective-permute-start.1 = (bf16[4,128,128]{2,1,0:T(8,128)(2,1)S(1)}, bf16[4,128,128]{2,1,0:T(8,128)(2,1)S(1)}, u32[]{:S(2)}, u32[]{:S(2)}) collective-permute-start(bf16[4,128,128]{2,1,0:T(8,128)(2,1)S(1)} %fusion.4), channel_id=1, source_target_pairs={{0,8},{4,12},{8,16},{12,20},{16,24},{20,28},{24,0},{28,4},{32,40},... | collective-permute-start | bytes 393224 | tf_op jit(solution)/shard_map/ppermute | solution.py:321
  22.1 119.4 %collective-permute-start.16 = (bf16[2,2048,256]{2,1,0:T(8,128)(2,1)}, bf16[2,2048,256]{2,1,0:T(8,128)(2,1)}, u32[]{:S(2)}, u32[]{:S(2)}) collective-permute-start(bf16[2,2048,256]{2,1,0:T(8,128)(2,1)} %get-tuple-element.40), channel_id=1, source_target_pairs={{0,1},{1,4},{2,5},{3,0},{4,3},{5,6},{6,7},{7,2},{8,9},{9,12},{10,1... | collective-permute-start | bytes 6291464 | tf_op jit(solution)/shard_map/ppermute | solution.py:289
  30.0 115.0 %collective-permute-start.19 = (bf16[2,2048,256]{2,1,0:T(8,128)(2,1)}, bf16[2,2048,256]{2,1,0:T(8,128)(2,1)}, u32[]{:S(2)}, u32[]{:S(2)}) collective-permute-start(bf16[2,2048,256]{2,1,0:T(8,128)(2,1)} %get-tuple-element.42.gu2), channel_id=1, source_target_pairs={{2,4},{3,5},{4,2},{5,3},{10,12},{11,13},{12,10},{13,11},{18,20},{1... | collective-permute-start | bytes 6291464 | tf_op jit(solution)/shard_map/ppermute | solution.py:289
  33.2 8.4 %collective-permute-start.6 = (bf16[4,128,128]{2,1,0:T(8,128)(2,1)S(1)}, bf16[4,128,128]{2,1,0:T(8,128)(2,1)S(1)}, u32[]{:S(2)}, u32[]{:S(2)}) collective-permute-start(bf16[4,128,128]{2,1,0:T(8,128)(2,1)S(1)} %get-tuple-element.54), channel_id=1, source_target_pairs={{0,96},{4,100},{8,104},{12,108},{16,112},{20,116},{24,120},{28,124... | collective-permute-start | bytes 393224 | tf_op jit(solution)/shard_map/ppermute | solution.py:321
  36.3 9.2 %collective-permute-start.4 = (bf16[4,128,128]{2,1,0:T(8,128)(2,1)S(1)}, bf16[4,128,128]{2,1,0:T(8,128)(2,1)S(1)}, u32[]{:S(2)}, u32[]{:S(2)}) collective-permute-start(bf16[4,128,128]{2,1,0:T(8,128)(2,1)S(1)} %get-tuple-element.54), channel_id=1, source_target_pairs={{0,32},{4,36},{8,40},{12,44},{16,48},{20,52},{24,56},{28,60},{32,6... | collective-permute-start | bytes 393224 | tf_op jit(solution)/shard_map/ppermute | solution.py:321
  50.4 28.9 %collective-permute-start.7 = (bf16[64,2048]{1,0:T(8,128)(2,1)}, bf16[64,2048]{1,0:T(8,128)(2,1)S(1)}, u32[]{:S(2)}, u32[]{:S(2)}) collective-permute-start(bf16[64,2048]{1,0:T(8,128)(2,1)} %get-tuple-element.35), channel_id=1, source_target_pairs={{0,1},{1,2},{2,3},{3,0},{4,5},{5,6},{6,7},{7,4},{8,9},{9,10},{10,1... | collective-permute-start | bytes 786440 | tf_op jit(solution)/shard_map/ppermute | solution.py:331
  50.5 32.6 %collective-permute-start.8 = (bf16[64,2048]{1,0:T(8,128)(2,1)}, bf16[64,2048]{1,0:T(8,128)(2,1)S(1)}, u32[]{:S(2)}, u32[]{:S(2)}) collective-permute-start(bf16[64,2048]{1,0:T(8,128)(2,1)} %get-tuple-element.36), channel_id=1, source_target_pairs={{0,2},{1,3},{2,0},{3,1},{4,6},{5,7},{6,4},{7,5},{8,10},{9,11},{10,... | collective-permute-start | bytes 786440 | tf_op jit(solution)/shard_map/ppermute | solution.py:331
  51.7 31.4 %collective-permute-start.9 = (bf16[64,2048]{1,0:T(8,128)(2,1)}, bf16[64,2048]{1,0:T(8,128)(2,1)S(1)}, u32[]{:S(2)}, u32[]{:S(2)}) collective-permute-start(bf16[64,2048]{1,0:T(8,128)(2,1)} %get-tuple-element.37), channel_id=1, source_target_pairs={{0,3},{1,0},{2,1},{3,2},{4,7},{5,4},{6,5},{7,6},{8,11},{9,8},{10,9... | collective-permute-start | bytes 786440 | tf_op jit(solution)/shard_map/ppermute | solution.py:331
  79.3 60.9 %collective-permute-start.21 = (bf16[256,2048]{1,0:T(8,128)(2,1)}, bf16[256,2048]{1,0:T(8,128)(2,1)}, u32[]{:S(2)}, u32[]{:S(2)}) collective-permute-start(bf16[256,2048]{1,0:T(8,128)(2,1)} %get-tuple-element.43), channel_id=1, source_target_pairs={{0,1},{1,4},{2,5},{3,0},{4,3},{5,6},{6,7},{7,2},{8,9},{9,12},{10,1... | collective-permute-start | bytes 3145736 | tf_op jit(solution)/shard_map/ppermute | solution.py:289
  84.6 26.3 %collective-permute-start.15 = (bf16[64,2048]{1,0:T(8,128)(2,1)S(1)}, bf16[64,2048]{1,0:T(8,128)(2,1)S(1)}, u32[]{:S(2)}, u32[]{:S(2)}) collective-permute-start(bf16[64,2048]{1,0:T(8,128)(2,1)S(1)} %multiply_convert_fusion.t0), channel_id=1, source_target_pairs={{0,3},{1,0},{2,1},{3,2},{4,7},{5,4},{6,5},{7,6},{8,11},{9,8},{10,9... | collective-permute-start | bytes 786440 | tf_op jit(solution)/shard_map/ppermute | solution.py:325
  87.5 13.9 %collective-permute-start.12 = (f32[64,16]{1,0:T(8,128)S(1)}, f32[64,16]{1,0:T(8,128)S(1)}, u32[]{:S(2)}, u32[]{:S(2)}) collective-permute-start(f32[64,16]{1,0:T(8,128)S(1)} %copy.16.t0), channel_id=1, source_target_pairs={{0,3},{1,0},{2,1},{3,2},{4,7},{5,4},{6,5},{7,6},{8,11},{9,8},{10,9... | collective-permute-start | bytes 12296 | tf_op jit(solution)/shard_map/ppermute | solution.py:325
  110.0 7.9 %collective-permute-start.14 = (bf16[64,2048]{1,0:T(8,128)(2,1)S(1)}, bf16[64,2048]{1,0:T(8,128)(2,1)S(1)}, u32[]{:S(2)}, u32[]{:S(2)}) collective-permute-start(bf16[64,2048]{1,0:T(8,128)(2,1)S(1)} %multiply_convert_fusion.t0), channel_id=1, source_target_pairs={{0,2},{1,3},{2,0},{3,1},{4,6},{5,7},{6,4},{7,5},{8,10},{9,11},{10,... | collective-permute-start | bytes 786440 | tf_op jit(solution)/shard_map/ppermute | solution.py:325
  110.9 14.4 %collective-permute-start.13 = (bf16[64,2048]{1,0:T(8,128)(2,1)S(1)}, bf16[64,2048]{1,0:T(8,128)(2,1)S(1)}, u32[]{:S(2)}, u32[]{:S(2)}) collective-permute-start(bf16[64,2048]{1,0:T(8,128)(2,1)S(1)} %multiply_convert_fusion.t0), channel_id=1, source_target_pairs={{0,1},{1,2},{2,3},{3,0},{4,5},{5,6},{6,7},{7,4},{8,9},{9,10},{10,1... | collective-permute-start | bytes 786440 | tf_op jit(solution)/shard_map/ppermute | solution.py:325
  129.6 35.4 %all-to-all-start = ((bf16[32,16,2304]{2,1,0:T(8,128)(2,1)}), bf16[32,16,2304]{2,1,0:T(8,128)(2,1)S(1)}, u32[]{:S(2)}, u32[]{:S(2)}) async-start(bf16[32,16,2304]{2,1,0:T(8,128)(2,1)} %bitcast.20), calls=%async_computation | async-start | bytes 4718592 | tf_op jit(solution)/shard_map/all_to_all | solution.py:398
  135.8 18.1 %collective-permute-start.24 = (bf16[256,2048]{1,0:T(8,128)(2,1)}, bf16[256,2048]{1,0:T(8,128)(2,1)}, u32[]{:S(2)}, u32[]{:S(2)}) collective-permute-start(bf16[256,2048]{1,0:T(8,128)(2,1)} %get-tuple-element.44.dn2), channel_id=1, source_target_pairs={{2,4},{3,5},{4,2},{5,3},{10,12},{11,13},{12,10},{13,11},{18,20},{1... | collective-permute-start | bytes 3145736 | tf_op jit(solution)/shard_map/ppermute | solution.py:289
  138.9 15.0 %collective-permute-start.23 = (bf16[256,2048]{1,0:T(8,128)(2,1)}, bf16[256,2048]{1,0:T(8,128)(2,1)}, u32[]{:S(2)}, u32[]{:S(2)}) collective-permute-start(bf16[256,2048]{1,0:T(8,128)(2,1)} %get-tuple-element.44.dn2), channel_id=1, source_target_pairs={{0,4},{1,5},{6,2},{7,3},{8,12},{9,13},{14,10},{15,11},{16,20},{17,... | collective-permute-start | bytes 3145736 | tf_op jit(solution)/shard_map/ppermute | solution.py:289
  140.2 18.7 %collective-permute-start.18 = (bf16[2,2048,256]{2,1,0:T(8,128)(2,1)}, bf16[2,2048,256]{2,1,0:T(8,128)(2,1)}, u32[]{:S(2)}, u32[]{:S(2)}) collective-permute-start(bf16[2,2048,256]{2,1,0:T(8,128)(2,1)} %get-tuple-element.42.gu2), channel_id=1, source_target_pairs={{0,4},{1,5},{6,2},{7,3},{8,12},{9,13},{14,10},{15,11},{16,20},{17,... | collective-permute-start | bytes 6291464 | tf_op jit(solution)/shard_map/ppermute | solution.py:289
  141.5 23.5 %collective-permute-start.17 = (bf16[2,2048,256]{2,1,0:T(8,128)(2,1)}, bf16[2,2048,256]{2,1,0:T(8,128)(2,1)}, u32[]{:S(2)}, u32[]{:S(2)}) collective-permute-start(bf16[2,2048,256]{2,1,0:T(8,128)(2,1)} %collective-permute-done.16.gu0), channel_id=1, source_target_pairs={{0,4},{4,0},{8,12},{12,8},{16,20},{20,16},{24,28},{28,24},{32,36},... | collective-permute-start | bytes 6291464 | tf_op jit(solution)/shard_map/ppermute | solution.py:289
  145.0 20.0 %collective-permute-start.20 = (bf16[2,2048,256]{2,1,0:T(8,128)(2,1)}, bf16[2,2048,256]{2,1,0:T(8,128)(2,1)}, u32[]{:S(2)}, u32[]{:S(2)}) collective-permute-start(bf16[2,2048,256]{2,1,0:T(8,128)(2,1)} %collective-permute-done.19.gu4), channel_id=1, source_target_pairs={{2,6},{3,7},{4,0},{5,1},{10,14},{11,15},{12,8},{13,9},{18,22},{19,... | collective-permute-start | bytes 6291464 | tf_op jit(solution)/shard_map/ppermute | solution.py:289
  220.7 15.0 %collective-permute-start.26 = (bf16[64,2048]{1,0:T(8,128)(2,1)}, bf16[64,2048]{1,0:T(8,128)(2,1)S(1)}, u32[]{:S(2)}, u32[]{:S(2)}) collective-permute-start(bf16[64,2048]{1,0:T(8,128)(2,1)} %get-tuple-element.46), channel_id=1, source_target_pairs={{0,1},{1,2},{2,3},{3,0},{4,5},{5,6},{6,7},{7,4},{8,9},{9,10},{10,1... | collective-permute-start | bytes 786440 | tf_op jit(solution)/shard_map/ppermute | solution.py:331
  220.7 15.0 %collective-permute-start.27 = (bf16[64,2048]{1,0:T(8,128)(2,1)}, bf16[64,2048]{1,0:T(8,128)(2,1)S(1)}, u32[]{:S(2)}, u32[]{:S(2)}) collective-permute-start(bf16[64,2048]{1,0:T(8,128)(2,1)} %get-tuple-element.47), channel_id=1, source_target_pairs={{0,2},{1,3},{2,0},{3,1},{4,6},{5,7},{6,4},{7,5},{8,10},{9,11},{10,... | collective-permute-start | bytes 786440 | tf_op jit(solution)/shard_map/ppermute | solution.py:331
  222.2 13.8 %collective-permute-start.28 = (bf16[64,2048]{1,0:T(8,128)(2,1)}, bf16[64,2048]{1,0:T(8,128)(2,1)S(1)}, u32[]{:S(2)}, u32[]{:S(2)}) collective-permute-start(bf16[64,2048]{1,0:T(8,128)(2,1)} %get-tuple-element.48), channel_id=1, source_target_pairs={{0,3},{1,0},{2,1},{3,2},{4,7},{5,4},{6,5},{7,6},{8,11},{9,8},{10,9... | collective-permute-start | bytes 786440 | tf_op jit(solution)/shard_map/ppermute | solution.py:331
  (22 other events, 259.7 us)
where the time goes:
time: 241 us; the launch traced here: 238 us
  waiting for transfers between devices  88.4 us (37%)
  starting transfers between devices  53 us (22%)
  Pallas kernels  43.6 us (18%)
  blocking collectives  37.6 us (16%)
  local copies, waits for them, and re-layouts  8.49 us (4%)
  other arithmetic  5.9 us (2%)
    ppermute x6, waiting for transfers between devices, scatter_head(): total = total + lax.ppermute(blocks[k], 'head', head_perm(k)).astype(F32)  38.5 us
    all_to_all x1, blocking collectives, on_device(): lax.all_to_all(results.reshape(32, 16, PACKED), 'seq', 0, 0, tiled=True)  37.6 us
    ppermute x6, waiting for transfers between devices, gather_head(): lax.ppermute(array, 'head', head_perm(k))  31.4 us
    ppermute x10, starting transfers between devices, permute_all(): return [lax.ppermute(a, axes, perm) for a in arrays]  25.4 us
    pallas_call x1, Pallas kernels, on_device(): call(expert_kernel, [SMEM] + [ANY] * 13, [out((MAIN, PACKED), BF)], [pltp...  12 us
    ppermute x6, starting transfers between devices, exchange(): lax.ppermute(array, 'seq', seq_perm(dy * k, dz * k, 0))  8.6 us
    ppermute x10, waiting for transfers between devices, permute_all(): return [lax.ppermute(a, axes, perm) for a in arrays]  7.28 us
    pallas_call x2, Pallas kernels, pick(): pl.pallas_call(pick_kernel, in_specs=[SMEM, ANY, ANY], out_specs=[VMEM, V...  7.17 us
  transfers between devices with their start and end apart: 30, of which 14 were waited for; matrix products, arithmetic and copies ran while one was open for 1% of the time, Pallas kernels for 9%

commit v1 on v0

--- a/solution.py
+++ b/solution.py
@@ -24,6 +24,7 @@
 VMEM = pl.BlockSpec(memory_space=pltpu.VMEM)
 SMEM = pl.BlockSpec(memory_space=pltpu.SMEM)
 ANY = pl.BlockSpec(memory_space=pl.ANY)
+HBM = pl.BlockSpec(memory_space=pltpu.HBM)
 
 
 def out(shape, dtype):
@@ -82,8 +83,9 @@
         send_ref[h] = state.astype(BF)
 
 
-def local_kernel(normed_ref, wq_ref, k_ref, v_ref, q_ref, local_ref):
-    query = dot(normed_ref[...], wq_ref[...]).astype(BF)
+def local_kernel(normed_ref, upper_ref, lower_ref, k_ref, v_ref, q_ref, local_ref):
+    query = dot(normed_ref[:, :D // 2], upper_ref[...]) + dot(normed_ref[:, D // 2:], lower_ref[...])
+    query = query.astype(BF)
     q_ref[...] = query
     row = lax.broadcasted_iota(jnp.int32, (TOK, TOK), 0)
     causal = lax.broadcasted_iota(jnp.int32, (TOK, TOK), 1) <= row
@@ -364,7 +366,8 @@
     sibling = lax.ppermute(send_state, "seq", seq_perm(0, 0, 1)).astype(F32)
     odd = (head & 1) + zero[0]
     rest = pick(w_gate_up, w_down, odd)
-    far = permute_all(rest, both, device_perm(far_target))
+    far_down = lax.ppermute(rest[1], both, device_perm(far_target))
+    far = [lax.ppermute(rest[0], both, device_perm(far_target)), far_down]
     rest_other = permute_all(rest, both, device_perm(keep_target))
     near_other = permute_all(near, "seq", seq_perm(0, 0, 1))
     far_other = permute_all(far, both, device_perm(pass_target))
@@ -377,9 +380,12 @@
         total = total + got.astype(F32)
     rows_y = exchange(total.astype(BF), (1, 0))
 
+    w_query = [
+        lax.dynamic_slice_in_dim(w_qkv, zero[0] + start, D // 2, 0)[:, 0] for start in (0, D // 2)
+    ]
     query, local = call(
-        local_kernel, [VMEM] * 4, [out((TOK, WIDE), BF), out((TOK, WIDE), F32)]
-    )(normed, w_qkv[:, 0], key, value)
+        local_kernel, [VMEM] * 5, [out((TOK, WIDE), BF), out((TOK, WIDE), F32)]
+    )(normed, *w_query, key, value)
     place = jnp.stack([y, head]).astype(jnp.int32)
     blocks = call(
         attend_kernel,
@@ -399,7 +405,7 @@
     keep = (head // 2 == core).astype(jnp.int32)[None]
     results = call(
         expert_kernel,
-        [SMEM] + [ANY] * 13,
+        [SMEM, HBM] + [ANY] * 12,
         [out((MAIN, PACKED), BF)],
         [
             pltpu.VMEM((SLOTS, D), BF),

time: 241 us -> 240 us (level)
  waiting for transfers between devices: 88.4 us -> 81.7 us
  between operations: 0.91 us -> 4.1 us
    ppermute x0 -> x2, waiting for transfers between devices: none -> 5.68 us  [the longest x1 5.67 us: on_device(): far_down = lax.ppermute(rest[1], both, device_perm(far_target))]
    ppermute x10 -> x8, waiting for transfers between devices: 7.28 us -> 1.66 us  [permute_all(): return [lax.ppermute(a, axes, perm) for a in arrays]]
    ppermute x10 -> x8, starting transfers between devices: 25.4 us -> 20.1 us  [permute_all(): return [lax.ppermute(a, axes, perm) for a in arrays]]
    ppermute x0 -> x2, starting transfers between devices: none -> 5.28 us  [the longest x1 3.09 us: on_device(): far_down = lax.ppermute(rest[1], both, device_perm(far_target))]
    ppermute x6, waiting for transfers between devices: 38.5 us -> 35.1 us  [scatter_head(): total = total + lax.ppermute(blocks[k], 'head', head_perm(k)).astype(F32)]
    ppermute x6, waiting for transfers between devices: 3.88 us -> 0.55 us  [exchange(): lax.ppermute(array, 'seq', seq_perm(dy * k, dz * k, 0))]
    squeeze x1 -> x2, local copies, waits for them, and re-layouts: 5.6 us -> 7.84 us  [the longest x1 4.48 us: on_device(): w_qkv[:, 2]]
  transfers between devices with their start and end apart: 30 -> 30, of which waited for: 14 -> 13; matrix products, arithmetic and copies ran while one was open for 1% -> 3% of each run, Pallas kernels for 9% -> 9%
where the time goes in v1:
time: 240 us; the launch traced here: 237 us
  waiting for transfers between devices  81.7 us (34%)
  starting transfers between devices  53.1 us (22%)
  Pallas kernels  43.6 us (18%)
  blocking collectives  37.6 us (16%)
  local copies, waits for them, and re-layouts  10.8 us (4%)
  other arithmetic  5.89 us (2%)
  between operations  4.1 us (2%)
    all_to_all x1, blocking collectives, on_device(): lax.all_to_all(results.reshape(32, 16, PACKED), 'seq', 0, 0, tiled=True)  37.6 us
    ppermute x6, waiting for transfers between devices, scatter_head(): total = total + lax.ppermute(blocks[k], 'head', head_perm(k)).astype(F32)  35.1 us
    ppermute x6, waiting for transfers between devices, gather_head(): lax.ppermute(array, 'head', head_perm(k))  31.4 us
    ppermute x8, starting transfers between devices, permute_all(): return [lax.ppermute(a, axes, perm) for a in arrays]  20.1 us
    pallas_call x1, Pallas kernels, on_device(): call(expert_kernel, [SMEM, HBM] + [ANY] * 12, [out((MAIN, PACKED), BF)],...  12 us
    ppermute x6, starting transfers between devices, exchange(): lax.ppermute(array, 'seq', seq_perm(dy * k, dz * k, 0))  8.6 us
    pallas_call x2, Pallas kernels, pick(): pl.pallas_call(pick_kernel, in_specs=[SMEM, ANY, ANY], out_specs=[VMEM, V...  7.18 us
    ppermute x6, starting transfers between devices, gather_head(): lax.ppermute(array, 'head', head_perm(k))  6.35 us
  transfers between devices with their start and end apart: 30, of which 13 were waited for; matrix products, arithmetic and copies ran while one was open for 3% of the time, Pallas kernels for 9%

profile of v1, /device:TPU:33, one launch (start us, length us, event | category | flops | bytes accessed | tf_op | source)
XLA Modules:
  0.0 236.8 jit_solution(14126113802632419283)
XLA Ops:
  0.0 4.5 %slice_bitcast_fusion = (bf16[2048,512]{1,0:T(8,128)(2,1)}, bf16[2048,512]{1,0:T(8,128)(2,1)}) fusion(bf16[2048,3,512]{2,0,1:T(8,128)(2,1)} %param.12), kind=kLoop, calls=%fused_computation | loop fusion | bytes 8388608 | tf_op jit(solution)/shard_map/squeeze | solution.py:365
  4.5 5.2 %shard_map.100 = (bf16[256,2048]{1,0:T(8,128)(2,1)}, bf16[256,512]{1,0:T(8,128)(2,1)}, bf16[256,512]{1,0:T(8,128)(2,1)}, f32[4,128,128]{2,1,0:T(8,128)}, bf16[4,128,128]{2,1,0:T(8,128)(2,1)}, /*index=5*/s32[1]{0:T(128)}) custom-call(bf16[256,2048]{1,0:T(8,128)(2,1)} %x_ref.1, f32[1,2048]{1,0:T(1,128)} %bitcast.24, ...), custom_call_target="tpu_custom_call" | custom-call | tf_op jit(solution)/shard_map/pallas_call | solution.py:353
  17.5 3.5 %pick.2 = (bf16[2,2048,256]{2,1,0:T(8,128)(2,1)}, bf16[256,2048]{1,0:T(8,128)(2,1)}) custom-call(s32[1]{0:T(128)} %bitcast.12.index_ref, bf16[2,2,2048,256]{3,2,1,0:T(8,128)(2,1)} %gu_ref.3, bf16[2,256,2048]{2,1,0:T(8,128)(2,1)} %dn_ref.3), custom_call_target="tpu_custom_call" | custom-call | tf_op jit(solution)/shard_map/pick/pallas_call | solution.py:311
  21.0 3.6 %collective-permute-start.16 = (bf16[2,2048,256]{2,1,0:T(8,128)(2,1)}, bf16[2,2048,256]{2,1,0:T(8,128)(2,1)}, u32[]{:S(2)}, u32[]{:S(2)}) collective-permute-start(bf16[2,2048,256]{2,1,0:T(8,128)(2,1)} %get-tuple-element.41), channel_id=1, source_target_pairs={{0,1},{1,4},{2,5},{3,0},{4,3},{5,6},{6,7},{7,2},{8,9},{9,12},{10,1... | collective-permute-start | bytes 6291464 | tf_op jit(solution)/shard_map/ppermute | solution.py:291
  25.3 3.7 %pick.3 = (bf16[2,2048,256]{2,1,0:T(8,128)(2,1)}, bf16[256,2048]{1,0:T(8,128)(2,1)}) custom-call(s32[1]{0:T(128)} %bitcast.13.index_ref, bf16[2,2,2048,256]{3,2,1,0:T(8,128)(2,1)} %gu_ref.3, bf16[2,256,2048]{2,1,0:T(8,128)(2,1)} %dn_ref.3), custom_call_target="tpu_custom_call" | custom-call | tf_op jit(solution)/shard_map/pick/pallas_call | solution.py:311
  39.0 3.4 %dynamic-slice_bitcast_fusion = (bf16[1024,512]{1,0:T(8,128)(2,1)}, bf16[1024,512]{1,0:T(8,128)(2,1)}) fusion(bf16[2048,3,512]{2,0,1:T(8,128)(2,1)} %param.12, s32[]{:T(128)S(6)} %select_n.70, s32[]{:T(128)S(6)} %select_n.69), kind=kLoop, calls=%fused_computation.2 | loop fusion | bytes 4194312 | tf_op jit(solution)/shard_map/squeeze | solution.py:384
  42.4 3.9 %shard_map.101 = (bf16[256,512]{1,0:T(8,128)(2,1)}, f32[256,512]{1,0:T(8,128)}) custom-call(bf16[256,2048]{1,0:T(8,128)(2,1)} %get-tuple-element.29.normed_ref, bf16[1024,512]{1,0:T(8,128)(2,1)} %get-tuple-element.52.upper_ref, bf16[1024,512]{1,0:T(8,128)(2,1)} %get-tuple-element.51.lower_ref, bf16[256,512]{1,0:T(8,128)(2,1)} %get-tuple-element.31.k_ref, ...), custom_call_target="tpu_custom_call" | custom-call | tf_op jit(solution)/shard_map/pallas_call | solution.py:386
  48.2 4.3 %shard_map.102 = (f32[64,2048]{1,0:T(8,128)}, bf16[64,2048]{1,0:T(8,128)(2,1)}, bf16[64,2048]{1,0:T(8,128)(2,1)}, bf16[64,2048]{1,0:T(8,128)(2,1)}) custom-call(s32[2]{0:T(128)} %pad_add_fusion.place_ref, f32[4,128,128]{2,1,0:T(8,128)} %get-tuple-element.56.prefix_ref, bf16[4,128,128]{2,1,0:T(8,128)(2,1)} %copy-done.8, bf16[4,128,128]{2,1,0:T(8,128)(2,1)} %copy-done.7, ...), custom_call_target="tpu_custom_call" | custom-call | tf_op jit(solution)/shard_map/pallas_call | solution.py:390
  55.4 22.8 %collective-permute-done.7 = bf16[64,2048]{1,0:T(8,128)(2,1)S(1)} collective-permute-done((bf16[64,2048]{1,0:T(8,128)(2,1)}, bf16[64,2048]{1,0:T(8,128)(2,1)S(1)}, u32[]{:S(2)}, u32[]{:S(2)}) %collective-permute-start.7) | collective-permute-done | bytes 262176 | tf_op jit(solution)/shard_map/ppermute | solution.py:333
  78.2 3.8 %collective-permute-start.21 = (bf16[256,2048]{1,0:T(8,128)(2,1)}, bf16[256,2048]{1,0:T(8,128)(2,1)}, u32[]{:S(2)}, u32[]{:S(2)}) collective-permute-start(bf16[256,2048]{1,0:T(8,128)(2,1)} %get-tuple-element.43), channel_id=1, source_target_pairs={{0,1},{1,4},{2,5},{3,0},{4,3},{5,6},{6,7},{7,2},{8,9},{9,12},{10,1... | collective-permute-start | bytes 3145736 | tf_op jit(solution)/shard_map/ppermute | solution.py:291
  86.4 13.8 %collective-permute-done.12.t3 = f32[64,16]{1,0:T(8,128)S(1)} collective-permute-done((f32[64,16]{1,0:T(8,128)S(1)}, f32[64,16]{1,0:T(8,128)S(1)}, u32[]{:S(2)}, u32[]{:S(2)}) %collective-permute-start.12) | collective-permute-done | bytes 4128 | tf_op jit(solution)/shard_map/ppermute | solution.py:327
  101.3 3.6 %collective-permute-done.11.t2 = f32[64,16]{1,0:T(8,128)S(1)} collective-permute-done((f32[64,16]{1,0:T(8,128)S(1)}, f32[64,16]{1,0:T(8,128)S(1)}, u32[]{:S(2)}, u32[]{:S(2)}) %collective-permute-start.11) | collective-permute-done | bytes 4128 | tf_op jit(solution)/shard_map/ppermute | solution.py:327
  105.2 3.7 %collective-permute-done.10.t1 = f32[64,16]{1,0:T(8,128)S(1)} collective-permute-done((f32[64,16]{1,0:T(8,128)S(1)}, f32[64,16]{1,0:T(8,128)S(1)}, u32[]{:S(2)}, u32[]{:S(2)}) %collective-permute-start.10) | collective-permute-done | bytes 4128 | tf_op jit(solution)/shard_map/ppermute | solution.py:327
  116.8 7.4 %collective-permute-done.13.t1 = bf16[64,2048]{1,0:T(8,128)(2,1)S(1)} collective-permute-done((bf16[64,2048]{1,0:T(8,128)(2,1)S(1)}, bf16[64,2048]{1,0:T(8,128)(2,1)S(1)}, u32[]{:S(2)}, u32[]{:S(2)}) %collective-permute-start.13) | collective-permute-done | bytes 262176 | tf_op jit(solution)/shard_map/ppermute | solution.py:327
  124.9 3.5 %shard_map.104 = bf16[512,2304]{1,0:T(8,128)(2,1)} custom-call(bf16[576,256]{1,0:T(8,128)(2,1)} %get-tuple-element.40.place_ref, bf16[64,2048]{1,0:T(8,128)(2,1)} %copy-done.1, bf16[64,2048]{1,0:T(8,128)(2,1)} %copy-done.5, bf16[64,2048]{1,0:T(8,128)(2,1)} %copy-done.4, bf16[64,2048]{1,0:T(8,128)(2,1)} %copy-done.3), custom_call_target="tpu_custom_call" | custom-call | tf_op jit(solution)/shard_map/pallas_call | solution.py:401
  128.4 6.2 %all-to-all-start = ((bf16[32,16,2304]{2,1,0:T(8,128)(2,1)}), bf16[32,16,2304]{2,1,0:T(8,128)(2,1)S(1)}, u32[]{:S(2)}, u32[]{:S(2)}) async-start(bf16[32,16,2304]{2,1,0:T(8,128)(2,1)} %bitcast.22), calls=%async_computation | async-start | bytes 4718592 | tf_op jit(solution)/shard_map/all_to_all | solution.py:404
  140.4 3.5 %collective-permute-start.17 = (bf16[2,2048,256]{2,1,0:T(8,128)(2,1)}, bf16[2,2048,256]{2,1,0:T(8,128)(2,1)}, u32[]{:S(2)}, u32[]{:S(2)}) collective-permute-start(bf16[2,2048,256]{2,1,0:T(8,128)(2,1)} %collective-permute-done.16.gu0), channel_id=1, source_target_pairs={{0,4},{4,0},{8,12},{12,8},{16,20},{20,16},{24,28},{28,24},{32,36},... | collective-permute-start | bytes 6291464 | tf_op jit(solution)/shard_map/ppermute | solution.py:291
  147.1 5.7 %collective-permute-done.24.dn4 = bf16[256,2048]{1,0:T(8,128)(2,1)} collective-permute-done((bf16[256,2048]{1,0:T(8,128)(2,1)}, bf16[256,2048]{1,0:T(8,128)(2,1)}, u32[]{:S(2)}, u32[]{:S(2)}) %collective-permute-start.24) | collective-permute-done | bytes 1048608 | tf_op jit(solution)/shard_map/ppermute | solution.py:369
  152.8 3.4 %collective-permute-start.25 = (bf16[256,2048]{1,0:T(8,128)(2,1)}, bf16[256,2048]{1,0:T(8,128)(2,1)}, u32[]{:S(2)}, u32[]{:S(2)}) collective-permute-start(bf16[256,2048]{1,0:T(8,128)(2,1)} %collective-permute-done.24.dn4), channel_id=1, source_target_pairs={{2,6},{3,7},{4,0},{5,1},{10,14},{11,15},{12,8},{13,9},{18,22},{19,... | collective-permute-start | bytes 3145736 | tf_op jit(solution)/shard_map/ppermute | solution.py:291
  157.8 6.1 %all-to-all-done = bf16[32,16,2304]{2,1,0:T(8,128)(2,1)S(1)} async-done(((bf16[32,16,2304]{2,1,0:T(8,128)(2,1)}), bf16[32,16,2304]{2,1,0:T(8,128)(2,1)S(1)}, u32[]{:S(2)}, u32[]{:S(2)}) %all-to-all-start) | async-done | bytes 2359328 | tf_op jit(solution)/shard_map/all_to_all | solution.py:404
  165.3 12.0 %shard_map.105 = bf16[512,2304]{1,0:T(8,128)(2,1)} custom-call(s32[1]{0:T(128)} %bitcast.9.keep_ref, bf16[512,2304]{1,0:T(8,128)(2,1)} %bitcast.20, bf16[2,2048,256]{2,1,0:T(8,128)(2,1)} %collective-permute-done.16.gu0, bf16[2,2048,256]{2,1,0:T(8,128)(2,1)} %collective-permute-done.17.gu1, bf16[2,2048,256]{2,1,0:T(8,128)(2,1)} %get-tuple-element.42.gu2, ...), custom_call_target="tpu_custom_call" | custom-call | tf_op jit(solution)/shard_map/pallas_call | solution.py:406
  177.4 37.6 %all_to_all.10 = bf16[32,16,2304]{2,1,0:T(8,128)(2,1)} all-to-all(bf16[32,16,2304]{2,1,0:T(8,128)(2,1)} %bitcast.21), channel_id=1, replica_groups=mesh['seq'=32,'head'=4] {'seq'}, dimensions={0} | all-to-all | bytes 4718592 | tf_op jit(solution)/shard_map/all_to_all | solution.py:420
  215.0 4.7 %shard_map.106 = (f32[64,2048]{1,0:T(8,128)}, bf16[64,2048]{1,0:T(8,128)(2,1)}, bf16[64,2048]{1,0:T(8,128)(2,1)}, bf16[64,2048]{1,0:T(8,128)(2,1)}) custom-call(bf16[512,576]{1,0:T(8,128)(2,1)} %get-tuple-element.39.weight_ref, bf16[512,2304]{1,0:T(8,128)(2,1)} %bitcast.23), custom_call_target="tpu_custom_call" | custom-call | tf_op jit(solution)/shard_map/pallas_call | solution.py:421
  222.6 12.0 %collective-permute-done.26 = bf16[64,2048]{1,0:T(8,128)(2,1)S(1)} collective-permute-done((bf16[64,2048]{1,0:T(8,128)(2,1)}, bf16[64,2048]{1,0:T(8,128)(2,1)S(1)}, u32[]{:S(2)}, u32[]{:S(2)}) %collective-permute-start.26) | collective-permute-done | bytes 262176 | tf_op jit(solution)/shard_map/ppermute | solution.py:333
  (90 shorter events, 51.1 us)
Async XLA Ops:
  12.6 21.7 %collective-permute-start.3 = (bf16[4,128,128]{2,1,0:T(8,128)(2,1)S(1)}, bf16[4,128,128]{2,1,0:T(8,128)(2,1)S(1)}, u32[]{:S(2)}, u32[]{:S(2)}) collective-permute-start(bf16[4,128,128]{2,1,0:T(8,128)(2,1)S(1)} %fusion.4), channel_id=1, source_target_pairs={{0,24},{4,28},{8,0},{12,4},{16,8},{20,12},{24,16},{28,20},{32,56},... | collective-permute-start | bytes 393224 | tf_op jit(solution)/shard_map/ppermute | solution.py:323
  12.7 21.7 %collective-permute-start.2 = (bf16[4,128,128]{2,1,0:T(8,128)(2,1)S(1)}, bf16[4,128,128]{2,1,0:T(8,128)(2,1)S(1)}, u32[]{:S(2)}, u32[]{:S(2)}) collective-permute-start(bf16[4,128,128]{2,1,0:T(8,128)(2,1)S(1)} %fusion.4), channel_id=1, source_target_pairs={{0,16},{4,20},{8,24},{12,28},{16,0},{20,4},{24,8},{28,12},{32,48},... | collective-permute-start | bytes 393224 | tf_op jit(solution)/shard_map/ppermute | solution.py:323
  15.5 18.9 %collective-permute-start.1 = (bf16[4,128,128]{2,1,0:T(8,128)(2,1)S(1)}, bf16[4,128,128]{2,1,0:T(8,128)(2,1)S(1)}, u32[]{:S(2)}, u32[]{:S(2)}) collective-permute-start(bf16[4,128,128]{2,1,0:T(8,128)(2,1)S(1)} %fusion.4), channel_id=1, source_target_pairs={{0,8},{4,12},{8,16},{12,20},{16,24},{20,28},{24,0},{28,4},{32,40},... | collective-permute-start | bytes 393224 | tf_op jit(solution)/shard_map/ppermute | solution.py:323
  21.0 119.4 %collective-permute-start.16 = (bf16[2,2048,256]{2,1,0:T(8,128)(2,1)}, bf16[2,2048,256]{2,1,0:T(8,128)(2,1)}, u32[]{:S(2)}, u32[]{:S(2)}) collective-permute-start(bf16[2,2048,256]{2,1,0:T(8,128)(2,1)} %get-tuple-element.41), channel_id=1, source_target_pairs={{0,1},{1,4},{2,5},{3,0},{4,3},{5,6},{6,7},{7,2},{8,9},{9,12},{10,1... | collective-permute-start | bytes 6291464 | tf_op jit(solution)/shard_map/ppermute | solution.py:291
  28.9 114.9 %collective-permute-start.19 = (bf16[2,2048,256]{2,1,0:T(8,128)(2,1)}, bf16[2,2048,256]{2,1,0:T(8,128)(2,1)}, u32[]{:S(2)}, u32[]{:S(2)}) collective-permute-start(bf16[2,2048,256]{2,1,0:T(8,128)(2,1)} %get-tuple-element.42.gu2), channel_id=1, source_target_pairs={{2,4},{3,5},{4,2},{5,3},{10,12},{11,13},{12,10},{13,11},{18,20},{1... | collective-permute-start | bytes 6291464 | tf_op jit(solution)/shard_map/ppermute | solution.py:370
  35.2 11.7 %collective-permute-start.6 = (bf16[4,128,128]{2,1,0:T(8,128)(2,1)S(1)}, bf16[4,128,128]{2,1,0:T(8,128)(2,1)S(1)}, u32[]{:S(2)}, u32[]{:S(2)}) collective-permute-start(bf16[4,128,128]{2,1,0:T(8,128)(2,1)S(1)} %get-tuple-element.55), channel_id=1, source_target_pairs={{0,96},{4,100},{8,104},{12,108},{16,112},{20,116},{24,120},{28,124... | collective-permute-start | bytes 393224 | tf_op jit(solution)/shard_map/ppermute | solution.py:323
  38.0 9.0 %collective-permute-start.5 = (bf16[4,128,128]{2,1,0:T(8,128)(2,1)S(1)}, bf16[4,128,128]{2,1,0:T(8,128)(2,1)S(1)}, u32[]{:S(2)}, u32[]{:S(2)}) collective-permute-start(bf16[4,128,128]{2,1,0:T(8,128)(2,1)S(1)} %get-tuple-element.55), channel_id=1, source_target_pairs={{0,64},{4,68},{8,72},{12,76},{16,80},{20,84},{24,88},{28,92},{32,9... | collective-permute-start | bytes 393224 | tf_op jit(solution)/shard_map/ppermute | solution.py:323
  38.3 9.2 %collective-permute-start.4 = (bf16[4,128,128]{2,1,0:T(8,128)(2,1)S(1)}, bf16[4,128,128]{2,1,0:T(8,128)(2,1)S(1)}, u32[]{:S(2)}, u32[]{:S(2)}) collective-permute-start(bf16[4,128,128]{2,1,0:T(8,128)(2,1)S(1)} %get-tuple-element.55), channel_id=1, source_target_pairs={{0,32},{4,36},{8,40},{12,44},{16,48},{20,52},{24,56},{28,60},{32,6... | collective-permute-start | bytes 393224 | tf_op jit(solution)/shard_map/ppermute | solution.py:323
  52.5 25.7 %collective-permute-start.7 = (bf16[64,2048]{1,0:T(8,128)(2,1)}, bf16[64,2048]{1,0:T(8,128)(2,1)S(1)}, u32[]{:S(2)}, u32[]{:S(2)}) collective-permute-start(bf16[64,2048]{1,0:T(8,128)(2,1)} %get-tuple-element.36), channel_id=1, source_target_pairs={{0,1},{1,2},{2,3},{3,0},{4,5},{5,6},{6,7},{7,4},{8,9},{9,10},{10,1... | collective-permute-start | bytes 786440 | tf_op jit(solution)/shard_map/ppermute | solution.py:333
  52.9 29.1 %collective-permute-start.8 = (bf16[64,2048]{1,0:T(8,128)(2,1)}, bf16[64,2048]{1,0:T(8,128)(2,1)S(1)}, u32[]{:S(2)}, u32[]{:S(2)}) collective-permute-start(bf16[64,2048]{1,0:T(8,128)(2,1)} %get-tuple-element.37), channel_id=1, source_target_pairs={{0,2},{1,3},{2,0},{3,1},{4,6},{5,7},{6,4},{7,5},{8,10},{9,11},{10,... | collective-permute-start | bytes 786440 | tf_op jit(solution)/shard_map/ppermute | solution.py:333
  53.8 28.1 %collective-permute-start.9 = (bf16[64,2048]{1,0:T(8,128)(2,1)}, bf16[64,2048]{1,0:T(8,128)(2,1)S(1)}, u32[]{:S(2)}, u32[]{:S(2)}) collective-permute-start(bf16[64,2048]{1,0:T(8,128)(2,1)} %get-tuple-element.38), channel_id=1, source_target_pairs={{0,3},{1,0},{2,1},{3,2},{4,7},{5,4},{6,5},{7,6},{8,11},{9,8},{10,9... | collective-permute-start | bytes 786440 | tf_op jit(solution)/shard_map/ppermute | solution.py:333
  78.2 60.9 %collective-permute-start.21 = (bf16[256,2048]{1,0:T(8,128)(2,1)}, bf16[256,2048]{1,0:T(8,128)(2,1)}, u32[]{:S(2)}, u32[]{:S(2)}) collective-permute-start(bf16[256,2048]{1,0:T(8,128)(2,1)} %get-tuple-element.43), channel_id=1, source_target_pairs={{0,1},{1,4},{2,5},{3,0},{4,3},{5,6},{6,7},{7,2},{8,9},{9,12},{10,1... | collective-permute-start | bytes 3145736 | tf_op jit(solution)/shard_map/ppermute | solution.py:291
  83.5 26.3 %collective-permute-start.15 = (bf16[64,2048]{1,0:T(8,128)(2,1)S(1)}, bf16[64,2048]{1,0:T(8,128)(2,1)S(1)}, u32[]{:S(2)}, u32[]{:S(2)}) collective-permute-start(bf16[64,2048]{1,0:T(8,128)(2,1)S(1)} %multiply_convert_fusion.t0), channel_id=1, source_target_pairs={{0,3},{1,0},{2,1},{3,2},{4,7},{5,4},{6,5},{7,6},{8,11},{9,8},{10,9... | collective-permute-start | bytes 786440 | tf_op jit(solution)/shard_map/ppermute | solution.py:327
  86.3 13.9 %collective-permute-start.12 = (f32[64,16]{1,0:T(8,128)S(1)}, f32[64,16]{1,0:T(8,128)S(1)}, u32[]{:S(2)}, u32[]{:S(2)}) collective-permute-start(f32[64,16]{1,0:T(8,128)S(1)} %copy.16.t0), channel_id=1, source_target_pairs={{0,3},{1,0},{2,1},{3,2},{4,7},{5,4},{6,5},{7,6},{8,11},{9,8},{10,9... | collective-permute-start | bytes 12296 | tf_op jit(solution)/shard_map/ppermute | solution.py:327
  109.8 14.4 %collective-permute-start.13 = (bf16[64,2048]{1,0:T(8,128)(2,1)S(1)}, bf16[64,2048]{1,0:T(8,128)(2,1)S(1)}, u32[]{:S(2)}, u32[]{:S(2)}) collective-permute-start(bf16[64,2048]{1,0:T(8,128)(2,1)S(1)} %multiply_convert_fusion.t0), channel_id=1, source_target_pairs={{0,1},{1,2},{2,3},{3,0},{4,5},{5,6},{6,7},{7,4},{8,9},{9,10},{10,1... | collective-permute-start | bytes 786440 | tf_op jit(solution)/shard_map/ppermute | solution.py:327
  128.4 35.5 %all-to-all-start = ((bf16[32,16,2304]{2,1,0:T(8,128)(2,1)}), bf16[32,16,2304]{2,1,0:T(8,128)(2,1)S(1)}, u32[]{:S(2)}, u32[]{:S(2)}) async-start(bf16[32,16,2304]{2,1,0:T(8,128)(2,1)} %bitcast.22), calls=%async_computation | async-start | bytes 4718592 | tf_op jit(solution)/shard_map/all_to_all | solution.py:404
  134.6 18.1 %collective-permute-start.24 = (bf16[256,2048]{1,0:T(8,128)(2,1)}, bf16[256,2048]{1,0:T(8,128)(2,1)}, u32[]{:S(2)}, u32[]{:S(2)}) collective-permute-start(bf16[256,2048]{1,0:T(8,128)(2,1)} %get-tuple-element.44.dn2), channel_id=1, source_target_pairs={{2,4},{3,5},{4,2},{5,3},{10,12},{11,13},{12,10},{13,11},{18,20},{1... | collective-permute-start | bytes 3145736 | tf_op jit(solution)/shard_map/ppermute | solution.py:369
  137.7 15.0 %collective-permute-start.23 = (bf16[256,2048]{1,0:T(8,128)(2,1)}, bf16[256,2048]{1,0:T(8,128)(2,1)}, u32[]{:S(2)}, u32[]{:S(2)}) collective-permute-start(bf16[256,2048]{1,0:T(8,128)(2,1)} %get-tuple-element.44.dn2), channel_id=1, source_target_pairs={{0,4},{1,5},{6,2},{7,3},{8,12},{9,13},{14,10},{15,11},{16,20},{17,... | collective-permute-start | bytes 3145736 | tf_op jit(solution)/shard_map/ppermute | solution.py:291
  139.0 18.7 %collective-permute-start.18 = (bf16[2,2048,256]{2,1,0:T(8,128)(2,1)}, bf16[2,2048,256]{2,1,0:T(8,128)(2,1)}, u32[]{:S(2)}, u32[]{:S(2)}) collective-permute-start(bf16[2,2048,256]{2,1,0:T(8,128)(2,1)} %get-tuple-element.42.gu2), channel_id=1, source_target_pairs={{0,4},{1,5},{6,2},{7,3},{8,12},{9,13},{14,10},{15,11},{16,20},{17,... | collective-permute-start | bytes 6291464 | tf_op jit(solution)/shard_map/ppermute | solution.py:291
  140.4 23.5 %collective-permute-start.17 = (bf16[2,2048,256]{2,1,0:T(8,128)(2,1)}, bf16[2,2048,256]{2,1,0:T(8,128)(2,1)}, u32[]{:S(2)}, u32[]{:S(2)}) collective-permute-start(bf16[2,2048,256]{2,1,0:T(8,128)(2,1)} %collective-permute-done.16.gu0), channel_id=1, source_target_pairs={{0,4},{4,0},{8,12},{12,8},{16,20},{20,16},{24,28},{28,24},{32,36},... | collective-permute-start | bytes 6291464 | tf_op jit(solution)/shard_map/ppermute | solution.py:291
  143.8 20.0 %collective-permute-start.20 = (bf16[2,2048,256]{2,1,0:T(8,128)(2,1)}, bf16[2,2048,256]{2,1,0:T(8,128)(2,1)}, u32[]{:S(2)}, u32[]{:S(2)}) collective-permute-start(bf16[2,2048,256]{2,1,0:T(8,128)(2,1)} %collective-permute-done.19.gu4), channel_id=1, source_target_pairs={{2,6},{3,7},{4,0},{5,1},{10,14},{11,15},{12,8},{13,9},{18,22},{19,... | collective-permute-start | bytes 6291464 | tf_op jit(solution)/shard_map/ppermute | solution.py:291
  219.6 15.0 %collective-permute-start.26 = (bf16[64,2048]{1,0:T(8,128)(2,1)}, bf16[64,2048]{1,0:T(8,128)(2,1)S(1)}, u32[]{:S(2)}, u32[]{:S(2)}) collective-permute-start(bf16[64,2048]{1,0:T(8,128)(2,1)} %get-tuple-element.46), channel_id=1, source_target_pairs={{0,1},{1,2},{2,3},{3,0},{4,5},{5,6},{6,7},{7,4},{8,9},{9,10},{10,1... | collective-permute-start | bytes 786440 | tf_op jit(solution)/shard_map/ppermute | solution.py:333
  219.6 15.0 %collective-permute-start.27 = (bf16[64,2048]{1,0:T(8,128)(2,1)}, bf16[64,2048]{1,0:T(8,128)(2,1)S(1)}, u32[]{:S(2)}, u32[]{:S(2)}) collective-permute-start(bf16[64,2048]{1,0:T(8,128)(2,1)} %get-tuple-element.47), channel_id=1, source_target_pairs={{0,2},{1,3},{2,0},{3,1},{4,6},{5,7},{6,4},{7,5},{8,10},{9,11},{10,... | collective-permute-start | bytes 786440 | tf_op jit(solution)/shard_map/ppermute | solution.py:333
  221.1 13.8 %collective-permute-start.28 = (bf16[64,2048]{1,0:T(8,128)(2,1)}, bf16[64,2048]{1,0:T(8,128)(2,1)S(1)}, u32[]{:S(2)}, u32[]{:S(2)}) collective-permute-start(bf16[64,2048]{1,0:T(8,128)(2,1)} %get-tuple-element.48), channel_id=1, source_target_pairs={{0,3},{1,0},{2,1},{3,2},{4,7},{5,4},{6,5},{7,6},{8,11},{9,8},{10,9... | collective-permute-start | bytes 786440 | tf_op jit(solution)/shard_map/ppermute | solution.py:333
  (22 other events, 249.1 us)

commit v2 on v1

--- a/solution.py
+++ b/solution.py
@@ -16,6 +16,7 @@
 MAIN = 512
 SLOTS = 576
 PACKED = D + 256
+HALF = D // 2
 EPSILON = 1e-06
 BF = jnp.bfloat16
 F32 = jnp.float32
@@ -139,8 +140,6 @@
     block = (head - lax.broadcasted_iota(jnp.int32, (TOK, 16), 0) // ROWS) & 3
     base = ((block >> 1) * 18 + (block & 1) * CAP).astype(F32)
     slot = jnp.where(chosen > 0, base + rank, -1.0).astype(BF)
-    high = gates.astype(BF)
-    low = (gates - high.astype(F32)).astype(BF)
 
     def of_row(shape, axis):
         row = lax.broadcasted_iota(jnp.int32, shape, axis)
@@ -156,8 +155,7 @@
     chip, want = of_row((16, SLOTS), 1)
     spread = (chip == lax.broadcasted_iota(jnp.int32, (16, SLOTS), 0)).astype(F32).astype(BF)
     at_row = dot(slot, spread) == want[:1, :]
-    weight_ref[:TOK, :] = jnp.where(at_row, dot(high, spread), 0.0).astype(BF)
-    weight_ref[TOK:, :] = jnp.where(at_row, dot(low, spread), 0.0).astype(BF)
+    weight_ref[...] = jnp.where(at_row, dot(gates.astype(BF), spread), 0.0).astype(BF)
 
 
 def dispatch_kernel(place_ref, t0, t1, t2, t3, out_ref, tokens):
@@ -175,74 +173,95 @@
         out_ref[:, D + t * 128:D + (t + 1) * 128] = piece
 
 
+def start_quarters(keep_ref, arrays, dest_of, sems, first):
+    def load(q, ref):
+        return pltpu.make_async_copy(ref, dest_of(q), sems.at[first + q])
+
+    keep = keep_ref[0] == 1
+    copies = [load(0, arrays[0]), load(1, arrays[1])]
+    copies[0].start()
+    copies[1].start()
+
+    @pl.when(keep)
+    def _():
+        load(2, arrays[2]).start()
+        load(3, arrays[5]).start()
+
+    @pl.when(jnp.logical_not(keep))
+    def _():
+        load(2, arrays[3]).start()
+        load(3, arrays[4]).start()
+
+    return copies + [load(2, arrays[2]), load(3, arrays[4])]
+
+
+def down_half(act, down, out_ref):
+    tail = []
+    for n in range(2):
+        cols = slice(n * 512, (n + 1) * 512)
+        result = dot(act, down[:, cols])
+        out_ref[:, cols] = result[:MAIN].astype(BF)
+        tail.append(result[MAIN:])
+    tail = jnp.concatenate(tail, axis=1)
+    pieces = [tail[t * 32:(t + 1) * 32].reshape(32, 8, 128) for t in range(2)]
+    out_ref[:, HALF:] = jnp.concatenate(pieces, axis=1).reshape(MAIN, 128).astype(BF)
+
+
 def expert_kernel(
     keep_ref, x_ref, gu0, gu1, gu2, gu3, gu4, gu5, dn0, dn1, dn2, dn3, dn4, dn5,
-    out_ref, rows, ends, gate_up, down, act, tail, sems,
+    out_ref, act, rows, ends, gate_up, down, sems,
 ):
-    copies = [
-        pltpu.make_async_copy(x_ref.at[:, :D], rows.at[:MAIN], sems.at[8]),
-        pltpu.make_async_copy(x_ref.at[:, D:], ends, sems.at[9]),
-    ]
-
-    def load(q, gu, dn):
-        return [
-            pltpu.make_async_copy(gu, gate_up.at[q], sems.at[q]),
-            pltpu.make_async_copy(dn, down.at[q * 256:(q + 1) * 256], sems.at[4 + q]),
-        ]
-
-    copies += load(0, gu0, dn0) + load(1, gu1, dn1)
-    for copy in copies:
-        copy.start()
-    keep = keep_ref[0] == 1
-
-    @pl.when(keep)
-    def _():
-        for copy in load(2, gu2, dn2) + load(3, gu5, dn5):
-            copy.start()
-
-    @pl.when(jnp.logical_not(keep))
-    def _():
-        for copy in load(2, gu3, dn3) + load(3, gu4, dn4):
-            copy.start()
-
-    copies += load(2, gu2, dn2) + load(3, gu4, dn4)
-    copies[1].wait()
+    copy_rows = pltpu.make_async_copy(x_ref.at[:, :D], rows.at[:MAIN], sems.at[8])
+    copy_ends = pltpu.make_async_copy(x_ref.at[:, D:], ends, sems.at[9])
+    copy_ends.start()
+    copy_rows.start()
+    copies = start_quarters(
+        keep_ref, (gu0, gu1, gu2, gu3, gu4, gu5), lambda q: gate_up.at[q], sems, 0
+    )
+    halves = [dn.at[:, :HALF] for dn in (dn0, dn1, dn2, dn3, dn4, dn5)]
+    down_copies = start_quarters(
+        keep_ref, halves, lambda q: down.at[q * 256:(q + 1) * 256], sems, 4
+    )
+    copy_ends.wait()
     for t in range(2):
         piece = ends[:, t * 128:(t + 1) * 128].astype(F32).reshape(32, D)
         rows[MAIN + t * 32:MAIN + (t + 1) * 32, :] = piece.astype(BF)
-    copies[0].wait()
+    copy_rows.wait()
     for q in range(4):
-        copies[2 + 2 * q].wait()
+        copies[q].wait()
         gate = dot(rows[...], gate_up[q, 0])
         up = dot(rows[...], gate_up[q, 1])
         act[:, q * 256:(q + 1) * 256] = (jax.nn.silu(gate) * up).astype(BF)
-    for q in range(4):
-        copies[3 + 2 * q].wait()
-    for n in range(4):
-        cols = slice(n * 512, (n + 1) * 512)
-        result = dot(act[...], down[:, cols])
-        out_ref[:, cols] = result[:MAIN].astype(BF)
-        tail[:, cols] = result[MAIN:]
+    for copy in down_copies:
+        copy.wait()
+    down_half(act[...], down, out_ref)
+
+
+def finish_kernel(keep_ref, act, dn0, dn1, dn2, dn3, dn4, dn5, out_ref, down, sems):
+    halves = [dn.at[:, HALF:] for dn in (dn0, dn1, dn2, dn3, dn4, dn5)]
+    copies = start_quarters(
+        keep_ref, halves, lambda q: down.at[q * 256:(q + 1) * 256], sems, 0
+    )
+    for copy in copies:
+        copy.wait()
+    down_half(act[...], down, out_ref)
+
+
+def combine_kernel(weight_ref, y_ref, own_ref, s1, s2, s3, tail):
+    ends = y_ref[:, HALF:].astype(F32).reshape(32, 16, 128)
     for t in range(2):
-        piece = tail[t * 32:(t + 1) * 32, :].reshape(MAIN, 128).astype(BF)
-        out_ref[:, D + t * 128:D + (t + 1) * 128] = piece
-
-
-def combine_kernel(weight_ref, y_ref, own_ref, s1, s2, s3, tail):
-    for t in range(2):
-        piece = y_ref[:, D + t * 128:D + (t + 1) * 128].astype(F32).reshape(32, D)
-        tail[t * 32:(t + 1) * 32, :] = piece.astype(BF)
-    for n in range(4):
+        tail[t * 32:(t + 1) * 32, :] = ends[:, t * 8:(t + 1) * 8].reshape(32, HALF).astype(BF)
+    for n in range(2):
         cols = slice(n * 512, (n + 1) * 512)
         rows = dot(weight_ref[:, :MAIN], y_ref[:, cols]) + dot(weight_ref[:, MAIN:], tail[:, cols])
-        rows = rows[:TOK] + rows[TOK:]
         own_ref[:, cols] = rows[:ROWS]
         s3[:, cols] = rows[ROWS:2 * ROWS].astype(BF)
         s2[:, cols] = rows[2 * ROWS:3 * ROWS].astype(BF)
         s1[:, cols] = rows[3 * ROWS:].astype(BF)
 
 
-BLOCKS_OUT = [out((ROWS, D), F32)] + [out((ROWS, D), BF)] * 3
+def blocks_out(columns):
+    return [out((ROWS, columns), F32)] + [out((ROWS, columns), BF)] * 3
 
 
 def seq_perm(dy, dz, dc):
@@ -347,7 +366,7 @@
     near = permute_all(pick(w_gate_up, w_down, 1 - (head & 1)), both, device_perm(near_target))
     tables = gather_head(jnp.concatenate([routes.astype(F32), gate_weights], axis=1))
     place_rows, weight = call(
-        routing_kernel, [SMEM] + [VMEM] * 4, [out((SLOTS, TOK), BF), out((2 * TOK, SLOTS), BF)]
+        routing_kernel, [SMEM] + [VMEM] * 4, [out((SLOTS, TOK), BF), out((TOK, SLOTS), BF)]
     )(head.astype(jnp.int32)[None], *tables)
 
     normed, key, value, own_state, send_state, zero = call(
@@ -381,7 +400,8 @@
     rows_y = exchange(total.astype(BF), (1, 0))
 
     w_query = [
-        lax.dynamic_slice_in_dim(w_qkv, zero[0] + start, D // 2, 0)[:, 0] for start in (0, D // 2)
+        lax.dynamic_slice_in_dim(w_qkv, zero[0] + start, D // 2, 0)[:, 0]
+        for start in (0, D // 2)
     ]
     query, local = call(
         local_kernel, [VMEM] * 5, [out((TOK, WIDE), BF), out((TOK, WIDE), F32)]
@@ -390,7 +410,7 @@
     blocks = call(
         attend_kernel,
         [SMEM] + [VMEM] * 8,
-        BLOCKS_OUT,
+        blocks_out(D),
         [pltpu.VMEM((TOK, WIDE), BF), pltpu.VMEM((TOK, WIDE), BF)],
     )(place, prefix, *rows_y, query, local, out_gain[None, :], w_out)
     attn_rows = scatter_head(blocks)
@@ -403,26 +423,34 @@
     )(place_rows, *tokens)[0]
     received = lax.all_to_all(sent.reshape(32, 16, PACKED), "seq", 0, 0, tiled=True)
     keep = (head // 2 == core).astype(jnp.int32)[None]
-    results = call(
+    gate_ups = [p[0] for p in pieces]
+    downs = [p[1] for p in pieces]
+    first, act = call(
         expert_kernel,
         [SMEM, HBM] + [ANY] * 12,
-        [out((MAIN, PACKED), BF)],
+        [out((MAIN, HALF + 128), BF), out((SLOTS, 1024), BF)],
         [
             pltpu.VMEM((SLOTS, D), BF),
             pltpu.VMEM((MAIN, 256), BF),
             pltpu.VMEM((4, 2, D, 256), BF),
-            pltpu.VMEM((1024, D), BF),
-            pltpu.VMEM((SLOTS, 1024), BF),
-            pltpu.VMEM((64, D), F32),
+            pltpu.VMEM((1024, HALF), BF),
             pltpu.SemaphoreType.DMA((10,)),
         ],
-    )(keep, received.reshape(MAIN, PACKED), *[p[0] for p in pieces], *[p[1] for p in pieces])[0]
-    back = lax.all_to_all(results.reshape(32, 16, PACKED), "seq", 0, 0, tiled=True)
-    blocks = call(
-        combine_kernel, [VMEM] * 2, BLOCKS_OUT, [pltpu.VMEM((64, D), BF)]
-    )(weight, back.reshape(MAIN, PACKED))
-    moe_sum = scatter_head(blocks)
-    return (resid + moe_sum).astype(BF)
+    )(keep, received.reshape(MAIN, PACKED), *gate_ups, *downs)
+    second = call(
+        finish_kernel,
+        [SMEM, VMEM] + [ANY] * 6,
+        [out((MAIN, HALF + 128), BF)],
+        [pltpu.VMEM((1024, HALF), BF), pltpu.SemaphoreType.DMA((4,))],
+    )(keep, act, *downs)[0]
+    moe_sum = []
+    for results in (first, second):
+        back = lax.all_to_all(results.reshape(32, 16, HALF + 128), "seq", 0, 0, tiled=True)
+        blocks = call(
+            combine_kernel, [VMEM] * 2, blocks_out(HALF), [pltpu.VMEM((64, HALF), BF)]
+        )(weight, back.reshape(MAIN, HALF + 128))
+        moe_sum.append(scatter_head(blocks))
+    return (resid + jnp.concatenate(moe_sum, axis=1)).astype(BF)
 
 
 def solution(mesh):

time: 240 us -> 240 us (level)
  blocking collectives: 37.6 us -> 0 us
  starting transfers between devices: 53.1 us -> 68.3 us
  waiting for transfers between devices: 81.7 us -> 96 us
  Pallas kernels: 43.6 us -> 47.9 us
    all_to_all x1 -> x0, blocking collectives: 37.6 us -> none  [on_device(): lax.all_to_all(results.reshape(32, 16, PACKED), 'seq', 0, 0, tiled=True)]
    all_to_all x0 -> x2, waiting for transfers between devices: none -> 21.7 us  [on_device(): lax.all_to_all(results.reshape(32, 16, HALF + 128), 'seq', 0, 0, tiled=True)]
    all_to_all x0 -> x2, starting transfers between devices: none -> 12.3 us  [on_device(): lax.all_to_all(results.reshape(32, 16, HALF + 128), 'seq', 0, 0, tiled=True)]
    ppermute x6 -> x9, waiting for transfers between devices: 35.1 us -> 27.5 us  [scatter_head(): total = total + lax.ppermute(blocks[k], 'head', head_perm(k)).astype(F32)]
    pallas_call x4 -> x6, Pallas kernels: 23.8 us -> 28.1 us  [the longest x1 10.4 us: on_device(): call(expert_kernel, [SMEM, HBM] + [ANY] * 12, [out((MAIN, HALF + 128), BF...]
    ppermute x6 -> x9, starting transfers between devices: 5.86 us -> 8.78 us  [scatter_head(): total = total + lax.ppermute(blocks[k], 'head', head_perm(k)).astype(F32)]
  transfers between devices with their start and end apart: 30 -> 35, of which waited for: 13 -> 14; matrix products, arithmetic and copies ran while one was open for 3% -> 3% of each run, Pallas kernels for 9% -> 14%
where the time goes in v2:
time: 240 us; the launch traced here: 235 us
  waiting for transfers between devices  96 us (40%)
  starting transfers between devices  68.3 us (28%)
  Pallas kernels  47.9 us (20%)
  local copies, waits for them, and re-layouts  11.8 us (5%)
  other arithmetic  6.76 us (3%)
  between operations  4.47 us (2%)
    ppermute x6, waiting for transfers between devices, gather_head(): lax.ppermute(array, 'head', head_perm(k))  31.6 us
    ppermute x9, waiting for transfers between devices, scatter_head(): total = total + lax.ppermute(blocks[k], 'head', head_perm(k)).astype(F32)  27.5 us
    all_to_all x2, waiting for transfers between devices, on_device(): lax.all_to_all(results.reshape(32, 16, HALF + 128), 'seq', 0, 0, tiled=True)  21.7 us
    ppermute x8, starting transfers between devices, permute_all(): return [lax.ppermute(a, axes, perm) for a in arrays]  20.1 us
    all_to_all x2, starting transfers between devices, on_device(): lax.all_to_all(results.reshape(32, 16, HALF + 128), 'seq', 0, 0, tiled=True)  12.3 us
    pallas_call x1, Pallas kernels, on_device(): call(expert_kernel, [SMEM, HBM] + [ANY] * 12, [out((MAIN, HALF + 128), BF...  10.4 us
    ppermute x9, starting transfers between devices, scatter_head(): total = total + lax.ppermute(blocks[k], 'head', head_perm(k)).astype(F32)  8.78 us
    ppermute x6, starting transfers between devices, exchange(): lax.ppermute(array, 'seq', seq_perm(dy * k, dz * k, 0))  8.6 us
  transfers between devices with their start and end apart: 35, of which 14 were waited for; matrix products, arithmetic and copies ran while one was open for 3% of the time, Pallas kernels for 14%

profile of v2, /device:TPU:33, one launch (start us, length us, event | category | flops | bytes accessed | tf_op | source)
XLA Modules:
  0.0 235.2 jit_solution(2323626872256416735)
XLA Ops:
  0.0 4.5 %slice_bitcast_fusion = (bf16[2048,512]{1,0:T(8,128)(2,1)}, bf16[2048,512]{1,0:T(8,128)(2,1)}) fusion(bf16[2048,3,512]{2,0,1:T(8,128)(2,1)} %param.12), kind=kLoop, calls=%fused_computation | loop fusion | bytes 8388608 | tf_op jit(solution)/shard_map/squeeze | solution.py:384
  4.5 5.2 %shard_map.100 = (bf16[256,2048]{1,0:T(8,128)(2,1)}, bf16[256,512]{1,0:T(8,128)(2,1)}, bf16[256,512]{1,0:T(8,128)(2,1)}, f32[4,128,128]{2,1,0:T(8,128)}, bf16[4,128,128]{2,1,0:T(8,128)(2,1)}, /*index=5*/s32[1]{0:T(128)}) custom-call(bf16[256,2048]{1,0:T(8,128)(2,1)} %x_ref.1, f32[1,2048]{1,0:T(1,128)} %bitcast.28, ...), custom_call_target="tpu_custom_call" | custom-call | tf_op jit(solution)/shard_map/pallas_call | solution.py:372
  17.5 3.5 %pick.2 = (bf16[2,2048,256]{2,1,0:T(8,128)(2,1)}, bf16[256,2048]{1,0:T(8,128)(2,1)}) custom-call(s32[1]{0:T(128)} %bitcast.12.index_ref, bf16[2,2,2048,256]{3,2,1,0:T(8,128)(2,1)} %gu_ref.3, bf16[2,256,2048]{2,1,0:T(8,128)(2,1)} %dn_ref.3), custom_call_target="tpu_custom_call" | custom-call | tf_op jit(solution)/shard_map/pick/pallas_call | solution.py:330
  21.0 3.6 %collective-permute-start.16 = (bf16[2,2048,256]{2,1,0:T(8,128)(2,1)}, bf16[2,2048,256]{2,1,0:T(8,128)(2,1)}, u32[]{:S(2)}, u32[]{:S(2)}) collective-permute-start(bf16[2,2048,256]{2,1,0:T(8,128)(2,1)} %get-tuple-element.47), channel_id=1, source_target_pairs={{0,1},{1,4},{2,5},{3,0},{4,3},{5,6},{6,7},{7,2},{8,9},{9,12},{10,1... | collective-permute-start | bytes 6291464 | tf_op jit(solution)/shard_map/ppermute | solution.py:310
  25.4 3.6 %pick.3 = (bf16[2,2048,256]{2,1,0:T(8,128)(2,1)}, bf16[256,2048]{1,0:T(8,128)(2,1)}) custom-call(s32[1]{0:T(128)} %bitcast.13.index_ref, bf16[2,2,2048,256]{3,2,1,0:T(8,128)(2,1)} %gu_ref.3, bf16[2,256,2048]{2,1,0:T(8,128)(2,1)} %dn_ref.3), custom_call_target="tpu_custom_call" | custom-call | tf_op jit(solution)/shard_map/pick/pallas_call | solution.py:330
  42.6 3.9 %shard_map.101 = (bf16[256,512]{1,0:T(8,128)(2,1)}, f32[256,512]{1,0:T(8,128)}) custom-call(bf16[256,2048]{1,0:T(8,128)(2,1)} %get-tuple-element.35.normed_ref, bf16[1024,512]{1,0:T(8,128)(2,1)} %get-tuple-element.64.upper_ref, bf16[1024,512]{1,0:T(8,128)(2,1)} %get-tuple-element.63.lower_ref, bf16[256,512]{1,0:T(8,128)(2,1)} %get-tuple-element.37.k_ref, ...), custom_call_target="tpu_custom_call" | custom-call | tf_op jit(solution)/shard_map/pallas_call | solution.py:406
  48.5 4.3 %shard_map.102 = (f32[64,2048]{1,0:T(8,128)}, bf16[64,2048]{1,0:T(8,128)(2,1)}, bf16[64,2048]{1,0:T(8,128)(2,1)}, bf16[64,2048]{1,0:T(8,128)(2,1)}) custom-call(s32[2]{0:T(128)} %pad_add_fusion.place_ref, f32[4,128,128]{2,1,0:T(8,128)} %get-tuple-element.68.prefix_ref, bf16[4,128,128]{2,1,0:T(8,128)(2,1)} %copy-done.10, bf16[4,128,128]{2,1,0:T(8,128)(2,1)} %copy-done.9, ...), custom_call_target="tpu_custom_call" | custom-call | tf_op jit(solution)/shard_map/pallas_call | solution.py:410
  55.6 22.6 %collective-permute-done.7 = bf16[64,2048]{1,0:T(8,128)(2,1)S(1)} collective-permute-done((bf16[64,2048]{1,0:T(8,128)(2,1)}, bf16[64,2048]{1,0:T(8,128)(2,1)S(1)}, u32[]{:S(2)}, u32[]{:S(2)}) %collective-permute-start.7) | collective-permute-done | bytes 262176 | tf_op jit(solution)/shard_map/ppermute | solution.py:352
  78.2 3.8 %collective-permute-start.21 = (bf16[256,2048]{1,0:T(8,128)(2,1)}, bf16[256,2048]{1,0:T(8,128)(2,1)}, u32[]{:S(2)}, u32[]{:S(2)}) collective-permute-start(bf16[256,2048]{1,0:T(8,128)(2,1)} %get-tuple-element.49), channel_id=1, source_target_pairs={{0,1},{1,4},{2,5},{3,0},{4,3},{5,6},{6,7},{7,2},{8,9},{9,12},{10,1... | collective-permute-start | bytes 3145736 | tf_op jit(solution)/shard_map/ppermute | solution.py:310
  86.5 13.8 %collective-permute-done.12.t3 = f32[64,16]{1,0:T(8,128)S(1)} collective-permute-done((f32[64,16]{1,0:T(8,128)S(1)}, f32[64,16]{1,0:T(8,128)S(1)}, u32[]{:S(2)}, u32[]{:S(2)}) %collective-permute-start.12) | collective-permute-done | bytes 4128 | tf_op jit(solution)/shard_map/ppermute | solution.py:346
  101.3 3.6 %collective-permute-done.11.t2 = f32[64,16]{1,0:T(8,128)S(1)} collective-permute-done((f32[64,16]{1,0:T(8,128)S(1)}, f32[64,16]{1,0:T(8,128)S(1)}, u32[]{:S(2)}, u32[]{:S(2)}) %collective-permute-start.11) | collective-permute-done | bytes 4128 | tf_op jit(solution)/shard_map/ppermute | solution.py:346
  105.2 3.7 %collective-permute-done.10.t1 = f32[64,16]{1,0:T(8,128)S(1)} collective-permute-done((f32[64,16]{1,0:T(8,128)S(1)}, f32[64,16]{1,0:T(8,128)S(1)}, u32[]{:S(2)}, u32[]{:S(2)}) %collective-permute-start.10) | collective-permute-done | bytes 4128 | tf_op jit(solution)/shard_map/ppermute | solution.py:346
  116.9 7.4 %collective-permute-done.13.t1 = bf16[64,2048]{1,0:T(8,128)(2,1)S(1)} collective-permute-done((bf16[64,2048]{1,0:T(8,128)(2,1)S(1)}, bf16[64,2048]{1,0:T(8,128)(2,1)S(1)}, u32[]{:S(2)}, u32[]{:S(2)}) %collective-permute-start.13) | collective-permute-done | bytes 262176 | tf_op jit(solution)/shard_map/ppermute | solution.py:346
  128.5 6.2 %all-to-all-start = ((bf16[32,16,2304]{2,1,0:T(8,128)(2,1)}), bf16[32,16,2304]{2,1,0:T(8,128)(2,1)S(1)}, u32[]{:S(2)}, u32[]{:S(2)}) async-start(bf16[32,16,2304]{2,1,0:T(8,128)(2,1)} %bitcast.23), calls=%async_computation | async-start | bytes 4718592 | tf_op jit(solution)/shard_map/all_to_all | solution.py:424
  140.4 3.5 %collective-permute-start.17 = (bf16[2,2048,256]{2,1,0:T(8,128)(2,1)}, bf16[2,2048,256]{2,1,0:T(8,128)(2,1)}, u32[]{:S(2)}, u32[]{:S(2)}) collective-permute-start(bf16[2,2048,256]{2,1,0:T(8,128)(2,1)} %collective-permute-done.16.gu0), channel_id=1, source_target_pairs={{0,4},{4,0},{8,12},{12,8},{16,20},{20,16},{24,28},{28,24},{32,36},... | collective-permute-start | bytes 6291464 | tf_op jit(solution)/shard_map/ppermute | solution.py:310
  147.2 5.6 %collective-permute-done.24.dn4 = bf16[256,2048]{1,0:T(8,128)(2,1)} collective-permute-done((bf16[256,2048]{1,0:T(8,128)(2,1)}, bf16[256,2048]{1,0:T(8,128)(2,1)}, u32[]{:S(2)}, u32[]{:S(2)}) %collective-permute-start.24) | collective-permute-done | bytes 1048608 | tf_op jit(solution)/shard_map/ppermute | solution.py:388
  157.8 6.1 %all-to-all-done = bf16[32,16,2304]{2,1,0:T(8,128)(2,1)S(1)} async-done(((bf16[32,16,2304]{2,1,0:T(8,128)(2,1)}), bf16[32,16,2304]{2,1,0:T(8,128)(2,1)S(1)}, u32[]{:S(2)}, u32[]{:S(2)}) %all-to-all-start) | async-done | bytes 2359328 | tf_op jit(solution)/shard_map/all_to_all | solution.py:424
  165.3 10.4 %shard_map.105 = (bf16[512,1152]{1,0:T(8,128)(2,1)}, bf16[576,1024]{1,0:T(8,128)(2,1)}) custom-call(s32[1]{0:T(128)} %bitcast.9.keep_ref, bf16[512,2304]{1,0:T(8,128)(2,1)} %bitcast.22, bf16[2,2048,256]{2,1,0:T(8,128)(2,1)} %collective-permute-done.16.gu0, bf16[2,2048,256]{2,1,0:T(8,128)(2,1)} %collective-permute-done.17.gu1, ...), custom_call_target="tpu_custom_call" | custom-call | tf_op jit(solution)/shard_map/pallas_call | solution.py:428
  175.8 6.4 %all-to-all-start.1 = ((bf16[32,16,1152]{2,1,0:T(8,128)(2,1)}), bf16[32,16,1152]{2,1,0:T(8,128)(2,1)S(1)}, u32[]{:S(2)}, u32[]{:S(2)}) async-start(bf16[32,16,1152]{2,1,0:T(8,128)(2,1)} %bitcast.27), calls=%async_computation.1 | async-start | bytes 2359296 | tf_op jit(solution)/shard_map/all_to_all | solution.py:448
  182.1 5.3 %shard_map.107 = bf16[512,1152]{1,0:T(8,128)(2,1)} custom-call(s32[1]{0:T(128)} %bitcast.9.keep_ref, bf16[576,1024]{1,0:T(8,128)(2,1)} %get-tuple-element.56.act, bf16[256,2048]{1,0:T(8,128)(2,1)} %collective-permute-done.21.dn0, bf16[256,2048]{1,0:T(8,128)(2,1)} %collective-permute-done.22.dn1, bf16[256,2048]{1,0:T(8,128)(2,1)} %get-tuple-element.50.dn2, ...), custom_call_target="tpu_custom_call" | custom-call | tf_op jit(solution)/shard_map/pallas_call | solution.py:440
  187.4 11.1 %all-to-all-done.1 = bf16[32,16,1152]{2,1,0:T(8,128)(2,1)S(1)} async-done(((bf16[32,16,1152]{2,1,0:T(8,128)(2,1)}), bf16[32,16,1152]{2,1,0:T(8,128)(2,1)S(1)}, u32[]{:S(2)}, u32[]{:S(2)}) %all-to-all-start.1) | async-done | bytes 1179680 | tf_op jit(solution)/shard_map/all_to_all | solution.py:448
  198.5 5.9 %all-to-all-start.2 = ((bf16[32,16,1152]{2,1,0:T(8,128)(2,1)}), bf16[32,16,1152]{2,1,0:T(8,128)(2,1)S(1)}, u32[]{:S(2)}, u32[]{:S(2)}) async-start(bf16[32,16,1152]{2,1,0:T(8,128)(2,1)} %bitcast.24), calls=%async_computation.2 | async-start | bytes 2359296 | tf_op jit(solution)/shard_map/all_to_all | solution.py:448
  210.2 10.6 %all-to-all-done.2 = bf16[32,16,1152]{2,1,0:T(8,128)(2,1)S(1)} async-done(((bf16[32,16,1152]{2,1,0:T(8,128)(2,1)}), bf16[32,16,1152]{2,1,0:T(8,128)(2,1)S(1)}, u32[]{:S(2)}, u32[]{:S(2)}) %all-to-all-start.2) | async-done | bytes 1179680 | tf_op jit(solution)/shard_map/all_to_all | solution.py:448
  228.6 4.9 %collective-permute-done.29 = bf16[64,1024]{1,0:T(8,128)(2,1)S(1)} collective-permute-done((bf16[64,1024]{1,0:T(8,128)(2,1)}, bf16[64,1024]{1,0:T(8,128)(2,1)S(1)}, u32[]{:S(2)}, u32[]{:S(2)}) %collective-permute-start.29) | collective-permute-done | bytes 131104 | tf_op jit(solution)/shard_map/ppermute | solution.py:352
  (107 shorter events, 71.4 us)
Async XLA Ops:
  12.6 22.0 %collective-permute-start.3 = (bf16[4,128,128]{2,1,0:T(8,128)(2,1)S(1)}, bf16[4,128,128]{2,1,0:T(8,128)(2,1)S(1)}, u32[]{:S(2)}, u32[]{:S(2)}) collective-permute-start(bf16[4,128,128]{2,1,0:T(8,128)(2,1)S(1)} %fusion.5), channel_id=1, source_target_pairs={{0,24},{4,28},{8,0},{12,4},{16,8},{20,12},{24,16},{28,20},{32,56},... | collective-permute-start | bytes 393224 | tf_op jit(solution)/shard_map/ppermute | solution.py:342
  12.7 21.9 %collective-permute-start.2 = (bf16[4,128,128]{2,1,0:T(8,128)(2,1)S(1)}, bf16[4,128,128]{2,1,0:T(8,128)(2,1)S(1)}, u32[]{:S(2)}, u32[]{:S(2)}) collective-permute-start(bf16[4,128,128]{2,1,0:T(8,128)(2,1)S(1)} %fusion.5), channel_id=1, source_target_pairs={{0,16},{4,20},{8,24},{12,28},{16,0},{20,4},{24,8},{28,12},{32,48},... | collective-permute-start | bytes 393224 | tf_op jit(solution)/shard_map/ppermute | solution.py:342
  15.5 19.1 %collective-permute-start.1 = (bf16[4,128,128]{2,1,0:T(8,128)(2,1)S(1)}, bf16[4,128,128]{2,1,0:T(8,128)(2,1)S(1)}, u32[]{:S(2)}, u32[]{:S(2)}) collective-permute-start(bf16[4,128,128]{2,1,0:T(8,128)(2,1)S(1)} %fusion.5), channel_id=1, source_target_pairs={{0,8},{4,12},{8,16},{12,20},{16,24},{20,28},{24,0},{28,4},{32,40},... | collective-permute-start | bytes 393224 | tf_op jit(solution)/shard_map/ppermute | solution.py:342
  21.0 119.4 %collective-permute-start.16 = (bf16[2,2048,256]{2,1,0:T(8,128)(2,1)}, bf16[2,2048,256]{2,1,0:T(8,128)(2,1)}, u32[]{:S(2)}, u32[]{:S(2)}) collective-permute-start(bf16[2,2048,256]{2,1,0:T(8,128)(2,1)} %get-tuple-element.47), channel_id=1, source_target_pairs={{0,1},{1,4},{2,5},{3,0},{4,3},{5,6},{6,7},{7,2},{8,9},{9,12},{10,1... | collective-permute-start | bytes 6291464 | tf_op jit(solution)/shard_map/ppermute | solution.py:310
  28.9 115.0 %collective-permute-start.19 = (bf16[2,2048,256]{2,1,0:T(8,128)(2,1)}, bf16[2,2048,256]{2,1,0:T(8,128)(2,1)}, u32[]{:S(2)}, u32[]{:S(2)}) collective-permute-start(bf16[2,2048,256]{2,1,0:T(8,128)(2,1)} %get-tuple-element.48.gu2), channel_id=1, source_target_pairs={{2,4},{3,5},{4,2},{5,3},{10,12},{11,13},{12,10},{13,11},{18,20},{1... | collective-permute-start | bytes 6291464 | tf_op jit(solution)/shard_map/ppermute | solution.py:389
  35.5 11.7 %collective-permute-start.6 = (bf16[4,128,128]{2,1,0:T(8,128)(2,1)S(1)}, bf16[4,128,128]{2,1,0:T(8,128)(2,1)S(1)}, u32[]{:S(2)}, u32[]{:S(2)}) collective-permute-start(bf16[4,128,128]{2,1,0:T(8,128)(2,1)S(1)} %get-tuple-element.67), channel_id=1, source_target_pairs={{0,96},{4,100},{8,104},{12,108},{16,112},{20,116},{24,120},{28,124... | collective-permute-start | bytes 393224 | tf_op jit(solution)/shard_map/ppermute | solution.py:342
  52.8 25.4 %collective-permute-start.7 = (bf16[64,2048]{1,0:T(8,128)(2,1)}, bf16[64,2048]{1,0:T(8,128)(2,1)S(1)}, u32[]{:S(2)}, u32[]{:S(2)}) collective-permute-start(bf16[64,2048]{1,0:T(8,128)(2,1)} %get-tuple-element.42), channel_id=1, source_target_pairs={{0,1},{1,2},{2,3},{3,0},{4,5},{5,6},{6,7},{7,4},{8,9},{9,10},{10,1... | collective-permute-start | bytes 786440 | tf_op jit(solution)/shard_map/ppermute | solution.py:352
  53.1 28.8 %collective-permute-start.8 = (bf16[64,2048]{1,0:T(8,128)(2,1)}, bf16[64,2048]{1,0:T(8,128)(2,1)S(1)}, u32[]{:S(2)}, u32[]{:S(2)}) collective-permute-start(bf16[64,2048]{1,0:T(8,128)(2,1)} %get-tuple-element.43), channel_id=1, source_target_pairs={{0,2},{1,3},{2,0},{3,1},{4,6},{5,7},{6,4},{7,5},{8,10},{9,11},{10,... | collective-permute-start | bytes 786440 | tf_op jit(solution)/shard_map/ppermute | solution.py:352
  54.2 27.8 %collective-permute-start.9 = (bf16[64,2048]{1,0:T(8,128)(2,1)}, bf16[64,2048]{1,0:T(8,128)(2,1)S(1)}, u32[]{:S(2)}, u32[]{:S(2)}) collective-permute-start(bf16[64,2048]{1,0:T(8,128)(2,1)} %get-tuple-element.44), channel_id=1, source_target_pairs={{0,3},{1,0},{2,1},{3,2},{4,7},{5,4},{6,5},{7,6},{8,11},{9,8},{10,9... | collective-permute-start | bytes 786440 | tf_op jit(solution)/shard_map/ppermute | solution.py:352
  78.2 60.9 %collective-permute-start.21 = (bf16[256,2048]{1,0:T(8,128)(2,1)}, bf16[256,2048]{1,0:T(8,128)(2,1)}, u32[]{:S(2)}, u32[]{:S(2)}) collective-permute-start(bf16[256,2048]{1,0:T(8,128)(2,1)} %get-tuple-element.49), channel_id=1, source_target_pairs={{0,1},{1,4},{2,5},{3,0},{4,3},{5,6},{6,7},{7,2},{8,9},{9,12},{10,1... | collective-permute-start | bytes 3145736 | tf_op jit(solution)/shard_map/ppermute | solution.py:310
  83.5 26.3 %collective-permute-start.15 = (bf16[64,2048]{1,0:T(8,128)(2,1)S(1)}, bf16[64,2048]{1,0:T(8,128)(2,1)S(1)}, u32[]{:S(2)}, u32[]{:S(2)}) collective-permute-start(bf16[64,2048]{1,0:T(8,128)(2,1)S(1)} %multiply_convert_fusion.t0), channel_id=1, source_target_pairs={{0,3},{1,0},{2,1},{3,2},{4,7},{5,4},{6,5},{7,6},{8,11},{9,8},{10,9... | collective-permute-start | bytes 786440 | tf_op jit(solution)/shard_map/ppermute | solution.py:346
  86.4 13.9 %collective-permute-start.12 = (f32[64,16]{1,0:T(8,128)S(1)}, f32[64,16]{1,0:T(8,128)S(1)}, u32[]{:S(2)}, u32[]{:S(2)}) collective-permute-start(f32[64,16]{1,0:T(8,128)S(1)} %copy.16.t0), channel_id=1, source_target_pairs={{0,3},{1,0},{2,1},{3,2},{4,7},{5,4},{6,5},{7,6},{8,11},{9,8},{10,9... | collective-permute-start | bytes 12296 | tf_op jit(solution)/shard_map/ppermute | solution.py:346
  109.8 14.4 %collective-permute-start.13 = (bf16[64,2048]{1,0:T(8,128)(2,1)S(1)}, bf16[64,2048]{1,0:T(8,128)(2,1)S(1)}, u32[]{:S(2)}, u32[]{:S(2)}) collective-permute-start(bf16[64,2048]{1,0:T(8,128)(2,1)S(1)} %multiply_convert_fusion.t0), channel_id=1, source_target_pairs={{0,1},{1,2},{2,3},{3,0},{4,5},{5,6},{6,7},{7,4},{8,9},{9,10},{10,1... | collective-permute-start | bytes 786440 | tf_op jit(solution)/shard_map/ppermute | solution.py:346
  128.5 35.5 %all-to-all-start = ((bf16[32,16,2304]{2,1,0:T(8,128)(2,1)}), bf16[32,16,2304]{2,1,0:T(8,128)(2,1)S(1)}, u32[]{:S(2)}, u32[]{:S(2)}) async-start(bf16[32,16,2304]{2,1,0:T(8,128)(2,1)} %bitcast.23), calls=%async_computation | async-start | bytes 4718592 | tf_op jit(solution)/shard_map/all_to_all | solution.py:424
  134.7 18.1 %collective-permute-start.24 = (bf16[256,2048]{1,0:T(8,128)(2,1)}, bf16[256,2048]{1,0:T(8,128)(2,1)}, u32[]{:S(2)}, u32[]{:S(2)}) collective-permute-start(bf16[256,2048]{1,0:T(8,128)(2,1)} %get-tuple-element.50.dn2), channel_id=1, source_target_pairs={{2,4},{3,5},{4,2},{5,3},{10,12},{11,13},{12,10},{13,11},{18,20},{1... | collective-permute-start | bytes 3145736 | tf_op jit(solution)/shard_map/ppermute | solution.py:388
  137.8 15.0 %collective-permute-start.23 = (bf16[256,2048]{1,0:T(8,128)(2,1)}, bf16[256,2048]{1,0:T(8,128)(2,1)}, u32[]{:S(2)}, u32[]{:S(2)}) collective-permute-start(bf16[256,2048]{1,0:T(8,128)(2,1)} %get-tuple-element.50.dn2), channel_id=1, source_target_pairs={{0,4},{1,5},{6,2},{7,3},{8,12},{9,13},{14,10},{15,11},{16,20},{17,... | collective-permute-start | bytes 3145736 | tf_op jit(solution)/shard_map/ppermute | solution.py:310
  139.1 18.7 %collective-permute-start.18 = (bf16[2,2048,256]{2,1,0:T(8,128)(2,1)}, bf16[2,2048,256]{2,1,0:T(8,128)(2,1)}, u32[]{:S(2)}, u32[]{:S(2)}) collective-permute-start(bf16[2,2048,256]{2,1,0:T(8,128)(2,1)} %get-tuple-element.48.gu2), channel_id=1, source_target_pairs={{0,4},{1,5},{6,2},{7,3},{8,12},{9,13},{14,10},{15,11},{16,20},{17,... | collective-permute-start | bytes 6291464 | tf_op jit(solution)/shard_map/ppermute | solution.py:310
  140.4 23.5 %collective-permute-start.17 = (bf16[2,2048,256]{2,1,0:T(8,128)(2,1)}, bf16[2,2048,256]{2,1,0:T(8,128)(2,1)}, u32[]{:S(2)}, u32[]{:S(2)}) collective-permute-start(bf16[2,2048,256]{2,1,0:T(8,128)(2,1)} %collective-permute-done.16.gu0), channel_id=1, source_target_pairs={{0,4},{4,0},{8,12},{12,8},{16,20},{20,16},{24,28},{28,24},{32,36},... | collective-permute-start | bytes 6291464 | tf_op jit(solution)/shard_map/ppermute | solution.py:310
  143.9 20.0 %collective-permute-start.20 = (bf16[2,2048,256]{2,1,0:T(8,128)(2,1)}, bf16[2,2048,256]{2,1,0:T(8,128)(2,1)}, u32[]{:S(2)}, u32[]{:S(2)}) collective-permute-start(bf16[2,2048,256]{2,1,0:T(8,128)(2,1)} %collective-permute-done.19.gu4), channel_id=1, source_target_pairs={{2,6},{3,7},{4,0},{5,1},{10,14},{11,15},{12,8},{13,9},{18,22},{19,... | collective-permute-start | bytes 6291464 | tf_op jit(solution)/shard_map/ppermute | solution.py:310
  175.8 22.8 %all-to-all-start.1 = ((bf16[32,16,1152]{2,1,0:T(8,128)(2,1)}), bf16[32,16,1152]{2,1,0:T(8,128)(2,1)S(1)}, u32[]{:S(2)}, u32[]{:S(2)}) async-start(bf16[32,16,1152]{2,1,0:T(8,128)(2,1)} %bitcast.27), calls=%async_computation.1 | async-start | bytes 2359296 | tf_op jit(solution)/shard_map/all_to_all | solution.py:448
  198.5 22.2 %all-to-all-start.2 = ((bf16[32,16,1152]{2,1,0:T(8,128)(2,1)}), bf16[32,16,1152]{2,1,0:T(8,128)(2,1)S(1)}, u32[]{:S(2)}, u32[]{:S(2)}) async-start(bf16[32,16,1152]{2,1,0:T(8,128)(2,1)} %bitcast.24), calls=%async_computation.2 | async-start | bytes 2359296 | tf_op jit(solution)/shard_map/all_to_all | solution.py:448
  207.2 18.8 %collective-permute-start.26 = (bf16[64,1024]{1,0:T(8,128)(2,1)}, bf16[64,1024]{1,0:T(8,128)(2,1)S(1)}, u32[]{:S(2)}, u32[]{:S(2)}) collective-permute-start(bf16[64,1024]{1,0:T(8,128)(2,1)} %get-tuple-element.53), channel_id=1, source_target_pairs={{0,1},{1,2},{2,3},{3,0},{4,5},{5,6},{6,7},{7,4},{8,9},{9,10},{10,1... | collective-permute-start | bytes 393224 | tf_op jit(solution)/shard_map/ppermute | solution.py:352
  207.2 20.3 %collective-permute-start.27 = (bf16[64,1024]{1,0:T(8,128)(2,1)}, bf16[64,1024]{1,0:T(8,128)(2,1)S(1)}, u32[]{:S(2)}, u32[]{:S(2)}) collective-permute-start(bf16[64,1024]{1,0:T(8,128)(2,1)} %get-tuple-element.54), channel_id=1, source_target_pairs={{0,2},{1,3},{2,0},{3,1},{4,6},{5,7},{6,4},{7,5},{8,10},{9,11},{10,... | collective-permute-start | bytes 393224 | tf_op jit(solution)/shard_map/ppermute | solution.py:352
  208.7 18.8 %collective-permute-start.28 = (bf16[64,1024]{1,0:T(8,128)(2,1)}, bf16[64,1024]{1,0:T(8,128)(2,1)S(1)}, u32[]{:S(2)}, u32[]{:S(2)}) collective-permute-start(bf16[64,1024]{1,0:T(8,128)(2,1)} %get-tuple-element.55), channel_id=1, source_target_pairs={{0,3},{1,0},{2,1},{3,2},{4,7},{5,4},{6,5},{7,6},{8,11},{9,8},{10,9... | collective-permute-start | bytes 393224 | tf_op jit(solution)/shard_map/ppermute | solution.py:352
  (29 other events, 299.0 us)

commit v3 on v1

--- a/solution.py
+++ b/solution.py
@@ -63,12 +63,12 @@
     return slice(h * DH, (h + 1) * DH)
 
 
-def front_kernel(x_ref, gain_ref, wk_ref, wv_ref, normed_ref, k_ref, v_ref, state_ref, send_ref, zero_ref, wk, wv, sems):
-    zero_ref[0] = 0
-    copy_k = pltpu.make_async_copy(wk_ref, wk, sems.at[0])
-    copy_v = pltpu.make_async_copy(wv_ref, wv, sems.at[1])
+def front_kernel(x_ref, gain_ref, w_ref, normed_ref, k_ref, v_ref, send_ref, zero_ref, wk, wv, sems):
+    copy_k = pltpu.make_async_copy(w_ref.at[1], wk, sems.at[0])
+    copy_v = pltpu.make_async_copy(w_ref.at[2], wv, sems.at[1])
     copy_k.start()
     copy_v.start()
+    zero_ref[0] = 0
     normed = rms_norm(x_ref[...].astype(F32), gain_ref[...]).astype(BF)
     normed_ref[...] = normed
     copy_k.wait()
@@ -79,16 +79,24 @@
     v_ref[...] = value
     for h in range(HEADS):
         state = dot_rows(key[:, of_head(h)], value[:, of_head(h)])
-        state_ref[h] = state
-        send_ref[h] = state.astype(BF)
-
-
-def local_kernel(normed_ref, upper_ref, lower_ref, k_ref, v_ref, q_ref, local_ref):
-    query = dot(normed_ref[:, :D // 2], upper_ref[...]) + dot(normed_ref[:, D // 2:], lower_ref[...])
-    query = query.astype(BF)
-    q_ref[...] = query
+        send_ref[of_head(h), :] = state.astype(BF)
+
+
+def prefix_kernel(states_ref, out_ref):
+    total = jnp.zeros((16, DH), F32)
+    for s in range(32):
+        out_ref[s] = total.astype(BF)
+        total = total + states_ref[s].astype(F32)
+
+
+def local_kernel(normed_ref, w_ref, k_ref, v_ref, q_ref, local_ref, wq, sems):
+    copy_q = pltpu.make_async_copy(w_ref.at[0], wq, sems.at[0])
+    copy_q.start()
     row = lax.broadcasted_iota(jnp.int32, (TOK, TOK), 0)
     causal = lax.broadcasted_iota(jnp.int32, (TOK, TOK), 1) <= row
+    copy_q.wait()
+    query = dot(normed_ref[...], wq[...]).astype(BF)
+    q_ref[...] = query
     for h in range(HEADS):
         scores = dot_cols(query[:, of_head(h)], k_ref[:, of_head(h)])
         scores = jnp.where(causal, scores, 0.0).astype(BF)
@@ -96,19 +104,12 @@
 
 
 def attend_kernel(
-    place_ref, prefix_ref, g1, g2, g3, q_ref, local_ref, gain_ref, w_ref,
+    head_ref, earlier_ref, q_ref, local_ref, gain_ref, w_ref,
     own_ref, s1, s2, s3, mixed_ref, turned_ref,
 ):
-    y = place_ref[0]
-    head = place_ref[1]
+    head = head_ref[0]
     for h in range(HEADS):
-        earlier = prefix_ref[h]
-        for k, got in ((1, g1), (2, g2), (3, g3)):
-            earlier = earlier + jnp.where(y >= k, got[h].astype(F32), 0.0)
-        high = earlier.astype(BF)
-        low = (earlier - high.astype(F32)).astype(BF)
-        query = q_ref[:, of_head(h)]
-        attended = local_ref[:, of_head(h)] + (dot(query, high) + dot(query, low))
+        attended = local_ref[:, of_head(h)] + dot(q_ref[:, of_head(h)], earlier_ref[of_head(h), :])
         mixed_ref[:, of_head(h)] = rms_norm(attended, gain_ref[:, of_head(h)]).astype(BF)
     for k in range(4):
         start = pl.multiple_of(((head - k) % 4) * ROWS, ROWS)
@@ -139,8 +140,6 @@
     block = (head - lax.broadcasted_iota(jnp.int32, (TOK, 16), 0) // ROWS) & 3
     base = ((block >> 1) * 18 + (block & 1) * CAP).astype(F32)
     slot = jnp.where(chosen > 0, base + rank, -1.0).astype(BF)
-    high = gates.astype(BF)
-    low = (gates - high.astype(F32)).astype(BF)
 
     def of_row(shape, axis):
         row = lax.broadcasted_iota(jnp.int32, shape, axis)
@@ -156,8 +155,7 @@
     chip, want = of_row((16, SLOTS), 1)
     spread = (chip == lax.broadcasted_iota(jnp.int32, (16, SLOTS), 0)).astype(F32).astype(BF)
     at_row = dot(slot, spread) == want[:1, :]
-    weight_ref[:TOK, :] = jnp.where(at_row, dot(high, spread), 0.0).astype(BF)
-    weight_ref[TOK:, :] = jnp.where(at_row, dot(low, spread), 0.0).astype(BF)
+    weight_ref[...] = jnp.where(at_row, dot(gates.astype(BF), spread), 0.0).astype(BF)
 
 
 def dispatch_kernel(place_ref, t0, t1, t2, t3, out_ref, tokens):
@@ -175,49 +173,53 @@
         out_ref[:, D + t * 128:D + (t + 1) * 128] = piece
 
 
+def start_quarters(keep_ref, arrays, dest_of, sems, first):
+    def load(q, ref):
+        return pltpu.make_async_copy(ref, dest_of(q), sems.at[first + q])
+
+    keep = keep_ref[0] == 1
+    copies = [load(0, arrays[0]), load(1, arrays[1])]
+    copies[0].start()
+    copies[1].start()
+
+    @pl.when(keep)
+    def _():
+        load(2, arrays[2]).start()
+        load(3, arrays[5]).start()
+
+    @pl.when(jnp.logical_not(keep))
+    def _():
+        load(2, arrays[3]).start()
+        load(3, arrays[4]).start()
+
+    return copies + [load(2, arrays[2]), load(3, arrays[4])]
+
+
 def expert_kernel(
     keep_ref, x_ref, gu0, gu1, gu2, gu3, gu4, gu5, dn0, dn1, dn2, dn3, dn4, dn5,
-    out_ref, rows, ends, gate_up, down, act, tail, sems,
+    out_ref, rows, gate_up, down, act, tail, sems,
 ):
-    copies = [
-        pltpu.make_async_copy(x_ref.at[:, :D], rows.at[:MAIN], sems.at[8]),
-        pltpu.make_async_copy(x_ref.at[:, D:], ends, sems.at[9]),
-    ]
-
-    def load(q, gu, dn):
-        return [
-            pltpu.make_async_copy(gu, gate_up.at[q], sems.at[q]),
-            pltpu.make_async_copy(dn, down.at[q * 256:(q + 1) * 256], sems.at[4 + q]),
-        ]
-
-    copies += load(0, gu0, dn0) + load(1, gu1, dn1)
-    for copy in copies:
-        copy.start()
-    keep = keep_ref[0] == 1
-
-    @pl.when(keep)
-    def _():
-        for copy in load(2, gu2, dn2) + load(3, gu5, dn5):
-            copy.start()
-
-    @pl.when(jnp.logical_not(keep))
-    def _():
-        for copy in load(2, gu3, dn3) + load(3, gu4, dn4):
-            copy.start()
-
-    copies += load(2, gu2, dn2) + load(3, gu4, dn4)
-    copies[1].wait()
+    copies = start_quarters(
+        keep_ref, (gu0, gu1, gu2, gu3, gu4, gu5), lambda q: gate_up.at[q], sems, 0
+    )
+    down_copies = start_quarters(
+        keep_ref,
+        (dn0, dn1, dn2, dn3, dn4, dn5),
+        lambda q: down.at[q * 256:(q + 1) * 256],
+        sems,
+        4,
+    )
+    rows[:MAIN, :] = x_ref[:, :D]
     for t in range(2):
-        piece = ends[:, t * 128:(t + 1) * 128].astype(F32).reshape(32, D)
+        piece = x_ref[:, D + t * 128:D + (t + 1) * 128].astype(F32).reshape(32, D)
         rows[MAIN + t * 32:MAIN + (t + 1) * 32, :] = piece.astype(BF)
-    copies[0].wait()
     for q in range(4):
-        copies[2 + 2 * q].wait()
+        copies[q].wait()
         gate = dot(rows[...], gate_up[q, 0])
         up = dot(rows[...], gate_up[q, 1])
         act[:, q * 256:(q + 1) * 256] = (jax.nn.silu(gate) * up).astype(BF)
-    for q in range(4):
-        copies[3 + 2 * q].wait()
+    for copy in down_copies:
+        copy.wait()
     for n in range(4):
         cols = slice(n * 512, (n + 1) * 512)
         result = dot(act[...], down[:, cols])
@@ -235,7 +237,6 @@
     for n in range(4):
         cols = slice(n * 512, (n + 1) * 512)
         rows = dot(weight_ref[:, :MAIN], y_ref[:, cols]) + dot(weight_ref[:, MAIN:], tail[:, cols])
-        rows = rows[:TOK] + rows[TOK:]
         own_ref[:, cols] = rows[:ROWS]
         s3[:, cols] = rows[ROWS:2 * ROWS].astype(BF)
         s2[:, cols] = rows[2 * ROWS:3 * ROWS].astype(BF)
@@ -291,36 +292,43 @@
     return [lax.ppermute(a, axes, perm) for a in arrays]
 
 
-def pick_kernel(index_ref, gu_ref, dn_ref, gu_out, dn_out, sems):
+def pick_kernel(index_ref, gu_ref, dn_ref, gu_out, dn_out, gu_buf, dn_buf, read_sems, write_sems):
     index = index_ref[0]
-    copies = []
+    reads = []
+    writes = []
     for half in range(2):
         for part in range(2):
             rows = pl.ds(part * (D // 2), D // 2)
-            copies.append((gu_ref.at[index, half, rows], gu_out.at[half, rows]))
+            reads.append((gu_ref.at[index, half, rows], gu_buf.at[half, rows]))
+            writes.append((gu_buf.at[half, rows], gu_out.at[half, rows]))
         rows = pl.ds(half * 128, 128)
-        copies.append((dn_ref.at[index, rows], dn_out.at[rows]))
-    copies = [pltpu.make_async_copy(a, b, sems.at[i]) for i, (a, b) in enumerate(copies)]
-    for copy in copies:
-        copy.start()
-    for copy in copies:
-        copy.wait()
+        reads.append((dn_ref.at[index, rows], dn_buf.at[rows]))
+        writes.append((dn_buf.at[rows], dn_out.at[rows]))
+    reads = [pltpu.make_async_copy(a, b, read_sems.at[i]) for i, (a, b) in enumerate(reads)]
+    writes = [pltpu.make_async_copy(a, b, write_sems.at[i]) for i, (a, b) in enumerate(writes)]
+    for read in reads:
+        read.start()
+    for read, write in zip(reads, writes):
+        read.wait()
+        write.start()
+    for write in writes:
+        write.wait()
 
 
 def pick(w_gate_up, w_down, index):
     return pl.pallas_call(
         pick_kernel,
         in_specs=[SMEM, ANY, ANY],
-        out_specs=[VMEM, VMEM],
+        out_specs=[HBM, HBM],
         out_shape=[out((2, D, 256), BF), out((256, D), BF)],
-        scratch_shapes=[pltpu.SemaphoreType.DMA((6,))],
+        scratch_shapes=[
+            pltpu.VMEM((2, D, 256), BF),
+            pltpu.VMEM((256, D), BF),
+            pltpu.SemaphoreType.DMA((6,)),
+            pltpu.SemaphoreType.DMA((6,)),
+        ],
         name="pick",
     )(index.astype(jnp.int32)[None], w_gate_up, w_down)
-
-
-def exchange(array, step):
-    dy, dz = step
-    return [lax.ppermute(array, "seq", seq_perm(dy * k, dz * k, 0)) for k in range(1, 4)]
 
 
 def gather_head(array):
@@ -340,30 +348,25 @@
     seq = lax.axis_index("seq")
     head = lax.axis_index("head")
     core = seq % 2
-    z = (seq // 2) % 4
-    y = seq // 8
 
     both = ("seq", "head")
     near = permute_all(pick(w_gate_up, w_down, 1 - (head & 1)), both, device_perm(near_target))
-    tables = gather_head(jnp.concatenate([routes.astype(F32), gate_weights], axis=1))
-    place_rows, weight = call(
-        routing_kernel, [SMEM] + [VMEM] * 4, [out((SLOTS, TOK), BF), out((2 * TOK, SLOTS), BF)]
-    )(head.astype(jnp.int32)[None], *tables)
-
-    normed, key, value, own_state, send_state, zero = call(
+    w_planes = w_qkv.transpose(1, 0, 2)
+    normed, key, value, send_state, zero = call(
         front_kernel,
-        [VMEM, VMEM, ANY, ANY],
+        [VMEM, VMEM, ANY],
         [
             out((TOK, D), BF),
             out((TOK, WIDE), BF),
             out((TOK, WIDE), BF),
-            out((HEADS, DH, DH), F32),
-            out((HEADS, DH, DH), BF),
+            out((WIDE, DH), BF),
             out((1,), jnp.int32),
         ],
         [pltpu.VMEM((D, WIDE), BF), pltpu.VMEM((D, WIDE), BF), pltpu.SemaphoreType.DMA((2,))],
-    )(hidden_in, attn_gain[None, :], w_qkv[:, 1], w_qkv[:, 2])
-    sibling = lax.ppermute(send_state, "seq", seq_perm(0, 0, 1)).astype(F32)
+    )(hidden_in, attn_gain[None, :], w_planes)
+    states = lax.all_to_all(send_state.reshape(32, 16, DH), "seq", 0, 0, tiled=True)
+    sums = call(prefix_kernel, [VMEM], [out((32, 16, DH), BF)])(states)[0]
+    earlier = lax.all_to_all(sums, "seq", 0, 0, tiled=True).reshape(WIDE, DH)
     odd = (head & 1) + zero[0]
     rest = pick(w_gate_up, w_down, odd)
     far_down = lax.ppermute(rest[1], both, device_perm(far_target))
@@ -372,27 +375,25 @@
     near_other = permute_all(near, "seq", seq_perm(0, 0, 1))
     far_other = permute_all(far, both, device_perm(pass_target))
     pieces = [near, near_other, rest, rest_other, far, far_other]
-    prefix = jnp.where(core == 1, sibling, 0.0)
-    total = own_state + sibling
-    rows_z = exchange(total.astype(BF), (0, 1))
-    for k, got in enumerate(rows_z):
-        prefix = prefix + jnp.where(z > k, got.astype(F32), 0.0)
-        total = total + got.astype(F32)
-    rows_y = exchange(total.astype(BF), (1, 0))
-
-    w_query = [
-        lax.dynamic_slice_in_dim(w_qkv, zero[0] + start, D // 2, 0)[:, 0] for start in (0, D // 2)
-    ]
+
     query, local = call(
-        local_kernel, [VMEM] * 5, [out((TOK, WIDE), BF), out((TOK, WIDE), F32)]
-    )(normed, *w_query, key, value)
-    place = jnp.stack([y, head]).astype(jnp.int32)
+        local_kernel,
+        [VMEM, ANY, VMEM, VMEM],
+        [out((TOK, WIDE), BF), out((TOK, WIDE), F32)],
+        [pltpu.VMEM((D, WIDE), BF), pltpu.SemaphoreType.DMA((1,))],
+    )(normed, w_planes, key, value)
+    here = head.astype(jnp.int32)[None]
     blocks = call(
         attend_kernel,
-        [SMEM] + [VMEM] * 8,
+        [SMEM] + [VMEM] * 5,
         BLOCKS_OUT,
         [pltpu.VMEM((TOK, WIDE), BF), pltpu.VMEM((TOK, WIDE), BF)],
-    )(place, prefix, *rows_y, query, local, out_gain[None, :], w_out)
+    )(here, earlier, query, local, out_gain[None, :], w_out)
+    tables = gather_head(jnp.concatenate([routes.astype(F32), gate_weights], axis=1))
+    place_rows, weight = call(
+        routing_kernel, [SMEM] + [VMEM] * 4, [out((SLOTS, TOK), BF), out((TOK, SLOTS), BF)]
+    )(here, *tables)
+
     attn_rows = scatter_head(blocks)
     resid = lax.dynamic_slice_in_dim(hidden_in, head * ROWS, ROWS, 0).astype(F32) + attn_rows
     normed2 = rms_norm(resid, moe_gain).astype(BF)
@@ -405,16 +406,15 @@
     keep = (head // 2 == core).astype(jnp.int32)[None]
     results = call(
         expert_kernel,
-        [SMEM, HBM] + [ANY] * 12,
+        [SMEM, VMEM] + [ANY] * 12,
         [out((MAIN, PACKED), BF)],
         [
             pltpu.VMEM((SLOTS, D), BF),
-            pltpu.VMEM((MAIN, 256), BF),
             pltpu.VMEM((4, 2, D, 256), BF),
             pltpu.VMEM((1024, D), BF),
             pltpu.VMEM((SLOTS, 1024), BF),
             pltpu.VMEM((64, D), F32),
-            pltpu.SemaphoreType.DMA((10,)),
+            pltpu.SemaphoreType.DMA((8,)),
         ],
     )(keep, received.reshape(MAIN, PACKED), *[p[0] for p in pieces], *[p[1] for p in pieces])[0]
     back = lax.all_to_all(results.reshape(32, 16, PACKED), "seq", 0, 0, tiled=True)

time: 240 us -> 241 us (level)
  starting transfers between devices: 53.1 us -> 74.1 us
  waiting for transfers between devices: 81.7 us -> 74.2 us
  local copies, waits for them, and re-layouts: 10.8 us -> 3.53 us
  between operations: 4.1 us -> 0.85 us
  other arithmetic: 5.89 us -> 3.39 us
    all_to_all x0 -> x2, starting transfers between devices: none -> 15.6 us  [the longest x1 8.5 us: on_device(): lax.all_to_all(send_state.reshape(32, 16, DH), 'seq', 0, 0, tiled=True)]
    ppermute x6, waiting for transfers between devices: 31.4 us -> 18.4 us  [gather_head(): lax.ppermute(array, 'head', head_perm(k))]
    all_to_all x1, starting transfers between devices: 6.19 us -> 16.1 us  [on_device(): lax.all_to_all(sent.reshape(32, 16, PACKED), 'seq', 0, 0, tiled=True)]
    ppermute x7 -> x0, starting transfers between devices: 9.35 us -> none  [the longest x6 8.6 us: exchange(): lax.ppermute(array, 'seq', seq_perm(dy * k, dz * k, 0))]
    squeeze x2 -> x0, local copies, waits for them, and re-layouts: 7.84 us -> none  [the longest x1 4.48 us: on_device(): w_qkv[:, 2]]
    ppermute x6, waiting for transfers between devices: 35.1 us -> 42.7 us  [scatter_head(): total = total + lax.ppermute(blocks[k], 'head', head_perm(k)).astype(F32)]
    ppermute x8, waiting for transfers between devices: 1.66 us -> 7.38 us  [permute_all(): return [lax.ppermute(a, axes, perm) for a in arrays]]
    ppermute x1, waiting for transfers between devices: 5.67 us -> 0.01 us  [on_device(): far_down = lax.ppermute(rest[1], both, device_perm(far_target))]
  transfers between devices with their start and end apart: 30 -> 25, of which waited for: 13 -> 13; matrix products, arithmetic and copies ran while one was open for 3% -> 1% of each run, Pallas kernels for 9% -> 9%
where the time goes in v3:
time: 241 us; the launch traced here: 238 us
  waiting for transfers between devices  74.2 us (31%)
  starting transfers between devices  74.1 us (31%)
  Pallas kernels  44.2 us (18%)
  blocking collectives  37.6 us (16%)
  local copies, waits for them, and re-layouts  3.53 us (1%)
  other arithmetic  3.39 us (1%)
    ppermute x6, waiting for transfers between devices, scatter_head(): total = total + lax.ppermute(blocks[k], 'head', head_perm(k)).astype(F32)  42.7 us
    all_to_all x1, blocking collectives, on_device(): lax.all_to_all(results.reshape(32, 16, PACKED), 'seq', 0, 0, tiled=True)  37.6 us
    ppermute x8, starting transfers between devices, permute_all(): return [lax.ppermute(a, axes, perm) for a in arrays]  18.6 us
    ppermute x6, waiting for transfers between devices, gather_head(): lax.ppermute(array, 'head', head_perm(k))  18.4 us
    all_to_all x1, starting transfers between devices, on_device(): lax.all_to_all(sent.reshape(32, 16, PACKED), 'seq', 0, 0, tiled=True)  16.1 us
    pallas_call x1, Pallas kernels, on_device(): call(expert_kernel, [SMEM, VMEM] + [ANY] * 12, [out((MAIN, PACKED), BF)],...  13 us
    ppermute x6, starting transfers between devices, gather_head(): lax.ppermute(array, 'head', head_perm(k))  10.5 us
    all_to_all x1, starting transfers between devices, on_device(): lax.all_to_all(send_state.reshape(32, 16, DH), 'seq', 0, 0, tiled=True)  8.5 us
  transfers between devices with their start and end apart: 25, of which 13 were waited for; matrix products, arithmetic and copies ran while one was open for 1% of the time, Pallas kernels for 9%

profile of v3, /device:TPU:33, one launch (start us, length us, event | category | flops | bytes accessed | tf_op | source)
XLA Modules:
  0.0 237.9 jit_solution(7182293995552343756)
XLA Ops:
  0.0 5.1 %shard_map.100 = (bf16[256,2048]{1,0:T(8,128)(2,1)}, bf16[256,512]{1,0:T(8,128)(2,1)}, bf16[256,512]{1,0:T(8,128)(2,1)}, bf16[512,128]{1,0:T(8,128)(2,1)}, s32[1]{0:T(128)}) custom-call(bf16[256,2048]{1,0:T(8,128)(2,1)} %x_ref.1, f32[1,2048]{1,0:T(1,128)} %bitcast.22, bf16[3,2048,512]{2,1,0:T(8,128)(2,1)} %bitcast.14), custom_call_target="tpu_custom_call" | custom-call | tf_op jit(solution)/shard_map/pallas_call | solution.py:355
  5.1 8.5 %all-to-all-start = ((bf16[32,16,128]{2,1,0:T(8,128)(2,1)}), bf16[32,16,128]{2,1,0:T(8,128)(2,1)S(1)}, u32[]{:S(2)}, u32[]{:S(2)}) async-start(bf16[32,16,128]{2,1,0:T(8,128)(2,1)} %bitcast.21), calls=%async_computation | async-start | bytes 262144 | tf_op jit(solution)/shard_map/all_to_all | solution.py:367
  14.3 2.8 %pick.3 = (bf16[2,2048,256]{2,1,0:T(8,128)(2,1)}, bf16[256,2048]{1,0:T(8,128)(2,1)}) custom-call(s32[1]{0:T(128)} %bitcast.11.index_ref, bf16[2,2,2048,256]{3,2,1,0:T(8,128)(2,1)} %gu_ref.3, bf16[2,256,2048]{2,1,0:T(8,128)(2,1)} %dn_ref.3), custom_call_target="tpu_custom_call" | custom-call | tf_op jit(solution)/shard_map/pick/pallas_call | solution.py:319
  17.1 4.9 %collective-permute-start.12 = (bf16[2,2048,256]{2,1,0:T(8,128)(2,1)}, bf16[2,2048,256]{2,1,0:T(8,128)(2,1)}, u32[]{:S(2)}, u32[]{:S(2)}) collective-permute-start(bf16[2,2048,256]{2,1,0:T(8,128)(2,1)} %get-tuple-element.40.gu2), channel_id=1, source_target_pairs={{2,4},{3,5},{4,2},{5,3},{10,12},{11,13},{12,10},{13,11},{18,20},{1... | collective-permute-start | bytes 6291464 | tf_op jit(solution)/shard_map/ppermute | solution.py:373
  22.0 2.9 %pick.2 = (bf16[2,2048,256]{2,1,0:T(8,128)(2,1)}, bf16[256,2048]{1,0:T(8,128)(2,1)}) custom-call(s32[1]{0:T(128)} %bitcast.9.index_ref, bf16[2,2,2048,256]{3,2,1,0:T(8,128)(2,1)} %gu_ref.3, bf16[2,256,2048]{2,1,0:T(8,128)(2,1)} %dn_ref.3), custom_call_target="tpu_custom_call" | custom-call | tf_op jit(solution)/shard_map/pick/pallas_call | solution.py:319
  28.1 7.1 %all-to-all-start.1 = ((bf16[32,16,128]{2,1,0:T(8,128)(2,1)}), bf16[32,16,128]{2,1,0:T(8,128)(2,1)S(1)}, u32[]{:S(2)}, u32[]{:S(2)}) async-start(bf16[32,16,128]{2,1,0:T(8,128)(2,1)} %shard_map.101), calls=%async_computation.1 | async-start | bytes 262144 | tf_op jit(solution)/shard_map/all_to_all | solution.py:369
  35.2 4.9 %shard_map.102 = (bf16[256,512]{1,0:T(8,128)(2,1)}, f32[256,512]{1,0:T(8,128)}) custom-call(bf16[256,2048]{1,0:T(8,128)(2,1)} %get-tuple-element.27.normed_ref, bf16[3,2048,512]{2,1,0:T(8,128)(2,1)} %bitcast.15, bf16[256,512]{1,0:T(8,128)(2,1)} %get-tuple-element.28.k_ref, bf16[256,512]{1,0:T(8,128)(2,1)} %get-tuple-element.29.v_ref), custom_call_target="tpu_custom_call" | custom-call | tf_op jit(solution)/shard_map/pallas_call | solution.py:379
  42.4 4.0 %shard_map.103 = (f32[64,2048]{1,0:T(8,128)}, bf16[64,2048]{1,0:T(8,128)(2,1)}, bf16[64,2048]{1,0:T(8,128)(2,1)}, bf16[64,2048]{1,0:T(8,128)(2,1)}) custom-call(s32[1]{0:T(128)} %bitcast.head_ref, bf16[512,128]{1,0:T(8,128)(2,1)} %bitcast.20, bf16[256,512]{1,0:T(8,128)(2,1)} %get-tuple-element.30.q_ref, f32[256,512]{1,0:T(8,128)} %get-tuple-element.31.local_ref, ...), custom_call_target="tpu_custom_call" | custom-call | tf_op jit(solution)/shard_map/pallas_call | solution.py:386
  50.1 21.2 %collective-permute-done = bf16[64,2048]{1,0:T(8,128)(2,1)S(1)} collective-permute-done((bf16[64,2048]{1,0:T(8,128)(2,1)}, bf16[64,2048]{1,0:T(8,128)(2,1)S(1)}, u32[]{:S(2)}, u32[]{:S(2)}) %collective-permute-start) | collective-permute-done | bytes 262176 | tf_op jit(solution)/shard_map/ppermute | solution.py:341
  73.1 8.9 %collective-permute-done.1 = bf16[64,2048]{1,0:T(8,128)(2,1)S(1)} collective-permute-done((bf16[64,2048]{1,0:T(8,128)(2,1)}, bf16[64,2048]{1,0:T(8,128)(2,1)S(1)}, u32[]{:S(2)}, u32[]{:S(2)}) %collective-permute-start.1) | collective-permute-done | bytes 262176 | tf_op jit(solution)/shard_map/ppermute | solution.py:341
  84.2 11.1 %collective-permute-done.5.t3 = f32[64,16]{1,0:T(8,128)S(1)} collective-permute-done((f32[64,16]{1,0:T(8,128)S(1)}, f32[64,16]{1,0:T(8,128)S(1)}, u32[]{:S(2)}, u32[]{:S(2)}) %collective-permute-start.5) | collective-permute-done | bytes 4128 | tf_op jit(solution)/shard_map/ppermute | solution.py:335
  95.3 4.3 %collective-permute-start.4 = (f32[64,16]{1,0:T(8,128)S(1)}, f32[64,16]{1,0:T(8,128)S(1)}, u32[]{:S(2)}, u32[]{:S(2)}) collective-permute-start(f32[64,16]{1,0:T(8,128)S(1)} %copy.16.t0), channel_id=1, source_target_pairs={{0,2},{1,3},{2,0},{3,1},{4,6},{5,7},{6,4},{7,5},{8,10},{9,11},{10,... | collective-permute-start | bytes 12296 | tf_op jit(solution)/shard_map/ppermute | solution.py:335
  100.9 3.4 %collective-permute-start.3 = (f32[64,16]{1,0:T(8,128)S(1)}, f32[64,16]{1,0:T(8,128)S(1)}, u32[]{:S(2)}, u32[]{:S(2)}) collective-permute-start(f32[64,16]{1,0:T(8,128)S(1)} %copy.16.t0), channel_id=1, source_target_pairs={{0,1},{1,2},{2,3},{3,0},{4,5},{5,6},{6,7},{7,4},{8,9},{9,10},{10,1... | collective-permute-start | bytes 12296 | tf_op jit(solution)/shard_map/ppermute | solution.py:335
  116.0 3.5 %shard_map.105 = bf16[512,2304]{1,0:T(8,128)(2,1)} custom-call(bf16[576,256]{1,0:T(8,128)(2,1)} %get-tuple-element.37.place_ref, bf16[64,2048]{1,0:T(8,128)(2,1)} %copy-done.1, bf16[64,2048]{1,0:T(8,128)(2,1)} %copy-done.6, bf16[64,2048]{1,0:T(8,128)(2,1)} %copy-done.5, bf16[64,2048]{1,0:T(8,128)(2,1)} %copy-done.4), custom_call_target="tpu_custom_call" | custom-call | tf_op jit(solution)/shard_map/pallas_call | solution.py:402
  119.5 16.1 %all-to-all-start.2 = ((bf16[32,16,2304]{2,1,0:T(8,128)(2,1)}), bf16[32,16,2304]{2,1,0:T(8,128)(2,1)S(1)}, u32[]{:S(2)}, u32[]{:S(2)}) async-start(bf16[32,16,2304]{2,1,0:T(8,128)(2,1)} %bitcast.18), calls=%async_computation.2 | async-start | bytes 4718592 | tf_op jit(solution)/shard_map/all_to_all | solution.py:405
  139.1 5.9 %collective-permute-start.13 = (bf16[2,2048,256]{2,1,0:T(8,128)(2,1)}, bf16[2,2048,256]{2,1,0:T(8,128)(2,1)}, u32[]{:S(2)}, u32[]{:S(2)}) collective-permute-start(bf16[2,2048,256]{2,1,0:T(8,128)(2,1)} %collective-permute-done.12.gu4), channel_id=1, source_target_pairs={{2,6},{3,7},{4,0},{5,1},{10,14},{11,15},{12,8},{13,9},{18,22},{19,... | collective-permute-start | bytes 6291464 | tf_op jit(solution)/shard_map/ppermute | solution.py:292
  145.0 3.4 %collective-permute-start.18 = (bf16[256,2048]{1,0:T(8,128)(2,1)}, bf16[256,2048]{1,0:T(8,128)(2,1)}, u32[]{:S(2)}, u32[]{:S(2)}) collective-permute-start(bf16[256,2048]{1,0:T(8,128)(2,1)} %collective-permute-done.17.dn4), channel_id=1, source_target_pairs={{2,6},{3,7},{4,0},{5,1},{10,14},{11,15},{12,8},{13,9},{18,22},{19,... | collective-permute-start | bytes 3145736 | tf_op jit(solution)/shard_map/ppermute | solution.py:292
  148.4 4.7 %collective-permute-done.14.dn0 = bf16[256,2048]{1,0:T(8,128)(2,1)} collective-permute-done((bf16[256,2048]{1,0:T(8,128)(2,1)}, bf16[256,2048]{1,0:T(8,128)(2,1)}, u32[]{:S(2)}, u32[]{:S(2)}) %collective-permute-start.14) | collective-permute-done | bytes 1048608 | tf_op jit(solution)/shard_map/ppermute | solution.py:292
  153.2 4.9 %collective-permute-start.15 = (bf16[256,2048]{1,0:T(8,128)(2,1)}, bf16[256,2048]{1,0:T(8,128)(2,1)}, u32[]{:S(2)}, u32[]{:S(2)}) collective-permute-start(bf16[256,2048]{1,0:T(8,128)(2,1)} %collective-permute-done.14.dn0), channel_id=1, source_target_pairs={{0,4},{4,0},{8,12},{12,8},{16,20},{20,16},{24,28},{28,24},{32,36},... | collective-permute-start | bytes 3145736 | tf_op jit(solution)/shard_map/ppermute | solution.py:292
  160.7 4.1 %all-to-all-done.2 = bf16[32,16,2304]{2,1,0:T(8,128)(2,1)S(1)} async-done(((bf16[32,16,2304]{2,1,0:T(8,128)(2,1)}), bf16[32,16,2304]{2,1,0:T(8,128)(2,1)S(1)}, u32[]{:S(2)}, u32[]{:S(2)}) %all-to-all-start.2) | async-done | bytes 2359328 | tf_op jit(solution)/shard_map/all_to_all | solution.py:405
  166.3 13.0 %shard_map.106 = bf16[512,2304]{1,0:T(8,128)(2,1)} custom-call(s32[1]{0:T(128)} %bitcast.6.keep_ref, bf16[512,2304]{1,0:T(8,128)(2,1)} %bitcast.16, bf16[2,2048,256]{2,1,0:T(8,128)(2,1)} %collective-permute-done.9.gu0, bf16[2,2048,256]{2,1,0:T(8,128)(2,1)} %collective-permute-done.10.gu1, bf16[2,2048,256]{2,1,0:T(8,128)(2,1)} %get-tuple-element.40.gu2, ...), custom_call_target="tpu_custom_call" | custom-call | tf_op jit(solution)/shard_map/pallas_call | solution.py:407
  179.3 37.6 %all_to_all.20 = bf16[32,16,2304]{2,1,0:T(8,128)(2,1)} all-to-all(bf16[32,16,2304]{2,1,0:T(8,128)(2,1)} %bitcast.17), channel_id=1, replica_groups=mesh['seq'=32,'head'=4] {'seq'}, dimensions={0} | all-to-all | bytes 4718592 | tf_op jit(solution)/shard_map/all_to_all | solution.py:420
  216.9 3.8 %shard_map.107 = (f32[64,2048]{1,0:T(8,128)}, bf16[64,2048]{1,0:T(8,128)(2,1)}, bf16[64,2048]{1,0:T(8,128)(2,1)}, bf16[64,2048]{1,0:T(8,128)(2,1)}) custom-call(bf16[256,576]{1,0:T(8,128)(2,1)} %get-tuple-element.36.weight_ref, bf16[512,2304]{1,0:T(8,128)(2,1)} %bitcast.19), custom_call_target="tpu_custom_call" | custom-call | tf_op jit(solution)/shard_map/pallas_call | solution.py:421
  223.4 12.3 %collective-permute-done.19 = bf16[64,2048]{1,0:T(8,128)(2,1)S(1)} collective-permute-done((bf16[64,2048]{1,0:T(8,128)(2,1)}, bf16[64,2048]{1,0:T(8,128)(2,1)S(1)}, u32[]{:S(2)}, u32[]{:S(2)}) %collective-permute-start.19) | collective-permute-done | bytes 262176 | tf_op jit(solution)/shard_map/ppermute | solution.py:341
  (72 shorter events, 38.6 us)
Async XLA Ops:
  5.1 20.7 %all-to-all-start = ((bf16[32,16,128]{2,1,0:T(8,128)(2,1)}), bf16[32,16,128]{2,1,0:T(8,128)(2,1)S(1)}, u32[]{:S(2)}, u32[]{:S(2)}) async-start(bf16[32,16,128]{2,1,0:T(8,128)(2,1)} %bitcast.21), calls=%async_computation | async-start | bytes 262144 | tf_op jit(solution)/shard_map/all_to_all | solution.py:367
  17.1 122.0 %collective-permute-start.12 = (bf16[2,2048,256]{2,1,0:T(8,128)(2,1)}, bf16[2,2048,256]{2,1,0:T(8,128)(2,1)}, u32[]{:S(2)}, u32[]{:S(2)}) collective-permute-start(bf16[2,2048,256]{2,1,0:T(8,128)(2,1)} %get-tuple-element.40.gu2), channel_id=1, source_target_pairs={{2,4},{3,5},{4,2},{5,3},{10,12},{11,13},{12,10},{13,11},{18,20},{1... | collective-permute-start | bytes 6291464 | tf_op jit(solution)/shard_map/ppermute | solution.py:373
  24.9 120.1 %collective-permute-start.9 = (bf16[2,2048,256]{2,1,0:T(8,128)(2,1)}, bf16[2,2048,256]{2,1,0:T(8,128)(2,1)}, u32[]{:S(2)}, u32[]{:S(2)}) collective-permute-start(bf16[2,2048,256]{2,1,0:T(8,128)(2,1)} %get-tuple-element.38), channel_id=1, source_target_pairs={{0,1},{1,4},{2,5},{3,0},{4,3},{5,6},{6,7},{7,2},{8,9},{9,12},{10,1... | collective-permute-start | bytes 6291464 | tf_op jit(solution)/shard_map/ppermute | solution.py:292
  28.1 13.7 %all-to-all-start.1 = ((bf16[32,16,128]{2,1,0:T(8,128)(2,1)}), bf16[32,16,128]{2,1,0:T(8,128)(2,1)S(1)}, u32[]{:S(2)}, u32[]{:S(2)}) async-start(bf16[32,16,128]{2,1,0:T(8,128)(2,1)} %shard_map.101), calls=%async_computation.1 | async-start | bytes 262144 | tf_op jit(solution)/shard_map/all_to_all | solution.py:369
  46.4 24.8 %collective-permute-start = (bf16[64,2048]{1,0:T(8,128)(2,1)}, bf16[64,2048]{1,0:T(8,128)(2,1)S(1)}, u32[]{:S(2)}, u32[]{:S(2)}) collective-permute-start(bf16[64,2048]{1,0:T(8,128)(2,1)} %get-tuple-element.33), channel_id=1, source_target_pairs={{0,1},{1,2},{2,3},{3,0},{4,5},{5,6},{6,7},{7,4},{8,9},{9,10},{10,1... | collective-permute-start | bytes 786440 | tf_op jit(solution)/shard_map/ppermute | solution.py:341
  47.4 34.7 %collective-permute-start.1 = (bf16[64,2048]{1,0:T(8,128)(2,1)}, bf16[64,2048]{1,0:T(8,128)(2,1)S(1)}, u32[]{:S(2)}, u32[]{:S(2)}) collective-permute-start(bf16[64,2048]{1,0:T(8,128)(2,1)} %get-tuple-element.34), channel_id=1, source_target_pairs={{0,2},{1,3},{2,0},{3,1},{4,6},{5,7},{6,4},{7,5},{8,10},{9,11},{10,... | collective-permute-start | bytes 786440 | tf_op jit(solution)/shard_map/ppermute | solution.py:341
  48.1 33.9 %collective-permute-start.2 = (bf16[64,2048]{1,0:T(8,128)(2,1)}, bf16[64,2048]{1,0:T(8,128)(2,1)S(1)}, u32[]{:S(2)}, u32[]{:S(2)}) collective-permute-start(bf16[64,2048]{1,0:T(8,128)(2,1)} %get-tuple-element.35), channel_id=1, source_target_pairs={{0,3},{1,0},{2,1},{3,2},{4,7},{5,4},{6,5},{7,6},{8,11},{9,8},{10,9... | collective-permute-start | bytes 786440 | tf_op jit(solution)/shard_map/ppermute | solution.py:341
  71.2 67.0 %collective-permute-start.17 = (bf16[256,2048]{1,0:T(8,128)(2,1)}, bf16[256,2048]{1,0:T(8,128)(2,1)}, u32[]{:S(2)}, u32[]{:S(2)}) collective-permute-start(bf16[256,2048]{1,0:T(8,128)(2,1)} %get-tuple-element.42.dn2), channel_id=1, source_target_pairs={{2,4},{3,5},{4,2},{5,3},{10,12},{11,13},{12,10},{13,11},{18,20},{1... | collective-permute-start | bytes 3145736 | tf_op jit(solution)/shard_map/ppermute | solution.py:372
  83.6 23.8 %collective-permute-start.8 = (bf16[64,2048]{1,0:T(8,128)(2,1)S(1)}, bf16[64,2048]{1,0:T(8,128)(2,1)S(1)}, u32[]{:S(2)}, u32[]{:S(2)}) collective-permute-start(bf16[64,2048]{1,0:T(8,128)(2,1)S(1)} %multiply_convert_fusion.t0), channel_id=1, source_target_pairs={{0,3},{1,0},{2,1},{3,2},{4,7},{5,4},{6,5},{7,6},{8,11},{9,8},{10,9... | collective-permute-start | bytes 786440 | tf_op jit(solution)/shard_map/ppermute | solution.py:335
  83.8 11.5 %collective-permute-start.5 = (f32[64,16]{1,0:T(8,128)S(1)}, f32[64,16]{1,0:T(8,128)S(1)}, u32[]{:S(2)}, u32[]{:S(2)}) collective-permute-start(f32[64,16]{1,0:T(8,128)S(1)} %copy.16.t0), channel_id=1, source_target_pairs={{0,3},{1,0},{2,1},{3,2},{4,7},{5,4},{6,5},{7,6},{8,11},{9,8},{10,9... | collective-permute-start | bytes 12296 | tf_op jit(solution)/shard_map/ppermute | solution.py:335
  95.3 5.6 %collective-permute-start.4 = (f32[64,16]{1,0:T(8,128)S(1)}, f32[64,16]{1,0:T(8,128)S(1)}, u32[]{:S(2)}, u32[]{:S(2)}) collective-permute-start(f32[64,16]{1,0:T(8,128)S(1)} %copy.16.t0), channel_id=1, source_target_pairs={{0,2},{1,3},{2,0},{3,1},{4,6},{5,7},{6,4},{7,5},{8,10},{9,11},{10,... | collective-permute-start | bytes 12296 | tf_op jit(solution)/shard_map/ppermute | solution.py:335
  105.3 7.2 %collective-permute-start.7 = (bf16[64,2048]{1,0:T(8,128)(2,1)S(1)}, bf16[64,2048]{1,0:T(8,128)(2,1)S(1)}, u32[]{:S(2)}, u32[]{:S(2)}) collective-permute-start(bf16[64,2048]{1,0:T(8,128)(2,1)S(1)} %multiply_convert_fusion.t0), channel_id=1, source_target_pairs={{0,2},{1,3},{2,0},{3,1},{4,6},{5,7},{6,4},{7,5},{8,10},{9,11},{10,... | collective-permute-start | bytes 786440 | tf_op jit(solution)/shard_map/ppermute | solution.py:335
  107.4 7.9 %collective-permute-start.6 = (bf16[64,2048]{1,0:T(8,128)(2,1)S(1)}, bf16[64,2048]{1,0:T(8,128)(2,1)S(1)}, u32[]{:S(2)}, u32[]{:S(2)}) collective-permute-start(bf16[64,2048]{1,0:T(8,128)(2,1)S(1)} %multiply_convert_fusion.t0), channel_id=1, source_target_pairs={{0,1},{1,2},{2,3},{3,0},{4,5},{5,6},{6,7},{7,4},{8,9},{9,10},{10,1... | collective-permute-start | bytes 786440 | tf_op jit(solution)/shard_map/ppermute | solution.py:335
  119.5 45.4 %all-to-all-start.2 = ((bf16[32,16,2304]{2,1,0:T(8,128)(2,1)}), bf16[32,16,2304]{2,1,0:T(8,128)(2,1)S(1)}, u32[]{:S(2)}, u32[]{:S(2)}) async-start(bf16[32,16,2304]{2,1,0:T(8,128)(2,1)} %bitcast.18), calls=%async_computation.2 | async-start | bytes 4718592 | tf_op jit(solution)/shard_map/all_to_all | solution.py:405
  135.6 9.4 %collective-permute-start.16 = (bf16[256,2048]{1,0:T(8,128)(2,1)}, bf16[256,2048]{1,0:T(8,128)(2,1)}, u32[]{:S(2)}, u32[]{:S(2)}) collective-permute-start(bf16[256,2048]{1,0:T(8,128)(2,1)} %get-tuple-element.42.dn2), channel_id=1, source_target_pairs={{0,4},{1,5},{6,2},{7,3},{8,12},{9,13},{14,10},{15,11},{16,20},{17,... | collective-permute-start | bytes 3145736 | tf_op jit(solution)/shard_map/ppermute | solution.py:292
  136.9 21.2 %collective-permute-start.11 = (bf16[2,2048,256]{2,1,0:T(8,128)(2,1)}, bf16[2,2048,256]{2,1,0:T(8,128)(2,1)}, u32[]{:S(2)}, u32[]{:S(2)}) collective-permute-start(bf16[2,2048,256]{2,1,0:T(8,128)(2,1)} %get-tuple-element.40.gu2), channel_id=1, source_target_pairs={{0,4},{1,5},{6,2},{7,3},{8,12},{9,13},{14,10},{15,11},{16,20},{17,... | collective-permute-start | bytes 6291464 | tf_op jit(solution)/shard_map/ppermute | solution.py:292
  138.2 15.0 %collective-permute-start.14 = (bf16[256,2048]{1,0:T(8,128)(2,1)}, bf16[256,2048]{1,0:T(8,128)(2,1)}, u32[]{:S(2)}, u32[]{:S(2)}) collective-permute-start(bf16[256,2048]{1,0:T(8,128)(2,1)} %get-tuple-element.41), channel_id=1, source_target_pairs={{0,1},{1,4},{2,5},{3,0},{4,3},{5,6},{6,7},{7,2},{8,9},{9,12},{10,1... | collective-permute-start | bytes 3145736 | tf_op jit(solution)/shard_map/ppermute | solution.py:292
  139.1 25.8 %collective-permute-start.13 = (bf16[2,2048,256]{2,1,0:T(8,128)(2,1)}, bf16[2,2048,256]{2,1,0:T(8,128)(2,1)}, u32[]{:S(2)}, u32[]{:S(2)}) collective-permute-start(bf16[2,2048,256]{2,1,0:T(8,128)(2,1)} %collective-permute-done.12.gu4), channel_id=1, source_target_pairs={{2,6},{3,7},{4,0},{5,1},{10,14},{11,15},{12,8},{13,9},{18,22},{19,... | collective-permute-start | bytes 6291464 | tf_op jit(solution)/shard_map/ppermute | solution.py:292
  145.0 19.9 %collective-permute-start.10 = (bf16[2,2048,256]{2,1,0:T(8,128)(2,1)}, bf16[2,2048,256]{2,1,0:T(8,128)(2,1)}, u32[]{:S(2)}, u32[]{:S(2)}) collective-permute-start(bf16[2,2048,256]{2,1,0:T(8,128)(2,1)} %collective-permute-done.9.gu0), channel_id=1, source_target_pairs={{0,4},{4,0},{8,12},{12,8},{16,20},{20,16},{24,28},{28,24},{32,36},... | collective-permute-start | bytes 6291464 | tf_op jit(solution)/shard_map/ppermute | solution.py:292
  145.0 13.1 %collective-permute-start.18 = (bf16[256,2048]{1,0:T(8,128)(2,1)}, bf16[256,2048]{1,0:T(8,128)(2,1)}, u32[]{:S(2)}, u32[]{:S(2)}) collective-permute-start(bf16[256,2048]{1,0:T(8,128)(2,1)} %collective-permute-done.17.dn4), channel_id=1, source_target_pairs={{2,6},{3,7},{4,0},{5,1},{10,14},{11,15},{12,8},{13,9},{18,22},{19,... | collective-permute-start | bytes 3145736 | tf_op jit(solution)/shard_map/ppermute | solution.py:292
  153.2 7.6 %collective-permute-start.15 = (bf16[256,2048]{1,0:T(8,128)(2,1)}, bf16[256,2048]{1,0:T(8,128)(2,1)}, u32[]{:S(2)}, u32[]{:S(2)}) collective-permute-start(bf16[256,2048]{1,0:T(8,128)(2,1)} %collective-permute-done.14.dn0), channel_id=1, source_target_pairs={{0,4},{4,0},{8,12},{12,8},{16,20},{20,16},{24,28},{28,24},{32,36},... | collective-permute-start | bytes 3145736 | tf_op jit(solution)/shard_map/ppermute | solution.py:292
  220.7 15.0 %collective-permute-start.19 = (bf16[64,2048]{1,0:T(8,128)(2,1)}, bf16[64,2048]{1,0:T(8,128)(2,1)S(1)}, u32[]{:S(2)}, u32[]{:S(2)}) collective-permute-start(bf16[64,2048]{1,0:T(8,128)(2,1)} %get-tuple-element.44), channel_id=1, source_target_pairs={{0,1},{1,2},{2,3},{3,0},{4,5},{5,6},{6,7},{7,4},{8,9},{9,10},{10,1... | collective-permute-start | bytes 786440 | tf_op jit(solution)/shard_map/ppermute | solution.py:341
  220.7 15.0 %collective-permute-start.20 = (bf16[64,2048]{1,0:T(8,128)(2,1)}, bf16[64,2048]{1,0:T(8,128)(2,1)S(1)}, u32[]{:S(2)}, u32[]{:S(2)}) collective-permute-start(bf16[64,2048]{1,0:T(8,128)(2,1)} %get-tuple-element.45), channel_id=1, source_target_pairs={{0,2},{1,3},{2,0},{3,1},{4,6},{5,7},{6,4},{7,5},{8,10},{9,11},{10,... | collective-permute-start | bytes 786440 | tf_op jit(solution)/shard_map/ppermute | solution.py:341
  222.4 13.6 %collective-permute-start.21 = (bf16[64,2048]{1,0:T(8,128)(2,1)}, bf16[64,2048]{1,0:T(8,128)(2,1)S(1)}, u32[]{:S(2)}, u32[]{:S(2)}) collective-permute-start(bf16[64,2048]{1,0:T(8,128)(2,1)} %get-tuple-element.46), channel_id=1, source_target_pairs={{0,3},{1,0},{2,1},{3,2},{4,7},{5,4},{6,5},{7,6},{8,11},{9,8},{10,9... | collective-permute-start | bytes 786440 | tf_op jit(solution)/shard_map/ppermute | solution.py:341
  (15 other events, 211.3 us)

commit v4 on v3

--- a/solution.py
+++ b/solution.py
@@ -27,18 +27,32 @@
 HBM = pl.BlockSpec(memory_space=pltpu.HBM)
 
 
+def on_chip(array):
+    return pltpu.with_memory_space_constraint(array, pltpu.VMEM)
+
+
 def out(shape, dtype):
     return jax.ShapeDtypeStruct(shape, dtype)
 
 
-def call(kernel, ins, outs, scratch=()):
+def chip(shape, dtype):
+    return pltpu.VMEM(shape, dtype)
+
+
+def spec_of(o):
+    if o.dtype == jnp.int32:
+        return SMEM
+    return HBM if o in QUARTER else VMEM
+
+
+def call(kernel, ins, outs, scratch=(), limit=54):
     return pl.pallas_call(
         kernel,
         in_specs=ins,
-        out_specs=[SMEM if o.dtype == jnp.int32 else VMEM for o in outs],
+        out_specs=[spec_of(o) for o in outs],
         out_shape=outs,
         scratch_shapes=list(scratch),
-        compiler_params=pltpu.CompilerParams(vmem_limit_bytes=56 << 20),
+        compiler_params=pltpu.CompilerParams(vmem_limit_bytes=limit << 20),
     )
 
 
@@ -63,11 +77,38 @@
     return slice(h * DH, (h + 1) * DH)
 
 
-def front_kernel(x_ref, gain_ref, w_ref, normed_ref, k_ref, v_ref, send_ref, zero_ref, wk, wv, sems):
+def pick_copies(index_ref, gu_ref, dn_ref, gu_out, dn_out, gu_buf, dn_buf, read_sems, write_sems):
+    index = index_ref[0]
+    reads = []
+    writes = []
+    for half in range(2):
+        for part in range(2):
+            rows = pl.ds(part * (D // 2), D // 2)
+            reads.append((gu_ref.at[index, half, rows], gu_buf.at[half, rows]))
+            writes.append((gu_buf.at[half, rows], gu_out.at[half, rows]))
+        rows = pl.ds(half * 128, 128)
+        reads.append((dn_ref.at[index, rows], dn_buf.at[rows]))
+        writes.append((dn_buf.at[rows], dn_out.at[rows]))
+    return (
+        [pltpu.make_async_copy(a, b, read_sems.at[i]) for i, (a, b) in enumerate(reads)],
+        [pltpu.make_async_copy(a, b, write_sems.at[i]) for i, (a, b) in enumerate(writes)],
+    )
+
+
+def front_kernel(
+    index_ref, x_ref, gain_ref, w_ref, gu_ref, dn_ref,
+    normed_ref, k_ref, v_ref, send_ref, zero_ref, gu_out, dn_out,
+    wk, wv, sems, gu_buf, dn_buf, read_sems, write_sems,
+):
     copy_k = pltpu.make_async_copy(w_ref.at[1], wk, sems.at[0])
     copy_v = pltpu.make_async_copy(w_ref.at[2], wv, sems.at[1])
     copy_k.start()
     copy_v.start()
+    reads, writes = pick_copies(
+        index_ref, gu_ref, dn_ref, gu_out, dn_out, gu_buf, dn_buf, read_sems, write_sems
+    )
+    for read in reads:
+        read.start()
     zero_ref[0] = 0
     normed = rms_norm(x_ref[...].astype(F32), gain_ref[...]).astype(BF)
     normed_ref[...] = normed
@@ -75,11 +116,16 @@
     key = dot(normed, wk[...]).astype(BF)
     k_ref[...] = key
     copy_v.wait()
+    for read, write in zip(reads, writes):
+        read.wait()
+        write.start()
     value = dot(normed, wv[...]).astype(BF)
     v_ref[...] = value
     for h in range(HEADS):
         state = dot_rows(key[:, of_head(h)], value[:, of_head(h)])
         send_ref[of_head(h), :] = state.astype(BF)
+    for write in writes:
+        write.wait()
 
 
 def prefix_kernel(states_ref, out_ref):
@@ -292,20 +338,8 @@
     return [lax.ppermute(a, axes, perm) for a in arrays]
 
 
-def pick_kernel(index_ref, gu_ref, dn_ref, gu_out, dn_out, gu_buf, dn_buf, read_sems, write_sems):
-    index = index_ref[0]
-    reads = []
-    writes = []
-    for half in range(2):
-        for part in range(2):
-            rows = pl.ds(part * (D // 2), D // 2)
-            reads.append((gu_ref.at[index, half, rows], gu_buf.at[half, rows]))
-            writes.append((gu_buf.at[half, rows], gu_out.at[half, rows]))
-        rows = pl.ds(half * 128, 128)
-        reads.append((dn_ref.at[index, rows], dn_buf.at[rows]))
-        writes.append((dn_buf.at[rows], dn_out.at[rows]))
-    reads = [pltpu.make_async_copy(a, b, read_sems.at[i]) for i, (a, b) in enumerate(reads)]
-    writes = [pltpu.make_async_copy(a, b, write_sems.at[i]) for i, (a, b) in enumerate(writes)]
+def pick_kernel(*refs):
+    reads, writes = pick_copies(*refs)
     for read in reads:
         read.start()
     for read, write in zip(reads, writes):
@@ -315,18 +349,23 @@
         write.wait()
 
 
+QUARTER = [out((2, D, 256), BF), out((256, D), BF)]
+PICK_SCRATCH = [
+    pltpu.VMEM((2, D, 256), BF),
+    pltpu.VMEM((256, D), BF),
+    pltpu.SemaphoreType.DMA((6,)),
+    pltpu.SemaphoreType.DMA((6,)),
+]
+
+
 def pick(w_gate_up, w_down, index):
     return pl.pallas_call(
         pick_kernel,
-        in_specs=[SMEM, ANY, ANY],
+        in_specs=[SMEM, HBM, HBM],
         out_specs=[HBM, HBM],
-        out_shape=[out((2, D, 256), BF), out((256, D), BF)],
-        scratch_shapes=[
-            pltpu.VMEM((2, D, 256), BF),
-            pltpu.VMEM((256, D), BF),
-            pltpu.SemaphoreType.DMA((6,)),
-            pltpu.SemaphoreType.DMA((6,)),
-        ],
+        out_shape=QUARTER,
+        scratch_shapes=PICK_SCRATCH,
+        compiler_params=pltpu.CompilerParams(vmem_limit_bytes=50 << 20),
         name="pick",
     )(index.astype(jnp.int32)[None], w_gate_up, w_down)
 
@@ -349,23 +388,32 @@
     head = lax.axis_index("head")
     core = seq % 2
 
-    both = ("seq", "head")
-    near = permute_all(pick(w_gate_up, w_down, 1 - (head & 1)), both, device_perm(near_target))
     w_planes = w_qkv.transpose(1, 0, 2)
-    normed, key, value, send_state, zero = call(
+    normed, key, value, send_state, zero, *near = call(
         front_kernel,
-        [VMEM, VMEM, ANY],
+        [SMEM, VMEM, VMEM, HBM, HBM, HBM],
         [
-            out((TOK, D), BF),
-            out((TOK, WIDE), BF),
-            out((TOK, WIDE), BF),
+            chip((TOK, D), BF),
+            chip((TOK, WIDE), BF),
+            chip((TOK, WIDE), BF),
             out((WIDE, DH), BF),
             out((1,), jnp.int32),
-        ],
-        [pltpu.VMEM((D, WIDE), BF), pltpu.VMEM((D, WIDE), BF), pltpu.SemaphoreType.DMA((2,))],
-    )(hidden_in, attn_gain[None, :], w_planes)
+        ]
+        + QUARTER,
+        [pltpu.VMEM((D, WIDE), BF), pltpu.VMEM((D, WIDE), BF), pltpu.SemaphoreType.DMA((2,))]
+        + PICK_SCRATCH,
+    )(
+        (1 - (head & 1)).astype(jnp.int32)[None],
+        hidden_in,
+        attn_gain[None, :],
+        w_planes,
+        w_gate_up,
+        w_down,
+    )
+    both = ("seq", "head")
+    near = permute_all(near, both, device_perm(near_target))
     states = lax.all_to_all(send_state.reshape(32, 16, DH), "seq", 0, 0, tiled=True)
-    sums = call(prefix_kernel, [VMEM], [out((32, 16, DH), BF)])(states)[0]
+    sums = call(prefix_kernel, [VMEM], [out((32, 16, DH), BF)])(on_chip(states))[0]
     earlier = lax.all_to_all(sums, "seq", 0, 0, tiled=True).reshape(WIDE, DH)
     odd = (head & 1) + zero[0]
     rest = pick(w_gate_up, w_down, odd)
@@ -378,21 +426,21 @@
 
     query, local = call(
         local_kernel,
-        [VMEM, ANY, VMEM, VMEM],
-        [out((TOK, WIDE), BF), out((TOK, WIDE), F32)],
+        [VMEM, HBM, VMEM, VMEM],
+        [chip((TOK, WIDE), BF), chip((TOK, WIDE), F32)],
         [pltpu.VMEM((D, WIDE), BF), pltpu.SemaphoreType.DMA((1,))],
-    )(normed, w_planes, key, value)
+    )(on_chip(normed), w_planes, on_chip(key), on_chip(value))
     here = head.astype(jnp.int32)[None]
     blocks = call(
         attend_kernel,
         [SMEM] + [VMEM] * 5,
         BLOCKS_OUT,
         [pltpu.VMEM((TOK, WIDE), BF), pltpu.VMEM((TOK, WIDE), BF)],
-    )(here, earlier, query, local, out_gain[None, :], w_out)
+    )(here, on_chip(earlier), on_chip(query), on_chip(local), out_gain[None, :], w_out)
     tables = gather_head(jnp.concatenate([routes.astype(F32), gate_weights], axis=1))
     place_rows, weight = call(
-        routing_kernel, [SMEM] + [VMEM] * 4, [out((SLOTS, TOK), BF), out((TOK, SLOTS), BF)]
-    )(here, *tables)
+        routing_kernel, [SMEM] + [VMEM] * 4, [chip((SLOTS, TOK), BF), chip((TOK, SLOTS), BF)]
+    )(here, *[on_chip(t) for t in tables])
 
     attn_rows = scatter_head(blocks)
     resid = lax.dynamic_slice_in_dim(hidden_in, head * ROWS, ROWS, 0).astype(F32) + attn_rows
@@ -401,7 +449,7 @@
 
     sent = call(
         dispatch_kernel, [VMEM] * 5, [out((MAIN, PACKED), BF)], [pltpu.VMEM((TOK, D), BF)]
-    )(place_rows, *tokens)[0]
+    )(on_chip(place_rows), *[on_chip(t) for t in tokens])[0]
     received = lax.all_to_all(sent.reshape(32, 16, PACKED), "seq", 0, 0, tiled=True)
     keep = (head // 2 == core).astype(jnp.int32)[None]
     results = call(
@@ -416,11 +464,11 @@
             pltpu.VMEM((64, D), F32),
             pltpu.SemaphoreType.DMA((8,)),
         ],
-    )(keep, received.reshape(MAIN, PACKED), *[p[0] for p in pieces], *[p[1] for p in pieces])[0]
+    )(keep, on_chip(received.reshape(MAIN, PACKED)), *[p[0] for p in pieces], *[p[1] for p in pieces])[0]
     back = lax.all_to_all(results.reshape(32, 16, PACKED), "seq", 0, 0, tiled=True)
     blocks = call(
         combine_kernel, [VMEM] * 2, BLOCKS_OUT, [pltpu.VMEM((64, D), BF)]
-    )(weight, back.reshape(MAIN, PACKED))
+    )(on_chip(weight), on_chip(back.reshape(MAIN, PACKED)))
     moe_sum = scatter_head(blocks)
     return (resid + moe_sum).astype(BF)
 

time: 241 us -> 226 us (0.938)
  starting transfers between devices: 74.1 us -> 62.5 us
  Pallas kernels: 44.2 us -> 33.1 us
  waiting for transfers between devices: 74.2 us -> 83.6 us
    ppermute x6, waiting for transfers between devices: 18.4 us -> 29.6 us  [gather_head(): lax.ppermute(array, 'head', head_perm(k))]
    all_to_all x1, starting transfers between devices: 16.1 us -> 7.74 us  [on_device(): lax.all_to_all(sent.reshape(32, 16, PACKED), 'seq', 0, 0, tiled=True)]
    ppermute x1, waiting for transfers between devices: 0.01 us -> 6.15 us  [on_device(): far_down = lax.ppermute(rest[1], both, device_perm(far_target))]
    pallas_call x6 -> x5, Pallas kernels: 19.9 us -> 13.9 us  [the longest x1 6.68 us: on_device(): call(front_kernel, [SMEM, VMEM, VMEM, HBM, HBM, HBM], [chip((TOK, D), BF)...]
    ppermute x6, waiting for transfers between devices: 42.7 us -> 36.9 us  [scatter_head(): total = total + lax.ppermute(blocks[k], 'head', head_perm(k)).astype(F32)]
    ppermute x8, waiting for transfers between devices: 7.38 us -> 2.22 us  [permute_all(): return [lax.ppermute(a, axes, perm) for a in arrays]]
    ppermute x1, starting transfers between devices: 4.93 us -> 2.43 us  [on_device(): far = [lax.ppermute(rest[0], both, device_perm(far_target)), far_down]]
  transfers between devices with their start and end apart: 25 -> 25, of which waited for: 13 -> 13; matrix products, arithmetic and copies ran while one was open for 1% -> 1% of each run, Pallas kernels for 9% -> 6%
where the time goes in v4:
time: 226 us; the launch traced here: 223 us
  waiting for transfers between devices  83.6 us (37%)
  starting transfers between devices  62.5 us (28%)
  blocking collectives  37 us (16%)
  Pallas kernels  33.1 us (15%)
  other arithmetic  3.39 us (2%)
  local copies, waits for them, and re-layouts  2.74 us (1%)
    all_to_all x1, blocking collectives, on_device(): lax.all_to_all(results.reshape(32, 16, PACKED), 'seq', 0, 0, tiled=True)  37 us
    ppermute x6, waiting for transfers between devices, scatter_head(): total = total + lax.ppermute(blocks[k], 'head', head_perm(k)).astype(F32)  36.9 us
    ppermute x6, waiting for transfers between devices, gather_head(): lax.ppermute(array, 'head', head_perm(k))  29.6 us
    ppermute x8, starting transfers between devices, permute_all(): return [lax.ppermute(a, axes, perm) for a in arrays]  16.7 us
    pallas_call x1, Pallas kernels, on_device(): call(expert_kernel, [SMEM, VMEM] + [ANY] * 12, [out((MAIN, PACKED), BF)],...  11.3 us
    ppermute x6, starting transfers between devices, gather_head(): lax.ppermute(array, 'head', head_perm(k))  9.03 us
    all_to_all x1, starting transfers between devices, on_device(): lax.all_to_all(send_state.reshape(32, 16, DH), 'seq', 0, 0, tiled=True)  8.5 us
    ppermute x6, starting transfers between devices, scatter_head(): total = total + lax.ppermute(blocks[k], 'head', head_perm(k)).astype(F32)  7.83 us
  transfers between devices with their start and end apart: 25, of which 13 were waited for; matrix products, arithmetic and copies ran while one was open for 1% of the time, Pallas kernels for 6%

profile of v4, /device:TPU:33, one launch (start us, length us, event | category | flops | bytes accessed | tf_op | source)
XLA Modules:
  0.0 223.2 jit_solution(2043970952411399191)
XLA Ops:
  0.0 6.7 %shard_map.100 = (bf16[256,2048]{1,0:T(8,128)(2,1)S(1)}, bf16[256,512]{1,0:T(8,128)(2,1)S(1)}, bf16[256,512]{1,0:T(8,128)(2,1)S(1)}, bf16[512,128]{1,0:T(8,128)(...) custom-call(s32[1]{0:T(128)} %bitcast.1.index_ref, bf16[256,2048]{1,0:T(8,128)(2,1)} %x_ref.1, ...), custom_call_target="tpu_custom_call" | custom-call | tf_op jit(solution)/shard_map/pallas_call | solution.py:392
  6.7 8.5 %all-to-all-start = ((bf16[32,16,128]{2,1,0:T(8,128)(2,1)}), bf16[32,16,128]{2,1,0:T(8,128)(2,1)S(1)}, u32[]{:S(2)}, u32[]{:S(2)}) async-start(bf16[32,16,128]{2,1,0:T(8,128)(2,1)} %bitcast.21), calls=%async_computation | async-start | bytes 262144 | tf_op jit(solution)/shard_map/all_to_all | solution.py:415
  15.2 2.8 %collective-permute-start.9 = (bf16[2,2048,256]{2,1,0:T(8,128)(2,1)}, bf16[2,2048,256]{2,1,0:T(8,128)(2,1)}, u32[]{:S(2)}, u32[]{:S(2)}) collective-permute-start(bf16[2,2048,256]{2,1,0:T(8,128)(2,1)} %get-tuple-element.38), channel_id=1, source_target_pairs={{0,1},{1,4},{2,5},{3,0},{4,3},{5,6},{6,7},{7,2},{8,9},{9,12},{10,1... | collective-permute-start | bytes 6291464 | tf_op jit(solution)/shard_map/ppermute | solution.py:338
  18.6 2.6 %pick.1 = (bf16[2,2048,256]{2,1,0:T(8,128)(2,1)}, bf16[256,2048]{1,0:T(8,128)(2,1)S(1)}) custom-call(s32[1]{0:T(128)} %bitcast.11.refs_0_, bf16[2,2,2048,256]{3,2,1,0:T(8,128)(2,1)} %refs_1_.1, bf16[2,256,2048]{2,1,0:T(8,128)(2,1)} %refs_2_.1), custom_call_target="tpu_custom_call" | custom-call | tf_op jit(solution)/shard_map/pick/pallas_call | solution.py:362
  24.4 7.1 %all-to-all-start.1 = ((bf16[32,16,128]{2,1,0:T(8,128)(2,1)}), bf16[32,16,128]{2,1,0:T(8,128)(2,1)S(1)}, u32[]{:S(2)}, u32[]{:S(2)}) async-start(bf16[32,16,128]{2,1,0:T(8,128)(2,1)} %shard_map.101), calls=%async_computation.1 | async-start | bytes 262144 | tf_op jit(solution)/shard_map/all_to_all | solution.py:417
  31.5 2.8 %shard_map.102 = (bf16[256,512]{1,0:T(8,128)(2,1)S(1)}, f32[256,512]{1,0:T(8,128)S(1)}) custom-call(bf16[256,2048]{1,0:T(8,128)(2,1)S(1)} %get-tuple-element.27.normed_ref, bf16[3,2048,512]{2,1,0:T(8,128)(2,1)} %bitcast.18, bf16[256,512]{1,0:T(8,128)(2,1)S(1)} %get-tuple-element.28.k_ref, bf16[256,512]{1,0:T(8,128)(2,1)S(1)} %get-tuple-element.29.v_ref), custom_call_target="tpu_custom_call" | custom-call | tf_op jit(solution)/shard_map/pallas_call | solution.py:427
  35.0 3.1 %all-to-all-done.1 = bf16[32,16,128]{2,1,0:T(8,128)(2,1)S(1)} async-done(((bf16[32,16,128]{2,1,0:T(8,128)(2,1)}), bf16[32,16,128]{2,1,0:T(8,128)(2,1)S(1)}, u32[]{:S(2)}, u32[]{:S(2)}) %all-to-all-start.1) | async-done | bytes 131104 | tf_op jit(solution)/shard_map/all_to_all | solution.py:417
  39.1 3.7 %shard_map.103 = (f32[64,2048]{1,0:T(8,128)}, bf16[64,2048]{1,0:T(8,128)(2,1)}, bf16[64,2048]{1,0:T(8,128)(2,1)}, bf16[64,2048]{1,0:T(8,128)(2,1)}) custom-call(s32[1]{0:T(128)} %bitcast.head_ref, bf16[512,128]{1,0:T(8,128)(2,1)S(1)} %bitcast.16, bf16[256,512]{1,0:T(8,128)(2,1)S(1)} %copy-done.4, f32[256,512]{1,0:T(8,128)S(1)} %get-tuple-element.31.local_ref, ...), custom_call_target="tpu_custom_call" | custom-call | tf_op jit(solution)/shard_map/pallas_call | solution.py:434
  47.6 24.0 %collective-permute-done = bf16[64,2048]{1,0:T(8,128)(2,1)S(1)} collective-permute-done((bf16[64,2048]{1,0:T(8,128)(2,1)}, bf16[64,2048]{1,0:T(8,128)(2,1)S(1)}, u32[]{:S(2)}, u32[]{:S(2)}) %collective-permute-start) | collective-permute-done | bytes 262176 | tf_op jit(solution)/shard_map/ppermute | solution.py:380
  71.6 2.8 %collective-permute-start.14 = (bf16[256,2048]{1,0:T(8,128)(2,1)}, bf16[256,2048]{1,0:T(8,128)(2,1)}, u32[]{:S(2)}, u32[]{:S(2)}) collective-permute-start(bf16[256,2048]{1,0:T(8,128)(2,1)} %get-tuple-element.41), channel_id=1, source_target_pairs={{0,1},{1,4},{2,5},{3,0},{4,3},{5,6},{6,7},{7,2},{8,9},{9,12},{10,1... | collective-permute-start | bytes 3145736 | tf_op jit(solution)/shard_map/ppermute | solution.py:338
  76.6 3.1 %collective-permute-start.8 = (bf16[64,2048]{1,0:T(8,128)(2,1)S(1)}, bf16[64,2048]{1,0:T(8,128)(2,1)S(1)}, u32[]{:S(2)}, u32[]{:S(2)}) collective-permute-start(bf16[64,2048]{1,0:T(8,128)(2,1)S(1)} %multiply_convert_fusion.t0), channel_id=1, source_target_pairs={{0,3},{1,0},{2,1},{3,2},{4,7},{5,4},{6,5},{7,6},{8,11},{9,8},{10,9... | collective-permute-start | bytes 786440 | tf_op jit(solution)/shard_map/ppermute | solution.py:374
  80.3 12.3 %collective-permute-done.5.t3 = f32[64,16]{1,0:T(8,128)S(1)} collective-permute-done((f32[64,16]{1,0:T(8,128)S(1)}, f32[64,16]{1,0:T(8,128)S(1)}, u32[]{:S(2)}, u32[]{:S(2)}) %collective-permute-start.5) | collective-permute-done | bytes 4128 | tf_op jit(solution)/shard_map/ppermute | solution.py:374
  97.6 3.7 %collective-permute-done.3.t1 = f32[64,16]{1,0:T(8,128)S(1)} collective-permute-done((f32[64,16]{1,0:T(8,128)S(1)}, f32[64,16]{1,0:T(8,128)S(1)}, u32[]{:S(2)}, u32[]{:S(2)}) %collective-permute-start.3) | collective-permute-done | bytes 4128 | tf_op jit(solution)/shard_map/ppermute | solution.py:374
  105.0 3.5 %collective-permute-done.7.t2 = bf16[64,2048]{1,0:T(8,128)(2,1)S(1)} collective-permute-done((bf16[64,2048]{1,0:T(8,128)(2,1)S(1)}, bf16[64,2048]{1,0:T(8,128)(2,1)S(1)}, u32[]{:S(2)}, u32[]{:S(2)}) %collective-permute-start.7) | collective-permute-done | bytes 262176 | tf_op jit(solution)/shard_map/ppermute | solution.py:374
  108.5 7.9 %collective-permute-done.6.t1 = bf16[64,2048]{1,0:T(8,128)(2,1)S(1)} collective-permute-done((bf16[64,2048]{1,0:T(8,128)(2,1)S(1)}, bf16[64,2048]{1,0:T(8,128)(2,1)S(1)}, u32[]{:S(2)}, u32[]{:S(2)}) %collective-permute-start.6) | collective-permute-done | bytes 262176 | tf_op jit(solution)/shard_map/ppermute | solution.py:374
  118.7 7.7 %all-to-all-start.2 = ((bf16[32,16,2304]{2,1,0:T(8,128)(2,1)}), bf16[32,16,2304]{2,1,0:T(8,128)(2,1)S(1)}, u32[]{:S(2)}, u32[]{:S(2)}) async-start(bf16[32,16,2304]{2,1,0:T(8,128)(2,1)} %bitcast.20), calls=%async_computation.2 | async-start | bytes 4718592 | tf_op jit(solution)/shard_map/all_to_all | solution.py:453
  126.4 3.2 %collective-permute-start.17 = (bf16[256,2048]{1,0:T(8,128)(2,1)S(1)}, bf16[256,2048]{1,0:T(8,128)(2,1)}, u32[]{:S(2)}, u32[]{:S(2)}) collective-permute-start(bf16[256,2048]{1,0:T(8,128)(2,1)S(1)} %get-tuple-element.42.dn2), channel_id=1, source_target_pairs={{2,4},{3,5},{4,2},{5,3},{10,12},{11,13},{12,10},{13,11},{18,20},{1... | collective-permute-start | bytes 3145736 | tf_op jit(solution)/shard_map/ppermute | solution.py:420
  134.8 3.2 %collective-permute-start.13 = (bf16[2,2048,256]{2,1,0:T(8,128)(2,1)}, bf16[2,2048,256]{2,1,0:T(8,128)(2,1)}, u32[]{:S(2)}, u32[]{:S(2)}) collective-permute-start(bf16[2,2048,256]{2,1,0:T(8,128)(2,1)} %collective-permute-done.12.gu4), channel_id=1, source_target_pairs={{2,6},{3,7},{4,0},{5,1},{10,14},{11,15},{12,8},{13,9},{18,22},{19,... | collective-permute-start | bytes 6291464 | tf_op jit(solution)/shard_map/ppermute | solution.py:338
  138.0 6.2 %collective-permute-done.17.dn4 = bf16[256,2048]{1,0:T(8,128)(2,1)} collective-permute-done((bf16[256,2048]{1,0:T(8,128)(2,1)S(1)}, bf16[256,2048]{1,0:T(8,128)(2,1)}, u32[]{:S(2)}, u32[]{:S(2)}) %collective-permute-start.17) | collective-permute-done | bytes 1048608 | tf_op jit(solution)/shard_map/ppermute | solution.py:420
  145.2 2.6 %collective-permute-start.18 = (bf16[256,2048]{1,0:T(8,128)(2,1)}, bf16[256,2048]{1,0:T(8,128)(2,1)S(1)}, u32[]{:S(2)}, u32[]{:S(2)}) collective-permute-start(bf16[256,2048]{1,0:T(8,128)(2,1)} %collective-permute-done.17.dn4), channel_id=1, source_target_pairs={{2,6},{3,7},{4,0},{5,1},{10,14},{11,15},{12,8},{13,9},{18,22},{19,... | collective-permute-start | bytes 3145736 | tf_op jit(solution)/shard_map/ppermute | solution.py:338
  150.0 5.6 %all-to-all-done.2 = bf16[32,16,2304]{2,1,0:T(8,128)(2,1)S(1)} async-done(((bf16[32,16,2304]{2,1,0:T(8,128)(2,1)}), bf16[32,16,2304]{2,1,0:T(8,128)(2,1)S(1)}, u32[]{:S(2)}, u32[]{:S(2)}) %all-to-all-start.2) | async-done | bytes 2359328 | tf_op jit(solution)/shard_map/all_to_all | solution.py:453
  155.7 11.3 %shard_map.106 = bf16[512,2304]{1,0:T(8,128)(2,1)} custom-call(s32[1]{0:T(128)} %bitcast.7.keep_ref, bf16[512,2304]{1,0:T(8,128)(2,1)S(1)} %bitcast.14, bf16[2,2048,256]{2,1,0:T(8,128)(2,1)} %collective-permute-done.9.gu0, bf16[2,2048,256]{2,1,0:T(8,128)(2,1)} %collective-permute-done.10.gu1, bf16[2,2048,256]{2,1,0:T(8,128)(2,1)} %get-tuple-element.40.gu2, ...), custom_call_target="tpu_custom_call" | custom-call | tf_op jit(solution)/shard_map/pallas_call | solution.py:455
  167.0 37.0 %all_to_all.20 = bf16[32,16,2304]{2,1,0:T(8,128)(2,1)S(1)} all-to-all(bf16[32,16,2304]{2,1,0:T(8,128)(2,1)} %bitcast.19), channel_id=1, replica_groups=mesh['seq'=32,'head'=4] {'seq'}, dimensions={0} | all-to-all | bytes 4718592 | tf_op jit(solution)/shard_map/all_to_all | solution.py:468
  209.0 11.9 %collective-permute-done.19 = bf16[64,2048]{1,0:T(8,128)(2,1)S(1)} collective-permute-done((bf16[64,2048]{1,0:T(8,128)(2,1)}, bf16[64,2048]{1,0:T(8,128)(2,1)S(1)}, u32[]{:S(2)}, u32[]{:S(2)}) %collective-permute-start.19) | collective-permute-done | bytes 262176 | tf_op jit(solution)/shard_map/ppermute | solution.py:380
  (67 shorter events, 39.0 us)
Async XLA Ops:
  6.7 17.0 %all-to-all-start = ((bf16[32,16,128]{2,1,0:T(8,128)(2,1)}), bf16[32,16,128]{2,1,0:T(8,128)(2,1)S(1)}, u32[]{:S(2)}, u32[]{:S(2)}) async-start(bf16[32,16,128]{2,1,0:T(8,128)(2,1)} %bitcast.21), calls=%async_computation | async-start | bytes 262144 | tf_op jit(solution)/shard_map/all_to_all | solution.py:415
  15.2 117.0 %collective-permute-start.9 = (bf16[2,2048,256]{2,1,0:T(8,128)(2,1)}, bf16[2,2048,256]{2,1,0:T(8,128)(2,1)}, u32[]{:S(2)}, u32[]{:S(2)}) collective-permute-start(bf16[2,2048,256]{2,1,0:T(8,128)(2,1)} %get-tuple-element.38), channel_id=1, source_target_pairs={{0,1},{1,4},{2,5},{3,0},{4,3},{5,6},{6,7},{7,2},{8,9},{9,12},{10,1... | collective-permute-start | bytes 6291464 | tf_op jit(solution)/shard_map/ppermute | solution.py:338
  21.3 113.5 %collective-permute-start.12 = (bf16[2,2048,256]{2,1,0:T(8,128)(2,1)}, bf16[2,2048,256]{2,1,0:T(8,128)(2,1)}, u32[]{:S(2)}, u32[]{:S(2)}) collective-permute-start(bf16[2,2048,256]{2,1,0:T(8,128)(2,1)} %get-tuple-element.40.gu2), channel_id=1, source_target_pairs={{2,4},{3,5},{4,2},{5,3},{10,12},{11,13},{12,10},{13,11},{18,20},{1... | collective-permute-start | bytes 6291464 | tf_op jit(solution)/shard_map/ppermute | solution.py:421
  24.4 13.7 %all-to-all-start.1 = ((bf16[32,16,128]{2,1,0:T(8,128)(2,1)}), bf16[32,16,128]{2,1,0:T(8,128)(2,1)S(1)}, u32[]{:S(2)}, u32[]{:S(2)}) async-start(bf16[32,16,128]{2,1,0:T(8,128)(2,1)} %shard_map.101), calls=%async_computation.1 | async-start | bytes 262144 | tf_op jit(solution)/shard_map/all_to_all | solution.py:417
  42.8 28.8 %collective-permute-start = (bf16[64,2048]{1,0:T(8,128)(2,1)}, bf16[64,2048]{1,0:T(8,128)(2,1)S(1)}, u32[]{:S(2)}, u32[]{:S(2)}) collective-permute-start(bf16[64,2048]{1,0:T(8,128)(2,1)} %get-tuple-element.33), channel_id=1, source_target_pairs={{0,1},{1,2},{2,3},{3,0},{4,5},{5,6},{6,7},{7,4},{8,9},{9,10},{10,1... | collective-permute-start | bytes 786440 | tf_op jit(solution)/shard_map/ppermute | solution.py:380
  43.3 31.1 %collective-permute-start.1 = (bf16[64,2048]{1,0:T(8,128)(2,1)}, bf16[64,2048]{1,0:T(8,128)(2,1)S(1)}, u32[]{:S(2)}, u32[]{:S(2)}) collective-permute-start(bf16[64,2048]{1,0:T(8,128)(2,1)} %get-tuple-element.34), channel_id=1, source_target_pairs={{0,2},{1,3},{2,0},{3,1},{4,6},{5,7},{6,4},{7,5},{8,10},{9,11},{10,... | collective-permute-start | bytes 786440 | tf_op jit(solution)/shard_map/ppermute | solution.py:380
  45.8 29.3 %collective-permute-start.2 = (bf16[64,2048]{1,0:T(8,128)(2,1)}, bf16[64,2048]{1,0:T(8,128)(2,1)S(1)}, u32[]{:S(2)}, u32[]{:S(2)}) collective-permute-start(bf16[64,2048]{1,0:T(8,128)(2,1)} %get-tuple-element.35), channel_id=1, source_target_pairs={{0,3},{1,0},{2,1},{3,2},{4,7},{5,4},{6,5},{7,6},{8,11},{9,8},{10,9... | collective-permute-start | bytes 786440 | tf_op jit(solution)/shard_map/ppermute | solution.py:380
  71.6 59.3 %collective-permute-start.14 = (bf16[256,2048]{1,0:T(8,128)(2,1)}, bf16[256,2048]{1,0:T(8,128)(2,1)}, u32[]{:S(2)}, u32[]{:S(2)}) collective-permute-start(bf16[256,2048]{1,0:T(8,128)(2,1)} %get-tuple-element.41), channel_id=1, source_target_pairs={{0,1},{1,4},{2,5},{3,0},{4,3},{5,6},{6,7},{7,2},{8,9},{9,12},{10,1... | collective-permute-start | bytes 3145736 | tf_op jit(solution)/shard_map/ppermute | solution.py:338
  76.6 25.7 %collective-permute-start.8 = (bf16[64,2048]{1,0:T(8,128)(2,1)S(1)}, bf16[64,2048]{1,0:T(8,128)(2,1)S(1)}, u32[]{:S(2)}, u32[]{:S(2)}) collective-permute-start(bf16[64,2048]{1,0:T(8,128)(2,1)S(1)} %multiply_convert_fusion.t0), channel_id=1, source_target_pairs={{0,3},{1,0},{2,1},{3,2},{4,7},{5,4},{6,5},{7,6},{8,11},{9,8},{10,9... | collective-permute-start | bytes 786440 | tf_op jit(solution)/shard_map/ppermute | solution.py:374
  79.7 12.9 %collective-permute-start.5 = (f32[64,16]{1,0:T(8,128)S(1)}, f32[64,16]{1,0:T(8,128)S(1)}, u32[]{:S(2)}, u32[]{:S(2)}) collective-permute-start(f32[64,16]{1,0:T(8,128)S(1)} %copy.16.t0), channel_id=1, source_target_pairs={{0,3},{1,0},{2,1},{3,2},{4,7},{5,4},{6,5},{7,6},{8,11},{9,8},{10,9... | collective-permute-start | bytes 12296 | tf_op jit(solution)/shard_map/ppermute | solution.py:374
  92.6 4.3 %collective-permute-start.4 = (f32[64,16]{1,0:T(8,128)S(1)}, f32[64,16]{1,0:T(8,128)S(1)}, u32[]{:S(2)}, u32[]{:S(2)}) collective-permute-start(f32[64,16]{1,0:T(8,128)S(1)} %copy.16.t0), channel_id=1, source_target_pairs={{0,2},{1,3},{2,0},{3,1},{4,6},{5,7},{6,4},{7,5},{8,10},{9,11},{10,... | collective-permute-start | bytes 12296 | tf_op jit(solution)/shard_map/ppermute | solution.py:374
  96.9 4.4 %collective-permute-start.3 = (f32[64,16]{1,0:T(8,128)S(1)}, f32[64,16]{1,0:T(8,128)S(1)}, u32[]{:S(2)}, u32[]{:S(2)}) collective-permute-start(f32[64,16]{1,0:T(8,128)S(1)} %copy.16.t0), channel_id=1, source_target_pairs={{0,1},{1,2},{2,3},{3,0},{4,5},{5,6},{6,7},{7,4},{8,9},{9,10},{10,1... | collective-permute-start | bytes 12296 | tf_op jit(solution)/shard_map/ppermute | solution.py:374
  101.3 7.2 %collective-permute-start.7 = (bf16[64,2048]{1,0:T(8,128)(2,1)S(1)}, bf16[64,2048]{1,0:T(8,128)(2,1)S(1)}, u32[]{:S(2)}, u32[]{:S(2)}) collective-permute-start(bf16[64,2048]{1,0:T(8,128)(2,1)S(1)} %multiply_convert_fusion.t0), channel_id=1, source_target_pairs={{0,2},{1,3},{2,0},{3,1},{4,6},{5,7},{6,4},{7,5},{8,10},{9,11},{10,... | collective-permute-start | bytes 786440 | tf_op jit(solution)/shard_map/ppermute | solution.py:374
  102.3 14.1 %collective-permute-start.6 = (bf16[64,2048]{1,0:T(8,128)(2,1)S(1)}, bf16[64,2048]{1,0:T(8,128)(2,1)S(1)}, u32[]{:S(2)}, u32[]{:S(2)}) collective-permute-start(bf16[64,2048]{1,0:T(8,128)(2,1)S(1)} %multiply_convert_fusion.t0), channel_id=1, source_target_pairs={{0,1},{1,2},{2,3},{3,0},{4,5},{5,6},{6,7},{7,4},{8,9},{9,10},{10,1... | collective-permute-start | bytes 786440 | tf_op jit(solution)/shard_map/ppermute | solution.py:374
  118.7 37.0 %all-to-all-start.2 = ((bf16[32,16,2304]{2,1,0:T(8,128)(2,1)}), bf16[32,16,2304]{2,1,0:T(8,128)(2,1)S(1)}, u32[]{:S(2)}, u32[]{:S(2)}) async-start(bf16[32,16,2304]{2,1,0:T(8,128)(2,1)} %bitcast.20), calls=%async_computation.2 | async-start | bytes 4718592 | tf_op jit(solution)/shard_map/all_to_all | solution.py:453
  126.4 17.8 %collective-permute-start.17 = (bf16[256,2048]{1,0:T(8,128)(2,1)S(1)}, bf16[256,2048]{1,0:T(8,128)(2,1)}, u32[]{:S(2)}, u32[]{:S(2)}) collective-permute-start(bf16[256,2048]{1,0:T(8,128)(2,1)S(1)} %get-tuple-element.42.dn2), channel_id=1, source_target_pairs={{2,4},{3,5},{4,2},{5,3},{10,12},{11,13},{12,10},{13,11},{18,20},{1... | collective-permute-start | bytes 3145736 | tf_op jit(solution)/shard_map/ppermute | solution.py:420
  129.6 14.6 %collective-permute-start.16 = (bf16[256,2048]{1,0:T(8,128)(2,1)S(1)}, bf16[256,2048]{1,0:T(8,128)(2,1)S(1)}, u32[]{:S(2)}, u32[]{:S(2)}) collective-permute-start(bf16[256,2048]{1,0:T(8,128)(2,1)S(1)} %get-tuple-element.42.dn2), channel_id=1, source_target_pairs={{0,4},{1,5},{6,2},{7,3},{8,12},{9,13},{14,10},{15,11},{16,20},{17,... | collective-permute-start | bytes 3145736 | tf_op jit(solution)/shard_map/ppermute | solution.py:338
  130.9 19.2 %collective-permute-start.11 = (bf16[2,2048,256]{2,1,0:T(8,128)(2,1)}, bf16[2,2048,256]{2,1,0:T(8,128)(2,1)}, u32[]{:S(2)}, u32[]{:S(2)}) collective-permute-start(bf16[2,2048,256]{2,1,0:T(8,128)(2,1)} %get-tuple-element.40.gu2), channel_id=1, source_target_pairs={{0,4},{1,5},{6,2},{7,3},{8,12},{9,13},{14,10},{15,11},{16,20},{17,... | collective-permute-start | bytes 6291464 | tf_op jit(solution)/shard_map/ppermute | solution.py:338
  132.2 23.5 %collective-permute-start.10 = (bf16[2,2048,256]{2,1,0:T(8,128)(2,1)}, bf16[2,2048,256]{2,1,0:T(8,128)(2,1)}, u32[]{:S(2)}, u32[]{:S(2)}) collective-permute-start(bf16[2,2048,256]{2,1,0:T(8,128)(2,1)} %collective-permute-done.9.gu0), channel_id=1, source_target_pairs={{0,4},{4,0},{8,12},{12,8},{16,20},{20,16},{24,28},{28,24},{32,36},... | collective-permute-start | bytes 6291464 | tf_op jit(solution)/shard_map/ppermute | solution.py:338
  134.8 20.9 %collective-permute-start.13 = (bf16[2,2048,256]{2,1,0:T(8,128)(2,1)}, bf16[2,2048,256]{2,1,0:T(8,128)(2,1)}, u32[]{:S(2)}, u32[]{:S(2)}) collective-permute-start(bf16[2,2048,256]{2,1,0:T(8,128)(2,1)} %collective-permute-done.12.gu4), channel_id=1, source_target_pairs={{2,6},{3,7},{4,0},{5,1},{10,14},{11,15},{12,8},{13,9},{18,22},{19,... | collective-permute-start | bytes 6291464 | tf_op jit(solution)/shard_map/ppermute | solution.py:338
  145.2 4.9 %collective-permute-start.18 = (bf16[256,2048]{1,0:T(8,128)(2,1)}, bf16[256,2048]{1,0:T(8,128)(2,1)S(1)}, u32[]{:S(2)}, u32[]{:S(2)}) collective-permute-start(bf16[256,2048]{1,0:T(8,128)(2,1)} %collective-permute-done.17.dn4), channel_id=1, source_target_pairs={{2,6},{3,7},{4,0},{5,1},{10,14},{11,15},{12,8},{13,9},{18,22},{19,... | collective-permute-start | bytes 3145736 | tf_op jit(solution)/shard_map/ppermute | solution.py:338
  206.0 15.0 %collective-permute-start.19 = (bf16[64,2048]{1,0:T(8,128)(2,1)}, bf16[64,2048]{1,0:T(8,128)(2,1)S(1)}, u32[]{:S(2)}, u32[]{:S(2)}) collective-permute-start(bf16[64,2048]{1,0:T(8,128)(2,1)} %get-tuple-element.44), channel_id=1, source_target_pairs={{0,1},{1,2},{2,3},{3,0},{4,5},{5,6},{6,7},{7,4},{8,9},{9,10},{10,1... | collective-permute-start | bytes 786440 | tf_op jit(solution)/shard_map/ppermute | solution.py:380
  206.0 15.0 %collective-permute-start.20 = (bf16[64,2048]{1,0:T(8,128)(2,1)}, bf16[64,2048]{1,0:T(8,128)(2,1)S(1)}, u32[]{:S(2)}, u32[]{:S(2)}) collective-permute-start(bf16[64,2048]{1,0:T(8,128)(2,1)} %get-tuple-element.45), channel_id=1, source_target_pairs={{0,2},{1,3},{2,0},{3,1},{4,6},{5,7},{6,4},{7,5},{8,10},{9,11},{10,... | collective-permute-start | bytes 786440 | tf_op jit(solution)/shard_map/ppermute | solution.py:380
  207.5 13.8 %collective-permute-start.21 = (bf16[64,2048]{1,0:T(8,128)(2,1)}, bf16[64,2048]{1,0:T(8,128)(2,1)S(1)}, u32[]{:S(2)}, u32[]{:S(2)}) collective-permute-start(bf16[64,2048]{1,0:T(8,128)(2,1)} %get-tuple-element.46), channel_id=1, source_target_pairs={{0,3},{1,0},{2,1},{3,2},{4,7},{5,4},{6,5},{7,6},{8,11},{9,8},{10,9... | collective-permute-start | bytes 786440 | tf_op jit(solution)/shard_map/ppermute | solution.py:380
  (13 other events, 302.6 us)

commit v5 on v4

--- a/solution.py
+++ b/solution.py
@@ -241,19 +241,9 @@
     return copies + [load(2, arrays[2]), load(3, arrays[4])]
 
 
-def expert_kernel(
-    keep_ref, x_ref, gu0, gu1, gu2, gu3, gu4, gu5, dn0, dn1, dn2, dn3, dn4, dn5,
-    out_ref, rows, gate_up, down, act, tail, sems,
-):
+def gate_kernel(keep_ref, x_ref, gu0, gu1, gu2, gu3, gu4, gu5, act_ref, rows, gate_up, sems):
     copies = start_quarters(
         keep_ref, (gu0, gu1, gu2, gu3, gu4, gu5), lambda q: gate_up.at[q], sems, 0
-    )
-    down_copies = start_quarters(
-        keep_ref,
-        (dn0, dn1, dn2, dn3, dn4, dn5),
-        lambda q: down.at[q * 256:(q + 1) * 256],
-        sems,
-        4,
     )
     rows[:MAIN, :] = x_ref[:, :D]
     for t in range(2):
@@ -263,11 +253,26 @@
         copies[q].wait()
         gate = dot(rows[...], gate_up[q, 0])
         up = dot(rows[...], gate_up[q, 1])
-        act[:, q * 256:(q + 1) * 256] = (jax.nn.silu(gate) * up).astype(BF)
-    for copy in down_copies:
-        copy.wait()
+        act_ref[:, q * 256:(q + 1) * 256] = (jax.nn.silu(gate) * up).astype(BF)
+
+
+def down_kernel(keep_ref, act, dn0, dn1, dn2, dn3, dn4, dn5, out_ref, down, tail, sems):
+    copies = []
     for n in range(4):
         cols = slice(n * 512, (n + 1) * 512)
+        copies.append(
+            start_quarters(
+                keep_ref,
+                [dn.at[:, cols] for dn in (dn0, dn1, dn2, dn3, dn4, dn5)],
+                lambda q: down.at[q * 256:(q + 1) * 256, cols],
+                sems,
+                4 * n,
+            )
+        )
+    for n in range(4):
+        cols = slice(n * 512, (n + 1) * 512)
+        for copy in copies[n]:
+            copy.wait()
         result = dot(act[...], down[:, cols])
         out_ref[:, cols] = result[:MAIN].astype(BF)
         tail[:, cols] = result[MAIN:]
@@ -421,13 +426,14 @@
     far = [lax.ppermute(rest[0], both, device_perm(far_target)), far_down]
     rest_other = permute_all(rest, both, device_perm(keep_target))
     near_other = permute_all(near, "seq", seq_perm(0, 0, 1))
-    far_other = permute_all(far, both, device_perm(pass_target))
+    far_other = [lax.ppermute(far[0], both, device_perm(pass_target))]
+    far_other.append(lax.ppermute(far[1], both, device_perm(pass_target)))
     pieces = [near, near_other, rest, rest_other, far, far_other]
 
     query, local = call(
         local_kernel,
         [VMEM, HBM, VMEM, VMEM],
-        [chip((TOK, WIDE), BF), chip((TOK, WIDE), F32)],
+        [out((TOK, WIDE), BF), chip((TOK, WIDE), F32)],
         [pltpu.VMEM((D, WIDE), BF), pltpu.SemaphoreType.DMA((1,))],
     )(on_chip(normed), w_planes, on_chip(key), on_chip(value))
     here = head.astype(jnp.int32)[None]
@@ -436,7 +442,7 @@
         [SMEM] + [VMEM] * 5,
         BLOCKS_OUT,
         [pltpu.VMEM((TOK, WIDE), BF), pltpu.VMEM((TOK, WIDE), BF)],
-    )(here, on_chip(earlier), on_chip(query), on_chip(local), out_gain[None, :], w_out)
+    )(here, on_chip(earlier), query, on_chip(local), out_gain[None, :], w_out)
     tables = gather_head(jnp.concatenate([routes.astype(F32), gate_weights], axis=1))
     place_rows, weight = call(
         routing_kernel, [SMEM] + [VMEM] * 4, [chip((SLOTS, TOK), BF), chip((TOK, SLOTS), BF)]
@@ -452,19 +458,26 @@
     )(on_chip(place_rows), *[on_chip(t) for t in tokens])[0]
     received = lax.all_to_all(sent.reshape(32, 16, PACKED), "seq", 0, 0, tiled=True)
     keep = (head // 2 == core).astype(jnp.int32)[None]
-    results = call(
-        expert_kernel,
-        [SMEM, VMEM] + [ANY] * 12,
-        [out((MAIN, PACKED), BF)],
+    act = call(
+        gate_kernel,
+        [SMEM, VMEM] + [ANY] * 6,
+        [chip((SLOTS, 1024), BF)],
         [
             pltpu.VMEM((SLOTS, D), BF),
             pltpu.VMEM((4, 2, D, 256), BF),
+            pltpu.SemaphoreType.DMA((4,)),
+        ],
+    )(keep, on_chip(received.reshape(MAIN, PACKED)), *[p[0] for p in pieces])[0]
+    results = call(
+        down_kernel,
+        [SMEM, VMEM] + [ANY] * 6,
+        [out((MAIN, PACKED), BF)],
+        [
             pltpu.VMEM((1024, D), BF),
-            pltpu.VMEM((SLOTS, 1024), BF),
             pltpu.VMEM((64, D), F32),
-            pltpu.SemaphoreType.DMA((8,)),
+            pltpu.SemaphoreType.DMA((16,)),
         ],
-    )(keep, on_chip(received.reshape(MAIN, PACKED)), *[p[0] for p in pieces], *[p[1] for p in pieces])[0]
+    )(keep, on_chip(act), *[p[1] for p in pieces])[0]
     back = lax.all_to_all(results.reshape(32, 16, PACKED), "seq", 0, 0, tiled=True)
     blocks = call(
         combine_kernel, [VMEM] * 2, BLOCKS_OUT, [pltpu.VMEM((64, D), BF)]

time: 226 us -> 232 us (1.027)
  waiting for transfers between devices: 83.6 us -> 93.2 us
  starting transfers between devices: 62.5 us -> 58.3 us
    ppermute x8 -> x6, waiting for transfers between devices: 2.22 us -> 21.4 us  [permute_all(): return [lax.ppermute(a, axes, perm) for a in arrays]]
    ppermute x6, waiting for transfers between devices: 36.9 us -> 44 us  [scatter_head(): total = total + lax.ppermute(blocks[k], 'head', head_perm(k)).astype(F32)]
    ppermute x0 -> x2, starting transfers between devices: none -> 6.21 us  [the longest x1 3.31 us: on_device(): far_other = [lax.ppermute(far[0], both, device_perm(pass_target))]]
    ppermute x1, waiting for transfers between devices: 6.15 us -> 0.01 us  [on_device(): far_down = lax.ppermute(rest[1], both, device_perm(far_target))]
    ppermute x8 -> x6, starting transfers between devices: 16.7 us -> 10.7 us  [permute_all(): return [lax.ppermute(a, axes, perm) for a in arrays]]
    ppermute x6, starting transfers between devices: 9.03 us -> 3.4 us  [gather_head(): lax.ppermute(array, 'head', head_perm(k))]
    all_to_all x1, waiting for transfers between devices: 5.62 us -> 0.01 us  [on_device(): lax.all_to_all(sent.reshape(32, 16, PACKED), 'seq', 0, 0, tiled=True)]
    ppermute x6, waiting for transfers between devices: 29.6 us -> 24.3 us  [gather_head(): lax.ppermute(array, 'head', head_perm(k))]
  transfers between devices with their start and end apart: 25 -> 25, of which waited for: 13 -> 10; matrix products, arithmetic and copies ran while one was open for 1% -> 1% of each run, Pallas kernels for 6% -> 9%
where the time goes in v5:
time: 232 us; the launch traced here: 229 us
  waiting for transfers between devices  93.2 us (40%)
  starting transfers between devices  58.3 us (25%)
  blocking collectives  37.5 us (16%)
  Pallas kernels  35.3 us (15%)
  other arithmetic  3.39 us (1%)
    ppermute x6, waiting for transfers between devices, scatter_head(): total = total + lax.ppermute(blocks[k], 'head', head_perm(k)).astype(F32)  44 us
    all_to_all x1, blocking collectives, on_device(): lax.all_to_all(results.reshape(32, 16, PACKED), 'seq', 0, 0, tiled=True)  37.5 us
    ppermute x6, waiting for transfers between devices, gather_head(): lax.ppermute(array, 'head', head_perm(k))  24.3 us
    ppermute x6, waiting for transfers between devices, permute_all(): return [lax.ppermute(a, axes, perm) for a in arrays]  21.4 us
    ppermute x6, starting transfers between devices, permute_all(): return [lax.ppermute(a, axes, perm) for a in arrays]  10.7 us
    all_to_all x1, starting transfers between devices, on_device(): lax.all_to_all(sent.reshape(32, 16, PACKED), 'seq', 0, 0, tiled=True)  10.4 us
    all_to_all x1, starting transfers between devices, on_device(): lax.all_to_all(send_state.reshape(32, 16, DH), 'seq', 0, 0, tiled=True)  8.5 us
    ppermute x6, starting transfers between devices, scatter_head(): total = total + lax.ppermute(blocks[k], 'head', head_perm(k)).astype(F32)  7.55 us
  transfers between devices with their start and end apart: 25, of which 10 were waited for; matrix products, arithmetic and copies ran while one was open for 1% of the time, Pallas kernels for 9%

profile of v5, /device:TPU:33, one launch (start us, length us, event | category | flops | bytes accessed | tf_op | source)
XLA Modules:
  0.0 229.2 jit_solution(14663486629332255285)
XLA Ops:
  0.0 6.7 %shard_map.100 = (bf16[256,2048]{1,0:T(8,128)(2,1)S(1)}, bf16[256,512]{1,0:T(8,128)(2,1)S(1)}, bf16[256,512]{1,0:T(8,128)(2,1)S(1)}, bf16[512,128]{1,0:T(8,128)(...) custom-call(s32[1]{0:T(128)} %bitcast.1.index_ref, bf16[256,2048]{1,0:T(8,128)(2,1)} %x_ref.1, ...), custom_call_target="tpu_custom_call" | custom-call | tf_op jit(solution)/shard_map/pallas_call | solution.py:397
  6.7 8.5 %all-to-all-start = ((bf16[32,16,128]{2,1,0:T(8,128)(2,1)}), bf16[32,16,128]{2,1,0:T(8,128)(2,1)S(1)}, u32[]{:S(2)}, u32[]{:S(2)}) async-start(bf16[32,16,128]{2,1,0:T(8,128)(2,1)} %bitcast.21), calls=%async_computation | async-start | bytes 262144 | tf_op jit(solution)/shard_map/all_to_all | solution.py:420
  15.2 2.8 %collective-permute-start.9 = (bf16[2,2048,256]{2,1,0:T(8,128)(2,1)}, bf16[2,2048,256]{2,1,0:T(8,128)(2,1)}, u32[]{:S(2)}, u32[]{:S(2)}) collective-permute-start(bf16[2,2048,256]{2,1,0:T(8,128)(2,1)} %get-tuple-element.38), channel_id=1, source_target_pairs={{0,1},{1,4},{2,5},{3,0},{4,3},{5,6},{6,7},{7,2},{8,9},{9,12},{10,1... | collective-permute-start | bytes 6291464 | tf_op jit(solution)/shard_map/ppermute | solution.py:343
  18.7 2.6 %pick.1 = (bf16[2,2048,256]{2,1,0:T(8,128)(2,1)}, bf16[256,2048]{1,0:T(8,128)(2,1)S(1)}) custom-call(s32[1]{0:T(128)} %bitcast.11.refs_0_, bf16[2,2,2048,256]{3,2,1,0:T(8,128)(2,1)} %refs_1_.1, bf16[2,256,2048]{2,1,0:T(8,128)(2,1)} %refs_2_.1), custom_call_target="tpu_custom_call" | custom-call | tf_op jit(solution)/shard_map/pick/pallas_call | solution.py:367
  24.4 7.1 %all-to-all-start.1 = ((bf16[32,16,128]{2,1,0:T(8,128)(2,1)}), bf16[32,16,128]{2,1,0:T(8,128)(2,1)S(1)}, u32[]{:S(2)}, u32[]{:S(2)}) async-start(bf16[32,16,128]{2,1,0:T(8,128)(2,1)} %shard_map.101), calls=%async_computation.1 | async-start | bytes 262144 | tf_op jit(solution)/shard_map/all_to_all | solution.py:422
  31.6 3.0 %shard_map.102 = (bf16[256,512]{1,0:T(8,128)(2,1)}, f32[256,512]{1,0:T(8,128)S(1)}) custom-call(bf16[256,2048]{1,0:T(8,128)(2,1)S(1)} %get-tuple-element.27.normed_ref, bf16[3,2048,512]{2,1,0:T(8,128)(2,1)} %bitcast.18, bf16[256,512]{1,0:T(8,128)(2,1)S(1)} %get-tuple-element.28.k_ref, bf16[256,512]{1,0:T(8,128)(2,1)S(1)} %get-tuple-element.29.v_ref), custom_call_target="tpu_custom_call" | custom-call | tf_op jit(solution)/shard_map/pallas_call | solution.py:433
  34.6 3.6 %all-to-all-done.1 = bf16[32,16,128]{2,1,0:T(8,128)(2,1)S(1)} async-done(((bf16[32,16,128]{2,1,0:T(8,128)(2,1)}), bf16[32,16,128]{2,1,0:T(8,128)(2,1)S(1)}, u32[]{:S(2)}, u32[]{:S(2)}) %all-to-all-start.1) | async-done | bytes 131104 | tf_op jit(solution)/shard_map/all_to_all | solution.py:422
  38.1 3.8 %shard_map.103 = (f32[64,2048]{1,0:T(8,128)}, bf16[64,2048]{1,0:T(8,128)(2,1)}, bf16[64,2048]{1,0:T(8,128)(2,1)}, bf16[64,2048]{1,0:T(8,128)(2,1)}) custom-call(s32[1]{0:T(128)} %bitcast.head_ref, bf16[512,128]{1,0:T(8,128)(2,1)S(1)} %bitcast.16, bf16[256,512]{1,0:T(8,128)(2,1)} %get-tuple-element.30.q_ref, f32[256,512]{1,0:T(8,128)S(1)} %get-tuple-element.31.local_ref, ...), custom_call_target="tpu_custom_call" | custom-call | tf_op jit(solution)/shard_map/pallas_call | solution.py:440
  45.5 29.6 %collective-permute-done.2 = bf16[64,2048]{1,0:T(8,128)(2,1)S(1)} collective-permute-done((bf16[64,2048]{1,0:T(8,128)(2,1)}, bf16[64,2048]{1,0:T(8,128)(2,1)S(1)}, u32[]{:S(2)}, u32[]{:S(2)}) %collective-permute-start.2) | collective-permute-done | bytes 262176 | tf_op jit(solution)/shard_map/ppermute | solution.py:385
  79.8 8.9 %collective-permute-done.3.t1 = f32[64,16]{1,0:T(8,128)S(1)} collective-permute-done((f32[64,16]{1,0:T(8,128)S(1)}, f32[64,16]{1,0:T(8,128)S(1)}, u32[]{:S(2)}, u32[]{:S(2)}) %collective-permute-start.3) | collective-permute-done | bytes 4128 | tf_op jit(solution)/shard_map/ppermute | solution.py:379
  88.7 4.3 %collective-permute-done.4.t2 = f32[64,16]{1,0:T(8,128)S(1)} collective-permute-done((f32[64,16]{1,0:T(8,128)S(1)}, f32[64,16]{1,0:T(8,128)S(1)}, u32[]{:S(2)}, u32[]{:S(2)}) %collective-permute-start.4) | collective-permute-done | bytes 4128 | tf_op jit(solution)/shard_map/ppermute | solution.py:379
  93.0 2.8 %collective-permute-done.5.t3 = f32[64,16]{1,0:T(8,128)S(1)} collective-permute-done((f32[64,16]{1,0:T(8,128)S(1)}, f32[64,16]{1,0:T(8,128)S(1)}, u32[]{:S(2)}, u32[]{:S(2)}) %collective-permute-start.5) | collective-permute-done | bytes 4128 | tf_op jit(solution)/shard_map/ppermute | solution.py:379
  99.0 3.5 %collective-permute-done.7.t2 = bf16[64,2048]{1,0:T(8,128)(2,1)S(1)} collective-permute-done((bf16[64,2048]{1,0:T(8,128)(2,1)S(1)}, bf16[64,2048]{1,0:T(8,128)(2,1)S(1)}, u32[]{:S(2)}, u32[]{:S(2)}) %collective-permute-start.7) | collective-permute-done | bytes 262176 | tf_op jit(solution)/shard_map/ppermute | solution.py:379
  102.5 4.9 %collective-permute-done.8.t3 = bf16[64,2048]{1,0:T(8,128)(2,1)S(1)} collective-permute-done((bf16[64,2048]{1,0:T(8,128)(2,1)S(1)}, bf16[64,2048]{1,0:T(8,128)(2,1)S(1)}, u32[]{:S(2)}, u32[]{:S(2)}) %collective-permute-start.8) | collective-permute-done | bytes 262176 | tf_op jit(solution)/shard_map/ppermute | solution.py:379
  109.6 10.4 %all-to-all-start.2 = ((bf16[32,16,2304]{2,1,0:T(8,128)(2,1)}), bf16[32,16,2304]{2,1,0:T(8,128)(2,1)S(1)}, u32[]{:S(2)}, u32[]{:S(2)}) async-start(bf16[32,16,2304]{2,1,0:T(8,128)(2,1)} %bitcast.20), calls=%async_computation.2 | async-start | bytes 4718592 | tf_op jit(solution)/shard_map/all_to_all | solution.py:459
  120.5 3.3 %collective-permute-start.13 = (bf16[2,2048,256]{2,1,0:T(8,128)(2,1)}, bf16[2,2048,256]{2,1,0:T(8,128)(2,1)}, u32[]{:S(2)}, u32[]{:S(2)}) collective-permute-start(bf16[2,2048,256]{2,1,0:T(8,128)(2,1)} %collective-permute-done.12.gu4), channel_id=1, source_target_pairs={{2,6},{3,7},{4,0},{5,1},{10,14},{11,15},{12,8},{13,9},{18,22},{19,... | collective-permute-start | bytes 6291464 | tf_op jit(solution)/shard_map/ppermute | solution.py:429
  128.3 21.3 %collective-permute-done.14.dn0 = bf16[256,2048]{1,0:T(8,128)(2,1)} collective-permute-done((bf16[256,2048]{1,0:T(8,128)(2,1)}, bf16[256,2048]{1,0:T(8,128)(2,1)}, u32[]{:S(2)}, u32[]{:S(2)}) %collective-permute-start.14) | collective-permute-done | bytes 1048608 | tf_op jit(solution)/shard_map/ppermute | solution.py:343
  153.3 2.9 %collective-permute-start.18 = (bf16[256,2048]{1,0:T(8,128)(2,1)}, bf16[256,2048]{1,0:T(8,128)(2,1)}, u32[]{:S(2)}, u32[]{:S(2)}) collective-permute-start(bf16[256,2048]{1,0:T(8,128)(2,1)} %collective-permute-done.17.dn4), channel_id=1, source_target_pairs={{2,6},{3,7},{4,0},{5,1},{10,14},{11,15},{12,8},{13,9},{18,22},{19,... | collective-permute-start | bytes 3145736 | tf_op jit(solution)/shard_map/ppermute | solution.py:430
  156.2 7.2 %shard_map.106.act = bf16[576,1024]{1,0:T(8,128)(2,1)S(1)} custom-call(s32[1]{0:T(128)} %bitcast.7.keep_ref, bf16[512,2304]{1,0:T(8,128)(2,1)S(1)} %bitcast.14, bf16[2,2048,256]{2,1,0:T(8,128)(2,1)} %collective-permute-done.9.gu0, bf16[2,2048,256]{2,1,0:T(8,128)(2,1)} %collective-permute-done.10.gu1, bf16[2,2048,256]{2,1,0:T(8,128)(2,1)} %get-tuple-element.40.gu2, ...), custom_call_target="tpu_custom_call" | custom-call | tf_op jit(solution)/shard_map/pallas_call | solution.py:461
  163.5 5.9 %shard_map.107 = bf16[512,2304]{1,0:T(8,128)(2,1)} custom-call(s32[1]{0:T(128)} %bitcast.7.keep_ref, bf16[576,1024]{1,0:T(8,128)(2,1)S(1)} %shard_map.106.act, bf16[256,2048]{1,0:T(8,128)(2,1)} %collective-permute-done.14.dn0, bf16[256,2048]{1,0:T(8,128)(2,1)} %collective-permute-done.15.dn1, bf16[256,2048]{1,0:T(8,128)(2,1)} %copy-done, ...), custom_call_target="tpu_custom_call" | custom-call | tf_op jit(solution)/shard_map/pallas_call | solution.py:471
  169.4 37.5 %all_to_all.20 = bf16[32,16,2304]{2,1,0:T(8,128)(2,1)S(1)} all-to-all(bf16[32,16,2304]{2,1,0:T(8,128)(2,1)} %bitcast.19), channel_id=1, replica_groups=mesh['seq'=32,'head'=4] {'seq'}, dimensions={0} | all-to-all | bytes 4718592 | tf_op jit(solution)/shard_map/all_to_all | solution.py:481
  209.0 3.4 %collective-permute-start.21 = (bf16[64,2048]{1,0:T(8,128)(2,1)}, bf16[64,2048]{1,0:T(8,128)(2,1)S(1)}, u32[]{:S(2)}, u32[]{:S(2)}) collective-permute-start(bf16[64,2048]{1,0:T(8,128)(2,1)} %get-tuple-element.46), channel_id=1, source_target_pairs={{0,3},{1,0},{2,1},{3,2},{4,7},{5,4},{6,5},{7,6},{8,11},{9,8},{10,9... | collective-permute-start | bytes 786440 | tf_op jit(solution)/shard_map/ppermute | solution.py:385
  212.9 11.1 %collective-permute-done.21 = bf16[64,2048]{1,0:T(8,128)(2,1)S(1)} collective-permute-done((bf16[64,2048]{1,0:T(8,128)(2,1)}, bf16[64,2048]{1,0:T(8,128)(2,1)S(1)}, u32[]{:S(2)}, u32[]{:S(2)}) %collective-permute-start.21) | collective-permute-done | bytes 262176 | tf_op jit(solution)/shard_map/ppermute | solution.py:385
  224.0 3.3 %collective-permute-done.19 = bf16[64,2048]{1,0:T(8,128)(2,1)S(1)} collective-permute-done((bf16[64,2048]{1,0:T(8,128)(2,1)}, bf16[64,2048]{1,0:T(8,128)(2,1)S(1)}, u32[]{:S(2)}, u32[]{:S(2)}) %collective-permute-start.19) | collective-permute-done | bytes 262176 | tf_op jit(solution)/shard_map/ppermute | solution.py:385
  (60 shorter events, 29.9 us)
Async XLA Ops:
  6.7 17.0 %all-to-all-start = ((bf16[32,16,128]{2,1,0:T(8,128)(2,1)}), bf16[32,16,128]{2,1,0:T(8,128)(2,1)S(1)}, u32[]{:S(2)}, u32[]{:S(2)}) async-start(bf16[32,16,128]{2,1,0:T(8,128)(2,1)} %bitcast.21), calls=%async_computation | async-start | bytes 262144 | tf_op jit(solution)/shard_map/all_to_all | solution.py:420
  15.2 104.8 %collective-permute-start.9 = (bf16[2,2048,256]{2,1,0:T(8,128)(2,1)}, bf16[2,2048,256]{2,1,0:T(8,128)(2,1)}, u32[]{:S(2)}, u32[]{:S(2)}) collective-permute-start(bf16[2,2048,256]{2,1,0:T(8,128)(2,1)} %get-tuple-element.38), channel_id=1, source_target_pairs={{0,1},{1,4},{2,5},{3,0},{4,3},{5,6},{6,7},{7,2},{8,9},{9,12},{10,1... | collective-permute-start | bytes 6291464 | tf_op jit(solution)/shard_map/ppermute | solution.py:343
  21.3 99.2 %collective-permute-start.12 = (bf16[2,2048,256]{2,1,0:T(8,128)(2,1)}, bf16[2,2048,256]{2,1,0:T(8,128)(2,1)}, u32[]{:S(2)}, u32[]{:S(2)}) collective-permute-start(bf16[2,2048,256]{2,1,0:T(8,128)(2,1)} %get-tuple-element.40.gu2), channel_id=1, source_target_pairs={{2,4},{3,5},{4,2},{5,3},{10,12},{11,13},{12,10},{13,11},{18,20},{1... | collective-permute-start | bytes 6291464 | tf_op jit(solution)/shard_map/ppermute | solution.py:426
  24.4 13.7 %all-to-all-start.1 = ((bf16[32,16,128]{2,1,0:T(8,128)(2,1)}), bf16[32,16,128]{2,1,0:T(8,128)(2,1)S(1)}, u32[]{:S(2)}, u32[]{:S(2)}) async-start(bf16[32,16,128]{2,1,0:T(8,128)(2,1)} %shard_map.101), calls=%async_computation.1 | async-start | bytes 262144 | tf_op jit(solution)/shard_map/all_to_all | solution.py:422
  41.9 33.2 %collective-permute-start.2 = (bf16[64,2048]{1,0:T(8,128)(2,1)}, bf16[64,2048]{1,0:T(8,128)(2,1)S(1)}, u32[]{:S(2)}, u32[]{:S(2)}) collective-permute-start(bf16[64,2048]{1,0:T(8,128)(2,1)} %get-tuple-element.35), channel_id=1, source_target_pairs={{0,3},{1,0},{2,1},{3,2},{4,7},{5,4},{6,5},{7,6},{8,11},{9,8},{10,9... | collective-permute-start | bytes 786440 | tf_op jit(solution)/shard_map/ppermute | solution.py:385
  43.7 32.6 %collective-permute-start.1 = (bf16[64,2048]{1,0:T(8,128)(2,1)}, bf16[64,2048]{1,0:T(8,128)(2,1)S(1)}, u32[]{:S(2)}, u32[]{:S(2)}) collective-permute-start(bf16[64,2048]{1,0:T(8,128)(2,1)} %get-tuple-element.34), channel_id=1, source_target_pairs={{0,2},{1,3},{2,0},{3,1},{4,6},{5,7},{6,4},{7,5},{8,10},{9,11},{10,... | collective-permute-start | bytes 786440 | tf_op jit(solution)/shard_map/ppermute | solution.py:385
  44.7 31.7 %collective-permute-start = (bf16[64,2048]{1,0:T(8,128)(2,1)}, bf16[64,2048]{1,0:T(8,128)(2,1)S(1)}, u32[]{:S(2)}, u32[]{:S(2)}) collective-permute-start(bf16[64,2048]{1,0:T(8,128)(2,1)} %get-tuple-element.33), channel_id=1, source_target_pairs={{0,1},{1,2},{2,3},{3,0},{4,5},{5,6},{6,7},{7,4},{8,9},{9,10},{10,1... | collective-permute-start | bytes 786440 | tf_op jit(solution)/shard_map/ppermute | solution.py:385
  75.1 78.2 %collective-permute-start.11 = (bf16[2,2048,256]{2,1,0:T(8,128)(2,1)}, bf16[2,2048,256]{2,1,0:T(8,128)(2,1)}, u32[]{:S(2)}, u32[]{:S(2)}) collective-permute-start(bf16[2,2048,256]{2,1,0:T(8,128)(2,1)} %get-tuple-element.40.gu2), channel_id=1, source_target_pairs={{0,4},{1,5},{6,2},{7,3},{8,12},{9,13},{14,10},{15,11},{16,20},{17,... | collective-permute-start | bytes 6291464 | tf_op jit(solution)/shard_map/ppermute | solution.py:343
  77.9 17.8 %collective-permute-start.6 = (bf16[64,2048]{1,0:T(8,128)(2,1)S(1)}, bf16[64,2048]{1,0:T(8,128)(2,1)S(1)}, u32[]{:S(2)}, u32[]{:S(2)}) collective-permute-start(bf16[64,2048]{1,0:T(8,128)(2,1)S(1)} %multiply_convert_fusion.t0), channel_id=1, source_target_pairs={{0,1},{1,2},{2,3},{3,0},{4,5},{5,6},{6,7},{7,4},{8,9},{9,10},{10,1... | collective-permute-start | bytes 786440 | tf_op jit(solution)/shard_map/ppermute | solution.py:379
  78.7 10.0 %collective-permute-start.3 = (f32[64,16]{1,0:T(8,128)S(1)}, f32[64,16]{1,0:T(8,128)S(1)}, u32[]{:S(2)}, u32[]{:S(2)}) collective-permute-start(f32[64,16]{1,0:T(8,128)S(1)} %copy.16.t0), channel_id=1, source_target_pairs={{0,1},{1,2},{2,3},{3,0},{4,5},{5,6},{6,7},{7,4},{8,9},{9,10},{10,1... | collective-permute-start | bytes 12296 | tf_op jit(solution)/shard_map/ppermute | solution.py:379
  88.7 4.3 %collective-permute-start.4 = (f32[64,16]{1,0:T(8,128)S(1)}, f32[64,16]{1,0:T(8,128)S(1)}, u32[]{:S(2)}, u32[]{:S(2)}) collective-permute-start(f32[64,16]{1,0:T(8,128)S(1)} %copy.16.t0), channel_id=1, source_target_pairs={{0,2},{1,3},{2,0},{3,1},{4,6},{5,7},{6,4},{7,5},{8,10},{9,11},{10,... | collective-permute-start | bytes 12296 | tf_op jit(solution)/shard_map/ppermute | solution.py:379
  95.7 6.7 %collective-permute-start.7 = (bf16[64,2048]{1,0:T(8,128)(2,1)S(1)}, bf16[64,2048]{1,0:T(8,128)(2,1)S(1)}, u32[]{:S(2)}, u32[]{:S(2)}) collective-permute-start(bf16[64,2048]{1,0:T(8,128)(2,1)S(1)} %multiply_convert_fusion.t0), channel_id=1, source_target_pairs={{0,2},{1,3},{2,0},{3,1},{4,6},{5,7},{6,4},{7,5},{8,10},{9,11},{10,... | collective-permute-start | bytes 786440 | tf_op jit(solution)/shard_map/ppermute | solution.py:379
  95.7 11.7 %collective-permute-start.8 = (bf16[64,2048]{1,0:T(8,128)(2,1)S(1)}, bf16[64,2048]{1,0:T(8,128)(2,1)S(1)}, u32[]{:S(2)}, u32[]{:S(2)}) collective-permute-start(bf16[64,2048]{1,0:T(8,128)(2,1)S(1)} %multiply_convert_fusion.t0), channel_id=1, source_target_pairs={{0,3},{1,0},{2,1},{3,2},{4,7},{5,4},{6,5},{7,6},{8,11},{9,8},{10,9... | collective-permute-start | bytes 786440 | tf_op jit(solution)/shard_map/ppermute | solution.py:379
  109.6 46.6 %all-to-all-start.2 = ((bf16[32,16,2304]{2,1,0:T(8,128)(2,1)}), bf16[32,16,2304]{2,1,0:T(8,128)(2,1)S(1)}, u32[]{:S(2)}, u32[]{:S(2)}) async-start(bf16[32,16,2304]{2,1,0:T(8,128)(2,1)} %bitcast.20), calls=%async_computation.2 | async-start | bytes 4718592 | tf_op jit(solution)/shard_map/all_to_all | solution.py:459
  120.0 36.2 %collective-permute-start.10 = (bf16[2,2048,256]{2,1,0:T(8,128)(2,1)}, bf16[2,2048,256]{2,1,0:T(8,128)(2,1)}, u32[]{:S(2)}, u32[]{:S(2)}) collective-permute-start(bf16[2,2048,256]{2,1,0:T(8,128)(2,1)} %collective-permute-done.9.gu0), channel_id=1, source_target_pairs={{0,4},{4,0},{8,12},{12,8},{16,20},{20,16},{24,28},{28,24},{32,36},... | collective-permute-start | bytes 6291464 | tf_op jit(solution)/shard_map/ppermute | solution.py:343
  120.5 35.7 %collective-permute-start.13 = (bf16[2,2048,256]{2,1,0:T(8,128)(2,1)}, bf16[2,2048,256]{2,1,0:T(8,128)(2,1)}, u32[]{:S(2)}, u32[]{:S(2)}) collective-permute-start(bf16[2,2048,256]{2,1,0:T(8,128)(2,1)} %collective-permute-done.12.gu4), channel_id=1, source_target_pairs={{2,6},{3,7},{4,0},{5,1},{10,14},{11,15},{12,8},{13,9},{18,22},{19,... | collective-permute-start | bytes 6291464 | tf_op jit(solution)/shard_map/ppermute | solution.py:429
  123.8 25.8 %collective-permute-start.14 = (bf16[256,2048]{1,0:T(8,128)(2,1)}, bf16[256,2048]{1,0:T(8,128)(2,1)}, u32[]{:S(2)}, u32[]{:S(2)}) collective-permute-start(bf16[256,2048]{1,0:T(8,128)(2,1)} %get-tuple-element.41), channel_id=1, source_target_pairs={{0,1},{1,4},{2,5},{3,0},{4,3},{5,6},{6,7},{7,2},{8,9},{9,12},{10,1... | collective-permute-start | bytes 3145736 | tf_op jit(solution)/shard_map/ppermute | solution.py:343
  126.3 24.6 %collective-permute-start.17 = (bf16[256,2048]{1,0:T(8,128)(2,1)S(1)}, bf16[256,2048]{1,0:T(8,128)(2,1)}, u32[]{:S(2)}, u32[]{:S(2)}) collective-permute-start(bf16[256,2048]{1,0:T(8,128)(2,1)S(1)} %get-tuple-element.42.dn2), channel_id=1, source_target_pairs={{2,4},{3,5},{4,2},{5,3},{10,12},{11,13},{12,10},{13,11},{18,20},{1... | collective-permute-start | bytes 3145736 | tf_op jit(solution)/shard_map/ppermute | solution.py:425
  149.6 13.8 %collective-permute-start.16 = (bf16[256,2048]{1,0:T(8,128)(2,1)S(1)}, bf16[256,2048]{1,0:T(8,128)(2,1)}, u32[]{:S(2)}, u32[]{:S(2)}) collective-permute-start(bf16[256,2048]{1,0:T(8,128)(2,1)S(1)} %get-tuple-element.42.dn2), channel_id=1, source_target_pairs={{0,4},{1,5},{6,2},{7,3},{8,12},{9,13},{14,10},{15,11},{16,20},{17,... | collective-permute-start | bytes 3145736 | tf_op jit(solution)/shard_map/ppermute | solution.py:343
  150.9 12.5 %collective-permute-start.15 = (bf16[256,2048]{1,0:T(8,128)(2,1)}, bf16[256,2048]{1,0:T(8,128)(2,1)}, u32[]{:S(2)}, u32[]{:S(2)}) collective-permute-start(bf16[256,2048]{1,0:T(8,128)(2,1)} %collective-permute-done.14.dn0), channel_id=1, source_target_pairs={{0,4},{4,0},{8,12},{12,8},{16,20},{20,16},{24,28},{28,24},{32,36},... | collective-permute-start | bytes 3145736 | tf_op jit(solution)/shard_map/ppermute | solution.py:343
  153.3 10.2 %collective-permute-start.18 = (bf16[256,2048]{1,0:T(8,128)(2,1)}, bf16[256,2048]{1,0:T(8,128)(2,1)}, u32[]{:S(2)}, u32[]{:S(2)}) collective-permute-start(bf16[256,2048]{1,0:T(8,128)(2,1)} %collective-permute-done.17.dn4), channel_id=1, source_target_pairs={{2,6},{3,7},{4,0},{5,1},{10,14},{11,15},{12,8},{13,9},{18,22},{19,... | collective-permute-start | bytes 3145736 | tf_op jit(solution)/shard_map/ppermute | solution.py:430
  209.0 15.0 %collective-permute-start.21 = (bf16[64,2048]{1,0:T(8,128)(2,1)}, bf16[64,2048]{1,0:T(8,128)(2,1)S(1)}, u32[]{:S(2)}, u32[]{:S(2)}) collective-permute-start(bf16[64,2048]{1,0:T(8,128)(2,1)} %get-tuple-element.46), channel_id=1, source_target_pairs={{0,3},{1,0},{2,1},{3,2},{4,7},{5,4},{6,5},{7,6},{8,11},{9,8},{10,9... | collective-permute-start | bytes 786440 | tf_op jit(solution)/shard_map/ppermute | solution.py:385
  212.4 11.7 %collective-permute-start.20 = (bf16[64,2048]{1,0:T(8,128)(2,1)}, bf16[64,2048]{1,0:T(8,128)(2,1)S(1)}, u32[]{:S(2)}, u32[]{:S(2)}) collective-permute-start(bf16[64,2048]{1,0:T(8,128)(2,1)} %get-tuple-element.45), channel_id=1, source_target_pairs={{0,2},{1,3},{2,0},{3,1},{4,6},{5,7},{6,4},{7,5},{8,10},{9,11},{10,... | collective-permute-start | bytes 786440 | tf_op jit(solution)/shard_map/ppermute | solution.py:385
  212.4 15.0 %collective-permute-start.19 = (bf16[64,2048]{1,0:T(8,128)(2,1)}, bf16[64,2048]{1,0:T(8,128)(2,1)S(1)}, u32[]{:S(2)}, u32[]{:S(2)}) collective-permute-start(bf16[64,2048]{1,0:T(8,128)(2,1)} %get-tuple-element.44), channel_id=1, source_target_pairs={{0,1},{1,2},{2,3},{3,0},{4,5},{5,6},{6,7},{7,4},{8,9},{9,10},{10,1... | collective-permute-start | bytes 786440 | tf_op jit(solution)/shard_map/ppermute | solution.py:385
  (9 other events, 313.1 us)

commit v6 on v4

--- a/solution.py
+++ b/solution.py
@@ -39,17 +39,17 @@
     return pltpu.VMEM(shape, dtype)
 
 
-def spec_of(o):
+def spec_of(o, direct):
     if o.dtype == jnp.int32:
         return SMEM
-    return HBM if o in QUARTER else VMEM
-
-
-def call(kernel, ins, outs, scratch=(), limit=54):
+    return HBM if o in direct else VMEM
+
+
+def call(kernel, ins, outs, scratch=(), limit=54, direct=()):
     return pl.pallas_call(
         kernel,
         in_specs=ins,
-        out_specs=[spec_of(o) for o in outs],
+        out_specs=[spec_of(o, direct) for o in outs],
         out_shape=outs,
         scratch_shapes=list(scratch),
         compiler_params=pltpu.CompilerParams(vmem_limit_bytes=limit << 20),
@@ -77,36 +77,28 @@
     return slice(h * DH, (h + 1) * DH)
 
 
-def pick_copies(index_ref, gu_ref, dn_ref, gu_out, dn_out, gu_buf, dn_buf, read_sems, write_sems):
+def pick_copies(index_ref, gu_ref, dn_ref, gu_buf, dn_buf, sems):
     index = index_ref[0]
-    reads = []
-    writes = []
+    copies = []
     for half in range(2):
         for part in range(2):
             rows = pl.ds(part * (D // 2), D // 2)
-            reads.append((gu_ref.at[index, half, rows], gu_buf.at[half, rows]))
-            writes.append((gu_buf.at[half, rows], gu_out.at[half, rows]))
+            copies.append((gu_ref.at[index, half, rows], gu_buf.at[half, rows]))
         rows = pl.ds(half * 128, 128)
-        reads.append((dn_ref.at[index, rows], dn_buf.at[rows]))
-        writes.append((dn_buf.at[rows], dn_out.at[rows]))
-    return (
-        [pltpu.make_async_copy(a, b, read_sems.at[i]) for i, (a, b) in enumerate(reads)],
-        [pltpu.make_async_copy(a, b, write_sems.at[i]) for i, (a, b) in enumerate(writes)],
-    )
+        copies.append((dn_ref.at[index, rows], dn_buf.at[rows]))
+    return [pltpu.make_async_copy(a, b, sems.at[i]) for i, (a, b) in enumerate(copies)]
 
 
 def front_kernel(
     index_ref, x_ref, gain_ref, w_ref, gu_ref, dn_ref,
     normed_ref, k_ref, v_ref, send_ref, zero_ref, gu_out, dn_out,
-    wk, wv, sems, gu_buf, dn_buf, read_sems, write_sems,
+    wk, wv, sems, read_sems,
 ):
     copy_k = pltpu.make_async_copy(w_ref.at[1], wk, sems.at[0])
     copy_v = pltpu.make_async_copy(w_ref.at[2], wv, sems.at[1])
     copy_k.start()
     copy_v.start()
-    reads, writes = pick_copies(
-        index_ref, gu_ref, dn_ref, gu_out, dn_out, gu_buf, dn_buf, read_sems, write_sems
-    )
+    reads = pick_copies(index_ref, gu_ref, dn_ref, gu_out, dn_out, read_sems)
     for read in reads:
         read.start()
     zero_ref[0] = 0
@@ -116,16 +108,13 @@
     key = dot(normed, wk[...]).astype(BF)
     k_ref[...] = key
     copy_v.wait()
-    for read, write in zip(reads, writes):
-        read.wait()
-        write.start()
     value = dot(normed, wv[...]).astype(BF)
     v_ref[...] = value
     for h in range(HEADS):
         state = dot_rows(key[:, of_head(h)], value[:, of_head(h)])
         send_ref[of_head(h), :] = state.astype(BF)
-    for write in writes:
-        write.wait()
+    for read in reads:
+        read.wait()
 
 
 def prefix_kernel(states_ref, out_ref):
@@ -169,6 +158,17 @@
         s1[:, cols] = rows[3 * ROWS:].astype(BF)
 
 
+def norm_kernel(head_ref, x_ref, own_ref, g1, g2, g3, gain_ref, resid_ref, normed_ref, rows, sems):
+    start = pl.multiple_of(head_ref[0] * ROWS, ROWS)
+    copy = pltpu.make_async_copy(x_ref.at[pl.ds(start, ROWS)], rows, sems.at[0])
+    copy.start()
+    total = own_ref[...] + g1[...].astype(F32) + g2[...].astype(F32) + g3[...].astype(F32)
+    copy.wait()
+    resid = rows[...].astype(F32) + total
+    resid_ref[...] = resid
+    normed_ref[...] = rms_norm(resid, gain_ref[...]).astype(BF)
+
+
 def routing_kernel(head_ref, t0, t1, t2, t3, place_ref, weight_ref):
     head = head_ref[0]
     tables = jnp.concatenate([t0[...], t1[...], t2[...], t3[...]], axis=0)
@@ -219,41 +219,44 @@
         out_ref[:, D + t * 128:D + (t + 1) * 128] = piece
 
 
-def start_quarters(keep_ref, arrays, dest_of, sems, first):
+def start_quarters(keep_ref, arrays, dest_of, sems, first, count=4):
     def load(q, ref):
         return pltpu.make_async_copy(ref, dest_of(q), sems.at[first + q])
 
     keep = keep_ref[0] == 1
-    copies = [load(0, arrays[0]), load(1, arrays[1])]
+    copies = [load(0, arrays[0]), load(1, arrays[1]), load(2, arrays[2])]
     copies[0].start()
     copies[1].start()
 
     @pl.when(keep)
     def _():
         load(2, arrays[2]).start()
-        load(3, arrays[5]).start()
+        if count == 4:
+            load(3, arrays[5]).start()
 
     @pl.when(jnp.logical_not(keep))
     def _():
         load(2, arrays[3]).start()
-        load(3, arrays[4]).start()
-
-    return copies + [load(2, arrays[2]), load(3, arrays[4])]
-
-
-def expert_kernel(
-    keep_ref, x_ref, gu0, gu1, gu2, gu3, gu4, gu5, dn0, dn1, dn2, dn3, dn4, dn5,
-    out_ref, rows, gate_up, down, act, tail, sems,
+        if count == 4:
+            load(3, arrays[4]).start()
+
+    return copies + ([load(3, arrays[4])] if count == 4 else [])
+
+
+def gate_kernel(
+    keep_ref, x_ref, gu0, gu1, gu2, gu3, gu4, gu5, dn0, dn1, dn2, dn3,
+    act_ref, down_ref, rows, gate_up, sems,
 ):
     copies = start_quarters(
         keep_ref, (gu0, gu1, gu2, gu3, gu4, gu5), lambda q: gate_up.at[q], sems, 0
     )
     down_copies = start_quarters(
         keep_ref,
-        (dn0, dn1, dn2, dn3, dn4, dn5),
-        lambda q: down.at[q * 256:(q + 1) * 256],
+        (dn0, dn1, dn2, dn3),
+        lambda q: down_ref.at[q * 256:(q + 1) * 256],
         sems,
         4,
+        3,
     )
     rows[:MAIN, :] = x_ref[:, :D]
     for t in range(2):
@@ -263,17 +266,41 @@
         copies[q].wait()
         gate = dot(rows[...], gate_up[q, 0])
         up = dot(rows[...], gate_up[q, 1])
-        act[:, q * 256:(q + 1) * 256] = (jax.nn.silu(gate) * up).astype(BF)
+        act_ref[:, q * 256:(q + 1) * 256] = (jax.nn.silu(gate) * up).astype(BF)
     for copy in down_copies:
         copy.wait()
+
+
+def down_kernel(keep_ref, act, down, dn4, dn5, out_ref, last, main, tail, ends, sems):
+    keep = keep_ref[0] == 1
+
+    @pl.when(keep)
+    def _():
+        pltpu.make_async_copy(dn5, last, sems.at[0]).start()
+
+    @pl.when(jnp.logical_not(keep))
+    def _():
+        pltpu.make_async_copy(dn4, last, sems.at[0]).start()
+
+    writes = []
     for n in range(4):
         cols = slice(n * 512, (n + 1) * 512)
-        result = dot(act[...], down[:, cols])
-        out_ref[:, cols] = result[:MAIN].astype(BF)
+        result = dot(act[:, :768], down[:, cols])
+        if n == 0:
+            pltpu.make_async_copy(dn4, last, sems.at[0]).wait()
+        result = result + dot(act[:, 768:], last[:, cols])
+        main[:, cols] = result[:MAIN].astype(BF)
         tail[:, cols] = result[MAIN:]
+        write = pltpu.make_async_copy(main.at[:, cols], out_ref.at[:, cols], sems.at[1 + n])
+        write.start()
+        writes.append(write)
     for t in range(2):
         piece = tail[t * 32:(t + 1) * 32, :].reshape(MAIN, 128).astype(BF)
-        out_ref[:, D + t * 128:D + (t + 1) * 128] = piece
+        ends[:, t * 128:(t + 1) * 128] = piece
+    write = pltpu.make_async_copy(ends, out_ref.at[:, D:], sems.at[5])
+    write.start()
+    for write in writes + [write]:
+        write.wait()
 
 
 def combine_kernel(weight_ref, y_ref, own_ref, s1, s2, s3, tail):
@@ -338,8 +365,16 @@
     return [lax.ppermute(a, axes, perm) for a in arrays]
 
 
-def pick_kernel(*refs):
-    reads, writes = pick_copies(*refs)
+def pick_kernel(index_ref, gu_ref, dn_ref, gu_out, dn_out, gu_buf, dn_buf, read_sems, write_sems):
+    reads = pick_copies(index_ref, gu_ref, dn_ref, gu_buf, dn_buf, read_sems)
+    writes = []
+    for half in range(2):
+        for part in range(2):
+            rows = pl.ds(part * (D // 2), D // 2)
+            writes.append((gu_buf.at[half, rows], gu_out.at[half, rows]))
+        rows = pl.ds(half * 128, 128)
+        writes.append((dn_buf.at[rows], dn_out.at[rows]))
+    writes = [pltpu.make_async_copy(a, b, write_sems.at[i]) for i, (a, b) in enumerate(writes)]
     for read in reads:
         read.start()
     for read, write in zip(reads, writes):
@@ -350,6 +385,7 @@
 
 
 QUARTER = [out((2, D, 256), BF), out((256, D), BF)]
+RESULTS = out((MAIN, PACKED), BF)
 PICK_SCRATCH = [
     pltpu.VMEM((2, D, 256), BF),
     pltpu.VMEM((256, D), BF),
@@ -398,10 +434,15 @@
             chip((TOK, WIDE), BF),
             out((WIDE, DH), BF),
             out((1,), jnp.int32),
-        ]
-        + QUARTER,
-        [pltpu.VMEM((D, WIDE), BF), pltpu.VMEM((D, WIDE), BF), pltpu.SemaphoreType.DMA((2,))]
-        + PICK_SCRATCH,
+            chip((2, D, 256), BF),
+            chip((256, D), BF),
+        ],
+        [
+            pltpu.VMEM((D, WIDE), BF),
+            pltpu.VMEM((D, WIDE), BF),
+            pltpu.SemaphoreType.DMA((2,)),
+            pltpu.SemaphoreType.DMA((6,)),
+        ],
     )(
         (1 - (head & 1)).astype(jnp.int32)[None],
         hidden_in,
@@ -421,30 +462,35 @@
     far = [lax.ppermute(rest[0], both, device_perm(far_target)), far_down]
     rest_other = permute_all(rest, both, device_perm(keep_target))
     near_other = permute_all(near, "seq", seq_perm(0, 0, 1))
-    far_other = permute_all(far, both, device_perm(pass_target))
+    far_other = [lax.ppermute(far[0], both, device_perm(pass_target))]
+    far_other.append(lax.ppermute(far[1], both, device_perm(pass_target)))
     pieces = [near, near_other, rest, rest_other, far, far_other]
 
     query, local = call(
         local_kernel,
         [VMEM, HBM, VMEM, VMEM],
-        [chip((TOK, WIDE), BF), chip((TOK, WIDE), F32)],
+        [out((TOK, WIDE), BF), chip((TOK, WIDE), F32)],
         [pltpu.VMEM((D, WIDE), BF), pltpu.SemaphoreType.DMA((1,))],
     )(on_chip(normed), w_planes, on_chip(key), on_chip(value))
     here = head.astype(jnp.int32)[None]
     blocks = call(
         attend_kernel,
         [SMEM] + [VMEM] * 5,
-        BLOCKS_OUT,
+        [chip((ROWS, D), F32)] + BLOCKS_OUT[1:],
         [pltpu.VMEM((TOK, WIDE), BF), pltpu.VMEM((TOK, WIDE), BF)],
-    )(here, on_chip(earlier), on_chip(query), on_chip(local), out_gain[None, :], w_out)
+    )(here, on_chip(earlier), query, on_chip(local), out_gain[None, :], w_out)
     tables = gather_head(jnp.concatenate([routes.astype(F32), gate_weights], axis=1))
     place_rows, weight = call(
         routing_kernel, [SMEM] + [VMEM] * 4, [chip((SLOTS, TOK), BF), chip((TOK, SLOTS), BF)]
     )(here, *[on_chip(t) for t in tables])
 
-    attn_rows = scatter_head(blocks)
-    resid = lax.dynamic_slice_in_dim(hidden_in, head * ROWS, ROWS, 0).astype(F32) + attn_rows
-    normed2 = rms_norm(resid, moe_gain).astype(BF)
+    got = [lax.ppermute(blocks[k], "head", head_perm(k)) for k in range(1, 4)]
+    resid, normed2 = call(
+        norm_kernel,
+        [SMEM, HBM] + [VMEM] * 5,
+        [out((ROWS, D), F32), chip((ROWS, D), BF)],
+        [pltpu.VMEM((ROWS, D), BF), pltpu.SemaphoreType.DMA((1,))],
+    )(here, hidden_in, on_chip(blocks[0]), *[on_chip(g) for g in got], moe_gain[None, :])
     tokens = gather_head(normed2)
 
     sent = call(
@@ -452,19 +498,31 @@
     )(on_chip(place_rows), *[on_chip(t) for t in tokens])[0]
     received = lax.all_to_all(sent.reshape(32, 16, PACKED), "seq", 0, 0, tiled=True)
     keep = (head // 2 == core).astype(jnp.int32)[None]
-    results = call(
-        expert_kernel,
-        [SMEM, VMEM] + [ANY] * 12,
-        [out((MAIN, PACKED), BF)],
+    gate_ups = [p[0] for p in pieces]
+    downs = [p[1] for p in pieces]
+    act, down = call(
+        gate_kernel,
+        [SMEM, VMEM] + [ANY] * 10,
+        [chip((SLOTS, 1024), BF), chip((768, D), BF)],
         [
             pltpu.VMEM((SLOTS, D), BF),
             pltpu.VMEM((4, 2, D, 256), BF),
-            pltpu.VMEM((1024, D), BF),
-            pltpu.VMEM((SLOTS, 1024), BF),
+            pltpu.SemaphoreType.DMA((7,)),
+        ],
+    )(keep, on_chip(received.reshape(MAIN, PACKED)), *gate_ups, *downs[:4])
+    results = call(
+        down_kernel,
+        [SMEM, VMEM, VMEM, ANY, ANY],
+        [RESULTS],
+        [
+            pltpu.VMEM((256, D), BF),
+            pltpu.VMEM((MAIN, D), BF),
             pltpu.VMEM((64, D), F32),
-            pltpu.SemaphoreType.DMA((8,)),
+            pltpu.VMEM((MAIN, 256), BF),
+            pltpu.SemaphoreType.DMA((6,)),
         ],
-    )(keep, on_chip(received.reshape(MAIN, PACKED)), *[p[0] for p in pieces], *[p[1] for p in pieces])[0]
+        direct=[RESULTS],
+    )(keep, on_chip(act), on_chip(down), *downs[4:])[0]
     back = lax.all_to_all(results.reshape(32, 16, PACKED), "seq", 0, 0, tiled=True)
     blocks = call(
         combine_kernel, [VMEM] * 2, BLOCKS_OUT, [pltpu.VMEM((64, D), BF)]

time: 226 us -> 228 us (level)
  starting transfers between devices: 62.5 us -> 44.5 us
  blocking collectives: 37 us -> 51.3 us
  waiting for transfers between devices: 83.6 us -> 87.8 us
  Pallas kernels: 33.1 us -> 36.9 us
    ppermute x0 -> x5, waiting for transfers between devices: none -> 29.7 us  [the longest x3 29.7 us: on_device(): got = [lax.ppermute(blocks[k], 'head', head_perm(k)) for k in range(1, 4)]]
    ppermute x6 -> x3, waiting for transfers between devices: 36.9 us -> 15 us  [scatter_head(): total = total + lax.ppermute(blocks[k], 'head', head_perm(k)).astype(F32)]
    all_to_all x0 -> x1, blocking collectives: none -> 14.3 us  [on_device(): lax.all_to_all(send_state.reshape(32, 16, DH), 'seq', 0, 0, tiled=True)]
    all_to_all x1 -> x0, starting transfers between devices: 8.5 us -> none  [on_device(): lax.all_to_all(send_state.reshape(32, 16, DH), 'seq', 0, 0, tiled=True)]
    ppermute x1, waiting for transfers between devices: 6.15 us -> 14 us  [on_device(): far_down = lax.ppermute(rest[1], both, device_perm(far_target))]
    ppermute x0 -> x5, starting transfers between devices: none -> 6.16 us  [the longest x1 3.24 us: on_device(): far_other = [lax.ppermute(far[0], both, device_perm(pass_target))]]
    ppermute x8 -> x6, starting transfers between devices: 16.7 us -> 10.9 us  [permute_all(): return [lax.ppermute(a, axes, perm) for a in arrays]]
    ppermute x6, starting transfers between devices: 9.03 us -> 3.32 us  [gather_head(): lax.ppermute(array, 'head', head_perm(k))]
  transfers between devices with their start and end apart: 25 -> 24, of which waited for: 13 -> 12; matrix products, arithmetic and copies ran while one was open for 1% -> 0% of each run, Pallas kernels for 6% -> 10%
where the time goes in v6:
time: 228 us; the launch traced here: 225 us
  waiting for transfers between devices  87.8 us (39%)
  blocking collectives  51.3 us (22%)
  starting transfers between devices  44.5 us (20%)
  Pallas kernels  36.9 us (16%)
    all_to_all x1, blocking collectives, on_device(): lax.all_to_all(results.reshape(32, 16, PACKED), 'seq', 0, 0, tiled=True)  37 us
    ppermute x3, waiting for transfers between devices, on_device(): got = [lax.ppermute(blocks[k], 'head', head_perm(k)) for k in range(1, 4)]  29.7 us
    ppermute x6, waiting for transfers between devices, gather_head(): lax.ppermute(array, 'head', head_perm(k))  24.1 us
    ppermute x3, waiting for transfers between devices, scatter_head(): total = total + lax.ppermute(blocks[k], 'head', head_perm(k)).astype(F32)  15 us
    all_to_all x1, blocking collectives, on_device(): lax.all_to_all(send_state.reshape(32, 16, DH), 'seq', 0, 0, tiled=True)  14.3 us
    ppermute x1, waiting for transfers between devices, on_device(): far_down = lax.ppermute(rest[1], both, device_perm(far_target))  14 us
    ppermute x6, starting transfers between devices, permute_all(): return [lax.ppermute(a, axes, perm) for a in arrays]  10.9 us
    all_to_all x1, starting transfers between devices, on_device(): lax.all_to_all(sent.reshape(32, 16, PACKED), 'seq', 0, 0, tiled=True)  10.4 us
  transfers between devices with their start and end apart: 24, of which 12 were waited for; matrix products, arithmetic and copies ran while one was open for 0% of the time, Pallas kernels for 10%

profile of v6, /device:TPU:33, one launch (start us, length us, event | category | flops | bytes accessed | tf_op | source)
XLA Modules:
  0.0 225.0 jit_solution(8033404605146393267)
XLA Ops:
  0.0 7.0 %shard_map.100 = (bf16[256,2048]{1,0:T(8,128)(2,1)S(1)}, bf16[256,512]{1,0:T(8,128)(2,1)S(1)}, bf16[256,512]{1,0:T(8,128)(2,1)S(1)}, bf16[512,128]{1,0:T(8,128)(...) custom-call(s32[1]{0:T(128)} %bitcast.1.index_ref, bf16[256,2048]{1,0:T(8,128)(2,1)} %x_ref.3, ...), custom_call_target="tpu_custom_call" | custom-call | tf_op jit(solution)/shard_map/pallas_call | solution.py:428
  7.0 3.1 %collective-permute-start.9 = (bf16[2,2048,256]{2,1,0:T(8,128)(2,1)}, bf16[2,2048,256]{2,1,0:T(8,128)(2,1)}, u32[]{:S(2)}, u32[]{:S(2)}) collective-permute-start(bf16[2,2048,256]{2,1,0:T(8,128)(2,1)} %get-tuple-element.44), channel_id=1, source_target_pairs={{0,1},{1,4},{2,5},{3,0},{4,3},{5,6},{6,7},{7,2},{8,9},{9,12},{10,1... | collective-permute-start | bytes 6291464 | tf_op jit(solution)/shard_map/ppermute | solution.py:365
  10.7 2.6 %pick.1 = (bf16[2,2048,256]{2,1,0:T(8,128)(2,1)}, bf16[256,2048]{1,0:T(8,128)(2,1)S(1)}) custom-call(s32[1]{0:T(128)} %bitcast.12.index_ref, bf16[2,2,2048,256]{3,2,1,0:T(8,128)(2,1)} %gu_ref.3, bf16[2,256,2048]{2,1,0:T(8,128)(2,1)} %dn_ref.3), custom_call_target="tpu_custom_call" | custom-call | tf_op jit(solution)/shard_map/pick/pallas_call | solution.py:398
  15.5 14.3 %all_to_all.20.states_ref = bf16[32,16,128]{2,1,0:T(8,128)(2,1)S(1)} all-to-all(bf16[32,16,128]{2,1,0:T(8,128)(2,1)S(1)} %bitcast.22), channel_id=1, replica_groups=mesh['seq'=32,'head'=4] {'seq'}, dimensions={0} | all-to-all | bytes 262144 | tf_op jit(solution)/shard_map/all_to_all | solution.py:456
  30.5 5.0 %all-to-all-start.1 = ((bf16[32,16,128]{2,1,0:T(8,128)(2,1)}), bf16[32,16,128]{2,1,0:T(8,128)(2,1)S(1)}, u32[]{:S(2)}, u32[]{:S(2)}) async-start(bf16[32,16,128]{2,1,0:T(8,128)(2,1)} %shard_map.101), calls=%async_computation.1 | async-start | bytes 262144 | tf_op jit(solution)/shard_map/all_to_all | solution.py:458
  35.5 3.0 %shard_map.102 = (bf16[256,512]{1,0:T(8,128)(2,1)}, f32[256,512]{1,0:T(8,128)S(1)}) custom-call(bf16[256,2048]{1,0:T(8,128)(2,1)S(1)} %get-tuple-element.31.normed_ref, bf16[3,2048,512]{2,1,0:T(8,128)(2,1)} %bitcast.19, bf16[256,512]{1,0:T(8,128)(2,1)S(1)} %get-tuple-element.32.k_ref, bf16[256,512]{1,0:T(8,128)(2,1)S(1)} %get-tuple-element.33.v_ref), custom_call_target="tpu_custom_call" | custom-call | tf_op jit(solution)/shard_map/pallas_call | solution.py:469
  38.6 3.7 %all-to-all-done.1 = bf16[32,16,128]{2,1,0:T(8,128)(2,1)S(1)} async-done(((bf16[32,16,128]{2,1,0:T(8,128)(2,1)}), bf16[32,16,128]{2,1,0:T(8,128)(2,1)S(1)}, u32[]{:S(2)}, u32[]{:S(2)}) %all-to-all-start.1) | async-done | bytes 131104 | tf_op jit(solution)/shard_map/all_to_all | solution.py:458
  42.2 3.7 %shard_map.103 = (f32[64,2048]{1,0:T(8,128)S(1)}, bf16[64,2048]{1,0:T(8,128)(2,1)}, bf16[64,2048]{1,0:T(8,128)(2,1)}, bf16[64,2048]{1,0:T(8,128)(2,1)}) custom-call(s32[1]{0:T(128)} %bitcast.head_ref, bf16[512,128]{1,0:T(8,128)(2,1)S(1)} %bitcast.17, bf16[256,512]{1,0:T(8,128)(2,1)} %get-tuple-element.34.q_ref, f32[256,512]{1,0:T(8,128)S(1)} %get-tuple-element.35.local_ref, ...), custom_call_target="tpu_custom_call" | custom-call | tf_op jit(solution)/shard_map/pallas_call | solution.py:476
  49.8 17.1 %collective-permute-done.g1 = bf16[64,2048]{1,0:T(8,128)(2,1)S(1)} collective-permute-done((bf16[64,2048]{1,0:T(8,128)(2,1)}, bf16[64,2048]{1,0:T(8,128)(2,1)S(1)}, u32[]{:S(2)}, u32[]{:S(2)}) %collective-permute-start) | collective-permute-done | bytes 262176 | tf_op jit(solution)/shard_map/ppermute | solution.py:487
  66.9 12.5 %collective-permute-done.1.g2 = bf16[64,2048]{1,0:T(8,128)(2,1)S(1)} collective-permute-done((bf16[64,2048]{1,0:T(8,128)(2,1)}, bf16[64,2048]{1,0:T(8,128)(2,1)S(1)}, u32[]{:S(2)}, u32[]{:S(2)}) %collective-permute-start.1) | collective-permute-done | bytes 262176 | tf_op jit(solution)/shard_map/ppermute | solution.py:487
  83.1 8.9 %collective-permute-done.3.t1 = f32[64,16]{1,0:T(8,128)S(1)} collective-permute-done((f32[64,16]{1,0:T(8,128)S(1)}, f32[64,16]{1,0:T(8,128)S(1)}, u32[]{:S(2)}, u32[]{:S(2)}) %collective-permute-start.3) | collective-permute-done | bytes 4128 | tf_op jit(solution)/shard_map/ppermute | solution.py:410
  92.0 4.3 %collective-permute-done.4.t2 = f32[64,16]{1,0:T(8,128)S(1)} collective-permute-done((f32[64,16]{1,0:T(8,128)S(1)}, f32[64,16]{1,0:T(8,128)S(1)}, u32[]{:S(2)}, u32[]{:S(2)}) %collective-permute-start.4) | collective-permute-done | bytes 4128 | tf_op jit(solution)/shard_map/ppermute | solution.py:410
  103.0 2.8 %collective-permute-done.7.t2 = bf16[64,2048]{1,0:T(8,128)(2,1)S(1)} collective-permute-done((bf16[64,2048]{1,0:T(8,128)(2,1)S(1)}, bf16[64,2048]{1,0:T(8,128)(2,1)S(1)}, u32[]{:S(2)}, u32[]{:S(2)}) %collective-permute-start.7) | collective-permute-done | bytes 262176 | tf_op jit(solution)/shard_map/ppermute | solution.py:410
  105.8 5.5 %collective-permute-done.8.t3 = bf16[64,2048]{1,0:T(8,128)(2,1)S(1)} collective-permute-done((bf16[64,2048]{1,0:T(8,128)(2,1)S(1)}, bf16[64,2048]{1,0:T(8,128)(2,1)S(1)}, u32[]{:S(2)}, u32[]{:S(2)}) %collective-permute-start.8) | collective-permute-done | bytes 262176 | tf_op jit(solution)/shard_map/ppermute | solution.py:410
  113.5 10.4 %all-to-all-start.2 = ((bf16[32,16,2304]{2,1,0:T(8,128)(2,1)}), bf16[32,16,2304]{2,1,0:T(8,128)(2,1)S(1)}, u32[]{:S(2)}, u32[]{:S(2)}) async-start(bf16[32,16,2304]{2,1,0:T(8,128)(2,1)} %bitcast.20), calls=%async_computation.2 | async-start | bytes 4718592 | tf_op jit(solution)/shard_map/all_to_all | solution.py:499
  126.6 2.7 %collective-permute-start.10 = (bf16[2,2048,256]{2,1,0:T(8,128)(2,1)}, bf16[2,2048,256]{2,1,0:T(8,128)(2,1)}, u32[]{:S(2)}, u32[]{:S(2)}) collective-permute-start(bf16[2,2048,256]{2,1,0:T(8,128)(2,1)} %collective-permute-done.9.gu0), channel_id=1, source_target_pairs={{0,4},{4,0},{8,12},{12,8},{16,20},{20,16},{24,28},{28,24},{32,36},... | collective-permute-start | bytes 6291464 | tf_op jit(solution)/shard_map/ppermute | solution.py:365
  129.2 3.2 %collective-permute-start.13 = (bf16[2,2048,256]{2,1,0:T(8,128)(2,1)}, bf16[2,2048,256]{2,1,0:T(8,128)(2,1)}, u32[]{:S(2)}, u32[]{:S(2)}) collective-permute-start(bf16[2,2048,256]{2,1,0:T(8,128)(2,1)} %collective-permute-done.12.gu4), channel_id=1, source_target_pairs={{2,6},{3,7},{4,0},{5,1},{10,14},{11,15},{12,8},{13,9},{18,22},{19,... | collective-permute-start | bytes 6291464 | tf_op jit(solution)/shard_map/ppermute | solution.py:465
  132.5 3.6 %collective-permute-start.17 = (bf16[256,2048]{1,0:T(8,128)(2,1)S(1)}, bf16[256,2048]{1,0:T(8,128)(2,1)}, u32[]{:S(2)}, u32[]{:S(2)}) collective-permute-start(bf16[256,2048]{1,0:T(8,128)(2,1)S(1)} %get-tuple-element.48.dn2), channel_id=1, source_target_pairs={{2,4},{3,5},{4,2},{5,3},{10,12},{11,13},{12,10},{13,11},{18,20},{1... | collective-permute-start | bytes 3145736 | tf_op jit(solution)/shard_map/ppermute | solution.py:461
  136.2 14.0 %collective-permute-done.17.dn4 = bf16[256,2048]{1,0:T(8,128)(2,1)} collective-permute-done((bf16[256,2048]{1,0:T(8,128)(2,1)S(1)}, bf16[256,2048]{1,0:T(8,128)(2,1)}, u32[]{:S(2)}, u32[]{:S(2)}) %collective-permute-start.17) | collective-permute-done | bytes 1048608 | tf_op jit(solution)/shard_map/ppermute | solution.py:461
  153.2 7.2 %shard_map.107 = (bf16[576,1024]{1,0:T(8,128)(2,1)S(1)}, bf16[768,2048]{1,0:T(8,128)(2,1)S(1)}) custom-call(s32[1]{0:T(128)} %bitcast.8.keep_ref, bf16[512,2304]{1,0:T(8,128)(2,1)S(1)} %bitcast.16, bf16[2,2048,256]{2,1,0:T(8,128)(2,1)} %collective-permute-done.9.gu0, bf16[2,2048,256]{2,1,0:T(8,128)(2,1)} %collective-permute-done.10.gu1, ...), custom_call_target="tpu_custom_call" | custom-call | tf_op jit(solution)/shard_map/pallas_call | solution.py:503
  161.4 4.9 %shard_map.108 = bf16[512,2304]{1,0:T(8,128)(2,1)} custom-call(s32[1]{0:T(128)} %bitcast.8.keep_ref, bf16[576,1024]{1,0:T(8,128)(2,1)S(1)} %get-tuple-element.49.act, bf16[768,2048]{1,0:T(8,128)(2,1)S(1)} %get-tuple-element.50.down, bf16[256,2048]{1,0:T(8,128)(2,1)} %collective-permute-done.17.dn4, bf16[256,2048]{1,0:T(8,128)(2,1)} %copy-done.4), custom_call_target="tpu_custom_call" | custom-call | tf_op jit(solution)/shard_map/pallas_call | solution.py:513
  166.3 37.0 %all_to_all.21 = bf16[32,16,2304]{2,1,0:T(8,128)(2,1)S(1)} all-to-all(bf16[32,16,2304]{2,1,0:T(8,128)(2,1)} %bitcast.21), channel_id=1, replica_groups=mesh['seq'=32,'head'=4] {'seq'}, dimensions={0} | all-to-all | bytes 4718592 | tf_op jit(solution)/shard_map/all_to_all | solution.py:526
  208.2 10.9 %collective-permute-done.21 = bf16[64,2048]{1,0:T(8,128)(2,1)S(1)} collective-permute-done((bf16[64,2048]{1,0:T(8,128)(2,1)}, bf16[64,2048]{1,0:T(8,128)(2,1)S(1)}, u32[]{:S(2)}, u32[]{:S(2)}) %collective-permute-start.21) | collective-permute-done | bytes 262176 | tf_op jit(solution)/shard_map/ppermute | solution.py:416
  219.1 4.1 %collective-permute-done.19 = bf16[64,2048]{1,0:T(8,128)(2,1)S(1)} collective-permute-done((bf16[64,2048]{1,0:T(8,128)(2,1)}, bf16[64,2048]{1,0:T(8,128)(2,1)S(1)}, u32[]{:S(2)}, u32[]{:S(2)}) %collective-permute-start.19) | collective-permute-done | bytes 262176 | tf_op jit(solution)/shard_map/ppermute | solution.py:416
  (59 shorter events, 32.8 us)
Async XLA Ops:
  7.0 119.6 %collective-permute-start.9 = (bf16[2,2048,256]{2,1,0:T(8,128)(2,1)}, bf16[2,2048,256]{2,1,0:T(8,128)(2,1)}, u32[]{:S(2)}, u32[]{:S(2)}) collective-permute-start(bf16[2,2048,256]{2,1,0:T(8,128)(2,1)} %get-tuple-element.44), channel_id=1, source_target_pairs={{0,1},{1,4},{2,5},{3,0},{4,3},{5,6},{6,7},{7,2},{8,9},{9,12},{10,1... | collective-permute-start | bytes 6291464 | tf_op jit(solution)/shard_map/ppermute | solution.py:365
  13.3 115.9 %collective-permute-start.12 = (bf16[2,2048,256]{2,1,0:T(8,128)(2,1)}, bf16[2,2048,256]{2,1,0:T(8,128)(2,1)}, u32[]{:S(2)}, u32[]{:S(2)}) collective-permute-start(bf16[2,2048,256]{2,1,0:T(8,128)(2,1)} %get-tuple-element.46.gu2), channel_id=1, source_target_pairs={{2,4},{3,5},{4,2},{5,3},{10,12},{11,13},{12,10},{13,11},{18,20},{1... | collective-permute-start | bytes 6291464 | tf_op jit(solution)/shard_map/ppermute | solution.py:462
  30.5 11.7 %all-to-all-start.1 = ((bf16[32,16,128]{2,1,0:T(8,128)(2,1)}), bf16[32,16,128]{2,1,0:T(8,128)(2,1)S(1)}, u32[]{:S(2)}, u32[]{:S(2)}) async-start(bf16[32,16,128]{2,1,0:T(8,128)(2,1)} %shard_map.101), calls=%async_computation.1 | async-start | bytes 262144 | tf_op jit(solution)/shard_map/all_to_all | solution.py:458
  45.9 21.0 %collective-permute-start = (bf16[64,2048]{1,0:T(8,128)(2,1)}, bf16[64,2048]{1,0:T(8,128)(2,1)S(1)}, u32[]{:S(2)}, u32[]{:S(2)}) collective-permute-start(bf16[64,2048]{1,0:T(8,128)(2,1)} %get-tuple-element.37), channel_id=1, source_target_pairs={{0,1},{1,2},{2,3},{3,0},{4,5},{5,6},{6,7},{7,4},{8,9},{9,10},{10,1... | collective-permute-start | bytes 786440 | tf_op jit(solution)/shard_map/ppermute | solution.py:487
  46.7 85.8 %collective-permute-start.14 = (bf16[256,2048]{1,0:T(8,128)(2,1)}, bf16[256,2048]{1,0:T(8,128)(2,1)}, u32[]{:S(2)}, u32[]{:S(2)}) collective-permute-start(bf16[256,2048]{1,0:T(8,128)(2,1)} %get-tuple-element.47), channel_id=1, source_target_pairs={{0,1},{1,4},{2,5},{3,0},{4,3},{5,6},{6,7},{7,2},{8,9},{9,12},{10,1... | collective-permute-start | bytes 3145736 | tf_op jit(solution)/shard_map/ppermute | solution.py:365
  49.1 30.3 %collective-permute-start.1 = (bf16[64,2048]{1,0:T(8,128)(2,1)}, bf16[64,2048]{1,0:T(8,128)(2,1)S(1)}, u32[]{:S(2)}, u32[]{:S(2)}) collective-permute-start(bf16[64,2048]{1,0:T(8,128)(2,1)} %get-tuple-element.38), channel_id=1, source_target_pairs={{0,2},{1,3},{2,0},{3,1},{4,6},{5,7},{6,4},{7,5},{8,10},{9,11},{10,... | collective-permute-start | bytes 786440 | tf_op jit(solution)/shard_map/ppermute | solution.py:487
  66.9 12.5 %collective-permute-start.2 = (bf16[64,2048]{1,0:T(8,128)(2,1)}, bf16[64,2048]{1,0:T(8,128)(2,1)S(1)}, u32[]{:S(2)}, u32[]{:S(2)}) collective-permute-start(bf16[64,2048]{1,0:T(8,128)(2,1)} %get-tuple-element.39), channel_id=1, source_target_pairs={{0,3},{1,0},{2,1},{3,2},{4,7},{5,4},{6,5},{7,6},{8,11},{9,8},{10,9... | collective-permute-start | bytes 786440 | tf_op jit(solution)/shard_map/ppermute | solution.py:487
  82.0 17.1 %collective-permute-start.6 = (bf16[64,2048]{1,0:T(8,128)(2,1)S(1)}, bf16[64,2048]{1,0:T(8,128)(2,1)S(1)}, u32[]{:S(2)}, u32[]{:S(2)}) collective-permute-start(bf16[64,2048]{1,0:T(8,128)(2,1)S(1)} %get-tuple-element.43.t0), channel_id=1, source_target_pairs={{0,1},{1,2},{2,3},{3,0},{4,5},{5,6},{6,7},{7,4},{8,9},{9,10},{10,1... | collective-permute-start | bytes 786440 | tf_op jit(solution)/shard_map/ppermute | solution.py:410
  82.9 9.1 %collective-permute-start.3 = (f32[64,16]{1,0:T(8,128)S(1)}, f32[64,16]{1,0:T(8,128)S(1)}, u32[]{:S(2)}, u32[]{:S(2)}) collective-permute-start(f32[64,16]{1,0:T(8,128)S(1)} %copy.16.t0), channel_id=1, source_target_pairs={{0,1},{1,2},{2,3},{3,0},{4,5},{5,6},{6,7},{7,4},{8,9},{9,10},{10,1... | collective-permute-start | bytes 12296 | tf_op jit(solution)/shard_map/ppermute | solution.py:410
  92.0 4.3 %collective-permute-start.4 = (f32[64,16]{1,0:T(8,128)S(1)}, f32[64,16]{1,0:T(8,128)S(1)}, u32[]{:S(2)}, u32[]{:S(2)}) collective-permute-start(f32[64,16]{1,0:T(8,128)S(1)} %copy.16.t0), channel_id=1, source_target_pairs={{0,2},{1,3},{2,0},{3,1},{4,6},{5,7},{6,4},{7,5},{8,10},{9,11},{10,... | collective-permute-start | bytes 12296 | tf_op jit(solution)/shard_map/ppermute | solution.py:410
  96.3 2.8 %collective-permute-start.5 = (f32[64,16]{1,0:T(8,128)S(1)}, f32[64,16]{1,0:T(8,128)S(1)}, u32[]{:S(2)}, u32[]{:S(2)}) collective-permute-start(f32[64,16]{1,0:T(8,128)S(1)} %copy.16.t0), channel_id=1, source_target_pairs={{0,3},{1,0},{2,1},{3,2},{4,7},{5,4},{6,5},{7,6},{8,11},{9,8},{10,9... | collective-permute-start | bytes 12296 | tf_op jit(solution)/shard_map/ppermute | solution.py:410
  99.1 6.7 %collective-permute-start.7 = (bf16[64,2048]{1,0:T(8,128)(2,1)S(1)}, bf16[64,2048]{1,0:T(8,128)(2,1)S(1)}, u32[]{:S(2)}, u32[]{:S(2)}) collective-permute-start(bf16[64,2048]{1,0:T(8,128)(2,1)S(1)} %get-tuple-element.43.t0), channel_id=1, source_target_pairs={{0,2},{1,3},{2,0},{3,1},{4,6},{5,7},{6,4},{7,5},{8,10},{9,11},{10,... | collective-permute-start | bytes 786440 | tf_op jit(solution)/shard_map/ppermute | solution.py:410
  99.1 12.2 %collective-permute-start.8 = (bf16[64,2048]{1,0:T(8,128)(2,1)S(1)}, bf16[64,2048]{1,0:T(8,128)(2,1)S(1)}, u32[]{:S(2)}, u32[]{:S(2)}) collective-permute-start(bf16[64,2048]{1,0:T(8,128)(2,1)S(1)} %get-tuple-element.43.t0), channel_id=1, source_target_pairs={{0,3},{1,0},{2,1},{3,2},{4,7},{5,4},{6,5},{7,6},{8,11},{9,8},{10,9... | collective-permute-start | bytes 786440 | tf_op jit(solution)/shard_map/ppermute | solution.py:410
  113.5 39.7 %all-to-all-start.2 = ((bf16[32,16,2304]{2,1,0:T(8,128)(2,1)}), bf16[32,16,2304]{2,1,0:T(8,128)(2,1)S(1)}, u32[]{:S(2)}, u32[]{:S(2)}) async-start(bf16[32,16,2304]{2,1,0:T(8,128)(2,1)} %bitcast.20), calls=%async_computation.2 | async-start | bytes 4718592 | tf_op jit(solution)/shard_map/all_to_all | solution.py:499
  123.9 27.8 %collective-permute-start.11 = (bf16[2,2048,256]{2,1,0:T(8,128)(2,1)}, bf16[2,2048,256]{2,1,0:T(8,128)(2,1)}, u32[]{:S(2)}, u32[]{:S(2)}) collective-permute-start(bf16[2,2048,256]{2,1,0:T(8,128)(2,1)} %get-tuple-element.46.gu2), channel_id=1, source_target_pairs={{0,4},{1,5},{6,2},{7,3},{8,12},{9,13},{14,10},{15,11},{16,20},{17,... | collective-permute-start | bytes 6291464 | tf_op jit(solution)/shard_map/ppermute | solution.py:365
  125.2 10.9 %collective-permute-start.16 = (bf16[256,2048]{1,0:T(8,128)(2,1)S(1)}, bf16[256,2048]{1,0:T(8,128)(2,1)S(1)}, u32[]{:S(2)}, u32[]{:S(2)}) collective-permute-start(bf16[256,2048]{1,0:T(8,128)(2,1)S(1)} %get-tuple-element.48.dn2), channel_id=1, source_target_pairs={{0,4},{1,5},{6,2},{7,3},{8,12},{9,13},{14,10},{15,11},{16,20},{17,... | collective-permute-start | bytes 3145736 | tf_op jit(solution)/shard_map/ppermute | solution.py:365
  126.6 26.6 %collective-permute-start.10 = (bf16[2,2048,256]{2,1,0:T(8,128)(2,1)}, bf16[2,2048,256]{2,1,0:T(8,128)(2,1)}, u32[]{:S(2)}, u32[]{:S(2)}) collective-permute-start(bf16[2,2048,256]{2,1,0:T(8,128)(2,1)} %collective-permute-done.9.gu0), channel_id=1, source_target_pairs={{0,4},{4,0},{8,12},{12,8},{16,20},{20,16},{24,28},{28,24},{32,36},... | collective-permute-start | bytes 6291464 | tf_op jit(solution)/shard_map/ppermute | solution.py:365
  129.2 24.0 %collective-permute-start.13 = (bf16[2,2048,256]{2,1,0:T(8,128)(2,1)}, bf16[2,2048,256]{2,1,0:T(8,128)(2,1)}, u32[]{:S(2)}, u32[]{:S(2)}) collective-permute-start(bf16[2,2048,256]{2,1,0:T(8,128)(2,1)} %collective-permute-done.12.gu4), channel_id=1, source_target_pairs={{2,6},{3,7},{4,0},{5,1},{10,14},{11,15},{12,8},{13,9},{18,22},{19,... | collective-permute-start | bytes 6291464 | tf_op jit(solution)/shard_map/ppermute | solution.py:465
  132.5 17.7 %collective-permute-start.17 = (bf16[256,2048]{1,0:T(8,128)(2,1)S(1)}, bf16[256,2048]{1,0:T(8,128)(2,1)}, u32[]{:S(2)}, u32[]{:S(2)}) collective-permute-start(bf16[256,2048]{1,0:T(8,128)(2,1)S(1)} %get-tuple-element.48.dn2), channel_id=1, source_target_pairs={{2,4},{3,5},{4,2},{5,3},{10,12},{11,13},{12,10},{13,11},{18,20},{1... | collective-permute-start | bytes 3145736 | tf_op jit(solution)/shard_map/ppermute | solution.py:461
  136.1 15.6 %collective-permute-start.15 = (bf16[256,2048]{1,0:T(8,128)(2,1)}, bf16[256,2048]{1,0:T(8,128)(2,1)}, u32[]{:S(2)}, u32[]{:S(2)}) collective-permute-start(bf16[256,2048]{1,0:T(8,128)(2,1)} %collective-permute-done.14.dn0), channel_id=1, source_target_pairs={{0,4},{4,0},{8,12},{12,8},{16,20},{20,16},{24,28},{28,24},{32,36},... | collective-permute-start | bytes 3145736 | tf_op jit(solution)/shard_map/ppermute | solution.py:365
  150.2 10.3 %collective-permute-start.18 = (bf16[256,2048]{1,0:T(8,128)(2,1)}, bf16[256,2048]{1,0:T(8,128)(2,1)S(1)}, u32[]{:S(2)}, u32[]{:S(2)}) collective-permute-start(bf16[256,2048]{1,0:T(8,128)(2,1)} %collective-permute-done.17.dn4), channel_id=1, source_target_pairs={{2,6},{3,7},{4,0},{5,1},{10,14},{11,15},{12,8},{13,9},{18,22},{19,... | collective-permute-start | bytes 3145736 | tf_op jit(solution)/shard_map/ppermute | solution.py:466
  205.3 13.8 %collective-permute-start.21 = (bf16[64,2048]{1,0:T(8,128)(2,1)}, bf16[64,2048]{1,0:T(8,128)(2,1)S(1)}, u32[]{:S(2)}, u32[]{:S(2)}) collective-permute-start(bf16[64,2048]{1,0:T(8,128)(2,1)} %get-tuple-element.54), channel_id=1, source_target_pairs={{0,3},{1,0},{2,1},{3,2},{4,7},{5,4},{6,5},{7,6},{8,11},{9,8},{10,9... | collective-permute-start | bytes 786440 | tf_op jit(solution)/shard_map/ppermute | solution.py:416
  207.6 11.5 %collective-permute-start.20 = (bf16[64,2048]{1,0:T(8,128)(2,1)}, bf16[64,2048]{1,0:T(8,128)(2,1)S(1)}, u32[]{:S(2)}, u32[]{:S(2)}) collective-permute-start(bf16[64,2048]{1,0:T(8,128)(2,1)} %get-tuple-element.53), channel_id=1, source_target_pairs={{0,2},{1,3},{2,0},{3,1},{4,6},{5,7},{6,4},{7,5},{8,10},{9,11},{10,... | collective-permute-start | bytes 786440 | tf_op jit(solution)/shard_map/ppermute | solution.py:416
  207.9 15.3 %collective-permute-start.19 = (bf16[64,2048]{1,0:T(8,128)(2,1)}, bf16[64,2048]{1,0:T(8,128)(2,1)S(1)}, u32[]{:S(2)}, u32[]{:S(2)}) collective-permute-start(bf16[64,2048]{1,0:T(8,128)(2,1)} %get-tuple-element.52), channel_id=1, source_target_pairs={{0,1},{1,2},{2,3},{3,0},{4,5},{5,6},{6,7},{7,4},{8,9},{9,10},{10,1... | collective-permute-start | bytes 786440 | tf_op jit(solution)/shard_map/ppermute | solution.py:416
  (9 other events, 277.8 us)

commit v7 on v6

--- a/solution.py
+++ b/solution.py
@@ -77,8 +77,7 @@
     return slice(h * DH, (h + 1) * DH)
 
 
-def pick_copies(index_ref, gu_ref, dn_ref, gu_buf, dn_buf, sems):
-    index = index_ref[0]
+def pick_copies(index, gu_ref, dn_ref, gu_buf, dn_buf, sems):
     copies = []
     for half in range(2):
         for part in range(2):
@@ -90,24 +89,26 @@
 
 
 def front_kernel(
-    index_ref, x_ref, gain_ref, w_ref, gu_ref, dn_ref,
-    normed_ref, k_ref, v_ref, send_ref, zero_ref, gu_out, dn_out,
+    head_ref, x_ref, gain_ref, w_ref, gu_ref, dn_ref,
+    normed_ref, k_ref, v_ref, send_ref, zero_ref, gu_out, dn_out, mine_ref,
     wk, wv, sems, read_sems,
 ):
     copy_k = pltpu.make_async_copy(w_ref.at[1], wk, sems.at[0])
     copy_v = pltpu.make_async_copy(w_ref.at[2], wv, sems.at[1])
     copy_k.start()
     copy_v.start()
-    reads = pick_copies(index_ref, gu_ref, dn_ref, gu_out, dn_out, read_sems)
-    for read in reads:
-        read.start()
+    head = head_ref[0]
+    reads = pick_copies(1 - (head & 1), gu_ref, dn_ref, gu_out, dn_out, read_sems)
     zero_ref[0] = 0
+    mine_ref[...] = x_ref[pl.ds(pl.multiple_of(head * ROWS, ROWS), ROWS), :]
     normed = rms_norm(x_ref[...].astype(F32), gain_ref[...]).astype(BF)
     normed_ref[...] = normed
     copy_k.wait()
+    copy_v.wait()
+    for read in reads:
+        read.start()
     key = dot(normed, wk[...]).astype(BF)
     k_ref[...] = key
-    copy_v.wait()
     value = dot(normed, wv[...]).astype(BF)
     v_ref[...] = value
     for h in range(HEADS):
@@ -158,15 +159,16 @@
         s1[:, cols] = rows[3 * ROWS:].astype(BF)
 
 
-def norm_kernel(head_ref, x_ref, own_ref, g1, g2, g3, gain_ref, resid_ref, normed_ref, rows, sems):
-    start = pl.multiple_of(head_ref[0] * ROWS, ROWS)
-    copy = pltpu.make_async_copy(x_ref.at[pl.ds(start, ROWS)], rows, sems.at[0])
-    copy.start()
+def norm_kernel(mine_ref, own_ref, g1, g2, g3, gain_ref, resid_ref, normed_ref):
     total = own_ref[...] + g1[...].astype(F32) + g2[...].astype(F32) + g3[...].astype(F32)
-    copy.wait()
-    resid = rows[...].astype(F32) + total
+    resid = mine_ref[...].astype(F32) + total
     resid_ref[...] = resid
     normed_ref[...] = rms_norm(resid, gain_ref[...]).astype(BF)
+
+
+def last_kernel(resid_ref, own_ref, g1, g2, g3, out_ref):
+    total = own_ref[...] + g1[...].astype(F32) + g2[...].astype(F32) + g3[...].astype(F32)
+    out_ref[...] = (resid_ref[...] + total).astype(BF)
 
 
 def routing_kernel(head_ref, t0, t1, t2, t3, place_ref, weight_ref):
@@ -366,7 +368,7 @@
 
 
 def pick_kernel(index_ref, gu_ref, dn_ref, gu_out, dn_out, gu_buf, dn_buf, read_sems, write_sems):
-    reads = pick_copies(index_ref, gu_ref, dn_ref, gu_buf, dn_buf, read_sems)
+    reads = pick_copies(index_ref[0], gu_ref, dn_ref, gu_buf, dn_buf, read_sems)
     writes = []
     for half in range(2):
         for part in range(2):
@@ -410,13 +412,6 @@
     return [array] + [lax.ppermute(array, "head", head_perm(k)) for k in range(1, 4)]
 
 
-def scatter_head(blocks):
-    total = blocks[0]
-    for k in range(1, 4):
-        total = total + lax.ppermute(blocks[k], "head", head_perm(k)).astype(F32)
-    return total
-
-
 def on_device(
     hidden_in, attn_gain, w_qkv, out_gain, w_out, moe_gain, routes, gate_weights, w_gate_up, w_down
 ):
@@ -425,7 +420,8 @@
     core = seq % 2
 
     w_planes = w_qkv.transpose(1, 0, 2)
-    normed, key, value, send_state, zero, *near = call(
+    here = head.astype(jnp.int32)[None]
+    normed, key, value, send_state, zero, *near, mine = call(
         front_kernel,
         [SMEM, VMEM, VMEM, HBM, HBM, HBM],
         [
@@ -436,6 +432,7 @@
             out((1,), jnp.int32),
             chip((2, D, 256), BF),
             chip((256, D), BF),
+            out((ROWS, D), BF),
         ],
         [
             pltpu.VMEM((D, WIDE), BF),
@@ -444,7 +441,7 @@
             pltpu.SemaphoreType.DMA((6,)),
         ],
     )(
-        (1 - (head & 1)).astype(jnp.int32)[None],
+        here,
         hidden_in,
         attn_gain[None, :],
         w_planes,
@@ -472,7 +469,6 @@
         [out((TOK, WIDE), BF), chip((TOK, WIDE), F32)],
         [pltpu.VMEM((D, WIDE), BF), pltpu.SemaphoreType.DMA((1,))],
     )(on_chip(normed), w_planes, on_chip(key), on_chip(value))
-    here = head.astype(jnp.int32)[None]
     blocks = call(
         attend_kernel,
         [SMEM] + [VMEM] * 5,
@@ -486,11 +482,8 @@
 
     got = [lax.ppermute(blocks[k], "head", head_perm(k)) for k in range(1, 4)]
     resid, normed2 = call(
-        norm_kernel,
-        [SMEM, HBM] + [VMEM] * 5,
-        [out((ROWS, D), F32), chip((ROWS, D), BF)],
-        [pltpu.VMEM((ROWS, D), BF), pltpu.SemaphoreType.DMA((1,))],
-    )(here, hidden_in, on_chip(blocks[0]), *[on_chip(g) for g in got], moe_gain[None, :])
+        norm_kernel, [VMEM] * 6, [out((ROWS, D), F32), chip((ROWS, D), BF)]
+    )(on_chip(mine), on_chip(blocks[0]), *[on_chip(g) for g in got], moe_gain[None, :])
     tokens = gather_head(normed2)
 
     sent = call(
@@ -525,10 +518,15 @@
     )(keep, on_chip(act), on_chip(down), *downs[4:])[0]
     back = lax.all_to_all(results.reshape(32, 16, PACKED), "seq", 0, 0, tiled=True)
     blocks = call(
-        combine_kernel, [VMEM] * 2, BLOCKS_OUT, [pltpu.VMEM((64, D), BF)]
+        combine_kernel,
+        [VMEM] * 2,
+        [chip((ROWS, D), F32)] + BLOCKS_OUT[1:],
+        [pltpu.VMEM((64, D), BF)],
     )(on_chip(weight), on_chip(back.reshape(MAIN, PACKED)))
-    moe_sum = scatter_head(blocks)
-    return (resid + moe_sum).astype(BF)
+    got = [lax.ppermute(blocks[k], "head", head_perm(k)) for k in range(1, 4)]
+    return call(last_kernel, [VMEM] * 5, [out((ROWS, D), BF)])(
+        on_chip(resid), on_chip(blocks[0]), *[on_chip(g) for g in got]
+    )[0]
 
 
 def solution(mesh):

time: 228 us -> 225 us (0.987)
  waiting for transfers between devices: 87.8 us -> 84.9 us
    ppermute x3 -> x0, waiting for transfers between devices: 15 us -> none  [scatter_head(): total = total + lax.ppermute(blocks[k], 'head', head_perm(k)).astype(F32)]
    ppermute x3 -> x6, waiting for transfers between devices: 29.7 us -> 41.9 us  [on_device(): got = [lax.ppermute(blocks[k], 'head', head_perm(k)) for k in range(1, 4)]]
    ppermute x3 -> x6, starting transfers between devices: 1.4 us -> 4.94 us  [on_device(): got = [lax.ppermute(blocks[k], 'head', head_perm(k)) for k in range(1, 4)]]
    ppermute x3 -> x0, starting transfers between devices: 2.88 us -> none  [scatter_head(): total = total + lax.ppermute(blocks[k], 'head', head_perm(k)).astype(F32)]
where the time goes in v7:
time: 225 us; the launch traced here: 222 us
  waiting for transfers between devices  84.9 us (38%)
  blocking collectives  51.3 us (23%)
  starting transfers between devices  45.2 us (20%)
  Pallas kernels  38.1 us (17%)
    ppermute x6, waiting for transfers between devices, on_device(): got = [lax.ppermute(blocks[k], 'head', head_perm(k)) for k in range(1, 4)]  41.9 us
    all_to_all x1, blocking collectives, on_device(): lax.all_to_all(results.reshape(32, 16, PACKED), 'seq', 0, 0, tiled=True)  37 us
    ppermute x6, waiting for transfers between devices, gather_head(): lax.ppermute(array, 'head', head_perm(k))  24 us
    all_to_all x1, blocking collectives, on_device(): lax.all_to_all(send_state.reshape(32, 16, DH), 'seq', 0, 0, tiled=True)  14.3 us
    ppermute x1, waiting for transfers between devices, on_device(): far_down = lax.ppermute(rest[1], both, device_perm(far_target))  13.9 us
    ppermute x6, starting transfers between devices, permute_all(): return [lax.ppermute(a, axes, perm) for a in arrays]  10.9 us
    all_to_all x1, starting transfers between devices, on_device(): lax.all_to_all(sent.reshape(32, 16, PACKED), 'seq', 0, 0, tiled=True)  10.4 us
    pallas_call x1, Pallas kernels, on_device(): call(front_kernel, [SMEM, VMEM, VMEM, HBM, HBM, HBM], [chip((TOK, D), BF)...  8.4 us
  transfers between devices with their start and end apart: 24, of which 12 were waited for; matrix products, arithmetic and copies ran while one was open for 0% of the time, Pallas kernels for 10%

profile of v7, /device:TPU:33, one launch (start us, length us, event | category | flops | bytes accessed | tf_op | source)
XLA Modules:
  0.0 222.2 jit_solution(8808034532786281298)
XLA Ops:
  0.0 8.4 %shard_map.100 = (bf16[256,2048]{1,0:T(8,128)(2,1)S(1)}, bf16[256,512]{1,0:T(8,128)(2,1)S(1)}, bf16[256,512]{1,0:T(8,128)(2,1)S(1)}, bf16[512,128]{1,0:T(8,128)(...) custom-call(s32[1]{0:T(128)} %bitcast.head_ref, ...), custom_call_target="tpu_custom_call" | custom-call | tf_op jit(solution)/shard_map/pallas_call | solution.py:424
  8.4 3.1 %collective-permute-start.9 = (bf16[2,2048,256]{2,1,0:T(8,128)(2,1)}, bf16[2,2048,256]{2,1,0:T(8,128)(2,1)}, u32[]{:S(2)}, u32[]{:S(2)}) collective-permute-start(bf16[2,2048,256]{2,1,0:T(8,128)(2,1)} %get-tuple-element.46), channel_id=1, source_target_pairs={{0,1},{1,4},{2,5},{3,0},{4,3},{5,6},{6,7},{7,2},{8,9},{9,12},{10,1... | collective-permute-start | bytes 6291464 | tf_op jit(solution)/shard_map/ppermute | solution.py:367
  17.0 14.3 %all_to_all.20.states_ref = bf16[32,16,128]{2,1,0:T(8,128)(2,1)S(1)} all-to-all(bf16[32,16,128]{2,1,0:T(8,128)(2,1)S(1)} %bitcast.21), channel_id=1, replica_groups=mesh['seq'=32,'head'=4] {'seq'}, dimensions={0} | all-to-all | bytes 262144 | tf_op jit(solution)/shard_map/all_to_all | solution.py:453
  32.0 5.0 %all-to-all-start.1 = ((bf16[32,16,128]{2,1,0:T(8,128)(2,1)}), bf16[32,16,128]{2,1,0:T(8,128)(2,1)S(1)}, u32[]{:S(2)}, u32[]{:S(2)}) async-start(bf16[32,16,128]{2,1,0:T(8,128)(2,1)} %shard_map.101), calls=%async_computation.1 | async-start | bytes 262144 | tf_op jit(solution)/shard_map/all_to_all | solution.py:455
  37.0 3.0 %shard_map.102 = (bf16[256,512]{1,0:T(8,128)(2,1)}, f32[256,512]{1,0:T(8,128)S(1)}) custom-call(bf16[256,2048]{1,0:T(8,128)(2,1)S(1)} %get-tuple-element.33.normed_ref, bf16[3,2048,512]{2,1,0:T(8,128)(2,1)} %bitcast.18, bf16[256,512]{1,0:T(8,128)(2,1)S(1)} %get-tuple-element.34.k_ref, bf16[256,512]{1,0:T(8,128)(2,1)S(1)} %get-tuple-element.35.v_ref), custom_call_target="tpu_custom_call" | custom-call | tf_op jit(solution)/shard_map/pallas_call | solution.py:466
  40.1 3.6 %all-to-all-done.1 = bf16[32,16,128]{2,1,0:T(8,128)(2,1)S(1)} async-done(((bf16[32,16,128]{2,1,0:T(8,128)(2,1)}), bf16[32,16,128]{2,1,0:T(8,128)(2,1)S(1)}, u32[]{:S(2)}, u32[]{:S(2)}) %all-to-all-start.1) | async-done | bytes 131104 | tf_op jit(solution)/shard_map/all_to_all | solution.py:455
  43.7 3.6 %shard_map.103 = (f32[64,2048]{1,0:T(8,128)S(1)}, bf16[64,2048]{1,0:T(8,128)(2,1)}, bf16[64,2048]{1,0:T(8,128)(2,1)}, bf16[64,2048]{1,0:T(8,128)(2,1)}) custom-call(s32[1]{0:T(128)} %bitcast.head_ref, bf16[512,128]{1,0:T(8,128)(2,1)S(1)} %bitcast.16, bf16[256,512]{1,0:T(8,128)(2,1)} %get-tuple-element.36.q_ref, f32[256,512]{1,0:T(8,128)S(1)} %get-tuple-element.37.local_ref, ...), custom_call_target="tpu_custom_call" | custom-call | tf_op jit(solution)/shard_map/pallas_call | solution.py:472
  51.2 17.1 %collective-permute-done.g1 = bf16[64,2048]{1,0:T(8,128)(2,1)S(1)} collective-permute-done((bf16[64,2048]{1,0:T(8,128)(2,1)}, bf16[64,2048]{1,0:T(8,128)(2,1)S(1)}, u32[]{:S(2)}, u32[]{:S(2)}) %collective-permute-start) | collective-permute-done | bytes 262176 | tf_op jit(solution)/shard_map/ppermute | solution.py:483
  68.4 12.5 %collective-permute-done.1.g2 = bf16[64,2048]{1,0:T(8,128)(2,1)S(1)} collective-permute-done((bf16[64,2048]{1,0:T(8,128)(2,1)}, bf16[64,2048]{1,0:T(8,128)(2,1)S(1)}, u32[]{:S(2)}, u32[]{:S(2)}) %collective-permute-start.1) | collective-permute-done | bytes 262176 | tf_op jit(solution)/shard_map/ppermute | solution.py:483
  83.6 8.8 %collective-permute-done.3.t1 = f32[64,16]{1,0:T(8,128)S(1)} collective-permute-done((f32[64,16]{1,0:T(8,128)S(1)}, f32[64,16]{1,0:T(8,128)S(1)}, u32[]{:S(2)}, u32[]{:S(2)}) %collective-permute-start.3) | collective-permute-done | bytes 4128 | tf_op jit(solution)/shard_map/ppermute | solution.py:412
  92.4 4.3 %collective-permute-done.4.t2 = f32[64,16]{1,0:T(8,128)S(1)} collective-permute-done((f32[64,16]{1,0:T(8,128)S(1)}, f32[64,16]{1,0:T(8,128)S(1)}, u32[]{:S(2)}, u32[]{:S(2)}) %collective-permute-start.4) | collective-permute-done | bytes 4128 | tf_op jit(solution)/shard_map/ppermute | solution.py:412
  103.4 2.8 %collective-permute-done.7.t2 = bf16[64,2048]{1,0:T(8,128)(2,1)S(1)} collective-permute-done((bf16[64,2048]{1,0:T(8,128)(2,1)S(1)}, bf16[64,2048]{1,0:T(8,128)(2,1)S(1)}, u32[]{:S(2)}, u32[]{:S(2)}) %collective-permute-start.7) | collective-permute-done | bytes 262176 | tf_op jit(solution)/shard_map/ppermute | solution.py:412
  106.2 5.5 %collective-permute-done.8.t3 = bf16[64,2048]{1,0:T(8,128)(2,1)S(1)} collective-permute-done((bf16[64,2048]{1,0:T(8,128)(2,1)S(1)}, bf16[64,2048]{1,0:T(8,128)(2,1)S(1)}, u32[]{:S(2)}, u32[]{:S(2)}) %collective-permute-start.8) | collective-permute-done | bytes 262176 | tf_op jit(solution)/shard_map/ppermute | solution.py:412
  114.0 10.4 %all-to-all-start.2 = ((bf16[32,16,2304]{2,1,0:T(8,128)(2,1)}), bf16[32,16,2304]{2,1,0:T(8,128)(2,1)S(1)}, u32[]{:S(2)}, u32[]{:S(2)}) async-start(bf16[32,16,2304]{2,1,0:T(8,128)(2,1)} %bitcast.19), calls=%async_computation.2 | async-start | bytes 4718592 | tf_op jit(solution)/shard_map/all_to_all | solution.py:492
  127.0 2.7 %collective-permute-start.10 = (bf16[2,2048,256]{2,1,0:T(8,128)(2,1)}, bf16[2,2048,256]{2,1,0:T(8,128)(2,1)}, u32[]{:S(2)}, u32[]{:S(2)}) collective-permute-start(bf16[2,2048,256]{2,1,0:T(8,128)(2,1)} %collective-permute-done.9.gu0), channel_id=1, source_target_pairs={{0,4},{4,0},{8,12},{12,8},{16,20},{20,16},{24,28},{28,24},{32,36},... | collective-permute-start | bytes 6291464 | tf_op jit(solution)/shard_map/ppermute | solution.py:367
  129.7 3.2 %collective-permute-start.13 = (bf16[2,2048,256]{2,1,0:T(8,128)(2,1)}, bf16[2,2048,256]{2,1,0:T(8,128)(2,1)}, u32[]{:S(2)}, u32[]{:S(2)}) collective-permute-start(bf16[2,2048,256]{2,1,0:T(8,128)(2,1)} %collective-permute-done.12.gu4), channel_id=1, source_target_pairs={{2,6},{3,7},{4,0},{5,1},{10,14},{11,15},{12,8},{13,9},{18,22},{19,... | collective-permute-start | bytes 6291464 | tf_op jit(solution)/shard_map/ppermute | solution.py:462
  132.9 3.6 %collective-permute-start.17 = (bf16[256,2048]{1,0:T(8,128)(2,1)S(1)}, bf16[256,2048]{1,0:T(8,128)(2,1)}, u32[]{:S(2)}, u32[]{:S(2)}) collective-permute-start(bf16[256,2048]{1,0:T(8,128)(2,1)S(1)} %get-tuple-element.50.dn2), channel_id=1, source_target_pairs={{2,4},{3,5},{4,2},{5,3},{10,12},{11,13},{12,10},{13,11},{18,20},{1... | collective-permute-start | bytes 3145736 | tf_op jit(solution)/shard_map/ppermute | solution.py:458
  136.7 13.9 %collective-permute-done.17.dn4 = bf16[256,2048]{1,0:T(8,128)(2,1)} collective-permute-done((bf16[256,2048]{1,0:T(8,128)(2,1)S(1)}, bf16[256,2048]{1,0:T(8,128)(2,1)}, u32[]{:S(2)}, u32[]{:S(2)}) %collective-permute-start.17) | collective-permute-done | bytes 1048608 | tf_op jit(solution)/shard_map/ppermute | solution.py:458
  153.7 7.2 %shard_map.107 = (bf16[576,1024]{1,0:T(8,128)(2,1)S(1)}, bf16[768,2048]{1,0:T(8,128)(2,1)S(1)}) custom-call(s32[1]{0:T(128)} %bitcast.7.keep_ref, bf16[512,2304]{1,0:T(8,128)(2,1)S(1)} %bitcast.15, bf16[2,2048,256]{2,1,0:T(8,128)(2,1)} %collective-permute-done.9.gu0, bf16[2,2048,256]{2,1,0:T(8,128)(2,1)} %collective-permute-done.10.gu1, ...), custom_call_target="tpu_custom_call" | custom-call | tf_op jit(solution)/shard_map/pallas_call | solution.py:496
  161.9 4.8 %shard_map.108 = bf16[512,2304]{1,0:T(8,128)(2,1)} custom-call(s32[1]{0:T(128)} %bitcast.7.keep_ref, bf16[576,1024]{1,0:T(8,128)(2,1)S(1)} %get-tuple-element.51.act, bf16[768,2048]{1,0:T(8,128)(2,1)S(1)} %get-tuple-element.52.down, bf16[256,2048]{1,0:T(8,128)(2,1)} %collective-permute-done.17.dn4, bf16[256,2048]{1,0:T(8,128)(2,1)} %copy-done.6), custom_call_target="tpu_custom_call" | custom-call | tf_op jit(solution)/shard_map/pallas_call | solution.py:506
  166.7 37.0 %all_to_all.21 = bf16[32,16,2304]{2,1,0:T(8,128)(2,1)S(1)} all-to-all(bf16[32,16,2304]{2,1,0:T(8,128)(2,1)} %bitcast.20), channel_id=1, replica_groups=mesh['seq'=32,'head'=4] {'seq'}, dimensions={0} | all-to-all | bytes 4718592 | tf_op jit(solution)/shard_map/all_to_all | solution.py:519
  206.4 2.7 %collective-permute-start.20 = (bf16[64,2048]{1,0:T(8,128)(2,1)}, bf16[64,2048]{1,0:T(8,128)(2,1)S(1)}, u32[]{:S(2)}, u32[]{:S(2)}) collective-permute-start(bf16[64,2048]{1,0:T(8,128)(2,1)} %get-tuple-element.55), channel_id=1, source_target_pairs={{0,2},{1,3},{2,0},{3,1},{4,6},{5,7},{6,4},{7,5},{8,10},{9,11},{10,... | collective-permute-start | bytes 786440 | tf_op jit(solution)/shard_map/ppermute | solution.py:526
  209.1 5.8 %collective-permute-done.19.g1 = bf16[64,2048]{1,0:T(8,128)(2,1)S(1)} collective-permute-done((bf16[64,2048]{1,0:T(8,128)(2,1)}, bf16[64,2048]{1,0:T(8,128)(2,1)S(1)}, u32[]{:S(2)}, u32[]{:S(2)}) %collective-permute-start.19) | collective-permute-done | bytes 262176 | tf_op jit(solution)/shard_map/ppermute | solution.py:526
  214.9 6.4 %collective-permute-done.20.g2 = bf16[64,2048]{1,0:T(8,128)(2,1)S(1)} collective-permute-done((bf16[64,2048]{1,0:T(8,128)(2,1)}, bf16[64,2048]{1,0:T(8,128)(2,1)S(1)}, u32[]{:S(2)}, u32[]{:S(2)}) %collective-permute-start.20) | collective-permute-done | bytes 262176 | tf_op jit(solution)/shard_map/ppermute | solution.py:526
  (61 shorter events, 31.3 us)
Async XLA Ops:
  8.4 118.6 %collective-permute-start.9 = (bf16[2,2048,256]{2,1,0:T(8,128)(2,1)}, bf16[2,2048,256]{2,1,0:T(8,128)(2,1)}, u32[]{:S(2)}, u32[]{:S(2)}) collective-permute-start(bf16[2,2048,256]{2,1,0:T(8,128)(2,1)} %get-tuple-element.46), channel_id=1, source_target_pairs={{0,1},{1,4},{2,5},{3,0},{4,3},{5,6},{6,7},{7,2},{8,9},{9,12},{10,1... | collective-permute-start | bytes 6291464 | tf_op jit(solution)/shard_map/ppermute | solution.py:367
  14.8 114.9 %collective-permute-start.12 = (bf16[2,2048,256]{2,1,0:T(8,128)(2,1)}, bf16[2,2048,256]{2,1,0:T(8,128)(2,1)}, u32[]{:S(2)}, u32[]{:S(2)}) collective-permute-start(bf16[2,2048,256]{2,1,0:T(8,128)(2,1)} %get-tuple-element.48.gu2), channel_id=1, source_target_pairs={{2,4},{3,5},{4,2},{5,3},{10,12},{11,13},{12,10},{13,11},{18,20},{1... | collective-permute-start | bytes 6291464 | tf_op jit(solution)/shard_map/ppermute | solution.py:459
  32.0 11.7 %all-to-all-start.1 = ((bf16[32,16,128]{2,1,0:T(8,128)(2,1)}), bf16[32,16,128]{2,1,0:T(8,128)(2,1)S(1)}, u32[]{:S(2)}, u32[]{:S(2)}) async-start(bf16[32,16,128]{2,1,0:T(8,128)(2,1)} %shard_map.101), calls=%async_computation.1 | async-start | bytes 262144 | tf_op jit(solution)/shard_map/all_to_all | solution.py:455
  47.4 21.0 %collective-permute-start = (bf16[64,2048]{1,0:T(8,128)(2,1)}, bf16[64,2048]{1,0:T(8,128)(2,1)S(1)}, u32[]{:S(2)}, u32[]{:S(2)}) collective-permute-start(bf16[64,2048]{1,0:T(8,128)(2,1)} %get-tuple-element.39), channel_id=1, source_target_pairs={{0,1},{1,2},{2,3},{3,0},{4,5},{5,6},{6,7},{7,4},{8,9},{9,10},{10,1... | collective-permute-start | bytes 786440 | tf_op jit(solution)/shard_map/ppermute | solution.py:483
  48.2 84.8 %collective-permute-start.14 = (bf16[256,2048]{1,0:T(8,128)(2,1)}, bf16[256,2048]{1,0:T(8,128)(2,1)}, u32[]{:S(2)}, u32[]{:S(2)}) collective-permute-start(bf16[256,2048]{1,0:T(8,128)(2,1)} %get-tuple-element.49), channel_id=1, source_target_pairs={{0,1},{1,4},{2,5},{3,0},{4,3},{5,6},{6,7},{7,2},{8,9},{9,12},{10,1... | collective-permute-start | bytes 3145736 | tf_op jit(solution)/shard_map/ppermute | solution.py:367
  50.6 30.2 %collective-permute-start.1 = (bf16[64,2048]{1,0:T(8,128)(2,1)}, bf16[64,2048]{1,0:T(8,128)(2,1)S(1)}, u32[]{:S(2)}, u32[]{:S(2)}) collective-permute-start(bf16[64,2048]{1,0:T(8,128)(2,1)} %get-tuple-element.40), channel_id=1, source_target_pairs={{0,2},{1,3},{2,0},{3,1},{4,6},{5,7},{6,4},{7,5},{8,10},{9,11},{10,... | collective-permute-start | bytes 786440 | tf_op jit(solution)/shard_map/ppermute | solution.py:483
  68.4 12.5 %collective-permute-start.2 = (bf16[64,2048]{1,0:T(8,128)(2,1)}, bf16[64,2048]{1,0:T(8,128)(2,1)S(1)}, u32[]{:S(2)}, u32[]{:S(2)}) collective-permute-start(bf16[64,2048]{1,0:T(8,128)(2,1)} %get-tuple-element.41), channel_id=1, source_target_pairs={{0,3},{1,0},{2,1},{3,2},{4,7},{5,4},{6,5},{7,6},{8,11},{9,8},{10,9... | collective-permute-start | bytes 786440 | tf_op jit(solution)/shard_map/ppermute | solution.py:483
  82.5 17.0 %collective-permute-start.6 = (bf16[64,2048]{1,0:T(8,128)(2,1)S(1)}, bf16[64,2048]{1,0:T(8,128)(2,1)S(1)}, u32[]{:S(2)}, u32[]{:S(2)}) collective-permute-start(bf16[64,2048]{1,0:T(8,128)(2,1)S(1)} %get-tuple-element.45.t0), channel_id=1, source_target_pairs={{0,1},{1,2},{2,3},{3,0},{4,5},{5,6},{6,7},{7,4},{8,9},{9,10},{10,1... | collective-permute-start | bytes 786440 | tf_op jit(solution)/shard_map/ppermute | solution.py:412
  83.4 9.1 %collective-permute-start.3 = (f32[64,16]{1,0:T(8,128)S(1)}, f32[64,16]{1,0:T(8,128)S(1)}, u32[]{:S(2)}, u32[]{:S(2)}) collective-permute-start(f32[64,16]{1,0:T(8,128)S(1)} %copy.16.t0), channel_id=1, source_target_pairs={{0,1},{1,2},{2,3},{3,0},{4,5},{5,6},{6,7},{7,4},{8,9},{9,10},{10,1... | collective-permute-start | bytes 12296 | tf_op jit(solution)/shard_map/ppermute | solution.py:412
  92.4 4.3 %collective-permute-start.4 = (f32[64,16]{1,0:T(8,128)S(1)}, f32[64,16]{1,0:T(8,128)S(1)}, u32[]{:S(2)}, u32[]{:S(2)}) collective-permute-start(f32[64,16]{1,0:T(8,128)S(1)} %copy.16.t0), channel_id=1, source_target_pairs={{0,2},{1,3},{2,0},{3,1},{4,6},{5,7},{6,4},{7,5},{8,10},{9,11},{10,... | collective-permute-start | bytes 12296 | tf_op jit(solution)/shard_map/ppermute | solution.py:412
  96.7 2.8 %collective-permute-start.5 = (f32[64,16]{1,0:T(8,128)S(1)}, f32[64,16]{1,0:T(8,128)S(1)}, u32[]{:S(2)}, u32[]{:S(2)}) collective-permute-start(f32[64,16]{1,0:T(8,128)S(1)} %copy.16.t0), channel_id=1, source_target_pairs={{0,3},{1,0},{2,1},{3,2},{4,7},{5,4},{6,5},{7,6},{8,11},{9,8},{10,9... | collective-permute-start | bytes 12296 | tf_op jit(solution)/shard_map/ppermute | solution.py:412
  99.5 6.7 %collective-permute-start.7 = (bf16[64,2048]{1,0:T(8,128)(2,1)S(1)}, bf16[64,2048]{1,0:T(8,128)(2,1)S(1)}, u32[]{:S(2)}, u32[]{:S(2)}) collective-permute-start(bf16[64,2048]{1,0:T(8,128)(2,1)S(1)} %get-tuple-element.45.t0), channel_id=1, source_target_pairs={{0,2},{1,3},{2,0},{3,1},{4,6},{5,7},{6,4},{7,5},{8,10},{9,11},{10,... | collective-permute-start | bytes 786440 | tf_op jit(solution)/shard_map/ppermute | solution.py:412
  99.5 12.3 %collective-permute-start.8 = (bf16[64,2048]{1,0:T(8,128)(2,1)S(1)}, bf16[64,2048]{1,0:T(8,128)(2,1)S(1)}, u32[]{:S(2)}, u32[]{:S(2)}) collective-permute-start(bf16[64,2048]{1,0:T(8,128)(2,1)S(1)} %get-tuple-element.45.t0), channel_id=1, source_target_pairs={{0,3},{1,0},{2,1},{3,2},{4,7},{5,4},{6,5},{7,6},{8,11},{9,8},{10,9... | collective-permute-start | bytes 786440 | tf_op jit(solution)/shard_map/ppermute | solution.py:412
  114.0 39.7 %all-to-all-start.2 = ((bf16[32,16,2304]{2,1,0:T(8,128)(2,1)}), bf16[32,16,2304]{2,1,0:T(8,128)(2,1)S(1)}, u32[]{:S(2)}, u32[]{:S(2)}) async-start(bf16[32,16,2304]{2,1,0:T(8,128)(2,1)} %bitcast.19), calls=%async_computation.2 | async-start | bytes 4718592 | tf_op jit(solution)/shard_map/all_to_all | solution.py:492
  124.4 27.8 %collective-permute-start.11 = (bf16[2,2048,256]{2,1,0:T(8,128)(2,1)}, bf16[2,2048,256]{2,1,0:T(8,128)(2,1)}, u32[]{:S(2)}, u32[]{:S(2)}) collective-permute-start(bf16[2,2048,256]{2,1,0:T(8,128)(2,1)} %get-tuple-element.48.gu2), channel_id=1, source_target_pairs={{0,4},{1,5},{6,2},{7,3},{8,12},{9,13},{14,10},{15,11},{16,20},{17,... | collective-permute-start | bytes 6291464 | tf_op jit(solution)/shard_map/ppermute | solution.py:367
  125.7 10.9 %collective-permute-start.16 = (bf16[256,2048]{1,0:T(8,128)(2,1)S(1)}, bf16[256,2048]{1,0:T(8,128)(2,1)S(1)}, u32[]{:S(2)}, u32[]{:S(2)}) collective-permute-start(bf16[256,2048]{1,0:T(8,128)(2,1)S(1)} %get-tuple-element.50.dn2), channel_id=1, source_target_pairs={{0,4},{1,5},{6,2},{7,3},{8,12},{9,13},{14,10},{15,11},{16,20},{17,... | collective-permute-start | bytes 3145736 | tf_op jit(solution)/shard_map/ppermute | solution.py:367
  127.0 26.6 %collective-permute-start.10 = (bf16[2,2048,256]{2,1,0:T(8,128)(2,1)}, bf16[2,2048,256]{2,1,0:T(8,128)(2,1)}, u32[]{:S(2)}, u32[]{:S(2)}) collective-permute-start(bf16[2,2048,256]{2,1,0:T(8,128)(2,1)} %collective-permute-done.9.gu0), channel_id=1, source_target_pairs={{0,4},{4,0},{8,12},{12,8},{16,20},{20,16},{24,28},{28,24},{32,36},... | collective-permute-start | bytes 6291464 | tf_op jit(solution)/shard_map/ppermute | solution.py:367
  129.7 24.0 %collective-permute-start.13 = (bf16[2,2048,256]{2,1,0:T(8,128)(2,1)}, bf16[2,2048,256]{2,1,0:T(8,128)(2,1)}, u32[]{:S(2)}, u32[]{:S(2)}) collective-permute-start(bf16[2,2048,256]{2,1,0:T(8,128)(2,1)} %collective-permute-done.12.gu4), channel_id=1, source_target_pairs={{2,6},{3,7},{4,0},{5,1},{10,14},{11,15},{12,8},{13,9},{18,22},{19,... | collective-permute-start | bytes 6291464 | tf_op jit(solution)/shard_map/ppermute | solution.py:462
  132.9 17.7 %collective-permute-start.17 = (bf16[256,2048]{1,0:T(8,128)(2,1)S(1)}, bf16[256,2048]{1,0:T(8,128)(2,1)}, u32[]{:S(2)}, u32[]{:S(2)}) collective-permute-start(bf16[256,2048]{1,0:T(8,128)(2,1)S(1)} %get-tuple-element.50.dn2), channel_id=1, source_target_pairs={{2,4},{3,5},{4,2},{5,3},{10,12},{11,13},{12,10},{13,11},{18,20},{1... | collective-permute-start | bytes 3145736 | tf_op jit(solution)/shard_map/ppermute | solution.py:458
  136.6 15.6 %collective-permute-start.15 = (bf16[256,2048]{1,0:T(8,128)(2,1)}, bf16[256,2048]{1,0:T(8,128)(2,1)}, u32[]{:S(2)}, u32[]{:S(2)}) collective-permute-start(bf16[256,2048]{1,0:T(8,128)(2,1)} %collective-permute-done.14.dn0), channel_id=1, source_target_pairs={{0,4},{4,0},{8,12},{12,8},{16,20},{20,16},{24,28},{28,24},{32,36},... | collective-permute-start | bytes 3145736 | tf_op jit(solution)/shard_map/ppermute | solution.py:367
  150.6 10.3 %collective-permute-start.18 = (bf16[256,2048]{1,0:T(8,128)(2,1)}, bf16[256,2048]{1,0:T(8,128)(2,1)S(1)}, u32[]{:S(2)}, u32[]{:S(2)}) collective-permute-start(bf16[256,2048]{1,0:T(8,128)(2,1)} %collective-permute-done.17.dn4), channel_id=1, source_target_pairs={{2,6},{3,7},{4,0},{5,1},{10,14},{11,15},{12,8},{13,9},{18,22},{19,... | collective-permute-start | bytes 3145736 | tf_op jit(solution)/shard_map/ppermute | solution.py:463
  205.6 9.3 %collective-permute-start.19 = (bf16[64,2048]{1,0:T(8,128)(2,1)}, bf16[64,2048]{1,0:T(8,128)(2,1)S(1)}, u32[]{:S(2)}, u32[]{:S(2)}) collective-permute-start(bf16[64,2048]{1,0:T(8,128)(2,1)} %get-tuple-element.54), channel_id=1, source_target_pairs={{0,1},{1,2},{2,3},{3,0},{4,5},{5,6},{6,7},{7,4},{8,9},{9,10},{10,1... | collective-permute-start | bytes 786440 | tf_op jit(solution)/shard_map/ppermute | solution.py:526
  206.4 15.0 %collective-permute-start.20 = (bf16[64,2048]{1,0:T(8,128)(2,1)}, bf16[64,2048]{1,0:T(8,128)(2,1)S(1)}, u32[]{:S(2)}, u32[]{:S(2)}) collective-permute-start(bf16[64,2048]{1,0:T(8,128)(2,1)} %get-tuple-element.55), channel_id=1, source_target_pairs={{0,2},{1,3},{2,0},{3,1},{4,6},{5,7},{6,4},{7,5},{8,10},{9,11},{10,... | collective-permute-start | bytes 786440 | tf_op jit(solution)/shard_map/ppermute | solution.py:526
  209.1 12.3 %collective-permute-start.21 = (bf16[64,2048]{1,0:T(8,128)(2,1)}, bf16[64,2048]{1,0:T(8,128)(2,1)S(1)}, u32[]{:S(2)}, u32[]{:S(2)}) collective-permute-start(bf16[64,2048]{1,0:T(8,128)(2,1)} %get-tuple-element.56), channel_id=1, source_target_pairs={{0,3},{1,0},{2,1},{3,2},{4,7},{5,4},{6,5},{7,6},{8,11},{9,8},{10,9... | collective-permute-start | bytes 786440 | tf_op jit(solution)/shard_map/ppermute | solution.py:526
  (10 other events, 313.3 us)

commit v8 on v7

--- a/solution.py
+++ b/solution.py
@@ -90,7 +90,7 @@
 
 def front_kernel(
     head_ref, x_ref, gain_ref, w_ref, gu_ref, dn_ref,
-    normed_ref, k_ref, v_ref, send_ref, zero_ref, gu_out, dn_out, mine_ref,
+    normed_ref, k_ref, v_ref, send_ref, zero_ref, gu_out, dn_out,
     wk, wv, sems, read_sems,
 ):
     copy_k = pltpu.make_async_copy(w_ref.at[1], wk, sems.at[0])
@@ -100,15 +100,14 @@
     head = head_ref[0]
     reads = pick_copies(1 - (head & 1), gu_ref, dn_ref, gu_out, dn_out, read_sems)
     zero_ref[0] = 0
-    mine_ref[...] = x_ref[pl.ds(pl.multiple_of(head * ROWS, ROWS), ROWS), :]
     normed = rms_norm(x_ref[...].astype(F32), gain_ref[...]).astype(BF)
     normed_ref[...] = normed
     copy_k.wait()
-    copy_v.wait()
     for read in reads:
         read.start()
     key = dot(normed, wk[...]).astype(BF)
     k_ref[...] = key
+    copy_v.wait()
     value = dot(normed, wv[...]).astype(BF)
     v_ref[...] = value
     for h in range(HEADS):
@@ -421,18 +420,17 @@
 
     w_planes = w_qkv.transpose(1, 0, 2)
     here = head.astype(jnp.int32)[None]
-    normed, key, value, send_state, zero, *near, mine = call(
+    normed, key, value, send_state, zero, *near = call(
         front_kernel,
         [SMEM, VMEM, VMEM, HBM, HBM, HBM],
         [
             chip((TOK, D), BF),
             chip((TOK, WIDE), BF),
-            chip((TOK, WIDE), BF),
+            out((TOK, WIDE), BF),
             out((WIDE, DH), BF),
             out((1,), jnp.int32),
             chip((2, D, 256), BF),
             chip((256, D), BF),
-            out((ROWS, D), BF),
         ],
         [
             pltpu.VMEM((D, WIDE), BF),
@@ -468,7 +466,7 @@
         [VMEM, HBM, VMEM, VMEM],
         [out((TOK, WIDE), BF), chip((TOK, WIDE), F32)],
         [pltpu.VMEM((D, WIDE), BF), pltpu.SemaphoreType.DMA((1,))],
-    )(on_chip(normed), w_planes, on_chip(key), on_chip(value))
+    )(on_chip(normed), w_planes, on_chip(key), value)
     blocks = call(
         attend_kernel,
         [SMEM] + [VMEM] * 5,
@@ -481,6 +479,7 @@
     )(here, *[on_chip(t) for t in tables])
 
     got = [lax.ppermute(blocks[k], "head", head_perm(k)) for k in range(1, 4)]
+    mine = lax.dynamic_slice_in_dim(hidden_in, head * ROWS + zero[0], ROWS, 0)
     resid, normed2 = call(
         norm_kernel, [VMEM] * 6, [out((ROWS, D), F32), chip((ROWS, D), BF)]
     )(on_chip(mine), on_chip(blocks[0]), *[on_chip(g) for g in got], moe_gain[None, :])

time: 225 us -> 223 us (level)
  waiting for transfers between devices: 84.9 us -> 82.4 us
  transfers between devices with their start and end apart: 24 -> 24, of which waited for: 12 -> 12; matrix products, arithmetic and copies ran while one was open for 0% -> 1% of each run, Pallas kernels for 10% -> 11%
where the time goes in v8:
time: 223 us; the launch traced here: 220 us
  waiting for transfers between devices  82.4 us (37%)
  blocking collectives  51.3 us (23%)
  starting transfers between devices  45.1 us (20%)
  Pallas kernels  37.4 us (17%)
  local copies, waits for them, and re-layouts  2.85 us (1%)
    ppermute x6, waiting for transfers between devices, on_device(): got = [lax.ppermute(blocks[k], 'head', head_perm(k)) for k in range(1, 4)]  40.2 us
    all_to_all x1, blocking collectives, on_device(): lax.all_to_all(results.reshape(32, 16, PACKED), 'seq', 0, 0, tiled=True)  37 us
    ppermute x6, waiting for transfers between devices, gather_head(): lax.ppermute(array, 'head', head_perm(k))  24 us
    all_to_all x1, blocking collectives, on_device(): lax.all_to_all(send_state.reshape(32, 16, DH), 'seq', 0, 0, tiled=True)  14.3 us
    ppermute x1, waiting for transfers between devices, on_device(): far_down = lax.ppermute(rest[1], both, device_perm(far_target))  13.9 us
    ppermute x6, starting transfers between devices, permute_all(): return [lax.ppermute(a, axes, perm) for a in arrays]  10.9 us
    all_to_all x1, starting transfers between devices, on_device(): lax.all_to_all(sent.reshape(32, 16, PACKED), 'seq', 0, 0, tiled=True)  10.4 us
    pallas_call x1, Pallas kernels, on_device(): call(gate_kernel, [SMEM, VMEM] + [ANY] * 10, [chip((SLOTS, 1024), BF), ch...  7.24 us
  transfers between devices with their start and end apart: 24, of which 12 were waited for; matrix products, arithmetic and copies ran while one was open for 1% of the time, Pallas kernels for 11%

profile of v8, /device:TPU:33, one launch (start us, length us, event | category | flops | bytes accessed | tf_op | source)
XLA Modules:
  0.0 220.5 jit_solution(3798640178679481975)
XLA Ops:
  0.0 6.7 %shard_map.100 = (bf16[256,2048]{1,0:T(8,128)(2,1)S(1)}, bf16[256,512]{1,0:T(8,128)(2,1)S(1)}, bf16[256,512]{1,0:T(8,128)(2,1)}, bf16[512,128]{1,0:T(8,128)(2,1)...) custom-call(s32[1]{0:T(128)} %bitcast.head_ref, bf16[256,2048]{1,0:T(8,128)(2,1)} %x_ref.1, ...), custom_call_target="tpu_custom_call" | custom-call | tf_op jit(solution)/shard_map/pallas_call | solution.py:423
  6.7 3.1 %collective-permute-start.9 = (bf16[2,2048,256]{2,1,0:T(8,128)(2,1)}, bf16[2,2048,256]{2,1,0:T(8,128)(2,1)}, u32[]{:S(2)}, u32[]{:S(2)}) collective-permute-start(bf16[2,2048,256]{2,1,0:T(8,128)(2,1)} %get-tuple-element.45), channel_id=1, source_target_pairs={{0,1},{1,4},{2,5},{3,0},{4,3},{5,6},{6,7},{7,2},{8,9},{9,12},{10,1... | collective-permute-start | bytes 6291464 | tf_op jit(solution)/shard_map/ppermute | solution.py:366
  15.3 14.3 %all_to_all.20.states_ref = bf16[32,16,128]{2,1,0:T(8,128)(2,1)S(1)} all-to-all(bf16[32,16,128]{2,1,0:T(8,128)(2,1)S(1)} %bitcast.21), channel_id=1, replica_groups=mesh['seq'=32,'head'=4] {'seq'}, dimensions={0} | all-to-all | bytes 262144 | tf_op jit(solution)/shard_map/all_to_all | solution.py:451
  30.3 5.0 %all-to-all-start.1 = ((bf16[32,16,128]{2,1,0:T(8,128)(2,1)}), bf16[32,16,128]{2,1,0:T(8,128)(2,1)S(1)}, u32[]{:S(2)}, u32[]{:S(2)}) async-start(bf16[32,16,128]{2,1,0:T(8,128)(2,1)} %shard_map.101), calls=%async_computation.1 | async-start | bytes 262144 | tf_op jit(solution)/shard_map/all_to_all | solution.py:453
  35.3 4.0 %shard_map.102 = (bf16[256,512]{1,0:T(8,128)(2,1)}, f32[256,512]{1,0:T(8,128)S(1)}) custom-call(bf16[256,2048]{1,0:T(8,128)(2,1)S(1)} %get-tuple-element.32.normed_ref, bf16[3,2048,512]{2,1,0:T(8,128)(2,1)} %bitcast.18, bf16[256,512]{1,0:T(8,128)(2,1)S(1)} %get-tuple-element.33.k_ref, bf16[256,512]{1,0:T(8,128)(2,1)} %get-tuple-element.34.v_ref), custom_call_target="tpu_custom_call" | custom-call | tf_op jit(solution)/shard_map/pallas_call | solution.py:464
  39.3 2.7 %all-to-all-done.1 = bf16[32,16,128]{2,1,0:T(8,128)(2,1)S(1)} async-done(((bf16[32,16,128]{2,1,0:T(8,128)(2,1)}), bf16[32,16,128]{2,1,0:T(8,128)(2,1)S(1)}, u32[]{:S(2)}, u32[]{:S(2)}) %all-to-all-start.1) | async-done | bytes 131104 | tf_op jit(solution)/shard_map/all_to_all | solution.py:453
  42.0 3.6 %shard_map.103 = (f32[64,2048]{1,0:T(8,128)S(1)}, bf16[64,2048]{1,0:T(8,128)(2,1)}, bf16[64,2048]{1,0:T(8,128)(2,1)}, bf16[64,2048]{1,0:T(8,128)(2,1)}) custom-call(s32[1]{0:T(128)} %bitcast.head_ref, bf16[512,128]{1,0:T(8,128)(2,1)S(1)} %bitcast.16, bf16[256,512]{1,0:T(8,128)(2,1)} %get-tuple-element.35.q_ref, f32[256,512]{1,0:T(8,128)S(1)} %get-tuple-element.36.local_ref, ...), custom_call_target="tpu_custom_call" | custom-call | tf_op jit(solution)/shard_map/pallas_call | solution.py:470
  49.5 17.2 %collective-permute-done.g1 = bf16[64,2048]{1,0:T(8,128)(2,1)S(1)} collective-permute-done((bf16[64,2048]{1,0:T(8,128)(2,1)}, bf16[64,2048]{1,0:T(8,128)(2,1)S(1)}, u32[]{:S(2)}, u32[]{:S(2)}) %collective-permute-start) | collective-permute-done | bytes 262176 | tf_op jit(solution)/shard_map/ppermute | solution.py:481
  68.3 10.8 %collective-permute-done.1.g2 = bf16[64,2048]{1,0:T(8,128)(2,1)S(1)} collective-permute-done((bf16[64,2048]{1,0:T(8,128)(2,1)}, bf16[64,2048]{1,0:T(8,128)(2,1)S(1)}, u32[]{:S(2)}, u32[]{:S(2)}) %collective-permute-start.1) | collective-permute-done | bytes 262176 | tf_op jit(solution)/shard_map/ppermute | solution.py:481
  81.9 8.9 %collective-permute-done.3.t1 = f32[64,16]{1,0:T(8,128)S(1)} collective-permute-done((f32[64,16]{1,0:T(8,128)S(1)}, f32[64,16]{1,0:T(8,128)S(1)}, u32[]{:S(2)}, u32[]{:S(2)}) %collective-permute-start.3) | collective-permute-done | bytes 4128 | tf_op jit(solution)/shard_map/ppermute | solution.py:411
  90.7 4.3 %collective-permute-done.4.t2 = f32[64,16]{1,0:T(8,128)S(1)} collective-permute-done((f32[64,16]{1,0:T(8,128)S(1)}, f32[64,16]{1,0:T(8,128)S(1)}, u32[]{:S(2)}, u32[]{:S(2)}) %collective-permute-start.4) | collective-permute-done | bytes 4128 | tf_op jit(solution)/shard_map/ppermute | solution.py:411
  101.7 2.8 %collective-permute-done.7.t2 = bf16[64,2048]{1,0:T(8,128)(2,1)S(1)} collective-permute-done((bf16[64,2048]{1,0:T(8,128)(2,1)S(1)}, bf16[64,2048]{1,0:T(8,128)(2,1)S(1)}, u32[]{:S(2)}, u32[]{:S(2)}) %collective-permute-start.7) | collective-permute-done | bytes 262176 | tf_op jit(solution)/shard_map/ppermute | solution.py:411
  104.5 5.5 %collective-permute-done.8.t3 = bf16[64,2048]{1,0:T(8,128)(2,1)S(1)} collective-permute-done((bf16[64,2048]{1,0:T(8,128)(2,1)S(1)}, bf16[64,2048]{1,0:T(8,128)(2,1)S(1)}, u32[]{:S(2)}, u32[]{:S(2)}) %collective-permute-start.8) | collective-permute-done | bytes 262176 | tf_op jit(solution)/shard_map/ppermute | solution.py:411
  112.3 10.4 %all-to-all-start.2 = ((bf16[32,16,2304]{2,1,0:T(8,128)(2,1)}), bf16[32,16,2304]{2,1,0:T(8,128)(2,1)S(1)}, u32[]{:S(2)}, u32[]{:S(2)}) async-start(bf16[32,16,2304]{2,1,0:T(8,128)(2,1)} %bitcast.19), calls=%async_computation.2 | async-start | bytes 4718592 | tf_op jit(solution)/shard_map/all_to_all | solution.py:491
  125.3 2.7 %collective-permute-start.10 = (bf16[2,2048,256]{2,1,0:T(8,128)(2,1)}, bf16[2,2048,256]{2,1,0:T(8,128)(2,1)}, u32[]{:S(2)}, u32[]{:S(2)}) collective-permute-start(bf16[2,2048,256]{2,1,0:T(8,128)(2,1)} %collective-permute-done.9.gu0), channel_id=1, source_target_pairs={{0,4},{4,0},{8,12},{12,8},{16,20},{20,16},{24,28},{28,24},{32,36},... | collective-permute-start | bytes 6291464 | tf_op jit(solution)/shard_map/ppermute | solution.py:366
  127.9 3.2 %collective-permute-start.13 = (bf16[2,2048,256]{2,1,0:T(8,128)(2,1)}, bf16[2,2048,256]{2,1,0:T(8,128)(2,1)}, u32[]{:S(2)}, u32[]{:S(2)}) collective-permute-start(bf16[2,2048,256]{2,1,0:T(8,128)(2,1)} %collective-permute-done.12.gu4), channel_id=1, source_target_pairs={{2,6},{3,7},{4,0},{5,1},{10,14},{11,15},{12,8},{13,9},{18,22},{19,... | collective-permute-start | bytes 6291464 | tf_op jit(solution)/shard_map/ppermute | solution.py:460
  131.2 3.6 %collective-permute-start.17 = (bf16[256,2048]{1,0:T(8,128)(2,1)S(1)}, bf16[256,2048]{1,0:T(8,128)(2,1)}, u32[]{:S(2)}, u32[]{:S(2)}) collective-permute-start(bf16[256,2048]{1,0:T(8,128)(2,1)S(1)} %get-tuple-element.48.dn2), channel_id=1, source_target_pairs={{2,4},{3,5},{4,2},{5,3},{10,12},{11,13},{12,10},{13,11},{18,20},{1... | collective-permute-start | bytes 3145736 | tf_op jit(solution)/shard_map/ppermute | solution.py:456
  135.0 13.9 %collective-permute-done.17.dn4 = bf16[256,2048]{1,0:T(8,128)(2,1)} collective-permute-done((bf16[256,2048]{1,0:T(8,128)(2,1)S(1)}, bf16[256,2048]{1,0:T(8,128)(2,1)}, u32[]{:S(2)}, u32[]{:S(2)}) %collective-permute-start.17) | collective-permute-done | bytes 1048608 | tf_op jit(solution)/shard_map/ppermute | solution.py:456
  151.9 7.2 %shard_map.107 = (bf16[576,1024]{1,0:T(8,128)(2,1)S(1)}, bf16[768,2048]{1,0:T(8,128)(2,1)S(1)}) custom-call(s32[1]{0:T(128)} %bitcast.8.keep_ref, bf16[512,2304]{1,0:T(8,128)(2,1)S(1)} %bitcast.15, bf16[2,2048,256]{2,1,0:T(8,128)(2,1)} %collective-permute-done.9.gu0, bf16[2,2048,256]{2,1,0:T(8,128)(2,1)} %collective-permute-done.10.gu1, ...), custom_call_target="tpu_custom_call" | custom-call | tf_op jit(solution)/shard_map/pallas_call | solution.py:495
  160.2 4.9 %shard_map.108 = bf16[512,2304]{1,0:T(8,128)(2,1)} custom-call(s32[1]{0:T(128)} %bitcast.8.keep_ref, bf16[576,1024]{1,0:T(8,128)(2,1)S(1)} %get-tuple-element.49.act, bf16[768,2048]{1,0:T(8,128)(2,1)S(1)} %get-tuple-element.50.down, bf16[256,2048]{1,0:T(8,128)(2,1)} %collective-permute-done.17.dn4, bf16[256,2048]{1,0:T(8,128)(2,1)} %copy-done.5), custom_call_target="tpu_custom_call" | custom-call | tf_op jit(solution)/shard_map/pallas_call | solution.py:505
  165.0 37.0 %all_to_all.21 = bf16[32,16,2304]{2,1,0:T(8,128)(2,1)S(1)} all-to-all(bf16[32,16,2304]{2,1,0:T(8,128)(2,1)} %bitcast.20), channel_id=1, replica_groups=mesh['seq'=32,'head'=4] {'seq'}, dimensions={0} | all-to-all | bytes 4718592 | tf_op jit(solution)/shard_map/all_to_all | solution.py:518
  204.7 2.7 %collective-permute-start.20 = (bf16[64,2048]{1,0:T(8,128)(2,1)}, bf16[64,2048]{1,0:T(8,128)(2,1)S(1)}, u32[]{:S(2)}, u32[]{:S(2)}) collective-permute-start(bf16[64,2048]{1,0:T(8,128)(2,1)} %get-tuple-element.53), channel_id=1, source_target_pairs={{0,2},{1,3},{2,0},{3,1},{4,6},{5,7},{6,4},{7,5},{8,10},{9,11},{10,... | collective-permute-start | bytes 786440 | tf_op jit(solution)/shard_map/ppermute | solution.py:525
  207.4 5.8 %collective-permute-done.19.g1 = bf16[64,2048]{1,0:T(8,128)(2,1)S(1)} collective-permute-done((bf16[64,2048]{1,0:T(8,128)(2,1)}, bf16[64,2048]{1,0:T(8,128)(2,1)S(1)}, u32[]{:S(2)}, u32[]{:S(2)}) %collective-permute-start.19) | collective-permute-done | bytes 262176 | tf_op jit(solution)/shard_map/ppermute | solution.py:525
  213.2 6.4 %collective-permute-done.20.g2 = bf16[64,2048]{1,0:T(8,128)(2,1)S(1)} collective-permute-done((bf16[64,2048]{1,0:T(8,128)(2,1)}, bf16[64,2048]{1,0:T(8,128)(2,1)S(1)}, u32[]{:S(2)}, u32[]{:S(2)}) %collective-permute-start.20) | collective-permute-done | bytes 262176 | tf_op jit(solution)/shard_map/ppermute | solution.py:525
  (60 shorter events, 32.3 us)
Async XLA Ops:
  6.7 118.6 %collective-permute-start.9 = (bf16[2,2048,256]{2,1,0:T(8,128)(2,1)}, bf16[2,2048,256]{2,1,0:T(8,128)(2,1)}, u32[]{:S(2)}, u32[]{:S(2)}) collective-permute-start(bf16[2,2048,256]{2,1,0:T(8,128)(2,1)} %get-tuple-element.45), channel_id=1, source_target_pairs={{0,1},{1,4},{2,5},{3,0},{4,3},{5,6},{6,7},{7,2},{8,9},{9,12},{10,1... | collective-permute-start | bytes 6291464 | tf_op jit(solution)/shard_map/ppermute | solution.py:366
  13.1 114.8 %collective-permute-start.12 = (bf16[2,2048,256]{2,1,0:T(8,128)(2,1)}, bf16[2,2048,256]{2,1,0:T(8,128)(2,1)}, u32[]{:S(2)}, u32[]{:S(2)}) collective-permute-start(bf16[2,2048,256]{2,1,0:T(8,128)(2,1)} %get-tuple-element.46.gu2), channel_id=1, source_target_pairs={{2,4},{3,5},{4,2},{5,3},{10,12},{11,13},{12,10},{13,11},{18,20},{1... | collective-permute-start | bytes 6291464 | tf_op jit(solution)/shard_map/ppermute | solution.py:457
  30.3 11.7 %all-to-all-start.1 = ((bf16[32,16,128]{2,1,0:T(8,128)(2,1)}), bf16[32,16,128]{2,1,0:T(8,128)(2,1)S(1)}, u32[]{:S(2)}, u32[]{:S(2)}) async-start(bf16[32,16,128]{2,1,0:T(8,128)(2,1)} %shard_map.101), calls=%async_computation.1 | async-start | bytes 262144 | tf_op jit(solution)/shard_map/all_to_all | solution.py:453
  45.6 21.0 %collective-permute-start = (bf16[64,2048]{1,0:T(8,128)(2,1)}, bf16[64,2048]{1,0:T(8,128)(2,1)S(1)}, u32[]{:S(2)}, u32[]{:S(2)}) collective-permute-start(bf16[64,2048]{1,0:T(8,128)(2,1)} %get-tuple-element.38), channel_id=1, source_target_pairs={{0,1},{1,2},{2,3},{3,0},{4,5},{5,6},{6,7},{7,4},{8,9},{9,10},{10,1... | collective-permute-start | bytes 786440 | tf_op jit(solution)/shard_map/ppermute | solution.py:481
  46.4 84.8 %collective-permute-start.14 = (bf16[256,2048]{1,0:T(8,128)(2,1)}, bf16[256,2048]{1,0:T(8,128)(2,1)}, u32[]{:S(2)}, u32[]{:S(2)}) collective-permute-start(bf16[256,2048]{1,0:T(8,128)(2,1)} %get-tuple-element.47), channel_id=1, source_target_pairs={{0,1},{1,4},{2,5},{3,0},{4,3},{5,6},{6,7},{7,2},{8,9},{9,12},{10,1... | collective-permute-start | bytes 3145736 | tf_op jit(solution)/shard_map/ppermute | solution.py:366
  48.9 30.3 %collective-permute-start.1 = (bf16[64,2048]{1,0:T(8,128)(2,1)}, bf16[64,2048]{1,0:T(8,128)(2,1)S(1)}, u32[]{:S(2)}, u32[]{:S(2)}) collective-permute-start(bf16[64,2048]{1,0:T(8,128)(2,1)} %get-tuple-element.39), channel_id=1, source_target_pairs={{0,2},{1,3},{2,0},{3,1},{4,6},{5,7},{6,4},{7,5},{8,10},{9,11},{10,... | collective-permute-start | bytes 786440 | tf_op jit(solution)/shard_map/ppermute | solution.py:481
  66.6 12.5 %collective-permute-start.2 = (bf16[64,2048]{1,0:T(8,128)(2,1)}, bf16[64,2048]{1,0:T(8,128)(2,1)S(1)}, u32[]{:S(2)}, u32[]{:S(2)}) collective-permute-start(bf16[64,2048]{1,0:T(8,128)(2,1)} %get-tuple-element.40), channel_id=1, source_target_pairs={{0,3},{1,0},{2,1},{3,2},{4,7},{5,4},{6,5},{7,6},{8,11},{9,8},{10,9... | collective-permute-start | bytes 786440 | tf_op jit(solution)/shard_map/ppermute | solution.py:481
  80.8 17.0 %collective-permute-start.6 = (bf16[64,2048]{1,0:T(8,128)(2,1)S(1)}, bf16[64,2048]{1,0:T(8,128)(2,1)S(1)}, u32[]{:S(2)}, u32[]{:S(2)}) collective-permute-start(bf16[64,2048]{1,0:T(8,128)(2,1)S(1)} %get-tuple-element.44.t0), channel_id=1, source_target_pairs={{0,1},{1,2},{2,3},{3,0},{4,5},{5,6},{6,7},{7,4},{8,9},{9,10},{10,1... | collective-permute-start | bytes 786440 | tf_op jit(solution)/shard_map/ppermute | solution.py:411
  81.6 9.1 %collective-permute-start.3 = (f32[64,16]{1,0:T(8,128)S(1)}, f32[64,16]{1,0:T(8,128)S(1)}, u32[]{:S(2)}, u32[]{:S(2)}) collective-permute-start(f32[64,16]{1,0:T(8,128)S(1)} %copy.16.t0), channel_id=1, source_target_pairs={{0,1},{1,2},{2,3},{3,0},{4,5},{5,6},{6,7},{7,4},{8,9},{9,10},{10,1... | collective-permute-start | bytes 12296 | tf_op jit(solution)/shard_map/ppermute | solution.py:411
  90.7 4.3 %collective-permute-start.4 = (f32[64,16]{1,0:T(8,128)S(1)}, f32[64,16]{1,0:T(8,128)S(1)}, u32[]{:S(2)}, u32[]{:S(2)}) collective-permute-start(f32[64,16]{1,0:T(8,128)S(1)} %copy.16.t0), channel_id=1, source_target_pairs={{0,2},{1,3},{2,0},{3,1},{4,6},{5,7},{6,4},{7,5},{8,10},{9,11},{10,... | collective-permute-start | bytes 12296 | tf_op jit(solution)/shard_map/ppermute | solution.py:411
  95.0 2.8 %collective-permute-start.5 = (f32[64,16]{1,0:T(8,128)S(1)}, f32[64,16]{1,0:T(8,128)S(1)}, u32[]{:S(2)}, u32[]{:S(2)}) collective-permute-start(f32[64,16]{1,0:T(8,128)S(1)} %copy.16.t0), channel_id=1, source_target_pairs={{0,3},{1,0},{2,1},{3,2},{4,7},{5,4},{6,5},{7,6},{8,11},{9,8},{10,9... | collective-permute-start | bytes 12296 | tf_op jit(solution)/shard_map/ppermute | solution.py:411
  97.8 6.7 %collective-permute-start.7 = (bf16[64,2048]{1,0:T(8,128)(2,1)S(1)}, bf16[64,2048]{1,0:T(8,128)(2,1)S(1)}, u32[]{:S(2)}, u32[]{:S(2)}) collective-permute-start(bf16[64,2048]{1,0:T(8,128)(2,1)S(1)} %get-tuple-element.44.t0), channel_id=1, source_target_pairs={{0,2},{1,3},{2,0},{3,1},{4,6},{5,7},{6,4},{7,5},{8,10},{9,11},{10,... | collective-permute-start | bytes 786440 | tf_op jit(solution)/shard_map/ppermute | solution.py:411
  97.8 12.3 %collective-permute-start.8 = (bf16[64,2048]{1,0:T(8,128)(2,1)S(1)}, bf16[64,2048]{1,0:T(8,128)(2,1)S(1)}, u32[]{:S(2)}, u32[]{:S(2)}) collective-permute-start(bf16[64,2048]{1,0:T(8,128)(2,1)S(1)} %get-tuple-element.44.t0), channel_id=1, source_target_pairs={{0,3},{1,0},{2,1},{3,2},{4,7},{5,4},{6,5},{7,6},{8,11},{9,8},{10,9... | collective-permute-start | bytes 786440 | tf_op jit(solution)/shard_map/ppermute | solution.py:411
  112.3 39.7 %all-to-all-start.2 = ((bf16[32,16,2304]{2,1,0:T(8,128)(2,1)}), bf16[32,16,2304]{2,1,0:T(8,128)(2,1)S(1)}, u32[]{:S(2)}, u32[]{:S(2)}) async-start(bf16[32,16,2304]{2,1,0:T(8,128)(2,1)} %bitcast.19), calls=%async_computation.2 | async-start | bytes 4718592 | tf_op jit(solution)/shard_map/all_to_all | solution.py:491
  122.7 27.8 %collective-permute-start.11 = (bf16[2,2048,256]{2,1,0:T(8,128)(2,1)}, bf16[2,2048,256]{2,1,0:T(8,128)(2,1)}, u32[]{:S(2)}, u32[]{:S(2)}) collective-permute-start(bf16[2,2048,256]{2,1,0:T(8,128)(2,1)} %get-tuple-element.46.gu2), channel_id=1, source_target_pairs={{0,4},{1,5},{6,2},{7,3},{8,12},{9,13},{14,10},{15,11},{16,20},{17,... | collective-permute-start | bytes 6291464 | tf_op jit(solution)/shard_map/ppermute | solution.py:366
  124.0 10.9 %collective-permute-start.16 = (bf16[256,2048]{1,0:T(8,128)(2,1)S(1)}, bf16[256,2048]{1,0:T(8,128)(2,1)S(1)}, u32[]{:S(2)}, u32[]{:S(2)}) collective-permute-start(bf16[256,2048]{1,0:T(8,128)(2,1)S(1)} %get-tuple-element.48.dn2), channel_id=1, source_target_pairs={{0,4},{1,5},{6,2},{7,3},{8,12},{9,13},{14,10},{15,11},{16,20},{17,... | collective-permute-start | bytes 3145736 | tf_op jit(solution)/shard_map/ppermute | solution.py:366
  125.3 26.6 %collective-permute-start.10 = (bf16[2,2048,256]{2,1,0:T(8,128)(2,1)}, bf16[2,2048,256]{2,1,0:T(8,128)(2,1)}, u32[]{:S(2)}, u32[]{:S(2)}) collective-permute-start(bf16[2,2048,256]{2,1,0:T(8,128)(2,1)} %collective-permute-done.9.gu0), channel_id=1, source_target_pairs={{0,4},{4,0},{8,12},{12,8},{16,20},{20,16},{24,28},{28,24},{32,36},... | collective-permute-start | bytes 6291464 | tf_op jit(solution)/shard_map/ppermute | solution.py:366
  127.9 24.0 %collective-permute-start.13 = (bf16[2,2048,256]{2,1,0:T(8,128)(2,1)}, bf16[2,2048,256]{2,1,0:T(8,128)(2,1)}, u32[]{:S(2)}, u32[]{:S(2)}) collective-permute-start(bf16[2,2048,256]{2,1,0:T(8,128)(2,1)} %collective-permute-done.12.gu4), channel_id=1, source_target_pairs={{2,6},{3,7},{4,0},{5,1},{10,14},{11,15},{12,8},{13,9},{18,22},{19,... | collective-permute-start | bytes 6291464 | tf_op jit(solution)/shard_map/ppermute | solution.py:460
  131.2 17.7 %collective-permute-start.17 = (bf16[256,2048]{1,0:T(8,128)(2,1)S(1)}, bf16[256,2048]{1,0:T(8,128)(2,1)}, u32[]{:S(2)}, u32[]{:S(2)}) collective-permute-start(bf16[256,2048]{1,0:T(8,128)(2,1)S(1)} %get-tuple-element.48.dn2), channel_id=1, source_target_pairs={{2,4},{3,5},{4,2},{5,3},{10,12},{11,13},{12,10},{13,11},{18,20},{1... | collective-permute-start | bytes 3145736 | tf_op jit(solution)/shard_map/ppermute | solution.py:456
  134.9 15.6 %collective-permute-start.15 = (bf16[256,2048]{1,0:T(8,128)(2,1)}, bf16[256,2048]{1,0:T(8,128)(2,1)}, u32[]{:S(2)}, u32[]{:S(2)}) collective-permute-start(bf16[256,2048]{1,0:T(8,128)(2,1)} %collective-permute-done.14.dn0), channel_id=1, source_target_pairs={{0,4},{4,0},{8,12},{12,8},{16,20},{20,16},{24,28},{28,24},{32,36},... | collective-permute-start | bytes 3145736 | tf_op jit(solution)/shard_map/ppermute | solution.py:366
  148.9 10.3 %collective-permute-start.18 = (bf16[256,2048]{1,0:T(8,128)(2,1)}, bf16[256,2048]{1,0:T(8,128)(2,1)S(1)}, u32[]{:S(2)}, u32[]{:S(2)}) collective-permute-start(bf16[256,2048]{1,0:T(8,128)(2,1)} %collective-permute-done.17.dn4), channel_id=1, source_target_pairs={{2,6},{3,7},{4,0},{5,1},{10,14},{11,15},{12,8},{13,9},{18,22},{19,... | collective-permute-start | bytes 3145736 | tf_op jit(solution)/shard_map/ppermute | solution.py:461
  203.9 9.3 %collective-permute-start.19 = (bf16[64,2048]{1,0:T(8,128)(2,1)}, bf16[64,2048]{1,0:T(8,128)(2,1)S(1)}, u32[]{:S(2)}, u32[]{:S(2)}) collective-permute-start(bf16[64,2048]{1,0:T(8,128)(2,1)} %get-tuple-element.52), channel_id=1, source_target_pairs={{0,1},{1,2},{2,3},{3,0},{4,5},{5,6},{6,7},{7,4},{8,9},{9,10},{10,1... | collective-permute-start | bytes 786440 | tf_op jit(solution)/shard_map/ppermute | solution.py:525
  204.7 15.0 %collective-permute-start.20 = (bf16[64,2048]{1,0:T(8,128)(2,1)}, bf16[64,2048]{1,0:T(8,128)(2,1)S(1)}, u32[]{:S(2)}, u32[]{:S(2)}) collective-permute-start(bf16[64,2048]{1,0:T(8,128)(2,1)} %get-tuple-element.53), channel_id=1, source_target_pairs={{0,2},{1,3},{2,0},{3,1},{4,6},{5,7},{6,4},{7,5},{8,10},{9,11},{10,... | collective-permute-start | bytes 786440 | tf_op jit(solution)/shard_map/ppermute | solution.py:525
  207.4 12.3 %collective-permute-start.21 = (bf16[64,2048]{1,0:T(8,128)(2,1)}, bf16[64,2048]{1,0:T(8,128)(2,1)S(1)}, u32[]{:S(2)}, u32[]{:S(2)}) collective-permute-start(bf16[64,2048]{1,0:T(8,128)(2,1)} %get-tuple-element.54), channel_id=1, source_target_pairs={{0,3},{1,0},{2,1},{3,2},{4,7},{5,4},{6,5},{7,6},{8,11},{9,8},{10,9... | collective-permute-start | bytes 786440 | tf_op jit(solution)/shard_map/ppermute | solution.py:525
  (9 other events, 272.5 us)

commit v9 on v8

--- a/solution.py
+++ b/solution.py
@@ -407,8 +407,15 @@
     )(index.astype(jnp.int32)[None], w_gate_up, w_down)
 
 
+def send_head(blocks):
+    got = [None] * 3
+    for k in (2, 1, 3):
+        got[k - 1] = lax.ppermute(blocks[k - 1], "head", head_perm(k))
+    return got
+
+
 def gather_head(array):
-    return [array] + [lax.ppermute(array, "head", head_perm(k)) for k in range(1, 4)]
+    return [array] + send_head([array] * 3)
 
 
 def on_device(
@@ -478,7 +485,7 @@
         routing_kernel, [SMEM] + [VMEM] * 4, [chip((SLOTS, TOK), BF), chip((TOK, SLOTS), BF)]
     )(here, *[on_chip(t) for t in tables])
 
-    got = [lax.ppermute(blocks[k], "head", head_perm(k)) for k in range(1, 4)]
+    got = send_head(blocks[1:])
     mine = lax.dynamic_slice_in_dim(hidden_in, head * ROWS + zero[0], ROWS, 0)
     resid, normed2 = call(
         norm_kernel, [VMEM] * 6, [out((ROWS, D), F32), chip((ROWS, D), BF)]
@@ -522,7 +529,7 @@
         [chip((ROWS, D), F32)] + BLOCKS_OUT[1:],
         [pltpu.VMEM((64, D), BF)],
     )(on_chip(weight), on_chip(back.reshape(MAIN, PACKED)))
-    got = [lax.ppermute(blocks[k], "head", head_perm(k)) for k in range(1, 4)]
+    got = send_head(blocks[1:])
     return call(last_kernel, [VMEM] * 5, [out((ROWS, D), BF)])(
         on_chip(resid), on_chip(blocks[0]), *[on_chip(g) for g in got]
     )[0]

time: 223 us -> 223 us (level)
  no operation moved by 1% of the time
where the time goes in v9:
time: 223 us; the launch traced here: 220 us
  waiting for transfers between devices  82.4 us (37%)
  blocking collectives  51.3 us (23%)
  starting transfers between devices  45.1 us (20%)
  Pallas kernels  37.4 us (17%)
  local copies, waits for them, and re-layouts  2.85 us (1%)
    ppermute x12, waiting for transfers between devices, send_head(): got[k - 1] = lax.ppermute(blocks[k - 1], 'head', head_perm(k))  64.2 us
    all_to_all x1, blocking collectives, on_device(): lax.all_to_all(results.reshape(32, 16, PACKED), 'seq', 0, 0, tiled=True)  37 us
    all_to_all x1, blocking collectives, on_device(): lax.all_to_all(send_state.reshape(32, 16, DH), 'seq', 0, 0, tiled=True)  14.3 us
    ppermute x1, waiting for transfers between devices, on_device(): far_down = lax.ppermute(rest[1], both, device_perm(far_target))  13.9 us
    ppermute x6, starting transfers between devices, permute_all(): return [lax.ppermute(a, axes, perm) for a in arrays]  10.9 us
    all_to_all x1, starting transfers between devices, on_device(): lax.all_to_all(sent.reshape(32, 16, PACKED), 'seq', 0, 0, tiled=True)  10.4 us
    ppermute x12, starting transfers between devices, send_head(): got[k - 1] = lax.ppermute(blocks[k - 1], 'head', head_perm(k))  8.21 us
    pallas_call x1, Pallas kernels, on_device(): call(gate_kernel, [SMEM, VMEM] + [ANY] * 10, [chip((SLOTS, 1024), BF), ch...  7.24 us
  transfers between devices with their start and end apart: 24, of which 12 were waited for; matrix products, arithmetic and copies ran while one was open for 1% of the time, Pallas kernels for 11%

profile of v9, /device:TPU:33, one launch (start us, length us, event | category | flops | bytes accessed | tf_op | source)
XLA Modules:
  0.0 220.5 jit_solution(3798640178679481975)
XLA Ops:
  0.0 6.7 %shard_map.100 = (bf16[256,2048]{1,0:T(8,128)(2,1)S(1)}, bf16[256,512]{1,0:T(8,128)(2,1)S(1)}, bf16[256,512]{1,0:T(8,128)(2,1)}, bf16[512,128]{1,0:T(8,128)(2,1)...) custom-call(s32[1]{0:T(128)} %bitcast.head_ref, bf16[256,2048]{1,0:T(8,128)(2,1)} %x_ref.1, ...), custom_call_target="tpu_custom_call" | custom-call | tf_op jit(solution)/shard_map/pallas_call | solution.py:430
  6.7 3.1 %collective-permute-start.9 = (bf16[2,2048,256]{2,1,0:T(8,128)(2,1)}, bf16[2,2048,256]{2,1,0:T(8,128)(2,1)}, u32[]{:S(2)}, u32[]{:S(2)}) collective-permute-start(bf16[2,2048,256]{2,1,0:T(8,128)(2,1)} %get-tuple-element.45), channel_id=1, source_target_pairs={{0,1},{1,4},{2,5},{3,0},{4,3},{5,6},{6,7},{7,2},{8,9},{9,12},{10,1... | collective-permute-start | bytes 6291464 | tf_op jit(solution)/shard_map/ppermute | solution.py:366
  15.3 14.3 %all_to_all.20.states_ref = bf16[32,16,128]{2,1,0:T(8,128)(2,1)S(1)} all-to-all(bf16[32,16,128]{2,1,0:T(8,128)(2,1)S(1)} %bitcast.21), channel_id=1, replica_groups=mesh['seq'=32,'head'=4] {'seq'}, dimensions={0} | all-to-all | bytes 262144 | tf_op jit(solution)/shard_map/all_to_all | solution.py:458
  30.3 5.0 %all-to-all-start.1 = ((bf16[32,16,128]{2,1,0:T(8,128)(2,1)}), bf16[32,16,128]{2,1,0:T(8,128)(2,1)S(1)}, u32[]{:S(2)}, u32[]{:S(2)}) async-start(bf16[32,16,128]{2,1,0:T(8,128)(2,1)} %shard_map.101), calls=%async_computation.1 | async-start | bytes 262144 | tf_op jit(solution)/shard_map/all_to_all | solution.py:460
  35.3 4.0 %shard_map.102 = (bf16[256,512]{1,0:T(8,128)(2,1)}, f32[256,512]{1,0:T(8,128)S(1)}) custom-call(bf16[256,2048]{1,0:T(8,128)(2,1)S(1)} %get-tuple-element.32.normed_ref, bf16[3,2048,512]{2,1,0:T(8,128)(2,1)} %bitcast.18, bf16[256,512]{1,0:T(8,128)(2,1)S(1)} %get-tuple-element.33.k_ref, bf16[256,512]{1,0:T(8,128)(2,1)} %get-tuple-element.34.v_ref), custom_call_target="tpu_custom_call" | custom-call | tf_op jit(solution)/shard_map/pallas_call | solution.py:471
  39.3 2.7 %all-to-all-done.1 = bf16[32,16,128]{2,1,0:T(8,128)(2,1)S(1)} async-done(((bf16[32,16,128]{2,1,0:T(8,128)(2,1)}), bf16[32,16,128]{2,1,0:T(8,128)(2,1)S(1)}, u32[]{:S(2)}, u32[]{:S(2)}) %all-to-all-start.1) | async-done | bytes 131104 | tf_op jit(solution)/shard_map/all_to_all | solution.py:460
  42.0 3.6 %shard_map.103 = (f32[64,2048]{1,0:T(8,128)S(1)}, bf16[64,2048]{1,0:T(8,128)(2,1)}, bf16[64,2048]{1,0:T(8,128)(2,1)}, bf16[64,2048]{1,0:T(8,128)(2,1)}) custom-call(s32[1]{0:T(128)} %bitcast.head_ref, bf16[512,128]{1,0:T(8,128)(2,1)S(1)} %bitcast.16, bf16[256,512]{1,0:T(8,128)(2,1)} %get-tuple-element.35.q_ref, f32[256,512]{1,0:T(8,128)S(1)} %get-tuple-element.36.local_ref, ...), custom_call_target="tpu_custom_call" | custom-call | tf_op jit(solution)/shard_map/pallas_call | solution.py:477
  49.5 17.2 %collective-permute-done.g1 = bf16[64,2048]{1,0:T(8,128)(2,1)S(1)} collective-permute-done((bf16[64,2048]{1,0:T(8,128)(2,1)}, bf16[64,2048]{1,0:T(8,128)(2,1)S(1)}, u32[]{:S(2)}, u32[]{:S(2)}) %collective-permute-start) | collective-permute-done | bytes 262176 | tf_op jit(solution)/shard_map/ppermute | solution.py:413
  68.3 10.8 %collective-permute-done.1.g2 = bf16[64,2048]{1,0:T(8,128)(2,1)S(1)} collective-permute-done((bf16[64,2048]{1,0:T(8,128)(2,1)}, bf16[64,2048]{1,0:T(8,128)(2,1)S(1)}, u32[]{:S(2)}, u32[]{:S(2)}) %collective-permute-start.1) | collective-permute-done | bytes 262176 | tf_op jit(solution)/shard_map/ppermute | solution.py:413
  81.9 8.9 %collective-permute-done.3.t1 = f32[64,16]{1,0:T(8,128)S(1)} collective-permute-done((f32[64,16]{1,0:T(8,128)S(1)}, f32[64,16]{1,0:T(8,128)S(1)}, u32[]{:S(2)}, u32[]{:S(2)}) %collective-permute-start.3) | collective-permute-done | bytes 4128 | tf_op jit(solution)/shard_map/ppermute | solution.py:413
  90.7 4.3 %collective-permute-done.4.t2 = f32[64,16]{1,0:T(8,128)S(1)} collective-permute-done((f32[64,16]{1,0:T(8,128)S(1)}, f32[64,16]{1,0:T(8,128)S(1)}, u32[]{:S(2)}, u32[]{:S(2)}) %collective-permute-start.4) | collective-permute-done | bytes 4128 | tf_op jit(solution)/shard_map/ppermute | solution.py:413
  101.7 2.8 %collective-permute-done.7.t2 = bf16[64,2048]{1,0:T(8,128)(2,1)S(1)} collective-permute-done((bf16[64,2048]{1,0:T(8,128)(2,1)S(1)}, bf16[64,2048]{1,0:T(8,128)(2,1)S(1)}, u32[]{:S(2)}, u32[]{:S(2)}) %collective-permute-start.7) | collective-permute-done | bytes 262176 | tf_op jit(solution)/shard_map/ppermute | solution.py:413
  104.5 5.5 %collective-permute-done.8.t3 = bf16[64,2048]{1,0:T(8,128)(2,1)S(1)} collective-permute-done((bf16[64,2048]{1,0:T(8,128)(2,1)S(1)}, bf16[64,2048]{1,0:T(8,128)(2,1)S(1)}, u32[]{:S(2)}, u32[]{:S(2)}) %collective-permute-start.8) | collective-permute-done | bytes 262176 | tf_op jit(solution)/shard_map/ppermute | solution.py:413
  112.3 10.4 %all-to-all-start.2 = ((bf16[32,16,2304]{2,1,0:T(8,128)(2,1)}), bf16[32,16,2304]{2,1,0:T(8,128)(2,1)S(1)}, u32[]{:S(2)}, u32[]{:S(2)}) async-start(bf16[32,16,2304]{2,1,0:T(8,128)(2,1)} %bitcast.19), calls=%async_computation.2 | async-start | bytes 4718592 | tf_op jit(solution)/shard_map/all_to_all | solution.py:498
  125.3 2.7 %collective-permute-start.10 = (bf16[2,2048,256]{2,1,0:T(8,128)(2,1)}, bf16[2,2048,256]{2,1,0:T(8,128)(2,1)}, u32[]{:S(2)}, u32[]{:S(2)}) collective-permute-start(bf16[2,2048,256]{2,1,0:T(8,128)(2,1)} %collective-permute-done.9.gu0), channel_id=1, source_target_pairs={{0,4},{4,0},{8,12},{12,8},{16,20},{20,16},{24,28},{28,24},{32,36},... | collective-permute-start | bytes 6291464 | tf_op jit(solution)/shard_map/ppermute | solution.py:366
  127.9 3.2 %collective-permute-start.13 = (bf16[2,2048,256]{2,1,0:T(8,128)(2,1)}, bf16[2,2048,256]{2,1,0:T(8,128)(2,1)}, u32[]{:S(2)}, u32[]{:S(2)}) collective-permute-start(bf16[2,2048,256]{2,1,0:T(8,128)(2,1)} %collective-permute-done.12.gu4), channel_id=1, source_target_pairs={{2,6},{3,7},{4,0},{5,1},{10,14},{11,15},{12,8},{13,9},{18,22},{19,... | collective-permute-start | bytes 6291464 | tf_op jit(solution)/shard_map/ppermute | solution.py:467
  131.2 3.6 %collective-permute-start.17 = (bf16[256,2048]{1,0:T(8,128)(2,1)S(1)}, bf16[256,2048]{1,0:T(8,128)(2,1)}, u32[]{:S(2)}, u32[]{:S(2)}) collective-permute-start(bf16[256,2048]{1,0:T(8,128)(2,1)S(1)} %get-tuple-element.48.dn2), channel_id=1, source_target_pairs={{2,4},{3,5},{4,2},{5,3},{10,12},{11,13},{12,10},{13,11},{18,20},{1... | collective-permute-start | bytes 3145736 | tf_op jit(solution)/shard_map/ppermute | solution.py:463
  135.0 13.9 %collective-permute-done.17.dn4 = bf16[256,2048]{1,0:T(8,128)(2,1)} collective-permute-done((bf16[256,2048]{1,0:T(8,128)(2,1)S(1)}, bf16[256,2048]{1,0:T(8,128)(2,1)}, u32[]{:S(2)}, u32[]{:S(2)}) %collective-permute-start.17) | collective-permute-done | bytes 1048608 | tf_op jit(solution)/shard_map/ppermute | solution.py:463
  151.9 7.2 %shard_map.107 = (bf16[576,1024]{1,0:T(8,128)(2,1)S(1)}, bf16[768,2048]{1,0:T(8,128)(2,1)S(1)}) custom-call(s32[1]{0:T(128)} %bitcast.8.keep_ref, bf16[512,2304]{1,0:T(8,128)(2,1)S(1)} %bitcast.15, bf16[2,2048,256]{2,1,0:T(8,128)(2,1)} %collective-permute-done.9.gu0, bf16[2,2048,256]{2,1,0:T(8,128)(2,1)} %collective-permute-done.10.gu1, ...), custom_call_target="tpu_custom_call" | custom-call | tf_op jit(solution)/shard_map/pallas_call | solution.py:502
  160.2 4.9 %shard_map.108 = bf16[512,2304]{1,0:T(8,128)(2,1)} custom-call(s32[1]{0:T(128)} %bitcast.8.keep_ref, bf16[576,1024]{1,0:T(8,128)(2,1)S(1)} %get-tuple-element.49.act, bf16[768,2048]{1,0:T(8,128)(2,1)S(1)} %get-tuple-element.50.down, bf16[256,2048]{1,0:T(8,128)(2,1)} %collective-permute-done.17.dn4, bf16[256,2048]{1,0:T(8,128)(2,1)} %copy-done.5), custom_call_target="tpu_custom_call" | custom-call | tf_op jit(solution)/shard_map/pallas_call | solution.py:512
  165.0 37.0 %all_to_all.21 = bf16[32,16,2304]{2,1,0:T(8,128)(2,1)S(1)} all-to-all(bf16[32,16,2304]{2,1,0:T(8,128)(2,1)} %bitcast.20), channel_id=1, replica_groups=mesh['seq'=32,'head'=4] {'seq'}, dimensions={0} | all-to-all | bytes 4718592 | tf_op jit(solution)/shard_map/all_to_all | solution.py:525
  204.7 2.7 %collective-permute-start.20 = (bf16[64,2048]{1,0:T(8,128)(2,1)}, bf16[64,2048]{1,0:T(8,128)(2,1)S(1)}, u32[]{:S(2)}, u32[]{:S(2)}) collective-permute-start(bf16[64,2048]{1,0:T(8,128)(2,1)} %get-tuple-element.53), channel_id=1, source_target_pairs={{0,2},{1,3},{2,0},{3,1},{4,6},{5,7},{6,4},{7,5},{8,10},{9,11},{10,... | collective-permute-start | bytes 786440 | tf_op jit(solution)/shard_map/ppermute | solution.py:413
  207.4 5.8 %collective-permute-done.19.g1 = bf16[64,2048]{1,0:T(8,128)(2,1)S(1)} collective-permute-done((bf16[64,2048]{1,0:T(8,128)(2,1)}, bf16[64,2048]{1,0:T(8,128)(2,1)S(1)}, u32[]{:S(2)}, u32[]{:S(2)}) %collective-permute-start.19) | collective-permute-done | bytes 262176 | tf_op jit(solution)/shard_map/ppermute | solution.py:413
  213.2 6.4 %collective-permute-done.20.g2 = bf16[64,2048]{1,0:T(8,128)(2,1)S(1)} collective-permute-done((bf16[64,2048]{1,0:T(8,128)(2,1)}, bf16[64,2048]{1,0:T(8,128)(2,1)S(1)}, u32[]{:S(2)}, u32[]{:S(2)}) %collective-permute-start.20) | collective-permute-done | bytes 262176 | tf_op jit(solution)/shard_map/ppermute | solution.py:413
  (60 shorter events, 32.3 us)
Async XLA Ops:
  6.7 118.6 %collective-permute-start.9 = (bf16[2,2048,256]{2,1,0:T(8,128)(2,1)}, bf16[2,2048,256]{2,1,0:T(8,128)(2,1)}, u32[]{:S(2)}, u32[]{:S(2)}) collective-permute-start(bf16[2,2048,256]{2,1,0:T(8,128)(2,1)} %get-tuple-element.45), channel_id=1, source_target_pairs={{0,1},{1,4},{2,5},{3,0},{4,3},{5,6},{6,7},{7,2},{8,9},{9,12},{10,1... | collective-permute-start | bytes 6291464 | tf_op jit(solution)/shard_map/ppermute | solution.py:366
  13.1 114.8 %collective-permute-start.12 = (bf16[2,2048,256]{2,1,0:T(8,128)(2,1)}, bf16[2,2048,256]{2,1,0:T(8,128)(2,1)}, u32[]{:S(2)}, u32[]{:S(2)}) collective-permute-start(bf16[2,2048,256]{2,1,0:T(8,128)(2,1)} %get-tuple-element.46.gu2), channel_id=1, source_target_pairs={{2,4},{3,5},{4,2},{5,3},{10,12},{11,13},{12,10},{13,11},{18,20},{1... | collective-permute-start | bytes 6291464 | tf_op jit(solution)/shard_map/ppermute | solution.py:464
  30.3 11.7 %all-to-all-start.1 = ((bf16[32,16,128]{2,1,0:T(8,128)(2,1)}), bf16[32,16,128]{2,1,0:T(8,128)(2,1)S(1)}, u32[]{:S(2)}, u32[]{:S(2)}) async-start(bf16[32,16,128]{2,1,0:T(8,128)(2,1)} %shard_map.101), calls=%async_computation.1 | async-start | bytes 262144 | tf_op jit(solution)/shard_map/all_to_all | solution.py:460
  45.6 21.0 %collective-permute-start = (bf16[64,2048]{1,0:T(8,128)(2,1)}, bf16[64,2048]{1,0:T(8,128)(2,1)S(1)}, u32[]{:S(2)}, u32[]{:S(2)}) collective-permute-start(bf16[64,2048]{1,0:T(8,128)(2,1)} %get-tuple-element.38), channel_id=1, source_target_pairs={{0,1},{1,2},{2,3},{3,0},{4,5},{5,6},{6,7},{7,4},{8,9},{9,10},{10,1... | collective-permute-start | bytes 786440 | tf_op jit(solution)/shard_map/ppermute | solution.py:413
  46.4 84.8 %collective-permute-start.14 = (bf16[256,2048]{1,0:T(8,128)(2,1)}, bf16[256,2048]{1,0:T(8,128)(2,1)}, u32[]{:S(2)}, u32[]{:S(2)}) collective-permute-start(bf16[256,2048]{1,0:T(8,128)(2,1)} %get-tuple-element.47), channel_id=1, source_target_pairs={{0,1},{1,4},{2,5},{3,0},{4,3},{5,6},{6,7},{7,2},{8,9},{9,12},{10,1... | collective-permute-start | bytes 3145736 | tf_op jit(solution)/shard_map/ppermute | solution.py:366
  48.9 30.3 %collective-permute-start.1 = (bf16[64,2048]{1,0:T(8,128)(2,1)}, bf16[64,2048]{1,0:T(8,128)(2,1)S(1)}, u32[]{:S(2)}, u32[]{:S(2)}) collective-permute-start(bf16[64,2048]{1,0:T(8,128)(2,1)} %get-tuple-element.39), channel_id=1, source_target_pairs={{0,2},{1,3},{2,0},{3,1},{4,6},{5,7},{6,4},{7,5},{8,10},{9,11},{10,... | collective-permute-start | bytes 786440 | tf_op jit(solution)/shard_map/ppermute | solution.py:413
  66.6 12.5 %collective-permute-start.2 = (bf16[64,2048]{1,0:T(8,128)(2,1)}, bf16[64,2048]{1,0:T(8,128)(2,1)S(1)}, u32[]{:S(2)}, u32[]{:S(2)}) collective-permute-start(bf16[64,2048]{1,0:T(8,128)(2,1)} %get-tuple-element.40), channel_id=1, source_target_pairs={{0,3},{1,0},{2,1},{3,2},{4,7},{5,4},{6,5},{7,6},{8,11},{9,8},{10,9... | collective-permute-start | bytes 786440 | tf_op jit(solution)/shard_map/ppermute | solution.py:413
  80.8 17.0 %collective-permute-start.6 = (bf16[64,2048]{1,0:T(8,128)(2,1)S(1)}, bf16[64,2048]{1,0:T(8,128)(2,1)S(1)}, u32[]{:S(2)}, u32[]{:S(2)}) collective-permute-start(bf16[64,2048]{1,0:T(8,128)(2,1)S(1)} %get-tuple-element.44.t0), channel_id=1, source_target_pairs={{0,1},{1,2},{2,3},{3,0},{4,5},{5,6},{6,7},{7,4},{8,9},{9,10},{10,1... | collective-permute-start | bytes 786440 | tf_op jit(solution)/shard_map/ppermute | solution.py:413
  81.6 9.1 %collective-permute-start.3 = (f32[64,16]{1,0:T(8,128)S(1)}, f32[64,16]{1,0:T(8,128)S(1)}, u32[]{:S(2)}, u32[]{:S(2)}) collective-permute-start(f32[64,16]{1,0:T(8,128)S(1)} %copy.16.t0), channel_id=1, source_target_pairs={{0,1},{1,2},{2,3},{3,0},{4,5},{5,6},{6,7},{7,4},{8,9},{9,10},{10,1... | collective-permute-start | bytes 12296 | tf_op jit(solution)/shard_map/ppermute | solution.py:413
  90.7 4.3 %collective-permute-start.4 = (f32[64,16]{1,0:T(8,128)S(1)}, f32[64,16]{1,0:T(8,128)S(1)}, u32[]{:S(2)}, u32[]{:S(2)}) collective-permute-start(f32[64,16]{1,0:T(8,128)S(1)} %copy.16.t0), channel_id=1, source_target_pairs={{0,2},{1,3},{2,0},{3,1},{4,6},{5,7},{6,4},{7,5},{8,10},{9,11},{10,... | collective-permute-start | bytes 12296 | tf_op jit(solution)/shard_map/ppermute | solution.py:413
  95.0 2.8 %collective-permute-start.5 = (f32[64,16]{1,0:T(8,128)S(1)}, f32[64,16]{1,0:T(8,128)S(1)}, u32[]{:S(2)}, u32[]{:S(2)}) collective-permute-start(f32[64,16]{1,0:T(8,128)S(1)} %copy.16.t0), channel_id=1, source_target_pairs={{0,3},{1,0},{2,1},{3,2},{4,7},{5,4},{6,5},{7,6},{8,11},{9,8},{10,9... | collective-permute-start | bytes 12296 | tf_op jit(solution)/shard_map/ppermute | solution.py:413
  97.8 6.7 %collective-permute-start.7 = (bf16[64,2048]{1,0:T(8,128)(2,1)S(1)}, bf16[64,2048]{1,0:T(8,128)(2,1)S(1)}, u32[]{:S(2)}, u32[]{:S(2)}) collective-permute-start(bf16[64,2048]{1,0:T(8,128)(2,1)S(1)} %get-tuple-element.44.t0), channel_id=1, source_target_pairs={{0,2},{1,3},{2,0},{3,1},{4,6},{5,7},{6,4},{7,5},{8,10},{9,11},{10,... | collective-permute-start | bytes 786440 | tf_op jit(solution)/shard_map/ppermute | solution.py:413
  97.8 12.3 %collective-permute-start.8 = (bf16[64,2048]{1,0:T(8,128)(2,1)S(1)}, bf16[64,2048]{1,0:T(8,128)(2,1)S(1)}, u32[]{:S(2)}, u32[]{:S(2)}) collective-permute-start(bf16[64,2048]{1,0:T(8,128)(2,1)S(1)} %get-tuple-element.44.t0), channel_id=1, source_target_pairs={{0,3},{1,0},{2,1},{3,2},{4,7},{5,4},{6,5},{7,6},{8,11},{9,8},{10,9... | collective-permute-start | bytes 786440 | tf_op jit(solution)/shard_map/ppermute | solution.py:413
  112.3 39.7 %all-to-all-start.2 = ((bf16[32,16,2304]{2,1,0:T(8,128)(2,1)}), bf16[32,16,2304]{2,1,0:T(8,128)(2,1)S(1)}, u32[]{:S(2)}, u32[]{:S(2)}) async-start(bf16[32,16,2304]{2,1,0:T(8,128)(2,1)} %bitcast.19), calls=%async_computation.2 | async-start | bytes 4718592 | tf_op jit(solution)/shard_map/all_to_all | solution.py:498
  122.7 27.8 %collective-permute-start.11 = (bf16[2,2048,256]{2,1,0:T(8,128)(2,1)}, bf16[2,2048,256]{2,1,0:T(8,128)(2,1)}, u32[]{:S(2)}, u32[]{:S(2)}) collective-permute-start(bf16[2,2048,256]{2,1,0:T(8,128)(2,1)} %get-tuple-element.46.gu2), channel_id=1, source_target_pairs={{0,4},{1,5},{6,2},{7,3},{8,12},{9,13},{14,10},{15,11},{16,20},{17,... | collective-permute-start | bytes 6291464 | tf_op jit(solution)/shard_map/ppermute | solution.py:366
  124.0 10.9 %collective-permute-start.16 = (bf16[256,2048]{1,0:T(8,128)(2,1)S(1)}, bf16[256,2048]{1,0:T(8,128)(2,1)S(1)}, u32[]{:S(2)}, u32[]{:S(2)}) collective-permute-start(bf16[256,2048]{1,0:T(8,128)(2,1)S(1)} %get-tuple-element.48.dn2), channel_id=1, source_target_pairs={{0,4},{1,5},{6,2},{7,3},{8,12},{9,13},{14,10},{15,11},{16,20},{17,... | collective-permute-start | bytes 3145736 | tf_op jit(solution)/shard_map/ppermute | solution.py:366
  125.3 26.6 %collective-permute-start.10 = (bf16[2,2048,256]{2,1,0:T(8,128)(2,1)}, bf16[2,2048,256]{2,1,0:T(8,128)(2,1)}, u32[]{:S(2)}, u32[]{:S(2)}) collective-permute-start(bf16[2,2048,256]{2,1,0:T(8,128)(2,1)} %collective-permute-done.9.gu0), channel_id=1, source_target_pairs={{0,4},{4,0},{8,12},{12,8},{16,20},{20,16},{24,28},{28,24},{32,36},... | collective-permute-start | bytes 6291464 | tf_op jit(solution)/shard_map/ppermute | solution.py:366
  127.9 24.0 %collective-permute-start.13 = (bf16[2,2048,256]{2,1,0:T(8,128)(2,1)}, bf16[2,2048,256]{2,1,0:T(8,128)(2,1)}, u32[]{:S(2)}, u32[]{:S(2)}) collective-permute-start(bf16[2,2048,256]{2,1,0:T(8,128)(2,1)} %collective-permute-done.12.gu4), channel_id=1, source_target_pairs={{2,6},{3,7},{4,0},{5,1},{10,14},{11,15},{12,8},{13,9},{18,22},{19,... | collective-permute-start | bytes 6291464 | tf_op jit(solution)/shard_map/ppermute | solution.py:467
  131.2 17.7 %collective-permute-start.17 = (bf16[256,2048]{1,0:T(8,128)(2,1)S(1)}, bf16[256,2048]{1,0:T(8,128)(2,1)}, u32[]{:S(2)}, u32[]{:S(2)}) collective-permute-start(bf16[256,2048]{1,0:T(8,128)(2,1)S(1)} %get-tuple-element.48.dn2), channel_id=1, source_target_pairs={{2,4},{3,5},{4,2},{5,3},{10,12},{11,13},{12,10},{13,11},{18,20},{1... | collective-permute-start | bytes 3145736 | tf_op jit(solution)/shard_map/ppermute | solution.py:463
  134.9 15.6 %collective-permute-start.15 = (bf16[256,2048]{1,0:T(8,128)(2,1)}, bf16[256,2048]{1,0:T(8,128)(2,1)}, u32[]{:S(2)}, u32[]{:S(2)}) collective-permute-start(bf16[256,2048]{1,0:T(8,128)(2,1)} %collective-permute-done.14.dn0), channel_id=1, source_target_pairs={{0,4},{4,0},{8,12},{12,8},{16,20},{20,16},{24,28},{28,24},{32,36},... | collective-permute-start | bytes 3145736 | tf_op jit(solution)/shard_map/ppermute | solution.py:366
  148.9 10.3 %collective-permute-start.18 = (bf16[256,2048]{1,0:T(8,128)(2,1)}, bf16[256,2048]{1,0:T(8,128)(2,1)S(1)}, u32[]{:S(2)}, u32[]{:S(2)}) collective-permute-start(bf16[256,2048]{1,0:T(8,128)(2,1)} %collective-permute-done.17.dn4), channel_id=1, source_target_pairs={{2,6},{3,7},{4,0},{5,1},{10,14},{11,15},{12,8},{13,9},{18,22},{19,... | collective-permute-start | bytes 3145736 | tf_op jit(solution)/shard_map/ppermute | solution.py:468
  203.9 9.3 %collective-permute-start.19 = (bf16[64,2048]{1,0:T(8,128)(2,1)}, bf16[64,2048]{1,0:T(8,128)(2,1)S(1)}, u32[]{:S(2)}, u32[]{:S(2)}) collective-permute-start(bf16[64,2048]{1,0:T(8,128)(2,1)} %get-tuple-element.52), channel_id=1, source_target_pairs={{0,1},{1,2},{2,3},{3,0},{4,5},{5,6},{6,7},{7,4},{8,9},{9,10},{10,1... | collective-permute-start | bytes 786440 | tf_op jit(solution)/shard_map/ppermute | solution.py:413
  204.7 15.0 %collective-permute-start.20 = (bf16[64,2048]{1,0:T(8,128)(2,1)}, bf16[64,2048]{1,0:T(8,128)(2,1)S(1)}, u32[]{:S(2)}, u32[]{:S(2)}) collective-permute-start(bf16[64,2048]{1,0:T(8,128)(2,1)} %get-tuple-element.53), channel_id=1, source_target_pairs={{0,2},{1,3},{2,0},{3,1},{4,6},{5,7},{6,4},{7,5},{8,10},{9,11},{10,... | collective-permute-start | bytes 786440 | tf_op jit(solution)/shard_map/ppermute | solution.py:413
  207.4 12.3 %collective-permute-start.21 = (bf16[64,2048]{1,0:T(8,128)(2,1)}, bf16[64,2048]{1,0:T(8,128)(2,1)S(1)}, u32[]{:S(2)}, u32[]{:S(2)}) collective-permute-start(bf16[64,2048]{1,0:T(8,128)(2,1)} %get-tuple-element.54), channel_id=1, source_target_pairs={{0,3},{1,0},{2,1},{3,2},{4,7},{5,4},{6,5},{7,6},{8,11},{9,8},{10,9... | collective-permute-start | bytes 786440 | tf_op jit(solution)/shard_map/ppermute | solution.py:413
  (9 other events, 272.5 us)
